TPU v7x, 32 devices: a whole 2x2x4 slice. The times are simulated.
32 devices in a mesh: seq: 8 (over z, y), head: 4 (over x, core).
Axes of the slice: x: 2, y: 2, z: 4, core: 2. Of those that a mesh axis runs over, the one named last changes fastest.
Arguments:
- queries: bfloat16 [4096, 4096], P('seq', 'head'), may hold values from -6 to 6
- keys: bfloat16 [4096, 4096], P('seq', 'head'), may hold values from -6 to 6
- values: bfloat16 [4096, 4096], P('seq', 'head'), may hold values from -6 to 6
- level_weights: float32 [5, 32, 4096], P(None, 'head', 'seq'), may hold values from 0.1 to 3, as said below
- norm_gain: float32 [4096], P('head'), may hold values from 0.25 to 1.75
Outputs:
- mixed: bfloat16 [4096, 4096], P('seq', 'head')
Inputs may be any that keep to these rules, and one draw needn't show every extreme that they name: `level_weights`: positive level weights.
All inputs are finite; a program needn't handle non-finite values.
Results may differ from a plain program's by a relative error of at most 0.0049.
Values may be sent and summed in bfloat16 or wider, within the bound.
No kernel may reach another device: no remote copies, remote signals or barrier semaphores. Data moves between devices by JAX's collectives and lax.ppermute only.
A program may use at most 64 MiB of HBM per device.

v0:
```python
import jax
import jax.numpy as jnp
from jax import lax
from jax.sharding import PartitionSpec as P

HEAD_DIM = 128
STRETCH = 256
D = 4096


EPSILON = 1e-06


def swapped(block, axis, stride):
    count = lax.axis_size(axis)
    route = []
    for low in range(count):
        high = low | 1 << stride
        if high != low and high < count:
            route += [(low, high), (high, low)]
    return lax.ppermute(block, axis, route)


def shifted(block, axis, distance):
    devices = range(lax.axis_size(axis))
    route = [(i - distance, i) for i in devices if i - distance in devices]
    return lax.ppermute(block, axis, route)


def local(queries, keys, values, level_weights, norm_gain):
    tok_rows = queries.shape[0]
    heads_here = queries.shape[1] // HEAD_DIM
    stretch_count = tok_rows // STRETCH
    block_shape = (stretch_count, STRETCH, heads_here, HEAD_DIM)
    query_block_list = queries.reshape(block_shape)
    key_blocks = keys.reshape(block_shape)
    value_blocks = values.reshape(block_shape)
    level_total = level_weights.shape[0]
    weights_here = level_weights.reshape(level_total, heads_here, stretch_count, STRETCH).transpose(
        0, 2, 3, 1
    )
    states = jnp.einsum(
        "cthk,cthv->chkv", key_blocks, value_blocks, preferred_element_type=jnp.float32
    )
    scores = jnp.einsum(
        "cthk,cshk->chts", query_block_list, key_blocks, preferred_element_type=jnp.float32
    )
    causal = lax.broadcasted_iota(jnp.int32, (STRETCH, STRETCH), 0) >= lax.broadcasted_iota(
        jnp.int32, (STRETCH, STRETCH), 1
    )
    attn_probs = jnp.where(causal[None, None], scores, 0.0).astype(jnp.bfloat16)
    intra_out = jnp.einsum(
        "chts,cshv->cthv", attn_probs, value_blocks, preferred_element_type=jnp.float32
    )
    combined = weights_here[0][..., None] * intra_out
    running = states
    local_bits = stretch_count.bit_length() - 1
    level_bit = 0
    groups = running.shape[0] // 2
    block_span = 2**level_bit
    halves = running.reshape(groups, 2, heads_here, HEAD_DIM, HEAD_DIM)
    leftward_sum = halves[:, 0].astype(jnp.bfloat16)
    rightward_queries = query_block_list.reshape(
        groups, 2, block_span * STRETCH, heads_here, HEAD_DIM
    )[:, 1]
    state_readout = jnp.einsum(
        "nthk,nhkv->nthv", rightward_queries, leftward_sum, preferred_element_type=jnp.float32
    )
    level_weight = weights_here[1 + level_bit].reshape(groups, 2, block_span * STRETCH, heads_here)[
        :, 1
    ]
    contrib = level_weight[..., None] * state_readout
    padded = jnp.stack([jnp.zeros_like(contrib), contrib], axis=1)
    combined = combined + padded.reshape(stretch_count, STRETCH, heads_here, HEAD_DIM)
    running = halves[:, 0] + halves[:, 1]
    device_sum = running[0]
    seq_count = lax.axis_size("seq")
    seq_bits = seq_count.bit_length() - 1
    position = lax.axis_index("seq")
    crossing_state_list = []
    for level_bit in range(seq_bits - 1):
        partner = swapped(device_sum, "seq", level_bit)
        is_right = position >> level_bit & 1 == 1
        crossing_state_list.append(
            jnp.where(is_right, partner, jnp.zeros_like(partner)).astype(jnp.bfloat16)
        )
        device_sum = device_sum + partner
    last_partner = shifted(device_sum.astype(jnp.bfloat16), "seq", seq_count // 2)
    crossing_state_list.append(last_partner)
    for number, state_per_level in enumerate(crossing_state_list):
        state_readout = jnp.einsum(
            "lwnx,nxq->lwnq", query_block_list, state_per_level, preferred_element_type=jnp.float32
        )
        combined = combined + weights_here[1 + local_bits + number][..., None] * state_readout
    squares = jnp.sum(combined * combined, axis=(2, 3)).reshape(tok_rows)
    total_squares = lax.psum(squares, "head")
    inverse_rms = lax.rsqrt(total_squares / D + EPSILON)
    flat_out = combined.reshape(tok_rows, heads_here * HEAD_DIM)
    mixed_out = flat_out * inverse_rms[:, None] * norm_gain[None, :]
    return mixed_out.astype(jnp.bfloat16)


def solution(mesh):
    return jax.shard_map(
        local,
        mesh=mesh,
        in_specs=(
            P("seq", "head"),
            P("seq", "head"),
            P("seq", "head"),
            P(None, "head", "seq"),
            P("head"),
        ),
        out_specs=P("seq", "head"),
        check_vma=False,
    )
```

profile of v0, /device:TPU:24, one launch (start us, length us, event | category | flops | bytes accessed | tf_op | source)
XLA Modules:
  0.0 59.7 jit_solution(3533077832521115567)
XLA Ops:
  0.0 0.0 copy-start.3
  0.0 1.6 %copy.53 = bf16[64,8,8,128]{3,2,1,0:T(8,128)(2,1)S(1)} copy(bf16[64,8,8,128]{3,1,2,0:T(8,128)(2,1)} %bitcast.103) | data formatting | bytes 2097152
  1.6 0.7 %copy.20 = bf16[2,256,8,128]{1,3,2,0:T(8,128)(2,1)S(1)} copy(bf16[2,256,8,128]{3,2,1,0:T(8,128)(2,1)S(1)} %bitcast.102) | data formatting | bytes 2097152 | tf_op jit(solution)/shard_map/reshape | solution.py:36
  2.3 0.0 copy-start
  2.3 0.0 copy-done.3
  2.3 0.3 copy.54
  2.6 0.0 copy-start.1
  2.6 0.0 copy-start.5
  2.6 0.0 copy-start.4
  2.6 0.4 convolution_bitcast_fusion.1
  3.0 0.2 copy-done
  3.2 0.8 %fusion.17 = f32[8,128,128]{2,1,0:T(8,128)} fusion(f32[1,2,8,128,128]{4,3,2,1,0:T(8,128)S(1)} %convolution_bitcast_fusion.1), kind=kLoop, calls=%fused_computation.27 | loop fusion | flops 131072 | bytes 1572864 | tf_op jit(solution)/shard_map/add | solution.py:75
  4.1 0.0 copy-done.1
  4.1 1.5 %collective-permute-start = (f32[8,128,128]{2,1,0:T(8,128)}, f32[8,128,128]{2,1,0:T(8,128)}, u32[]{:S(2)}, u32[]{:S(2)}) collective-permute-start(f32[8,128,128]{2,1,0:T(8,128)} %fusion.17), channel_id=1, source_target_pairs={{0,4},{4,0},{8,12},{12,8},{16,20},{20,16},{24,28},{28,24},{1,5},{5... | collective-permute-start | bytes 1572872 | tf_op jit(solution)/shard_map/ppermute | solution.py:21
  5.7 0.0 copy-done.5
  5.7 0.0 copy-done.4
  5.7 0.3 copy.52
  6.0 0.3 fusion.7
  6.4 4.2 %fusion.5 = f32[2,8,256,128]{2,3,1,0:T(8,128)} fusion(bf16[2,256,8,128]{1,3,2,0:T(8,128)(2,1)} %copy-done, pred[256,256]{1,0:T(8,128)(4,1)S(1)} %iota_compare_fusion, bf16[2,256,8,128]{3,2,1,0:T(8,128)(2,1)} %bitcast.101, bf16[2,256,8,128]{3,2,1,0:T(8,128)(2,1)S(1)} %bitcast.95), kind=kOutput, calls=%fused_computation.13 | convolution fusion | flops 538968064 | bytes 5308416 | tf_op jit(solution)/shard_map/chts,cshv->cthv/dot_general | solution.py:52
  10.6 7.5 %collective-permute-done = f32[8,128,128]{2,1,0:T(8,128)} collective-permute-done((f32[8,128,128]{2,1,0:T(8,128)}, f32[8,128,128]{2,1,0:T(8,128)}, u32[]{:S(2)}, u32[]{:S(2)}) %collective-permute-start) | collective-permute-done | bytes 524320 | tf_op jit(solution)/shard_map/ppermute | solution.py:21
  18.1 1.1 %fusion.34 = f32[8,128,128]{2,1,0:T(8,128)S(1)} fusion(f32[8,128,128]{2,1,0:T(8,128)} %collective-permute-done, f32[1,2,8,128,128]{4,3,2,1,0:T(8,128)S(1)} %convolution_bitcast_fusion.1), kind=kLoop, calls=%fused_computation.51 | loop fusion | flops 262144 | bytes 2097152 | tf_op jit(solution)/shard_map/add | solution.py:87
  19.2 0.5 collective-permute-start.1
  19.7 0.5 fusion.13
  20.2 11.8 %collective-permute-done.1 = f32[8,128,128]{2,1,0:T(8,128)S(1)} collective-permute-done((f32[8,128,128]{2,1,0:T(8,128)S(1)}, f32[8,128,128]{2,1,0:T(8,128)S(1)}, u32[]{:S(2)}, u32[]{:S(2)}) %collective-permute-start.1) | collective-permute-done | bytes 524320 | tf_op jit(solution)/shard_map/ppermute | solution.py:21
  32.1 0.1 add_convert_fusion
  32.1 0.0 copy-start.2
  32.1 1.4 %collective-permute-start.2 = (bf16[8,128,128]{2,1,0:T(8,128)(2,1)S(1)}, bf16[8,128,128]{2,1,0:T(8,128)(2,1)S(1)}, u32[]{:S(2)}, u32[]{:S(2)}) collective-permute-start(bf16[8,128,128]{2,1,0:T(8,128)(2,1)S(1)} %add_convert_fusion), channel_id=1, source_target_pairs={{0,16},{4,20},{8,24},{12,28},{1,17},{5,21},{9,25},{13,29},{2,18},{... | collective-permute-start | bytes 786440 | tf_op jit(solution)/shard_map/ppermute | solution.py:27
  33.6 0.5 fusion.11
  34.1 12.8 %collective-permute-done.2 = bf16[8,128,128]{2,1,0:T(8,128)(2,1)S(1)} collective-permute-done((bf16[8,128,128]{2,1,0:T(8,128)(2,1)S(1)}, bf16[8,128,128]{2,1,0:T(8,128)(2,1)S(1)}, u32[]{:S(2)}, u32[]{:S(2)}) %collective-permute-start.2) | collective-permute-done | bytes 262176 | tf_op jit(solution)/shard_map/ppermute | solution.py:27
  46.9 0.0 copy-done.2
  46.9 2.4 %multiply_reduce_fusion = (f32[2,256]{1,0:T(2,128)S(1)}, f32[2,256,8,128]{1,3,2,0:T(8,128)}) fusion(bf16[2,256,8,128]{3,2,1,0:T(8,128)(2,1)S(1)} %bitcast.98, bf16[8,128,128]{2,1,0:T(8,128)(2,1)S(1)} %collective-permute-done.2, f32[2,256,8]{1,2,0:T(8,128)S(1)} %get-tuple-element.6, f32[8,128,2,256]{3,1,0,2:T(8,128)S(1)} %fusion.11, ...), kind=kOutput, calls=%fused_computation.12 | convolution fusion | flops 139460096 | bytes 10815488 | tf_op jit(solution)/shard_map/lwnx,nxq->lwnq/dot_general | solution.py:91
  49.3 6.8 %psum.7 = f32[512]{0:T(512)S(1)} all-reduce(f32[512]{0:T(512)S(1)} %bitcast.109), channel_id=1, replica_groups=mesh['seq'=8,'head'=4] {'head'}, use_global_device_ids=true, to_apply=%region_1.2 | all-reduce | flops 512 | bytes 4096 | tf_op jit(solution)/shard_map/psum | solution.py:96
  56.1 0.0 copy-start.6
  56.1 2.1 %copy.33 = f32[2,256,8,128]{3,2,1,0:T(8,128)S(1)} copy(f32[2,256,8,128]{1,3,2,0:T(8,128)} %get-tuple-element.10) | data formatting | bytes 4194304 | tf_op jit(solution)/shard_map/add | solution.py:94
  58.3 0.0 copy-done.6
  58.3 1.4 %fusion.1 = bf16[512,1024]{1,0:T(8,128)(2,1)} fusion(f32[64,8,8,128]{3,2,1,0:T(8,128)S(1)} %bitcast.99, f32[1024]{0:T(1024)S(1)} %copy-done.6, f32[512]{0:T(512)S(1)} %add_rsqrt_fusion), kind=kLoop, calls=%fused_computation.3 | loop fusion | flops 1572864 | bytes 3151872 | tf_op jit(solution)/shard_map/convert_element_type | solution.py:100
  (6 shorter events, 0.1 us)
Async XLA Ops:
  0.0 2.3 %copy-start.3 = (bf16[512,1024]{1,0:T(8,128)(2,1)S(1)}, bf16[512,1024]{1,0:T(8,128)(2,1)}, u32[]{:S(2)}) copy-start(bf16[512,1024]{1,0:T(8,128)(2,1)} %param.7) | copy-start | bytes 3145732
  2.3 1.0 %copy-start = (bf16[2,256,8,128]{1,3,2,0:T(8,128)(2,1)}, bf16[2,256,8,128]{1,3,2,0:T(8,128)(2,1)S(1)}, u32[]{:S(2)}) copy-start(bf16[2,256,8,128]{1,3,2,0:T(8,128)(2,1)S(1)} %copy.20) | copy-start | bytes 3145732
  2.6 1.5 %copy-start.1 = (bf16[64,8,8,128]{3,2,1,0:T(8,128)(2,1)}, bf16[64,8,8,128]{3,2,1,0:T(8,128)(2,1)S(1)}, u32[]{:S(2)}) copy-start(bf16[64,8,8,128]{3,2,1,0:T(8,128)(2,1)S(1)} %copy.54) | copy-start | bytes 3145732
  2.6 3.1 %copy-start.5 = (f32[5,8,512]{2,1,0:T(8,128)S(1)}, f32[5,8,512]{2,1,0:T(8,128)}, u32[]{:S(2)}) copy-start(f32[5,8,512]{2,1,0:T(8,128)} %param.8) | copy-start | bytes 245764
  2.6 3.1 %copy-start.4 = (bf16[512,1024]{1,0:T(8,128)(2,1)S(1)}, bf16[512,1024]{1,0:T(8,128)(2,1)}, u32[]{:S(2)}) copy-start(bf16[512,1024]{1,0:T(8,128)(2,1)} %param.5) | copy-start | bytes 3145732
  4.1 14.0 %collective-permute-start = (f32[8,128,128]{2,1,0:T(8,128)}, f32[8,128,128]{2,1,0:T(8,128)}, u32[]{:S(2)}, u32[]{:S(2)}) collective-permute-start(f32[8,128,128]{2,1,0:T(8,128)} %fusion.17), channel_id=1, source_target_pairs={{0,4},{4,0},{8,12},{12,8},{16,20},{20,16},{24,28},{28,24},{1,5},{5... | collective-permute-start | bytes 1572872 | tf_op jit(solution)/shard_map/ppermute | solution.py:21
  19.2 12.9 %collective-permute-start.1 = (f32[8,128,128]{2,1,0:T(8,128)S(1)}, f32[8,128,128]{2,1,0:T(8,128)S(1)}, u32[]{:S(2)}, u32[]{:S(2)}) collective-permute-start(f32[8,128,128]{2,1,0:T(8,128)S(1)} %fusion.34), channel_id=1, source_target_pairs={{0,8},{8,0},{4,12},{12,4},{16,24},{24,16},{20,28},{28,20},{1,9},{9... | collective-permute-start | bytes 1572872 | tf_op jit(solution)/shard_map/ppermute | solution.py:21
  32.1 14.8 %copy-start.2 = (f32[2,8,256,128]{2,3,1,0:T(8,128)S(1)}, f32[2,8,256,128]{2,3,1,0:T(8,128)}, u32[]{:S(2)}) copy-start(f32[2,8,256,128]{2,3,1,0:T(8,128)} %fusion.5) | copy-start | bytes 6291460
  32.1 14.8 %collective-permute-start.2 = (bf16[8,128,128]{2,1,0:T(8,128)(2,1)S(1)}, bf16[8,128,128]{2,1,0:T(8,128)(2,1)S(1)}, u32[]{:S(2)}, u32[]{:S(2)}) collective-permute-start(bf16[8,128,128]{2,1,0:T(8,128)(2,1)S(1)} %add_convert_fusion), channel_id=1, source_target_pairs={{0,16},{4,20},{8,24},{12,28},{1,17},{5,21},{9,25},{13,29},{2,18},{... | collective-permute-start | bytes 786440 | tf_op jit(solution)/shard_map/ppermute | solution.py:27
  56.1 2.1 %copy-start.6 = (f32[1024]{0:T(1024)S(1)}, f32[1024]{0:T(1024)}, u32[]{:S(2)}) copy-start(f32[1024]{0:T(1024)} %param.9) | copy-start | bytes 12292
where the time goes:
time: 60 us; the launch traced here: 59.7 us
  waiting for transfers between devices  32.2 us (54%)
  matrix products  8.38 us (14%)
  blocking collectives  6.83 us (11%)
  local copies, waits for them, and re-layouts  5.2 us (9%)
  starting transfers between devices  3.46 us (6%)
  other arithmetic  3.45 us (6%)
    ppermute x2, waiting for transfers between devices, swapped(): return lax.ppermute(block, axis, route)  19.3 us
    ppermute x1, waiting for transfers between devices, shifted(): return lax.ppermute(block, axis, route)  12.8 us
    psum x1, blocking collectives, local(): total_squares = lax.psum(squares, 'head')  6.83 us
    dot_general x1, matrix products, local(): jnp.einsum('chts,cshv->cthv', attn_probs, value_blocks, preferred_element...  4.22 us
    dot_general x3, matrix products, local(): jnp.einsum('lwnx,nxq->lwnq', query_block_list, state_per_level, preferred...  3.39 us
    unnamed x18, local copies, waits for them, and re-layouts  2.36 us
    add x1, local copies, waits for them, and re-layouts, local(): combined + weights_here[1 + local_bits + number][..., None] * state_readout  2.12 us
    ppermute x2, starting transfers between devices, swapped(): return lax.ppermute(block, axis, route)  2.03 us
  transfers between devices with their start and end apart: 3, of which 3 were waited for; matrix products, arithmetic and copies ran while one was open for 10% of the time, Pallas kernels for 0%

commit v1 on v0

v1 whole, which is shorter than its diff:
```python
import functools

import jax
import jax.numpy as jnp
from jax import lax
from jax.experimental import pallas as pl
from jax.experimental.pallas import tpu as pltpu
from jax.sharding import PartitionSpec as P

HEAD_DIM = 128
STRETCH = 256
EPSILON = 1e-06
QUAD = 4
F32 = jnp.float32
BF16 = jnp.bfloat16
VMEM = pl.BlockSpec(memory_space=pltpu.VMEM)
SMEM = pl.BlockSpec(memory_space=pltpu.SMEM)
ANY = pl.BlockSpec(memory_space=pl.ANY)
GRANT = 24 << 20


def params():
    return pltpu.CompilerParams(vmem_limit_bytes=GRANT)


def cost(flops, moved):
    return pl.CostEstimate(flops=flops, bytes_accessed=moved, transcendentals=0)


def exchanged(block, axis, mask):
    count = lax.axis_size(axis)
    return lax.ppermute(block, axis, [(i, i ^ mask) for i in range(count)])


def nn(a, b):
    return jnp.dot(a, b, preferred_element_type=F32)


def nt(a, b):
    return lax.dot_general(a, b, (((1,), (1,)), ((), ())), preferred_element_type=F32)


def tn(a, b):
    return lax.dot_general(a, b, (((0,), (0,)), ((), ())), preferred_element_type=F32)


def column(head):
    return pl.ds(head * HEAD_DIM, HEAD_DIM)


def states_kernel(group, place_ref, k_hbm, v_hbm, own_ref, one_ref, two_ref, three_ref, rest_ref, k_buf, v_buf, sems):
    width = group * HEAD_DIM
    place = place_ref[0]
    order = (1, 3, 2, 0)
    copies = []
    for slot, r in enumerate(order):
        cols = pl.ds(pl.multiple_of((place ^ r) * width, width), width)
        pair = (
            pltpu.make_async_copy(k_hbm.at[:, cols], k_buf.at[slot], sems.at[0, slot]),
            pltpu.make_async_copy(v_hbm.at[:, cols], v_buf.at[slot], sems.at[1, slot]),
        )
        for copy in pair:
            copy.start()
        copies.append(pair)
    sent = {1: one_ref, 2: two_ref, 3: three_ref}
    spot = {0: 0, 3: 1, 2: 2}
    for slot, r in enumerate(order):
        for copy in copies[slot]:
            copy.wait()
        for j in range(group):
            state = tn(k_buf[slot, :, column(j)], v_buf[slot, :, column(j)])
            if r == 0:
                own_ref[j] = state
            else:
                sent[r][j] = state.astype(BF16)
            if r in spot:
                rest_ref[spot[r] * group + j] = state.astype(BF16)


def intra_kernel(group, q_ref, k_ref, v_ref, w_ref, out_ref):
    rows = q_ref.shape[0]
    heads = QUAD * group
    base = pl.program_id(0) * group
    causal = lax.broadcasted_iota(jnp.int32, (STRETCH, STRETCH), 0) >= lax.broadcasted_iota(
        jnp.int32, (STRETCH, STRETCH), 1
    )
    local_bits = (rows // STRETCH).bit_length() - 1
    weights = [jnp.transpose(w_ref[level, 0], (1, 0)) for level in range(1 + local_bits)]
    for j in range(group):
        states = []
        for c in range(rows // STRETCH):
            here = pl.ds(c * STRETCH, STRETCH)
            q, k, v = (ref[here, column(j)] for ref in (q_ref, k_ref, v_ref))
            probs = jnp.where(causal, nt(q, k), 0.0).astype(BF16)
            total = weights[0][c * STRETCH : (c + 1) * STRETCH, j : j + 1] * nn(probs, v)
            for bit in range(local_bits):
                if c >> bit & 1:
                    low = (c >> bit + 1) << bit + 1
                    left = functools.reduce(jnp.add, states[low : low + (1 << bit)])
                    scale = weights[1 + bit][c * STRETCH : (c + 1) * STRETCH, j : j + 1]
                    total += scale * nn(q, left.astype(BF16))
            out_ref[here, column(j)] = total
            if c + 1 < rows // STRETCH:
                states.append(tn(k, v))
    del heads, base


def readout(group, place, q_ref, w_list, total_ref, r, blocks):
    width = group * HEAD_DIM
    start = pl.multiple_of((place ^ r) * width, width)
    first = (place ^ r) * group
    return width, start, first


def far_kernel(group, bits, place_ref, q_ref, w_ref, *refs):
    n = len(bits)
    state_refs, total_ref, out_ref = refs[: QUAD * n], refs[QUAD * n], refs[QUAD * n + 1]
    place = place_ref[0]
    for r in range(QUAD):
        for j in range(group):
            head = (place & (QUAD - 1) ^ r) * group + j
            cols = pl.ds(pl.multiple_of(head * HEAD_DIM, HEAD_DIM), HEAD_DIM)
            q = q_ref[:, cols]
            total = total_ref[:, cols]
            for i, bit in enumerate(bits):
                row = w_ref[i, pl.ds(head, 1), :]
                row = jnp.where(place >> bit & 1 == 1, row, 0.0)
                scale = jnp.transpose(jnp.broadcast_to(row, (8, row.shape[1])), (1, 0))[:, :1]
                total += scale * nn(q, state_refs[QUAD * i + r][j])
            out_ref[:, cols] = total


def last_kernel(group, bits, place_ref, q_ref, w_ref, *refs):
    n = len(bits)
    state_refs = refs[:QUAD]
    total_ref, out_ref, sq_ref = refs[QUAD:]
    place = place_ref[0]
    squares = jnp.zeros((q_ref.shape[0], HEAD_DIM), F32)
    for r in range(QUAD):
        for j in range(group):
            head = (place & (QUAD - 1) ^ r) * group + j
            cols = pl.ds(pl.multiple_of(head * HEAD_DIM, HEAD_DIM), HEAD_DIM)
            q = q_ref[:, cols]
            total = total_ref[:, cols]
            for i, bit in enumerate(bits):
                row = w_ref[i, pl.ds(head, 1), :]
                row = jnp.where(place >> bit & 1 == 1, row, 0.0)
                scale = jnp.transpose(jnp.broadcast_to(row, (8, row.shape[1])), (1, 0))[:, :1]
                total += scale * nn(q, state_refs[r][i * group + j])
            out_ref[:, cols] = total
            squares += total * total
    sq_ref[...] = jnp.sum(jnp.transpose(squares, (1, 0)), axis=0, keepdims=True)


def norm_kernel(width, x_ref, sq_ref, gain_ref, out_hbm, buf, sems):
    rows = x_ref.shape[0]
    step = rows // sems.shape[0]
    inverse = lax.rsqrt(sq_ref[...] / width + EPSILON)
    scale = jnp.transpose(jnp.broadcast_to(inverse, (8, rows)), (1, 0))[:, :1]
    gain = gain_ref[...]
    copies = []
    for i in range(rows // step):
        here = pl.ds(i * step, step)
        buf[here, :] = (x_ref[here, :] * scale[i * step : (i + 1) * step] * gain).astype(BF16)
        copies.append(pltpu.make_async_copy(buf.at[here, :], out_hbm.at[here, :], sems.at[i]))
        copies[-1].start()
    for copy in copies:
        copy.wait()


def local(queries, keys, values, level_weights, norm_gain):
    rows, width = queries.shape
    heads = width // HEAD_DIM
    group = heads // QUAD
    levels = level_weights.shape[0]
    local_bits = (rows // STRETCH).bit_length() - 1
    seq_bits = lax.axis_size("seq").bit_length() - 1
    full_width = width * lax.axis_size("head")
    position = lax.axis_index("seq").astype(jnp.int32)
    place = (position & (QUAD - 1)).reshape(1)
    whole = position.reshape(1)
    block = (group, HEAD_DIM, HEAD_DIM)
    sds = jax.ShapeDtypeStruct

    own, one, two, three, rest = pl.pallas_call(
        functools.partial(states_kernel, group),
        out_shape=(sds(block, F32), sds(block, BF16), sds(block, BF16), sds(block, BF16), sds((3 * group,) + block[1:], BF16)),
        in_specs=[SMEM, ANY, ANY],
        out_specs=(VMEM,) * 5,
        scratch_shapes=[
            pltpu.VMEM((QUAD, rows, group * HEAD_DIM), BF16),
            pltpu.VMEM((QUAD, rows, group * HEAD_DIM), BF16),
            pltpu.SemaphoreType.DMA((2, QUAD)),
        ],
        compiler_params=params(),
        cost_estimate=cost(2 * rows * width * HEAD_DIM, 4 * rows * width),
        name="states",
    )(place, keys, values)

    got1, got2, got3 = exchanged(one, "seq", 1), exchanged(two, "seq", 2), exchanged(three, "seq", 3)

    weights4 = level_weights.reshape(levels, QUAD, group, rows)
    total = pl.pallas_call(
        functools.partial(intra_kernel, group),
        grid=(QUAD,),
        out_shape=sds((rows, width), F32),
        in_specs=[pl.BlockSpec((rows, group * HEAD_DIM), lambda i: (0, i))] * 3
        + [pl.BlockSpec((1 + local_bits, 1, group, rows), lambda i: (0, i, 0, 0))],
        out_specs=pl.BlockSpec((rows, group * HEAD_DIM), lambda i: (0, i)),
        compiler_params=params(),
        cost_estimate=cost(6 * rows * STRETCH * width, 10 * rows * width),
        name="intra",
    )(queries, keys, values, weights4)

    pair = own + got1.astype(F32)
    other = got2.astype(F32) + got3.astype(F32)
    running = pair + other
    left_pair = jnp.where(position >> 1 & 1 == 1, other, pair).astype(BF16)
    upper = []
    for bit in range(2, seq_bits):
        came = exchanged(running.astype(BF16), "seq", 1 << bit)
        upper.append(came)
        running = running + came.astype(F32)
    rest_got = exchanged(rest, "seq", 1)
    near = [got1] + [rest_got[i * group : (i + 1) * group] for i in range(3)]
    middle = [left_pair] + [exchanged(left_pair, "seq", r) for r in range(1, QUAD)]
    top = jnp.concatenate(upper, axis=0) if len(upper) > 1 else upper[0]
    tops = [top] + [exchanged(top, "seq", r) for r in range(1, QUAD)]

    first = 1 + local_bits
    total = pl.pallas_call(
        functools.partial(far_kernel, group, (0, 1)),
        out_shape=sds((rows, width), F32),
        in_specs=[SMEM] + [VMEM] * (2 + 2 * QUAD + 1),
        out_specs=VMEM,
        input_output_aliases={3 + 2 * QUAD: 0},
        compiler_params=params(),
        cost_estimate=cost(4 * rows * width * HEAD_DIM, 8 * rows * width),
        name="far",
    )(whole, queries, level_weights[first : first + 2], *near, *middle, total)

    total, squares = pl.pallas_call(
        functools.partial(last_kernel, group, tuple(range(2, seq_bits))),
        out_shape=(sds((rows, width), F32), sds((1, rows), F32)),
        in_specs=[SMEM] + [VMEM] * (2 + QUAD + 1),
        out_specs=(VMEM, VMEM),
        input_output_aliases={3 + QUAD: 0},
        compiler_params=params(),
        cost_estimate=cost(2 * (seq_bits - 2) * rows * width * HEAD_DIM, 8 * rows * width),
        name="last",
    )(whole, queries, level_weights[first + 2 :], *tops, total)

    mask = 1
    while mask < lax.axis_size("head"):
        squares = squares + exchanged(squares, "head", mask)
        mask *= 2

    return pl.pallas_call(
        functools.partial(norm_kernel, full_width),
        out_shape=sds((rows, width), BF16),
        in_specs=[VMEM] * 3,
        out_specs=ANY,
        scratch_shapes=[pltpu.VMEM((rows, width), BF16), pltpu.SemaphoreType.DMA((4,))],
        compiler_params=params(),
        cost_estimate=cost(2 * rows * width, 2 * rows * width),
        name="norm",
    )(total, squares, norm_gain.reshape(1, width))


def solution(mesh):
    return jax.shard_map(
        local,
        mesh=mesh,
        in_specs=(P("seq", "head"), P("seq", "head"), P("seq", "head"), P(None, "head", "seq"), P("head")),
        out_specs=P("seq", "head"),
        check_vma=False,
    )
```

time: 60 us -> 39.9 us (0.66)
  the two profiles are of different devices: /device:TPU:24 before, /device:TPU:0 now
where the time goes in v1:
time: 39.9 us; the launch traced here: 39.7 us
  starting transfers between devices  17.8 us (45%)
  Pallas kernels  11.1 us (28%)
  waiting for transfers between devices  5.81 us (15%)
  local copies, waits for them, and re-layouts  4.73 us (12%)
    ppermute x13, starting transfers between devices, exchanged(): return lax.ppermute(block, axis, [(i, i ^ mask) for i in range(count)])  17.8 us
    ppermute x13, waiting for transfers between devices, exchanged(): return lax.ppermute(block, axis, [(i, i ^ mask) for i in range(count)])  5.81 us
    pallas_call x1, Pallas kernels, local(): pl.pallas_call(functools.partial(intra_kernel, group), grid=(QUAD,), out_...  3.9 us
    unnamed x14, local copies, waits for them, and re-layouts  3.78 us
    pallas_call x1, Pallas kernels, local(): pl.pallas_call(functools.partial(far_kernel, group, (0, 1)), out_shape=sd...  2.69 us
    pallas_call x1, Pallas kernels, local(): pl.pallas_call(functools.partial(last_kernel, group, tuple(range(2, seq_b...  1.88 us
    pallas_call x1, Pallas kernels, local(): pl.pallas_call(functools.partial(states_kernel, group), out_shape=(sds(bl...  1.47 us
    pallas_call x1, Pallas kernels, local(): pl.pallas_call(functools.partial(norm_kernel, full_width), out_shape=sds(...  1.22 us
  transfers between devices with their start and end apart: 13, of which 5 were waited for; matrix products, arithmetic and copies ran while one was open for 3% of the time, Pallas kernels for 17%

profile of v1, /device:TPU:0, one launch (start us, length us, event | category | flops | bytes accessed | tf_op | source)
XLA Modules:
  0.0 39.7 jit_solution(5056752016444442501)
XLA Ops:
  0.0 0.0 copy-start
  0.0 0.0 copy-start.1
  0.0 1.3 %copy-done.1 = bf16[512,1024]{1,0:T(8,128)(2,1)S(1)} copy-done((bf16[512,1024]{1,0:T(8,128)(2,1)S(1)}, bf16[512,1024]{1,0:T(8,128)(2,1)}, u32[]{:S(2)}) %copy-start.1) | copy-done | bytes 1048600
  1.3 0.0 copy-start.3
  1.3 1.2 %copy-done.3 = bf16[512,1024]{1,0:T(8,128)(2,1)S(1)} copy-done((bf16[512,1024]{1,0:T(8,128)(2,1)S(1)}, bf16[512,1024]{1,0:T(8,128)(2,1)}, u32[]{:S(2)}) %copy-start.3) | copy-done | bytes 1048600
  2.5 0.0 copy-start.6
  2.5 0.0 copy-start.2
  2.5 1.5 %states.1 = (f32[2,128,128]{2,1,0:T(8,128)S(1)}, bf16[2,128,128]{2,1,0:T(8,128)(2,1)S(1)}, bf16[2,128,128]{2,1,0:T(8,128)(2,1)S(1)}, bf16[2,128,128]{2,1,0:T(8,128)(2,1)S(1)}, bf16[6,128,128]{2,1,0:T(8,128)(2,1)S(1)}) custom-call(s32[1]{0:T(128)} %bitcast.1.place_ref, bf16[512,1024]{1,0:T(8,128)(2,1)S(1)} %copy-done.1, bf16[512,1024]{1,0:T(8,128)(2,1)S(1)} %copy-done.3), custom_call_target="tpu_custom_call" | custom-call | flops 134217728 | bytes 2097152 | tf_op jit(solution)/shard_map/states/pallas_call | solution.py:185
  4.0 3.1 %collective-permute-start = (bf16[2,128,128]{2,1,0:T(8,128)(2,1)S(1)}, bf16[2,128,128]{2,1,0:T(8,128)(2,1)S(1)}, u32[]{:S(2)}, u32[]{:S(2)}) collective-permute-start(bf16[2,128,128]{2,1,0:T(8,128)(2,1)S(1)} %get-tuple-element.13), channel_id=1, source_target_pairs={{0,4},{4,0},{8,12},{12,8},{16,20},{20,16},{24,28},{28,24},{1,5},{5... | collective-permute-start | bytes 196616 | tf_op jit(solution)/shard_map/ppermute | solution.py:32
  7.1 1.6 %collective-permute-start.1 = (bf16[2,128,128]{2,1,0:T(8,128)(2,1)S(1)}, bf16[2,128,128]{2,1,0:T(8,128)(2,1)S(1)}, u32[]{:S(2)}, u32[]{:S(2)}) collective-permute-start(bf16[2,128,128]{2,1,0:T(8,128)(2,1)S(1)} %get-tuple-element.14), channel_id=1, source_target_pairs={{0,8},{4,12},{8,0},{12,4},{16,24},{20,28},{24,16},{28,20},{1,9},{5... | collective-permute-start | bytes 196616 | tf_op jit(solution)/shard_map/ppermute | solution.py:32
  8.7 0.0 collective-permute-start.2
  8.7 1.9 %collective-permute-start.7 = (bf16[6,128,128]{2,1,0:T(8,128)(2,1)S(1)}, bf16[6,128,128]{2,1,0:T(8,128)(2,1)S(1)}, u32[]{:S(2)}, u32[]{:S(2)}) collective-permute-start(bf16[6,128,128]{2,1,0:T(8,128)(2,1)S(1)} %get-tuple-element.16), channel_id=1, source_target_pairs={{0,4},{4,0},{8,12},{12,8},{16,20},{20,16},{24,28},{28,24},{1,5},{5... | collective-permute-start | bytes 589832 | tf_op jit(solution)/shard_map/ppermute | solution.py:32
  10.6 0.9 %reshape.14.w_ref = f32[5,4,2,512]{3,2,1,0:T(2,128)S(1)} reshape(f32[5,8,512]{2,1,0:T(8,128)} %param.8) | data formatting | bytes 163840 | tf_op jit(solution)/shard_map/reshape | solution.py:202
  11.5 0.0 copy-done.6
  11.5 0.0 collective-permute-done.refs_0_
  11.6 0.3 collective-permute-done.1
  11.9 2.1 %collective-permute-done.2 = bf16[2,128,128]{2,1,0:T(8,128)(2,1)S(1)} collective-permute-done((bf16[2,128,128]{2,1,0:T(8,128)(2,1)S(1)}, bf16[2,128,128]{2,1,0:T(8,128)(2,1)S(1)}, u32[]{:S(2)}, u32[]{:S(2)}) %collective-permute-start.2) | collective-permute-done | bytes 65568 | tf_op jit(solution)/shard_map/ppermute | solution.py:32
  14.0 0.8 %collective-permute-start.10 = (bf16[2,128,128]{2,1,0:T(8,128)(2,1)S(1)}, bf16[2,128,128]{2,1,0:T(8,128)(2,1)S(1)}, u32[]{:S(2)}, u32[]{:S(2)}) collective-permute-start(bf16[2,128,128]{2,1,0:T(8,128)(2,1)S(1)} %get-tuple-element.19.refs_4_), channel_id=1, source_target_pairs={{0,12},{4,8},{8,4},{12,0},{16,28},{20,24},{24,20},{28,16},{1,13},{... | collective-permute-start | bytes 196616 | tf_op jit(solution)/shard_map/ppermute | solution.py:32
  14.7 2.6 %collective-permute-start.3 = (bf16[2,128,128]{2,1,0:T(8,128)(2,1)S(1)}, bf16[2,128,128]{2,1,0:T(8,128)(2,1)S(1)}, u32[]{:S(2)}, u32[]{:S(2)}) collective-permute-start(bf16[2,128,128]{2,1,0:T(8,128)(2,1)S(1)} %get-tuple-element.20), channel_id=1, source_target_pairs={{0,16},{4,20},{8,24},{12,28},{16,0},{20,4},{24,8},{28,12},{1,17},{... | collective-permute-start | bytes 196616 | tf_op jit(solution)/shard_map/ppermute | solution.py:32
  17.3 0.0 copy-done
  17.3 0.0 copy-done.2
  17.3 0.0 copy-start.4
  17.3 1.2 %copy-done.4 = bf16[512,1024]{1,0:T(8,128)(2,1)S(1)} copy-done((bf16[512,1024]{1,0:T(8,128)(2,1)S(1)}, bf16[512,1024]{1,0:T(8,128)(2,1)}, u32[]{:S(2)}) %copy-start.4) | copy-done | bytes 1048600
  18.6 3.9 %intra.1.refs_8_ = f32[512,1024]{1,0:T(8,128)S(1)} custom-call(bf16[512,1024]{1,0:T(8,128)(2,1)S(1)} %copy-done, bf16[512,1024]{1,0:T(8,128)(2,1)S(1)} %copy-done.2, bf16[512,1024]{1,0:T(8,128)(2,1)S(1)} %copy-done.4, f32[5,4,2,512]{3,2,1,0:T(2,128)S(1)} %reshape.14.w_ref), custom_call_target="tpu_custom_call" | custom-call | flops 805306368 | bytes 5242880 | tf_op jit(solution)/shard_map/intra/pallas_call | solution.py:203
  22.5 1.3 %collective-permute-start.8 = (bf16[2,128,128]{2,1,0:T(8,128)(2,1)S(1)}, bf16[2,128,128]{2,1,0:T(8,128)(2,1)S(1)}, u32[]{:S(2)}, u32[]{:S(2)}) collective-permute-start(bf16[2,128,128]{2,1,0:T(8,128)(2,1)S(1)} %get-tuple-element.19.refs_4_), channel_id=1, source_target_pairs={{0,4},{4,0},{8,12},{12,8},{16,20},{20,16},{24,28},{28,24},{1,5},{5... | collective-permute-start | bytes 196616 | tf_op jit(solution)/shard_map/ppermute | solution.py:32
  23.7 1.6 %collective-permute-start.9 = (bf16[2,128,128]{2,1,0:T(8,128)(2,1)S(1)}, bf16[2,128,128]{2,1,0:T(8,128)(2,1)S(1)}, u32[]{:S(2)}, u32[]{:S(2)}) collective-permute-start(bf16[2,128,128]{2,1,0:T(8,128)(2,1)S(1)} %get-tuple-element.19.refs_4_), channel_id=1, source_target_pairs={{0,8},{4,12},{8,0},{12,4},{16,24},{20,28},{24,16},{28,20},{1,9},{5... | collective-permute-start | bytes 196616 | tf_op jit(solution)/shard_map/ppermute | solution.py:32
  25.3 0.0 collective-permute-done.3.refs_0_
  25.3 0.5 %collective-permute-start.4 = (bf16[2,128,128]{2,1,0:T(8,128)(2,1)S(1)}, bf16[2,128,128]{2,1,0:T(8,128)(2,1)S(1)}, u32[]{:S(2)}, u32[]{:S(2)}) collective-permute-start(bf16[2,128,128]{2,1,0:T(8,128)(2,1)S(1)} %collective-permute-done.3.refs_0_), channel_id=1, source_target_pairs={{0,4},{4,0},{8,12},{12,8},{16,20},{20,16},{24,28},{28,24},{1,5},{5... | collective-permute-start | bytes 196616 | tf_op jit(solution)/shard_map/ppermute | solution.py:32
  25.8 0.0 collective-permute-done.10.refs_7_
  25.8 0.8 %collective-permute-start.5 = (bf16[2,128,128]{2,1,0:T(8,128)(2,1)S(1)}, bf16[2,128,128]{2,1,0:T(8,128)(2,1)S(1)}, u32[]{:S(2)}, u32[]{:S(2)}) collective-permute-start(bf16[2,128,128]{2,1,0:T(8,128)(2,1)S(1)} %collective-permute-done.3.refs_0_), channel_id=1, source_target_pairs={{0,8},{4,12},{8,0},{12,4},{16,24},{20,28},{24,16},{28,20},{1,9},{5... | collective-permute-start | bytes 196616 | tf_op jit(solution)/shard_map/ppermute | solution.py:32
  26.6 0.0 collective-permute-done.7
  26.6 2.2 %collective-permute-start.6 = (bf16[2,128,128]{2,1,0:T(8,128)(2,1)S(1)}, bf16[2,128,128]{2,1,0:T(8,128)(2,1)S(1)}, u32[]{:S(2)}, u32[]{:S(2)}) collective-permute-start(bf16[2,128,128]{2,1,0:T(8,128)(2,1)S(1)} %collective-permute-done.3.refs_0_), channel_id=1, source_target_pairs={{0,12},{4,8},{8,4},{12,0},{16,28},{20,24},{24,20},{28,16},{1,13},{... | collective-permute-start | bytes 196616 | tf_op jit(solution)/shard_map/ppermute | solution.py:32
  28.8 0.0 collective-permute-done.8.refs_5_
  28.9 0.0 collective-permute-done.9.refs_6_
  28.9 2.7 %far.1.refs_4_ = f32[512,1024]{1,0:T(8,128)S(1)} custom-call(s32[1]{0:T(128)} %bitcast.place_ref, bf16[512,1024]{1,0:T(8,128)(2,1)S(1)} %copy-done, f32[2,8,512]{2,1,0:T(8,128)S(1)} %slice.16.w_ref, bf16[2,128,128]{2,1,0:T(8,128)(2,1)S(1)} %collective-permute-done.refs_0_, ...), custom_call_target="tpu_custom_call", output_to_operand_aliasing={{}: (11, {})} | custom-call | flops 268435456 | bytes 4194304 | tf_op jit(solution)/shard_map/far/pallas_call | solution.py:231
  31.6 0.0 copy-start.5
  31.6 0.0 collective-permute-done.4.refs_1_
  31.6 0.0 collective-permute-done.5.refs_2_
  31.6 0.2 collective-permute-done.6.refs_3_
  31.8 1.9 %last.1 = (f32[512,1024]{1,0:T(8,128)S(1)}, f32[1,512]{1,0:T(1,128)S(1)}) custom-call(s32[1]{0:T(128)} %bitcast.place_ref, bf16[512,1024]{1,0:T(8,128)(2,1)S(1)} %copy-done, f32[1,8,512]{2,1,0:T(8,128)S(1)} %slice.15.w_ref, bf16[2,128,128]{2,1,0:T(8,128)(2,1)S(1)} %collective-permute-done.3.refs_0_, ...), custom_call_target="tpu_custom_call", output_to_operand_aliasing={{0}: (7, {})} | custom-call | flops 134217728 | bytes 4194304 | tf_op jit(solution)/shard_map/last/pallas_call | solution.py:242
  33.6 0.1 collective-permute-start.11
  33.7 1.1 %collective-permute-done.11 = f32[1,512]{1,0:T(1,128)S(1)} collective-permute-done((f32[1,512]{1,0:T(1,128)S(1)}, f32[1,512]{1,0:T(1,128)S(1)}, u32[]{:S(2)}, u32[]{:S(2)}) %collective-permute-start.11) | collective-permute-done | bytes 2080 | tf_op jit(solution)/shard_map/ppermute | solution.py:32
  34.9 1.5 %collective-permute-start.12 = (f32[1,512]{1,0:T(1,128)S(1)}, f32[1,512]{1,0:T(1,128)S(1)}, u32[]{:S(2)}, u32[]{:S(2)}) collective-permute-start(f32[1,512]{1,0:T(1,128)S(1)} %add.18), channel_id=1, source_target_pairs={{0,2},{1,3},{2,0},{3,1},{4,6},{5,7},{6,4},{7,5},{8,10},{9,11},{10,... | collective-permute-start | bytes 6152 | tf_op jit(solution)/shard_map/ppermute | solution.py:32
  36.4 2.1 %collective-permute-done.12 = f32[1,512]{1,0:T(1,128)S(1)} collective-permute-done((f32[1,512]{1,0:T(1,128)S(1)}, f32[1,512]{1,0:T(1,128)S(1)}, u32[]{:S(2)}, u32[]{:S(2)}) %collective-permute-start.12) | collective-permute-done | bytes 2080 | tf_op jit(solution)/shard_map/ppermute | solution.py:32
  38.5 0.0 copy-done.5
  38.5 1.2 %norm.1 = bf16[512,1024]{1,0:T(8,128)(2,1)} custom-call(f32[512,1024]{1,0:T(8,128)S(1)} %get-tuple-element.17.x_ref, f32[1,512]{1,0:T(1,128)S(1)} %add.19.sq_ref, f32[1,1024]{1,0:T(1,128)S(1)} %bitcast.3), custom_call_target="tpu_custom_call" | custom-call | flops 1048576 | bytes 1048576 | tf_op jit(solution)/shard_map/norm/pallas_call | solution.py:258
  (6 shorter events, 0.1 us)
Async XLA Ops:
  0.0 17.3 %copy-start = (bf16[512,1024]{1,0:T(8,128)(2,1)S(1)}, bf16[512,1024]{1,0:T(8,128)(2,1)}, u32[]{:S(2)}) copy-start(bf16[512,1024]{1,0:T(8,128)(2,1)} %q_ref.5) | copy-start | bytes 3145732
  0.0 1.3 %copy-start.1 = (bf16[512,1024]{1,0:T(8,128)(2,1)S(1)}, bf16[512,1024]{1,0:T(8,128)(2,1)}, u32[]{:S(2)}) copy-start(bf16[512,1024]{1,0:T(8,128)(2,1)} %k_ref.1) | copy-start | bytes 3145732
  1.3 1.2 %copy-start.3 = (bf16[512,1024]{1,0:T(8,128)(2,1)S(1)}, bf16[512,1024]{1,0:T(8,128)(2,1)}, u32[]{:S(2)}) copy-start(bf16[512,1024]{1,0:T(8,128)(2,1)} %v_ref.1) | copy-start | bytes 3145732
  2.5 9.0 %copy-start.6 = (f32[5,8,512]{2,1,0:T(8,128)S(1)}, f32[5,8,512]{2,1,0:T(8,128)}, u32[]{:S(2)}) copy-start(f32[5,8,512]{2,1,0:T(8,128)} %param.8) | copy-start | bytes 245764
  2.5 14.8 %copy-start.2 = (bf16[512,1024]{1,0:T(8,128)(2,1)S(1)}, bf16[512,1024]{1,0:T(8,128)(2,1)}, u32[]{:S(2)}) copy-start(bf16[512,1024]{1,0:T(8,128)(2,1)} %k_ref.1) | copy-start | bytes 3145732
  4.0 7.5 %collective-permute-start = (bf16[2,128,128]{2,1,0:T(8,128)(2,1)S(1)}, bf16[2,128,128]{2,1,0:T(8,128)(2,1)S(1)}, u32[]{:S(2)}, u32[]{:S(2)}) collective-permute-start(bf16[2,128,128]{2,1,0:T(8,128)(2,1)S(1)} %get-tuple-element.13), channel_id=1, source_target_pairs={{0,4},{4,0},{8,12},{12,8},{16,20},{20,16},{24,28},{28,24},{1,5},{5... | collective-permute-start | bytes 196616 | tf_op jit(solution)/shard_map/ppermute | solution.py:32
  7.1 4.8 %collective-permute-start.1 = (bf16[2,128,128]{2,1,0:T(8,128)(2,1)S(1)}, bf16[2,128,128]{2,1,0:T(8,128)(2,1)S(1)}, u32[]{:S(2)}, u32[]{:S(2)}) collective-permute-start(bf16[2,128,128]{2,1,0:T(8,128)(2,1)S(1)} %get-tuple-element.14), channel_id=1, source_target_pairs={{0,8},{4,12},{8,0},{12,4},{16,24},{20,28},{24,16},{28,20},{1,9},{5... | collective-permute-start | bytes 196616 | tf_op jit(solution)/shard_map/ppermute | solution.py:32
  8.7 5.3 %collective-permute-start.2 = (bf16[2,128,128]{2,1,0:T(8,128)(2,1)S(1)}, bf16[2,128,128]{2,1,0:T(8,128)(2,1)S(1)}, u32[]{:S(2)}, u32[]{:S(2)}) collective-permute-start(bf16[2,128,128]{2,1,0:T(8,128)(2,1)S(1)} %get-tuple-element.15), channel_id=1, source_target_pairs={{0,12},{4,8},{8,4},{12,0},{16,28},{20,24},{24,20},{28,16},{1,13},{... | collective-permute-start | bytes 196616 | tf_op jit(solution)/shard_map/ppermute | solution.py:32
  8.7 17.9 %collective-permute-start.7 = (bf16[6,128,128]{2,1,0:T(8,128)(2,1)S(1)}, bf16[6,128,128]{2,1,0:T(8,128)(2,1)S(1)}, u32[]{:S(2)}, u32[]{:S(2)}) collective-permute-start(bf16[6,128,128]{2,1,0:T(8,128)(2,1)S(1)} %get-tuple-element.16), channel_id=1, source_target_pairs={{0,4},{4,0},{8,12},{12,8},{16,20},{20,16},{24,28},{28,24},{1,5},{5... | collective-permute-start | bytes 589832 | tf_op jit(solution)/shard_map/ppermute | solution.py:32
  14.0 11.9 %collective-permute-start.10 = (bf16[2,128,128]{2,1,0:T(8,128)(2,1)S(1)}, bf16[2,128,128]{2,1,0:T(8,128)(2,1)S(1)}, u32[]{:S(2)}, u32[]{:S(2)}) collective-permute-start(bf16[2,128,128]{2,1,0:T(8,128)(2,1)S(1)} %get-tuple-element.19.refs_4_), channel_id=1, source_target_pairs={{0,12},{4,8},{8,4},{12,0},{16,28},{20,24},{24,20},{28,16},{1,13},{... | collective-permute-start | bytes 196616 | tf_op jit(solution)/shard_map/ppermute | solution.py:32
  14.7 10.6 %collective-permute-start.3 = (bf16[2,128,128]{2,1,0:T(8,128)(2,1)S(1)}, bf16[2,128,128]{2,1,0:T(8,128)(2,1)S(1)}, u32[]{:S(2)}, u32[]{:S(2)}) collective-permute-start(bf16[2,128,128]{2,1,0:T(8,128)(2,1)S(1)} %get-tuple-element.20), channel_id=1, source_target_pairs={{0,16},{4,20},{8,24},{12,28},{16,0},{20,4},{24,8},{28,12},{1,17},{... | collective-permute-start | bytes 196616 | tf_op jit(solution)/shard_map/ppermute | solution.py:32
  17.3 1.2 %copy-start.4 = (bf16[512,1024]{1,0:T(8,128)(2,1)S(1)}, bf16[512,1024]{1,0:T(8,128)(2,1)}, u32[]{:S(2)}) copy-start(bf16[512,1024]{1,0:T(8,128)(2,1)} %v_ref.1) | copy-start | bytes 3145732
  22.5 6.4 %collective-permute-start.8 = (bf16[2,128,128]{2,1,0:T(8,128)(2,1)S(1)}, bf16[2,128,128]{2,1,0:T(8,128)(2,1)S(1)}, u32[]{:S(2)}, u32[]{:S(2)}) collective-permute-start(bf16[2,128,128]{2,1,0:T(8,128)(2,1)S(1)} %get-tuple-element.19.refs_4_), channel_id=1, source_target_pairs={{0,4},{4,0},{8,12},{12,8},{16,20},{20,16},{24,28},{28,24},{1,5},{5... | collective-permute-start | bytes 196616 | tf_op jit(solution)/shard_map/ppermute | solution.py:32
  23.7 5.1 %collective-permute-start.9 = (bf16[2,128,128]{2,1,0:T(8,128)(2,1)S(1)}, bf16[2,128,128]{2,1,0:T(8,128)(2,1)S(1)}, u32[]{:S(2)}, u32[]{:S(2)}) collective-permute-start(bf16[2,128,128]{2,1,0:T(8,128)(2,1)S(1)} %get-tuple-element.19.refs_4_), channel_id=1, source_target_pairs={{0,8},{4,12},{8,0},{12,4},{16,24},{20,28},{24,16},{28,20},{1,9},{5... | collective-permute-start | bytes 196616 | tf_op jit(solution)/shard_map/ppermute | solution.py:32
  25.3 6.2 %collective-permute-start.4 = (bf16[2,128,128]{2,1,0:T(8,128)(2,1)S(1)}, bf16[2,128,128]{2,1,0:T(8,128)(2,1)S(1)}, u32[]{:S(2)}, u32[]{:S(2)}) collective-permute-start(bf16[2,128,128]{2,1,0:T(8,128)(2,1)S(1)} %collective-permute-done.3.refs_0_), channel_id=1, source_target_pairs={{0,4},{4,0},{8,12},{12,8},{16,20},{20,16},{24,28},{28,24},{1,5},{5... | collective-permute-start | bytes 196616 | tf_op jit(solution)/shard_map/ppermute | solution.py:32
  25.8 5.7 %collective-permute-start.5 = (bf16[2,128,128]{2,1,0:T(8,128)(2,1)S(1)}, bf16[2,128,128]{2,1,0:T(8,128)(2,1)S(1)}, u32[]{:S(2)}, u32[]{:S(2)}) collective-permute-start(bf16[2,128,128]{2,1,0:T(8,128)(2,1)S(1)} %collective-permute-done.3.refs_0_), channel_id=1, source_target_pairs={{0,8},{4,12},{8,0},{12,4},{16,24},{20,28},{24,16},{28,20},{1,9},{5... | collective-permute-start | bytes 196616 | tf_op jit(solution)/shard_map/ppermute | solution.py:32
  26.6 5.2 %collective-permute-start.6 = (bf16[2,128,128]{2,1,0:T(8,128)(2,1)S(1)}, bf16[2,128,128]{2,1,0:T(8,128)(2,1)S(1)}, u32[]{:S(2)}, u32[]{:S(2)}) collective-permute-start(bf16[2,128,128]{2,1,0:T(8,128)(2,1)S(1)} %collective-permute-done.3.refs_0_), channel_id=1, source_target_pairs={{0,12},{4,8},{8,4},{12,0},{16,28},{20,24},{24,20},{28,16},{1,13},{... | collective-permute-start | bytes 196616 | tf_op jit(solution)/shard_map/ppermute | solution.py:32
  31.6 6.9 %copy-start.5 = (f32[1024]{0:T(1024)S(1)}, f32[1024]{0:T(1024)}, u32[]{:S(2)}) copy-start(f32[1024]{0:T(1024)} %param.9) | copy-start | bytes 12292
  33.6 1.2 %collective-permute-start.11 = (f32[1,512]{1,0:T(1,128)S(1)}, f32[1,512]{1,0:T(1,128)S(1)}, u32[]{:S(2)}, u32[]{:S(2)}) collective-permute-start(f32[1,512]{1,0:T(1,128)S(1)} %get-tuple-element.18), channel_id=1, source_target_pairs={{0,1},{1,0},{2,3},{3,2},{4,5},{5,4},{6,7},{7,6},{8,9},{9,8},{10,11... | collective-permute-start | bytes 6152 | tf_op jit(solution)/shard_map/ppermute | solution.py:32
  34.9 3.6 %collective-permute-start.12 = (f32[1,512]{1,0:T(1,128)S(1)}, f32[1,512]{1,0:T(1,128)S(1)}, u32[]{:S(2)}, u32[]{:S(2)}) collective-permute-start(f32[1,512]{1,0:T(1,128)S(1)} %add.18), channel_id=1, source_target_pairs={{0,2},{1,3},{2,0},{3,1},{4,6},{5,7},{6,4},{7,5},{8,10},{9,11},{10,... | collective-permute-start | bytes 6152 | tf_op jit(solution)/shard_map/ppermute | solution.py:32

commit v2 on v1

v2 whole, which is shorter than its diff:
```python
import functools

import jax
import jax.numpy as jnp
from jax import lax
from jax.experimental import pallas as pl
from jax.experimental.pallas import tpu as pltpu
from jax.sharding import PartitionSpec as P


HEAD_DIM = 128
STRETCH = 256
EPSILON = 1e-06
QUAD = 4
F32 = jnp.float32
BF16 = jnp.bfloat16
VMEM = pl.BlockSpec(memory_space=pltpu.VMEM)
SMEM = pl.BlockSpec(memory_space=pltpu.SMEM)
ANY = pl.BlockSpec(memory_space=pl.ANY)
HBM = pl.BlockSpec(memory_space=pltpu.HBM)
GRANT = 24 << 20
STATES_GRANT = 51968 << 10


def params(grant=GRANT):
    return pltpu.CompilerParams(vmem_limit_bytes=grant)


def cost(flops, moved):
    return pl.CostEstimate(flops=flops, bytes_accessed=moved, transcendentals=0)


def exchanged(block, axis, mask):
    count = lax.axis_size(axis)
    return lax.ppermute(block, axis, [(i, i ^ mask) for i in range(count)])


def nt(a, b):
    return lax.dot_general(a, b, (((1,), (1,)), ((), ())), preferred_element_type=F32)


def tn(a, b):
    return lax.dot_general(a, b, (((0,), (0,)), ((), ())), preferred_element_type=F32)


def column(head):
    return pl.ds(head * HEAD_DIM, HEAD_DIM)


def states_kernel(group, place_ref, k_hbm, v_hbm, k_ref, v_ref, own_ref, one_ref, two_ref, three_ref, rest_ref, sems):
    width = group * HEAD_DIM
    place = place_ref[0] & (QUAD - 1)
    order = (3, 1, 2, 0)
    copies = {}
    for r in order:
        cols = pl.ds(pl.multiple_of((place ^ r) * width, width), width)
        copies[r] = (
            pltpu.make_async_copy(k_hbm.at[:, cols], k_ref.at[r], sems.at[0, r]),
            pltpu.make_async_copy(v_hbm.at[:, cols], v_ref.at[r], sems.at[1, r]),
        )
        for copy in copies[r]:
            copy.start()
    sent = {1: one_ref, 2: two_ref, 3: three_ref}
    spot = {0: 0, 3: 1, 2: 2}
    for r in order:
        for copy in copies[r]:
            copy.wait()
        for j in range(group):
            state = tn(v_ref[r, :, column(j)], k_ref[r, :, column(j)])
            if r == 0:
                own_ref[j] = state
            else:
                sent[r][j] = state.astype(BF16)
            if r in spot:
                rest_ref[spot[r] * group + j] = state.astype(BF16)


def intra_kernel(group, groups, place_ref, q_ref, k_ref, v_ref, w_ref, out_ref):
    count = q_ref.shape[0] // STRETCH
    local_bits = count.bit_length() - 1
    place = place_ref[0] & (QUAD - 1)
    causal = lax.broadcasted_iota(jnp.int32, (STRETCH, STRETCH), 0) <= lax.broadcasted_iota(
        jnp.int32, (STRETCH, STRETCH), 1
    )
    for at, r in enumerate(groups):
        for j in range(group):
            head = (place ^ r) * group + j
            cols = pl.ds(pl.multiple_of(head * HEAD_DIM, HEAD_DIM), HEAD_DIM)
            states = []
            for c in range(count):
                here = slice(c * STRETCH, (c + 1) * STRETCH)
                q, k, v = q_ref[here, cols], k_ref[r, here, column(j)], v_ref[r, here, column(j)]
                probs = jnp.where(causal, nt(k, q), 0.0).astype(BF16)
                total = w_ref[0, pl.ds(head, 1), here] * tn(v, probs)
                for bit in range(local_bits):
                    if c >> bit & 1:
                        low = (c >> bit + 1) << bit + 1
                        left = functools.reduce(jnp.add, states[low : low + (1 << bit)])
                        total += w_ref[1 + bit, pl.ds(head, 1), here] * nt(left.astype(BF16), q)
                out_ref[at, column(j), here] = total
                if c + 1 < count:
                    states.append(tn(v, k))


def weight_of(w_ref, level, head, place, bit):
    return jnp.where(place >> bit & 1 == 1, w_ref[level, pl.ds(head, 1), :], 0.0)


def far_kernel(group, first, bits, place_ref, q_ref, w_ref, *refs):
    n = len(bits)
    state_refs, total_refs, out_refs = refs[: 2 * n], refs[2 * n : 2 * n + 2], refs[2 * n + 2 :]
    place = place_ref[0]
    for r in range(QUAD):
        for j in range(group):
            head = (place & (QUAD - 1) ^ r) * group + j
            q = q_ref[:, pl.ds(pl.multiple_of(head * HEAD_DIM, HEAD_DIM), HEAD_DIM)]
            total = total_refs[r // 2][r % 2, column(j), :]
            for i, bit in enumerate(bits):
                state = state_refs[2 * i][j] if r == 0 else state_refs[2 * i + 1][(r - 1) * group + j]
                total += weight_of(w_ref, first + bit, head, place, bit) * nt(state, q)
            out_refs[r // 2][r % 2, column(j), :] = total


def last_kernel(group, first, bits, place_ref, q_ref, w_ref, *refs):
    state_refs, total_refs, out_refs, sq_ref = refs[:QUAD], refs[QUAD : QUAD + 2], refs[QUAD + 2 : QUAD + 4], refs[QUAD + 4]
    place = place_ref[0]
    squares = jnp.zeros(sq_ref.shape, F32)
    for r in range(QUAD):
        for j in range(group):
            head = (place & (QUAD - 1) ^ r) * group + j
            q = q_ref[:, pl.ds(pl.multiple_of(head * HEAD_DIM, HEAD_DIM), HEAD_DIM)]
            total = total_refs[r // 2][r % 2, column(j), :]
            for i, bit in enumerate(bits):
                total += weight_of(w_ref, first + bit, head, place, bit) * nt(state_refs[r][i * group + j], q)
            out_refs[r // 2][r % 2, column(j), :] = total
            squares += jnp.sum(total * total, axis=0, keepdims=True)
    sq_ref[...] = squares


def norm_kernel(group, full_width, place_ref, a_ref, b_ref, sq_ref, gain_ref, out_hbm, buf, sems):
    width = group * HEAD_DIM
    place = place_ref[0] & (QUAD - 1)
    scale = lax.rsqrt(sq_ref[...] / full_width + EPSILON)
    copies = []
    for r in range(QUAD):
        cols = pl.ds(pl.multiple_of((place ^ r) * width, width), width)
        x = jnp.transpose((a_ref, b_ref)[r // 2][r % 2] * scale, (1, 0))
        buf[r] = (x * gain_ref[:, cols]).astype(BF16)
        copies.append(pltpu.make_async_copy(buf.at[r], out_hbm.at[:, cols], sems.at[r]))
        copies[-1].start()
    for copy in copies:
        copy.wait()


def local(queries, keys, values, level_weights, norm_gain):
    rows, width = queries.shape
    group = width // HEAD_DIM // QUAD
    local_bits = (rows // STRETCH).bit_length() - 1
    seq_bits = lax.axis_size("seq").bit_length() - 1
    full_width = width * lax.axis_size("head")
    position = lax.axis_index("seq").astype(jnp.int32)
    place = position.reshape(1)
    block = (group, HEAD_DIM, HEAD_DIM)
    others = (3 * group, HEAD_DIM, HEAD_DIM)
    panel = (QUAD, rows, group * HEAD_DIM)
    half = jax.ShapeDtypeStruct((2, group * HEAD_DIM, rows), F32)
    sds = jax.ShapeDtypeStruct

    k_here, v_here, own, one, two, three, rest = pl.pallas_call(
        functools.partial(states_kernel, group),
        out_shape=(sds(panel, BF16), sds(panel, BF16), sds(block, F32), sds(block, BF16), sds(block, BF16), sds(block, BF16), sds(others, BF16)),
        in_specs=[SMEM, HBM, HBM],
        out_specs=(VMEM,) * 7,
        scratch_shapes=[pltpu.SemaphoreType.DMA((2, QUAD))],
        compiler_params=params(STATES_GRANT),
        cost_estimate=cost(2 * rows * width * HEAD_DIM, 4 * rows * width),
        name="states",
    )(place, keys, values)

    got3 = exchanged(three, "seq", 3)
    got1 = exchanged(one, "seq", 1)
    got2 = exchanged(two, "seq", 2)
    near = exchanged(rest, "seq", 1)

    totals = []
    for groups in ((0, 1), (2, 3)):
        totals.append(
            pl.pallas_call(
                functools.partial(intra_kernel, group, groups),
                out_shape=half,
                in_specs=[SMEM] + [VMEM] * 4,
                out_specs=VMEM,
                compiler_params=params(),
                cost_estimate=cost(3 * rows * STRETCH * width, 2 * rows * width),
                name="intra",
            )(place, queries, k_here, v_here, level_weights)
        )

    pair = own + got1.astype(F32)
    other = got2.astype(F32) + got3.astype(F32)
    running = pair + other
    upper = []
    for bit in range(2, seq_bits):
        came = exchanged(running.astype(BF16), "seq", 1 << bit)
        upper.append(came)
        running = running + came.astype(F32)
    top = jnp.concatenate(upper, axis=0) if len(upper) > 1 else upper[0]
    gathered = {r: exchanged(top, "seq", r) for r in (3, 1, 2)}
    tops = [top] + [gathered[r] for r in (1, 2, 3)]

    sums = [
        three.astype(F32) + near[2 * group :].astype(F32),
        pair,
        one.astype(F32) + near[:group].astype(F32),
    ]
    middle = exchanged(jnp.concatenate(sums, axis=0).astype(BF16), "seq", 2)

    first = 1 + local_bits
    totals = pl.pallas_call(
        functools.partial(far_kernel, group, first, (0, 1)),
        out_shape=(half, half),
        in_specs=[SMEM] + [VMEM] * 8,
        out_specs=(VMEM, VMEM),
        input_output_aliases={7: 0, 8: 1},
        compiler_params=params(),
        cost_estimate=cost(4 * rows * width * HEAD_DIM, 8 * rows * width),
        name="far",
    )(place, queries, level_weights, got1, near, other.astype(BF16), middle, *totals)

    *totals, squares = pl.pallas_call(
        functools.partial(last_kernel, group, first, tuple(range(2, seq_bits))),
        out_shape=(half, half, sds((1, rows), F32)),
        in_specs=[SMEM] + [VMEM] * (2 + QUAD + 2),
        out_specs=(VMEM, VMEM, VMEM),
        input_output_aliases={3 + QUAD: 0, 4 + QUAD: 1},
        compiler_params=params(),
        cost_estimate=cost(2 * (seq_bits - 2) * rows * width * HEAD_DIM, 8 * rows * width),
        name="last",
    )(place, queries, level_weights, *tops, *totals)

    mask = 1
    while mask < lax.axis_size("head"):
        squares = squares + exchanged(squares, "head", mask)
        mask *= 2

    return pl.pallas_call(
        functools.partial(norm_kernel, group, full_width),
        out_shape=sds((rows, width), BF16),
        in_specs=[SMEM] + [VMEM] * 4,
        out_specs=ANY,
        scratch_shapes=[pltpu.VMEM(panel, BF16), pltpu.SemaphoreType.DMA((QUAD,))],
        compiler_params=params(),
        cost_estimate=cost(2 * rows * width, 2 * rows * width),
        name="norm",
    )(place, *totals, squares, norm_gain.reshape(1, width))


def solution(mesh):
    return jax.shard_map(
        local,
        mesh=mesh,
        in_specs=(P("seq", "head"), P("seq", "head"), P("seq", "head"), P(None, "head", "seq"), P("head")),
        out_specs=P("seq", "head"),
        check_vma=False,
    )
```

time: 39.9 us -> 38 us (0.952)
  waiting for transfers between devices: 5.81 us -> 13 us
  local copies, waits for them, and re-layouts: 4.73 us -> 0.7 us
  Pallas kernels: 11.1 us -> 7.73 us
  starting transfers between devices: 17.8 us -> 16.2 us
    ppermute x13 -> x11, waiting for transfers between devices: 5.81 us -> 13 us  [exchanged(): return lax.ppermute(block, axis, [(i, i ^ mask) for i in range(count)])]
    pallas_call x5 -> x6, Pallas kernels: 11.1 us -> 7.73 us  [the longest x2 2.23 us: local(): pl.pallas_call(functools.partial(intra_kernel, group, groups), out_shape=...]
    unnamed x14 -> x6, local copies, waits for them, and re-layouts: 3.78 us -> 0.7 us
    ppermute x13 -> x11, starting transfers between devices: 17.8 us -> 16.2 us  [exchanged(): return lax.ppermute(block, axis, [(i, i ^ mask) for i in range(count)])]
    reshape x1 -> x0, local copies, waits for them, and re-layouts: 0.93 us -> none  [local(): weights4 = level_weights.reshape(levels, QUAD, group, rows)]
  transfers between devices with their start and end apart: 13 -> 11, of which waited for: 5 -> 6; matrix products, arithmetic and copies ran while one was open for 3% -> 0% of each run, Pallas kernels for 17% -> 9%
where the time goes in v2:
time: 38 us; the launch traced here: 37.9 us
  starting transfers between devices  16.2 us (43%)
  waiting for transfers between devices  13 us (34%)
  Pallas kernels  7.73 us (20%)
  local copies, waits for them, and re-layouts  0.7 us (2%)
    ppermute x11, starting transfers between devices, exchanged(): return lax.ppermute(block, axis, [(i, i ^ mask) for i in range(count)])  16.2 us
    ppermute x11, waiting for transfers between devices, exchanged(): return lax.ppermute(block, axis, [(i, i ^ mask) for i in range(count)])  13 us
    pallas_call x2, Pallas kernels, local(): pl.pallas_call(functools.partial(intra_kernel, group, groups), out_shape=...  2.23 us
    pallas_call x1, Pallas kernels, local(): pl.pallas_call(functools.partial(states_kernel, group), out_shape=(sds(pa...  2.21 us
    pallas_call x1, Pallas kernels, local(): pl.pallas_call(functools.partial(norm_kernel, group, full_width), out_sha...  1.35 us
    pallas_call x1, Pallas kernels, local(): pl.pallas_call(functools.partial(far_kernel, group, first, (0, 1)), out_s...  1.07 us
    pallas_call x1, Pallas kernels, local(): pl.pallas_call(functools.partial(last_kernel, group, first, tuple(range(2...  0.86 us
  transfers between devices with their start and end apart: 11, of which 6 were waited for; matrix products, arithmetic and copies ran while one was open for 0% of the time, Pallas kernels for 9%

profile of v2, /device:TPU:0, one launch (start us, length us, event | category | flops | bytes accessed | tf_op | source)
XLA Modules:
  0.0 37.9 jit_solution(3162701470991638824)
XLA Ops:
  0.0 2.2 %states.1 = (bf16[4,512,256]{2,1,0:T(8,128)(2,1)S(1)}, bf16[4,512,256]{2,1,0:T(8,128)(2,1)S(1)}, f32[2,128,128]{2,1,0:T(8,128)S(1)}, bf16[2,128,128]{2,1,0:T(8,1...) custom-call(s32[1]{0:T(128)} %bitcast.place_ref, ...), custom_call_target="tpu_custom_call" | custom-call | flops 134217728 | bytes 2097152 | tf_op jit(solution)/shard_map/states/pallas_call | solution.py:169
  2.2 0.0 copy-start
  2.2 3.1 %collective-permute-start = (bf16[2,128,128]{2,1,0:T(8,128)(2,1)S(1)}, bf16[2,128,128]{2,1,0:T(8,128)(2,1)S(1)}, u32[]{:S(2)}, u32[]{:S(2)}) collective-permute-start(bf16[2,128,128]{2,1,0:T(8,128)(2,1)S(1)} %get-tuple-element.18), channel_id=1, source_target_pairs={{0,4},{4,0},{8,12},{12,8},{16,20},{20,16},{24,28},{28,24},{1,5},{5... | collective-permute-start | bytes 196616 | tf_op jit(solution)/shard_map/ppermute | solution.py:35
  5.3 1.5 %collective-permute-start.2 = (bf16[2,128,128]{2,1,0:T(8,128)(2,1)S(1)}, bf16[2,128,128]{2,1,0:T(8,128)(2,1)S(1)}, u32[]{:S(2)}, u32[]{:S(2)}) collective-permute-start(bf16[2,128,128]{2,1,0:T(8,128)(2,1)S(1)} %get-tuple-element.20), channel_id=1, source_target_pairs={{0,12},{4,8},{8,4},{12,0},{16,28},{20,24},{24,20},{28,16},{1,13},{... | collective-permute-start | bytes 196616 | tf_op jit(solution)/shard_map/ppermute | solution.py:35
  6.8 0.1 collective-permute-start.1
  6.9 1.9 %collective-permute-start.7 = (bf16[6,128,128]{2,1,0:T(8,128)(2,1)S(1)}, bf16[6,128,128]{2,1,0:T(8,128)(2,1)S(1)}, u32[]{:S(2)}, u32[]{:S(2)}) collective-permute-start(bf16[6,128,128]{2,1,0:T(8,128)(2,1)S(1)} %get-tuple-element.21), channel_id=1, source_target_pairs={{0,4},{4,0},{8,12},{12,8},{16,20},{20,16},{24,28},{28,24},{1,5},{5... | collective-permute-start | bytes 589832 | tf_op jit(solution)/shard_map/ppermute | solution.py:35
  8.8 0.0 collective-permute-done.refs_0_
  8.8 2.4 %collective-permute-done.2 = bf16[2,128,128]{2,1,0:T(8,128)(2,1)S(1)} collective-permute-done((bf16[2,128,128]{2,1,0:T(8,128)(2,1)S(1)}, bf16[2,128,128]{2,1,0:T(8,128)(2,1)S(1)}, u32[]{:S(2)}, u32[]{:S(2)}) %collective-permute-start.2) | collective-permute-done | bytes 65568 | tf_op jit(solution)/shard_map/ppermute | solution.py:35
  11.1 0.0 collective-permute-done.1
  11.2 2.8 %collective-permute-done.7.refs_1_ = bf16[6,128,128]{2,1,0:T(8,128)(2,1)S(1)} collective-permute-done((bf16[6,128,128]{2,1,0:T(8,128)(2,1)S(1)}, bf16[6,128,128]{2,1,0:T(8,128)(2,1)S(1)}, u32[]{:S(2)}, u32[]{:S(2)}) %collective-permute-start.7) | collective-permute-done | bytes 196640 | tf_op jit(solution)/shard_map/ppermute | solution.py:35
  14.0 0.0 copy-start.1
  14.0 1.6 %collective-permute-start.8 = (bf16[6,128,128]{2,1,0:T(8,128)(2,1)S(1)}, bf16[6,128,128]{2,1,0:T(8,128)(2,1)S(1)}, u32[]{:S(2)}, u32[]{:S(2)}) collective-permute-start(bf16[6,128,128]{2,1,0:T(8,128)(2,1)S(1)} %pad_maximum_fusion), channel_id=1, source_target_pairs={{0,8},{4,12},{8,0},{12,4},{16,24},{20,28},{24,16},{28,20},{1,9},{5... | collective-permute-start | bytes 589832 | tf_op jit(solution)/shard_map/ppermute | solution.py:35
  15.7 2.6 %collective-permute-start.3 = (bf16[2,128,128]{2,1,0:T(8,128)(2,1)S(1)}, bf16[2,128,128]{2,1,0:T(8,128)(2,1)S(1)}, u32[]{:S(2)}, u32[]{:S(2)}) collective-permute-start(bf16[2,128,128]{2,1,0:T(8,128)(2,1)S(1)} %get-tuple-element.32), channel_id=1, source_target_pairs={{0,16},{4,20},{8,24},{12,28},{16,0},{20,4},{24,8},{28,12},{1,17},{... | collective-permute-start | bytes 196616 | tf_op jit(solution)/shard_map/ppermute | solution.py:35
  18.3 3.1 %collective-permute-done.3.refs_0_ = bf16[2,128,128]{2,1,0:T(8,128)(2,1)S(1)} collective-permute-done((bf16[2,128,128]{2,1,0:T(8,128)(2,1)S(1)}, bf16[2,128,128]{2,1,0:T(8,128)(2,1)S(1)}, u32[]{:S(2)}, u32[]{:S(2)}) %collective-permute-start.3) | collective-permute-done | bytes 65568 | tf_op jit(solution)/shard_map/ppermute | solution.py:35
  21.4 1.1 %collective-permute-start.4 = (bf16[2,128,128]{2,1,0:T(8,128)(2,1)S(1)}, bf16[2,128,128]{2,1,0:T(8,128)(2,1)S(1)}, u32[]{:S(2)}, u32[]{:S(2)}) collective-permute-start(bf16[2,128,128]{2,1,0:T(8,128)(2,1)S(1)} %collective-permute-done.3.refs_0_), channel_id=1, source_target_pairs={{0,4},{4,0},{8,12},{12,8},{16,20},{20,16},{24,28},{28,24},{1,5},{5... | collective-permute-start | bytes 196616 | tf_op jit(solution)/shard_map/ppermute | solution.py:35
  22.5 2.5 %collective-permute-start.5 = (bf16[2,128,128]{2,1,0:T(8,128)(2,1)S(1)}, bf16[2,128,128]{2,1,0:T(8,128)(2,1)S(1)}, u32[]{:S(2)}, u32[]{:S(2)}) collective-permute-start(bf16[2,128,128]{2,1,0:T(8,128)(2,1)S(1)} %collective-permute-done.3.refs_0_), channel_id=1, source_target_pairs={{0,8},{4,12},{8,0},{12,4},{16,24},{20,28},{24,16},{28,20},{1,9},{5... | collective-permute-start | bytes 196616 | tf_op jit(solution)/shard_map/ppermute | solution.py:35
  25.0 0.3 collective-permute-start.6
  25.2 0.0 copy-done
  25.2 0.0 copy-done.1
  25.3 1.1 %intra.3.refs_5_ = f32[2,256,512]{2,1,0:T(8,128)S(1)} custom-call(s32[1]{0:T(128)} %bitcast.place_ref, bf16[512,1024]{1,0:T(8,128)(2,1)S(1)} %copy-done, bf16[4,512,256]{2,1,0:T(8,128)(2,1)S(1)} %get-tuple-element.22.k_ref, bf16[4,512,256]{2,1,0:T(8,128)(2,1)S(1)} %get-tuple-element.23.v_ref, f32[5,8,512]{2,1,0:T(8,128)S(1)} %copy-done.1), custom_call_target="tpu_custom_call" | custom-call | flops 402653184 | bytes 1048576 | tf_op jit(solution)/shard_map/intra/pallas_call | solution.py:188
  26.4 1.1 %intra.2.refs_4_ = f32[2,256,512]{2,1,0:T(8,128)S(1)} custom-call(s32[1]{0:T(128)} %bitcast.place_ref, bf16[512,1024]{1,0:T(8,128)(2,1)S(1)} %copy-done, bf16[4,512,256]{2,1,0:T(8,128)(2,1)S(1)} %get-tuple-element.22.k_ref, bf16[4,512,256]{2,1,0:T(8,128)(2,1)S(1)} %get-tuple-element.23.v_ref, f32[5,8,512]{2,1,0:T(8,128)S(1)} %copy-done.1), custom_call_target="tpu_custom_call" | custom-call | flops 402653184 | bytes 1048576 | tf_op jit(solution)/shard_map/intra/pallas_call | solution.py:188
  27.5 0.0 collective-permute-done.8.refs_3_
  27.5 1.1 %far.1 = (f32[2,256,512]{2,1,0:T(8,128)S(1)}, f32[2,256,512]{2,1,0:T(8,128)S(1)}) custom-call(s32[1]{0:T(128)} %bitcast.place_ref, bf16[512,1024]{1,0:T(8,128)(2,1)S(1)} %copy-done, f32[5,8,512]{2,1,0:T(8,128)S(1)} %copy-done.1, bf16[2,128,128]{2,1,0:T(8,128)(2,1)S(1)} %collective-permute-done.refs_0_, ...), custom_call_target="tpu_custom_call", output_to_operand_aliasing={{0}: (7, {}), {1}: (8, {})} | custom-call | flops 268435456 | bytes 4194304 | tf_op jit(solution)/shard_map/far/pallas_call | solution.py:219
  28.6 0.0 collective-permute-done.4.refs_1_
  28.6 0.0 collective-permute-done.5.refs_2_
  28.6 1.5 %collective-permute-done.6.refs_3_ = bf16[2,128,128]{2,1,0:T(8,128)(2,1)S(1)} collective-permute-done((bf16[2,128,128]{2,1,0:T(8,128)(2,1)S(1)}, bf16[2,128,128]{2,1,0:T(8,128)(2,1)S(1)}, u32[]{:S(2)}, u32[]{:S(2)}) %collective-permute-start.6) | collective-permute-done | bytes 65568 | tf_op jit(solution)/shard_map/ppermute | solution.py:35
  30.1 0.9 %last.1 = (f32[2,256,512]{2,1,0:T(8,128)S(1)}, f32[2,256,512]{2,1,0:T(8,128)S(1)}, f32[1,512]{1,0:T(1,128)S(1)}) custom-call(s32[1]{0:T(128)} %bitcast.place_ref, bf16[512,1024]{1,0:T(8,128)(2,1)S(1)} %copy-done, f32[5,8,512]{2,1,0:T(8,128)S(1)} %copy-done.1, ...), custom_call_target="tpu_custom_call", output_to_operand_aliasing={{0}: (7, {}), {1}: (8, {})} | custom-call | flops 134217728 | bytes 4194304 | tf_op jit(solution)/shard_map/last/pallas_call | solution.py:230
  31.0 0.1 collective-permute-start.9
  31.1 1.1 %collective-permute-done.9 = f32[1,512]{1,0:T(1,128)S(1)} collective-permute-done((f32[1,512]{1,0:T(1,128)S(1)}, f32[1,512]{1,0:T(1,128)S(1)}, u32[]{:S(2)}, u32[]{:S(2)}) %collective-permute-start.9) | collective-permute-done | bytes 2080 | tf_op jit(solution)/shard_map/ppermute | solution.py:35
  32.2 1.5 %collective-permute-start.10 = (f32[1,512]{1,0:T(1,128)S(1)}, f32[1,512]{1,0:T(1,128)S(1)}, u32[]{:S(2)}, u32[]{:S(2)}) collective-permute-start(f32[1,512]{1,0:T(1,128)S(1)} %add.26), channel_id=1, source_target_pairs={{0,2},{1,3},{2,0},{3,1},{4,6},{5,7},{6,4},{7,5},{8,10},{9,11},{10,... | collective-permute-start | bytes 6152 | tf_op jit(solution)/shard_map/ppermute | solution.py:35
  33.7 2.1 %collective-permute-done.10 = f32[1,512]{1,0:T(1,128)S(1)} collective-permute-done((f32[1,512]{1,0:T(1,128)S(1)}, f32[1,512]{1,0:T(1,128)S(1)}, u32[]{:S(2)}, u32[]{:S(2)}) %collective-permute-start.10) | collective-permute-done | bytes 2080 | tf_op jit(solution)/shard_map/ppermute | solution.py:35
  35.8 0.0 copy-start.2
  35.8 0.7 %copy-done.2 = f32[1024]{0:T(1024)S(1)} copy-done((f32[1024]{0:T(1024)S(1)}, f32[1024]{0:T(1024)}, u32[]{:S(2)}) %copy-start.2) | copy-done | bytes 4120
  36.5 1.4 %norm.1 = bf16[512,1024]{1,0:T(8,128)(2,1)} custom-call(s32[1]{0:T(128)} %bitcast.place_ref, f32[2,256,512]{2,1,0:T(8,128)S(1)} %get-tuple-element.26.a_ref, f32[2,256,512]{2,1,0:T(8,128)S(1)} %get-tuple-element.27.b_ref, f32[1,512]{1,0:T(1,128)S(1)} %add.27.sq_ref, f32[1,1024]{1,0:T(1,128)S(1)} %bitcast.2), custom_call_target="tpu_custom_call" | custom-call | flops 1048576 | bytes 1048576 | tf_op jit(solution)/shard_map/norm/pallas_call | solution.py:246
  (5 shorter events, 0.1 us)
Async XLA Ops:
  2.2 23.0 %copy-start = (bf16[512,1024]{1,0:T(8,128)(2,1)S(1)}, bf16[512,1024]{1,0:T(8,128)(2,1)}, u32[]{:S(2)}) copy-start(bf16[512,1024]{1,0:T(8,128)(2,1)} %q_ref.7) | copy-start | bytes 3145732
  2.2 6.6 %collective-permute-start = (bf16[2,128,128]{2,1,0:T(8,128)(2,1)S(1)}, bf16[2,128,128]{2,1,0:T(8,128)(2,1)S(1)}, u32[]{:S(2)}, u32[]{:S(2)}) collective-permute-start(bf16[2,128,128]{2,1,0:T(8,128)(2,1)S(1)} %get-tuple-element.18), channel_id=1, source_target_pairs={{0,4},{4,0},{8,12},{12,8},{16,20},{20,16},{24,28},{28,24},{1,5},{5... | collective-permute-start | bytes 196616 | tf_op jit(solution)/shard_map/ppermute | solution.py:35
  5.3 5.9 %collective-permute-start.2 = (bf16[2,128,128]{2,1,0:T(8,128)(2,1)S(1)}, bf16[2,128,128]{2,1,0:T(8,128)(2,1)S(1)}, u32[]{:S(2)}, u32[]{:S(2)}) collective-permute-start(bf16[2,128,128]{2,1,0:T(8,128)(2,1)S(1)} %get-tuple-element.20), channel_id=1, source_target_pairs={{0,12},{4,8},{8,4},{12,0},{16,28},{20,24},{24,20},{28,16},{1,13},{... | collective-permute-start | bytes 196616 | tf_op jit(solution)/shard_map/ppermute | solution.py:35
  6.8 4.3 %collective-permute-start.1 = (bf16[2,128,128]{2,1,0:T(8,128)(2,1)S(1)}, bf16[2,128,128]{2,1,0:T(8,128)(2,1)S(1)}, u32[]{:S(2)}, u32[]{:S(2)}) collective-permute-start(bf16[2,128,128]{2,1,0:T(8,128)(2,1)S(1)} %get-tuple-element.19), channel_id=1, source_target_pairs={{0,8},{4,12},{8,0},{12,4},{16,24},{20,28},{24,16},{28,20},{1,9},{5... | collective-permute-start | bytes 196616 | tf_op jit(solution)/shard_map/ppermute | solution.py:35
  6.9 7.1 %collective-permute-start.7 = (bf16[6,128,128]{2,1,0:T(8,128)(2,1)S(1)}, bf16[6,128,128]{2,1,0:T(8,128)(2,1)S(1)}, u32[]{:S(2)}, u32[]{:S(2)}) collective-permute-start(bf16[6,128,128]{2,1,0:T(8,128)(2,1)S(1)} %get-tuple-element.21), channel_id=1, source_target_pairs={{0,4},{4,0},{8,12},{12,8},{16,20},{20,16},{24,28},{28,24},{1,5},{5... | collective-permute-start | bytes 589832 | tf_op jit(solution)/shard_map/ppermute | solution.py:35
  14.0 11.3 %copy-start.1 = (f32[5,8,512]{2,1,0:T(8,128)S(1)}, f32[5,8,512]{2,1,0:T(8,128)}, u32[]{:S(2)}) copy-start(f32[5,8,512]{2,1,0:T(8,128)} %w_ref.7) | copy-start | bytes 245764
  14.0 13.5 %collective-permute-start.8 = (bf16[6,128,128]{2,1,0:T(8,128)(2,1)S(1)}, bf16[6,128,128]{2,1,0:T(8,128)(2,1)S(1)}, u32[]{:S(2)}, u32[]{:S(2)}) collective-permute-start(bf16[6,128,128]{2,1,0:T(8,128)(2,1)S(1)} %pad_maximum_fusion), channel_id=1, source_target_pairs={{0,8},{4,12},{8,0},{12,4},{16,24},{20,28},{24,16},{28,20},{1,9},{5... | collective-permute-start | bytes 589832 | tf_op jit(solution)/shard_map/ppermute | solution.py:35
  15.7 5.7 %collective-permute-start.3 = (bf16[2,128,128]{2,1,0:T(8,128)(2,1)S(1)}, bf16[2,128,128]{2,1,0:T(8,128)(2,1)S(1)}, u32[]{:S(2)}, u32[]{:S(2)}) collective-permute-start(bf16[2,128,128]{2,1,0:T(8,128)(2,1)S(1)} %get-tuple-element.32), channel_id=1, source_target_pairs={{0,16},{4,20},{8,24},{12,28},{16,0},{20,4},{24,8},{28,12},{1,17},{... | collective-permute-start | bytes 196616 | tf_op jit(solution)/shard_map/ppermute | solution.py:35
  21.4 7.2 %collective-permute-start.4 = (bf16[2,128,128]{2,1,0:T(8,128)(2,1)S(1)}, bf16[2,128,128]{2,1,0:T(8,128)(2,1)S(1)}, u32[]{:S(2)}, u32[]{:S(2)}) collective-permute-start(bf16[2,128,128]{2,1,0:T(8,128)(2,1)S(1)} %collective-permute-done.3.refs_0_), channel_id=1, source_target_pairs={{0,4},{4,0},{8,12},{12,8},{16,20},{20,16},{24,28},{28,24},{1,5},{5... | collective-permute-start | bytes 196616 | tf_op jit(solution)/shard_map/ppermute | solution.py:35
  22.5 6.1 %collective-permute-start.5 = (bf16[2,128,128]{2,1,0:T(8,128)(2,1)S(1)}, bf16[2,128,128]{2,1,0:T(8,128)(2,1)S(1)}, u32[]{:S(2)}, u32[]{:S(2)}) collective-permute-start(bf16[2,128,128]{2,1,0:T(8,128)(2,1)S(1)} %collective-permute-done.3.refs_0_), channel_id=1, source_target_pairs={{0,8},{4,12},{8,0},{12,4},{16,24},{20,28},{24,16},{28,20},{1,9},{5... | collective-permute-start | bytes 196616 | tf_op jit(solution)/shard_map/ppermute | solution.py:35
  25.0 5.2 %collective-permute-start.6 = (bf16[2,128,128]{2,1,0:T(8,128)(2,1)S(1)}, bf16[2,128,128]{2,1,0:T(8,128)(2,1)S(1)}, u32[]{:S(2)}, u32[]{:S(2)}) collective-permute-start(bf16[2,128,128]{2,1,0:T(8,128)(2,1)S(1)} %collective-permute-done.3.refs_0_), channel_id=1, source_target_pairs={{0,12},{4,8},{8,4},{12,0},{16,28},{20,24},{24,20},{28,16},{1,13},{... | collective-permute-start | bytes 196616 | tf_op jit(solution)/shard_map/ppermute | solution.py:35
  31.0 1.2 %collective-permute-start.9 = (f32[1,512]{1,0:T(1,128)S(1)}, f32[1,512]{1,0:T(1,128)S(1)}, u32[]{:S(2)}, u32[]{:S(2)}) collective-permute-start(f32[1,512]{1,0:T(1,128)S(1)} %get-tuple-element.28), channel_id=1, source_target_pairs={{0,1},{1,0},{2,3},{3,2},{4,5},{5,4},{6,7},{7,6},{8,9},{9,8},{10,11... | collective-permute-start | bytes 6152 | tf_op jit(solution)/shard_map/ppermute | solution.py:35
  32.2 3.6 %collective-permute-start.10 = (f32[1,512]{1,0:T(1,128)S(1)}, f32[1,512]{1,0:T(1,128)S(1)}, u32[]{:S(2)}, u32[]{:S(2)}) collective-permute-start(f32[1,512]{1,0:T(1,128)S(1)} %add.26), channel_id=1, source_target_pairs={{0,2},{1,3},{2,0},{3,1},{4,6},{5,7},{6,4},{7,5},{8,10},{9,11},{10,... | collective-permute-start | bytes 6152 | tf_op jit(solution)/shard_map/ppermute | solution.py:35
  35.8 0.7 %copy-start.2 = (f32[1024]{0:T(1024)S(1)}, f32[1024]{0:T(1024)}, u32[]{:S(2)}) copy-start(f32[1024]{0:T(1024)} %param.9) | copy-start | bytes 12292

commit v3 on v2

v3 whole, which is shorter than its diff:
```python
import functools

import jax
import jax.numpy as jnp
from jax import lax
from jax.experimental import pallas as pl
from jax.experimental.pallas import tpu as pltpu
from jax.sharding import PartitionSpec as P


HEAD_DIM = 128
STRETCH = 256
EPSILON = 1e-06
QUAD = 4
F32 = jnp.float32
BF16 = jnp.bfloat16
VMEM = pl.BlockSpec(memory_space=pltpu.VMEM)
SMEM = pl.BlockSpec(memory_space=pltpu.SMEM)
ANY = pl.BlockSpec(memory_space=pl.ANY)
HBM = pl.BlockSpec(memory_space=pltpu.HBM)
GRANT = 24 << 20
TILE = 256
STATES_GRANT = 52992 << 10
OWN_GRANT = 53248 << 10


def params(grant=GRANT):
    return pltpu.CompilerParams(vmem_limit_bytes=grant)


def cost(flops, moved):
    return pl.CostEstimate(flops=flops, bytes_accessed=moved, transcendentals=0)


def exchanged(block, axis, mask):
    count = lax.axis_size(axis)
    return lax.ppermute(block, axis, [(i, i ^ mask) for i in range(count)])


def nt(a, b):
    return lax.dot_general(a, b, (((1,), (1,)), ((), ())), preferred_element_type=F32)


def tn(a, b):
    return lax.dot_general(a, b, (((0,), (0,)), ((), ())), preferred_element_type=F32)


def column(head):
    return pl.ds(head * HEAD_DIM, HEAD_DIM)


def states_of(group, groups, place, k_hbm, v_hbm, k_ref, v_ref, sems, use):
    width = group * HEAD_DIM
    copies = []
    for at, r in enumerate(groups):
        cols = pl.ds(pl.multiple_of((place ^ r) * width, width), width)
        copies.append(
            (
                pltpu.make_async_copy(k_hbm.at[:, cols], k_ref.at[at], sems.at[0, at]),
                pltpu.make_async_copy(v_hbm.at[:, cols], v_ref.at[at], sems.at[1, at]),
            )
        )
        for copy in copies[-1]:
            copy.start()
    for at, r in enumerate(groups):
        for copy in copies[at]:
            copy.wait()
        for j in range(group):
            use(r, j, tn(v_ref[at, :, column(j)], k_ref[at, :, column(j)]))


def sent_kernel(group, groups, place_ref, k_hbm, v_hbm, k_ref, v_ref, *refs):
    sent = dict(zip(groups, refs))

    def use(r, j, state):
        sent[r][j] = state.astype(BF16)

    states_of(group, groups, place_ref[0] & (QUAD - 1), k_hbm, v_hbm, k_ref, v_ref, refs[-1], use)


def own_kernel(group, place_ref, k_hbm, v_hbm, gain_hbm, three_ref, two_ref, k_ref, v_ref, gain_ref, own_ref, rest_ref, sems, gain_sem):
    gain = pltpu.make_async_copy(gain_hbm, gain_ref, gain_sem)
    gain.start()
    rest_ref[group : 2 * group] = three_ref[...]
    rest_ref[2 * group :] = two_ref[...]

    def use(r, j, state):
        own_ref[j] = state
        rest_ref[j] = state.astype(BF16)

    states_of(group, (0,), place_ref[0] & (QUAD - 1), k_hbm, v_hbm, k_ref, v_ref, sems, use)
    gain.wait()


def intra_kernel(group, work, place_ref, q_ref, w_ref, *refs):
    n = len(work)
    sources, out_refs = refs[:-n], refs[-n:]
    count = q_ref.shape[0] // STRETCH
    local_bits = count.bit_length() - 1
    place = place_ref[0] & (QUAD - 1)
    causal = lax.broadcasted_iota(jnp.int32, (STRETCH, STRETCH), 0) <= lax.broadcasted_iota(
        jnp.int32, (STRETCH, STRETCH), 1
    )
    for (r, source, slot), out_ref in zip(work, out_refs):
        k_ref, v_ref = sources[2 * source : 2 * source + 2]
        for j in range(group):
            head = (place ^ r) * group + j
            cols = pl.ds(pl.multiple_of(head * HEAD_DIM, HEAD_DIM), HEAD_DIM)
            states = []
            for c in range(count):
                here = slice(c * STRETCH, (c + 1) * STRETCH)
                q, k, v = q_ref[here, cols], k_ref[slot, here, column(j)], v_ref[slot, here, column(j)]
                probs = jnp.where(causal, nt(k, q), 0.0).astype(BF16)
                total = w_ref[0, pl.ds(head, 1), here] * tn(v, probs)
                for bit in range(local_bits):
                    if c >> bit & 1:
                        low = (c >> bit + 1) << bit + 1
                        left = functools.reduce(jnp.add, states[low : low + (1 << bit)])
                        total += w_ref[1 + bit, pl.ds(head, 1), here] * nt(left.astype(BF16), q)
                out_ref[column(j), here] = total
                if c + 1 < count:
                    states.append(tn(v, k))


def readout_kernel(group, first, work, n_states, carry, finish, place_ref, q_ref, w_ref, *refs):
    n = len(work)
    state_refs, total_refs, refs = refs[:n_states], refs[n_states : n_states + n], refs[n_states + n :]
    carried_ref = refs[0] if carry else None
    out_refs, squares_ref = refs[carry : carry + n], refs[carry + n]
    rows = q_ref.shape[0]
    place = place_ref[0]
    for t in range(0, rows, TILE):
        here = slice(t, t + TILE)
        squares = carried_ref[:, here] if carry else jnp.zeros((8, TILE), F32)
        for (r, complete, reads), total_ref, out_ref in zip(work, total_refs, out_refs):
            for j in range(group):
                head = (place & (QUAD - 1) ^ r) * group + j
                q = q_ref[here, pl.ds(pl.multiple_of(head * HEAD_DIM, HEAD_DIM), HEAD_DIM)]
                total = total_ref[column(j), here]
                for bit, ref, slot in reads:
                    row = w_ref[first + bit, pl.ds(head, 1), here]
                    row = jnp.where(place >> bit & 1 == 1, row, 0.0)
                    total += row * nt(state_refs[ref][slot + j], q)
                out_ref[column(j), here] = total
                if complete:
                    squares += jnp.sum((total * total).reshape(HEAD_DIM // 8, 8, TILE), axis=0)
        squares_ref[:, here] = jnp.sum(squares, axis=0, keepdims=True) if finish else squares


def norm_kernel(group, full_width, place_ref, *refs):
    total_refs, (sq_ref, gain_ref, out_hbm, buf, sems) = refs[:QUAD], refs[QUAD:]
    width = group * HEAD_DIM
    place = place_ref[0] & (QUAD - 1)
    scale = lax.rsqrt(sq_ref[...] / full_width + EPSILON)
    copies = []
    for r in range(QUAD):
        cols = pl.ds(pl.multiple_of((place ^ r) * width, width), width)
        x = jnp.transpose(total_refs[r][...] * scale, (1, 0))
        buf[r] = (x * gain_ref[:, cols]).astype(BF16)
        copies.append(pltpu.make_async_copy(buf.at[r], out_hbm.at[:, cols], sems.at[r]))
        copies[-1].start()
    for copy in copies:
        copy.wait()


def local(queries, keys, values, level_weights, norm_gain):
    rows, width = queries.shape
    group = width // HEAD_DIM // QUAD
    local_bits = (rows // STRETCH).bit_length() - 1
    seq_bits = lax.axis_size("seq").bit_length() - 1
    full_width = width * lax.axis_size("head")
    position = lax.axis_index("seq").astype(jnp.int32)
    place = position.reshape(1)
    sds = jax.ShapeDtypeStruct
    block = (group, HEAD_DIM, HEAD_DIM)
    others = (3 * group, HEAD_DIM, HEAD_DIM)
    panel = (rows, group * HEAD_DIM)
    part = sds((group * HEAD_DIM, rows), F32)

    groups = (3, 1, 2)
    k_sent, v_sent, three, one, two = pl.pallas_call(
        functools.partial(sent_kernel, group, groups),
        out_shape=(sds((3,) + panel, BF16),) * 2 + (sds(block, BF16),) * 3,
        in_specs=[SMEM, HBM, HBM],
        out_specs=(VMEM,) * 5,
        scratch_shapes=[pltpu.SemaphoreType.DMA((2, 3))],
        compiler_params=params(STATES_GRANT),
        cost_estimate=cost(3 * rows * width * HEAD_DIM // 2, 3 * rows * width),
        name="sent",
    )(place, keys, values)

    got3 = exchanged(three, "seq", 3)
    got1 = exchanged(one, "seq", 1)
    got2 = exchanged(two, "seq", 2)

    k_own, v_own, gain, own, rest = pl.pallas_call(
        functools.partial(own_kernel, group),
        out_shape=(sds((1,) + panel, BF16),) * 2 + (sds((1, width), F32), sds(block, F32), sds(others, BF16)),
        in_specs=[SMEM, HBM, HBM, HBM, VMEM, VMEM],
        out_specs=(VMEM,) * 5,
        scratch_shapes=[pltpu.SemaphoreType.DMA((2, 1)), pltpu.SemaphoreType.DMA],
        compiler_params=params(OWN_GRANT),
        cost_estimate=cost(rows * width * HEAD_DIM // 2, rows * width),
        name="own",
    )(place, keys, values, norm_gain.reshape(1, width), three, two)
    near = exchanged(rest, "seq", 1)

    totals = {}
    for work, sources in (
        (((3, 0, 0), (1, 0, 1)), (k_sent, v_sent)),
        (((2, 0, 2), (0, 1, 0)), (k_sent, v_sent, k_own, v_own)),
    ):
        outs = pl.pallas_call(
            functools.partial(intra_kernel, group, work),
            out_shape=(part,) * len(work),
            in_specs=[SMEM] + [VMEM] * (2 + len(sources)),
            out_specs=(VMEM,) * len(work),
            compiler_params=params(),
            cost_estimate=cost(3 * rows * STRETCH * width, 2 * rows * width),
            name="intra",
        )(place, queries, level_weights, *sources)
        totals |= {r: out for (r, _, _), out in zip(work, outs)}

    pair = own + got1.astype(F32)
    other = got2.astype(F32) + got3.astype(F32)
    running = pair + other
    upper = []
    for bit in range(2, seq_bits):
        came = exchanged(running.astype(BF16), "seq", 1 << bit)
        upper.append(came)
        running = running + came.astype(F32)
    top = jnp.concatenate(upper, axis=0) if len(upper) > 1 else upper[0]
    tops = {0: top} | {r: exchanged(top, "seq", r) for r in (3, 1, 2)}

    sums = [
        three.astype(F32) + near[2 * group :].astype(F32),
        pair,
        one.astype(F32) + near[:group].astype(F32),
    ]
    middle = exchanged(jnp.concatenate(sums, axis=0).astype(BF16), "seq", 2)

    def top_reads(ref):
        return tuple((bit, ref, (bit - 2) * group) for bit in range(2, seq_bits))

    def readout(work, states, squares, finish=False):
        n, carry = len(work), squares is not None
        kernel = functools.partial(readout_kernel, group, 1 + local_bits, work, len(states), carry, finish)
        ins = [place, queries, level_weights, *states, *(totals[r] for r, _, _ in work)] + [squares] * carry
        shapes = [part] * n + [sds((1 if finish else 8, rows), F32)]
        outs = pl.pallas_call(
            kernel,
            out_shape=tuple(shapes),
            in_specs=[SMEM] + [VMEM] * (len(ins) - 1),
            out_specs=(VMEM,) * len(shapes),
            compiler_params=params(),
            cost_estimate=cost(n * rows * width * HEAD_DIM, 2 * n * rows * width),
        )(*ins)
        totals.update({r: out for (r, _, _), out in zip(work, outs)})
        return outs[n]

    below = {0: ((0, 0, 0), (1, 2, 0))} | {r: ((0, 1, (r - 1) * group), (1, 3, (r - 1) * group)) for r in (1, 2, 3)}
    work = tuple((r, r == 0, below[r] + (top_reads(4) if r == 0 else ())) for r in (3, 1, 2, 0))
    squares = readout(work, (got1, near, other.astype(BF16), middle, top), None)
    squares = readout(((3, True, top_reads(0)), (1, True, top_reads(1))), (tops[3], tops[1]), squares)
    squares = readout(((2, True, top_reads(0)),), (tops[2],), squares, finish=True)

    mask = 1
    while mask < lax.axis_size("head"):
        squares = squares + exchanged(squares, "head", mask)
        mask *= 2

    return pl.pallas_call(
        functools.partial(norm_kernel, group, full_width),
        out_shape=sds((rows, width), BF16),
        in_specs=[SMEM] + [VMEM] * (QUAD + 2),
        out_specs=ANY,
        scratch_shapes=[pltpu.VMEM((QUAD,) + panel, BF16), pltpu.SemaphoreType.DMA((QUAD,))],
        compiler_params=params(),
        cost_estimate=cost(2 * rows * width, 2 * rows * width),
        name="norm",
    )(place, *(totals[r] for r in range(QUAD)), squares, gain)


def solution(mesh):
    return jax.shard_map(
        local,
        mesh=mesh,
        in_specs=(P("seq", "head"), P("seq", "head"), P("seq", "head"), P(None, "head", "seq"), P("head")),
        out_specs=P("seq", "head"),
        check_vma=False,
    )
```

time: 38 us -> 37.8 us (level)
  local copies, waits for them, and re-layouts: 0.7 us -> 0.02 us
  Pallas kernels: 7.73 us -> 8.31 us
    unnamed x6, local copies, waits for them, and re-layouts: 0.7 us -> 0.02 us
    pallas_call x5 -> x7, Pallas kernels: 6.37 us -> 6.95 us  [the longest x2 2.24 us: local(): pl.pallas_call(functools.partial(intra_kernel, group, work), out_shape=(p...]
  transfers between devices with their start and end apart: 11 -> 11, of which waited for: 6 -> 6; matrix products, arithmetic and copies ran while one was open for 0% -> 0% of each run, Pallas kernels for 9% -> 13%
where the time goes in v3:
time: 37.8 us; the launch traced here: 37.6 us
  starting transfers between devices  16.3 us (43%)
  waiting for transfers between devices  12.8 us (34%)
  Pallas kernels  8.31 us (22%)
    ppermute x11, starting transfers between devices, exchanged(): return lax.ppermute(block, axis, [(i, i ^ mask) for i in range(count)])  16.3 us
    ppermute x11, waiting for transfers between devices, exchanged(): return lax.ppermute(block, axis, [(i, i ^ mask) for i in range(count)])  12.8 us
    pallas_call x2, Pallas kernels, local(): pl.pallas_call(functools.partial(intra_kernel, group, work), out_shape=(p...  2.24 us
    pallas_call x1, Pallas kernels, local(): pl.pallas_call(functools.partial(sent_kernel, group, groups), out_shape=(...  1.92 us
    pallas_call x3, Pallas kernels, readout(): pl.pallas_call(kernel, out_shape=tuple(shapes), in_specs=[SMEM] + [VMEM]...  1.45 us
    pallas_call x1, Pallas kernels, local(): pl.pallas_call(functools.partial(norm_kernel, group, full_width), out_sha...  1.36 us
    pallas_call x1, Pallas kernels, local(): pl.pallas_call(functools.partial(own_kernel, group), out_shape=(sds((1,)...  1.34 us
  transfers between devices with their start and end apart: 11, of which 6 were waited for; matrix products, arithmetic and copies ran while one was open for 0% of the time, Pallas kernels for 13%

profile of v3, /device:TPU:0, one launch (start us, length us, event | category | flops | bytes accessed | tf_op | source)
XLA Modules:
  0.0 37.6 jit_solution(13998191262738377)
XLA Ops:
  0.0 1.9 %sent.1 = (bf16[3,512,256]{2,1,0:T(8,128)(2,1)S(1)}, bf16[3,512,256]{2,1,0:T(8,128)(2,1)S(1)}, bf16[2,128,128]{2,1,0:T(8,128)(2,1)S(1)}, bf16[2,128,128]{2,1,0:T(8,128)(2,1)S(1)}, bf16[2,128,128]{2,1,0:T(8,128)(2,1)S(1)}) custom-call(s32[1]{0:T(128)} %bitcast.place_ref, bf16[512,1024]{1,0:T(8,128)(2,1)} %k_hbm.3, bf16[512,1024]{1,0:T(8,128)(2,1)} %v_hbm.3), custom_call_target="tpu_custom_call" | custom-call | flops 100663296 | bytes 1572864 | tf_op jit(solution)/shard_map/sent/pallas_call | solution.py:181
  1.9 0.0 copy-start.2
  1.9 3.1 %collective-permute-start = (bf16[2,128,128]{2,1,0:T(8,128)(2,1)S(1)}, bf16[2,128,128]{2,1,0:T(8,128)(2,1)S(1)}, u32[]{:S(2)}, u32[]{:S(2)}) collective-permute-start(bf16[2,128,128]{2,1,0:T(8,128)(2,1)S(1)} %get-tuple-element.29), channel_id=1, source_target_pairs={{0,4},{4,0},{8,12},{12,8},{16,20},{20,16},{24,28},{28,24},{1,5},{5... | collective-permute-start | bytes 196616 | tf_op jit(solution)/shard_map/ppermute | solution.py:37
  5.0 1.5 %collective-permute-start.3 = (bf16[2,128,128]{2,1,0:T(8,128)(2,1)S(1)}, bf16[2,128,128]{2,1,0:T(8,128)(2,1)S(1)}, u32[]{:S(2)}, u32[]{:S(2)}) collective-permute-start(bf16[2,128,128]{2,1,0:T(8,128)(2,1)S(1)} %get-tuple-element.30.three_ref), channel_id=1, source_target_pairs={{0,12},{4,8},{8,4},{12,0},{16,28},{20,24},{24,20},{28,16},{1,13},{... | collective-permute-start | bytes 196616 | tf_op jit(solution)/shard_map/ppermute | solution.py:37
  6.5 0.1 collective-permute-start.2
  6.6 0.0 copy-done.2
  6.6 1.3 %own.1 = (bf16[1,512,256]{2,1,0:T(8,128)(2,1)S(1)}, bf16[1,512,256]{2,1,0:T(8,128)(2,1)S(1)}, f32[1,1024]{1,0:T(1,128)S(1)}, f32[2,128,128]{2,1,0:T(8,128)S(1)}, bf16[6,128,128]{2,1,0:T(8,128)(2,1)S(1)}) custom-call(s32[1]{0:T(128)} %bitcast.place_ref, bf16[512,1024]{1,0:T(8,128)(2,1)} %k_hbm.3, bf16[512,1024]{1,0:T(8,128)(2,1)} %v_hbm.3, ...), custom_call_target="tpu_custom_call" | custom-call | flops 33554432 | bytes 524288 | tf_op jit(solution)/shard_map/own/pallas_call | solution.py:196
  7.9 0.0 copy-start
  7.9 2.0 %collective-permute-start.1 = (bf16[6,128,128]{2,1,0:T(8,128)(2,1)S(1)}, bf16[6,128,128]{2,1,0:T(8,128)(2,1)S(1)}, u32[]{:S(2)}, u32[]{:S(2)}) collective-permute-start(bf16[6,128,128]{2,1,0:T(8,128)(2,1)S(1)} %get-tuple-element.32), channel_id=1, source_target_pairs={{0,4},{4,0},{8,12},{12,8},{16,20},{20,16},{24,28},{28,24},{1,5},{5... | collective-permute-start | bytes 589832 | tf_op jit(solution)/shard_map/ppermute | solution.py:37
  9.9 0.0 collective-permute-done.refs_0_
  9.9 0.9 %collective-permute-done.3 = bf16[2,128,128]{2,1,0:T(8,128)(2,1)S(1)} collective-permute-done((bf16[2,128,128]{2,1,0:T(8,128)(2,1)S(1)}, bf16[2,128,128]{2,1,0:T(8,128)(2,1)S(1)}, u32[]{:S(2)}, u32[]{:S(2)}) %collective-permute-start.3) | collective-permute-done | bytes 65568 | tf_op jit(solution)/shard_map/ppermute | solution.py:37
  10.8 0.0 collective-permute-done.2
  10.9 3.7 %collective-permute-done.1.refs_1_ = bf16[6,128,128]{2,1,0:T(8,128)(2,1)S(1)} collective-permute-done((bf16[6,128,128]{2,1,0:T(8,128)(2,1)S(1)}, bf16[6,128,128]{2,1,0:T(8,128)(2,1)S(1)}, u32[]{:S(2)}, u32[]{:S(2)}) %collective-permute-start.1) | collective-permute-done | bytes 196640 | tf_op jit(solution)/shard_map/ppermute | solution.py:37
  14.6 0.0 copy-start.1
  14.7 1.4 %collective-permute-start.4 = (bf16[6,128,128]{2,1,0:T(8,128)(2,1)S(1)}, bf16[6,128,128]{2,1,0:T(8,128)(2,1)S(1)}, u32[]{:S(2)}, u32[]{:S(2)}) collective-permute-start(bf16[6,128,128]{2,1,0:T(8,128)(2,1)S(1)} %pad_maximum_fusion), channel_id=1, source_target_pairs={{0,8},{4,12},{8,0},{12,4},{16,24},{20,28},{24,16},{28,20},{1,9},{5... | collective-permute-start | bytes 589832 | tf_op jit(solution)/shard_map/ppermute | solution.py:37
  16.1 2.6 %collective-permute-start.5 = (bf16[2,128,128]{2,1,0:T(8,128)(2,1)S(1)}, bf16[2,128,128]{2,1,0:T(8,128)(2,1)S(1)}, u32[]{:S(2)}, u32[]{:S(2)}) collective-permute-start(bf16[2,128,128]{2,1,0:T(8,128)(2,1)S(1)} %get-tuple-element.53), channel_id=1, source_target_pairs={{0,16},{4,20},{8,24},{12,28},{16,0},{20,4},{24,8},{28,12},{1,17},{... | collective-permute-start | bytes 196616 | tf_op jit(solution)/shard_map/ppermute | solution.py:37
  18.7 3.0 %collective-permute-done.5.refs_4_ = bf16[2,128,128]{2,1,0:T(8,128)(2,1)S(1)} collective-permute-done((bf16[2,128,128]{2,1,0:T(8,128)(2,1)S(1)}, bf16[2,128,128]{2,1,0:T(8,128)(2,1)S(1)}, u32[]{:S(2)}, u32[]{:S(2)}) %collective-permute-start.5) | collective-permute-done | bytes 65568 | tf_op jit(solution)/shard_map/ppermute | solution.py:37
  21.7 2.6 %collective-permute-start.6 = (bf16[2,128,128]{2,1,0:T(8,128)(2,1)S(1)}, bf16[2,128,128]{2,1,0:T(8,128)(2,1)S(1)}, u32[]{:S(2)}, u32[]{:S(2)}) collective-permute-start(bf16[2,128,128]{2,1,0:T(8,128)(2,1)S(1)} %collective-permute-done.5.refs_4_), channel_id=1, source_target_pairs={{0,12},{4,8},{8,4},{12,0},{16,28},{20,24},{24,20},{28,16},{1,13},{... | collective-permute-start | bytes 196616 | tf_op jit(solution)/shard_map/ppermute | solution.py:37
  24.3 1.4 %collective-permute-start.7 = (bf16[2,128,128]{2,1,0:T(8,128)(2,1)S(1)}, bf16[2,128,128]{2,1,0:T(8,128)(2,1)S(1)}, u32[]{:S(2)}, u32[]{:S(2)}) collective-permute-start(bf16[2,128,128]{2,1,0:T(8,128)(2,1)S(1)} %collective-permute-done.5.refs_4_), channel_id=1, source_target_pairs={{0,4},{4,0},{8,12},{12,8},{16,20},{20,16},{24,28},{28,24},{1,5},{5... | collective-permute-start | bytes 196616 | tf_op jit(solution)/shard_map/ppermute | solution.py:37
  25.7 0.0 copy-done
  25.7 0.0 copy-done.1
  25.7 1.1 %intra.2 = (f32[256,512]{1,0:T(8,128)S(1)}, f32[256,512]{1,0:T(8,128)S(1)}) custom-call(s32[1]{0:T(128)} %bitcast.place_ref, bf16[512,1024]{1,0:T(8,128)(2,1)S(1)} %copy-done, f32[5,8,512]{2,1,0:T(8,128)S(1)} %copy-done.1, bf16[3,512,256]{2,1,0:T(8,128)(2,1)S(1)} %get-tuple-element.34.refs_0_, bf16[3,512,256]{2,1,0:T(8,128)(2,1)S(1)} %get-tuple-element.35.refs_1_), custom_call_target="tpu_custom_call" | custom-call | flops 402653184 | bytes 1048576 | tf_op jit(solution)/shard_map/intra/pallas_call | solution.py:213
  26.8 0.1 collective-permute-start.8
  26.9 1.1 %intra.3 = (f32[256,512]{1,0:T(8,128)S(1)}, f32[256,512]{1,0:T(8,128)S(1)}) custom-call(s32[1]{0:T(128)} %bitcast.place_ref, bf16[512,1024]{1,0:T(8,128)(2,1)S(1)} %copy-done, f32[5,8,512]{2,1,0:T(8,128)S(1)} %copy-done.1, bf16[3,512,256]{2,1,0:T(8,128)(2,1)S(1)} %get-tuple-element.34.refs_0_, bf16[3,512,256]{2,1,0:T(8,128)(2,1)S(1)} %get-tuple-element.35.refs_1_, ...), custom_call_target="tpu_custom_call" | custom-call | flops 402653184 | bytes 1048576 | tf_op jit(solution)/shard_map/intra/pallas_call | solution.py:213
  28.0 0.0 collective-permute-done.4.refs_3_
  28.0 0.8 %shard_map.55 = (f32[256,512]{1,0:T(8,128)S(1)}, f32[256,512]{1,0:T(8,128)S(1)}, f32[256,512]{1,0:T(8,128)S(1)}, f32[256,512]{1,0:T(8,128)S(1)}, f32[8,512]{1,0:T(8,128)S(1)}) custom-call(s32[1]{0:T(128)} %bitcast.place_ref, bf16[512,1024]{1,0:T(8,128)(2,1)S(1)} %copy-done, f32[5,8,512]{2,1,0:T(8,128)S(1)} %copy-done.1, ...), custom_call_target="tpu_custom_call" | custom-call | flops 268435456 | bytes 4194304 | tf_op jit(solution)/shard_map/pallas_call | solution.py:250
  28.9 0.0 collective-permute-done.6.refs_0_
  28.9 0.0 collective-permute-done.7.refs_1_
  28.9 0.3 shard_map.56
  29.3 1.9 %collective-permute-done.8.refs_0_ = bf16[2,128,128]{2,1,0:T(8,128)(2,1)S(1)} collective-permute-done((bf16[2,128,128]{2,1,0:T(8,128)(2,1)S(1)}, bf16[2,128,128]{2,1,0:T(8,128)(2,1)S(1)}, u32[]{:S(2)}, u32[]{:S(2)}) %collective-permute-start.8) | collective-permute-done | bytes 65568 | tf_op jit(solution)/shard_map/ppermute | solution.py:37
  31.2 0.3 shard_map.57
  31.4 0.1 collective-permute-start.9
  31.5 1.1 %collective-permute-done.9 = f32[1,512]{1,0:T(1,128)S(1)} collective-permute-done((f32[1,512]{1,0:T(1,128)S(1)}, f32[1,512]{1,0:T(1,128)S(1)}, u32[]{:S(2)}, u32[]{:S(2)}) %collective-permute-start.9) | collective-permute-done | bytes 2080 | tf_op jit(solution)/shard_map/ppermute | solution.py:37
  32.7 1.5 %collective-permute-start.10 = (f32[1,512]{1,0:T(1,128)S(1)}, f32[1,512]{1,0:T(1,128)S(1)}, u32[]{:S(2)}, u32[]{:S(2)}) collective-permute-start(f32[1,512]{1,0:T(1,128)S(1)} %add.26), channel_id=1, source_target_pairs={{0,2},{1,3},{2,0},{3,1},{4,6},{5,7},{6,4},{7,5},{8,10},{9,11},{10,... | collective-permute-start | bytes 6152 | tf_op jit(solution)/shard_map/ppermute | solution.py:37
  34.1 2.1 %collective-permute-done.10 = f32[1,512]{1,0:T(1,128)S(1)} collective-permute-done((f32[1,512]{1,0:T(1,128)S(1)}, f32[1,512]{1,0:T(1,128)S(1)}, u32[]{:S(2)}, u32[]{:S(2)}) %collective-permute-start.10) | collective-permute-done | bytes 2080 | tf_op jit(solution)/shard_map/ppermute | solution.py:37
  36.3 1.4 %norm.1 = bf16[512,1024]{1,0:T(8,128)(2,1)} custom-call(s32[1]{0:T(128)} %bitcast.place_ref, f32[256,512]{1,0:T(8,128)S(1)} %get-tuple-element.42.refs_0_, f32[256,512]{1,0:T(8,128)S(1)} %get-tuple-element.46.refs_1_, f32[256,512]{1,0:T(8,128)S(1)} %get-tuple-element.49.refs_2_, f32[256,512]{1,0:T(8,128)S(1)} %get-tuple-element.50.refs_3_, ...), custom_call_target="tpu_custom_call" | custom-call | flops 1048576 | bytes 1048576 | tf_op jit(solution)/shard_map/norm/pallas_call | solution.py:272
  (5 shorter events, 0.1 us)
Async XLA Ops:
  1.9 4.7 %copy-start.2 = (f32[1024]{0:T(1024)S(1)}, f32[1024]{0:T(1024)}, u32[]{:S(2)}) copy-start(f32[1024]{0:T(1024)} %param.9) | copy-start | bytes 12292
  1.9 8.0 %collective-permute-start = (bf16[2,128,128]{2,1,0:T(8,128)(2,1)S(1)}, bf16[2,128,128]{2,1,0:T(8,128)(2,1)S(1)}, u32[]{:S(2)}, u32[]{:S(2)}) collective-permute-start(bf16[2,128,128]{2,1,0:T(8,128)(2,1)S(1)} %get-tuple-element.29), channel_id=1, source_target_pairs={{0,4},{4,0},{8,12},{12,8},{16,20},{20,16},{24,28},{28,24},{1,5},{5... | collective-permute-start | bytes 196616 | tf_op jit(solution)/shard_map/ppermute | solution.py:37
  5.0 5.9 %collective-permute-start.3 = (bf16[2,128,128]{2,1,0:T(8,128)(2,1)S(1)}, bf16[2,128,128]{2,1,0:T(8,128)(2,1)S(1)}, u32[]{:S(2)}, u32[]{:S(2)}) collective-permute-start(bf16[2,128,128]{2,1,0:T(8,128)(2,1)S(1)} %get-tuple-element.30.three_ref), channel_id=1, source_target_pairs={{0,12},{4,8},{8,4},{12,0},{16,28},{20,24},{24,20},{28,16},{1,13},{... | collective-permute-start | bytes 196616 | tf_op jit(solution)/shard_map/ppermute | solution.py:37
  6.5 4.3 %collective-permute-start.2 = (bf16[2,128,128]{2,1,0:T(8,128)(2,1)S(1)}, bf16[2,128,128]{2,1,0:T(8,128)(2,1)S(1)}, u32[]{:S(2)}, u32[]{:S(2)}) collective-permute-start(bf16[2,128,128]{2,1,0:T(8,128)(2,1)S(1)} %get-tuple-element.31.two_ref), channel_id=1, source_target_pairs={{0,8},{4,12},{8,0},{12,4},{16,24},{20,28},{24,16},{28,20},{1,9},{5... | collective-permute-start | bytes 196616 | tf_op jit(solution)/shard_map/ppermute | solution.py:37
  7.9 17.8 %copy-start = (bf16[512,1024]{1,0:T(8,128)(2,1)S(1)}, bf16[512,1024]{1,0:T(8,128)(2,1)}, u32[]{:S(2)}) copy-start(bf16[512,1024]{1,0:T(8,128)(2,1)} %q_ref.9) | copy-start | bytes 3145732
  7.9 6.6 %collective-permute-start.1 = (bf16[6,128,128]{2,1,0:T(8,128)(2,1)S(1)}, bf16[6,128,128]{2,1,0:T(8,128)(2,1)S(1)}, u32[]{:S(2)}, u32[]{:S(2)}) collective-permute-start(bf16[6,128,128]{2,1,0:T(8,128)(2,1)S(1)} %get-tuple-element.32), channel_id=1, source_target_pairs={{0,4},{4,0},{8,12},{12,8},{16,20},{20,16},{24,28},{28,24},{1,5},{5... | collective-permute-start | bytes 589832 | tf_op jit(solution)/shard_map/ppermute | solution.py:37
  14.6 11.1 %copy-start.1 = (f32[5,8,512]{2,1,0:T(8,128)S(1)}, f32[5,8,512]{2,1,0:T(8,128)}, u32[]{:S(2)}) copy-start(f32[5,8,512]{2,1,0:T(8,128)} %w_ref.9) | copy-start | bytes 245764
  14.7 13.4 %collective-permute-start.4 = (bf16[6,128,128]{2,1,0:T(8,128)(2,1)S(1)}, bf16[6,128,128]{2,1,0:T(8,128)(2,1)S(1)}, u32[]{:S(2)}, u32[]{:S(2)}) collective-permute-start(bf16[6,128,128]{2,1,0:T(8,128)(2,1)S(1)} %pad_maximum_fusion), channel_id=1, source_target_pairs={{0,8},{4,12},{8,0},{12,4},{16,24},{20,28},{24,16},{28,20},{1,9},{5... | collective-permute-start | bytes 589832 | tf_op jit(solution)/shard_map/ppermute | solution.py:37
  16.1 5.6 %collective-permute-start.5 = (bf16[2,128,128]{2,1,0:T(8,128)(2,1)S(1)}, bf16[2,128,128]{2,1,0:T(8,128)(2,1)S(1)}, u32[]{:S(2)}, u32[]{:S(2)}) collective-permute-start(bf16[2,128,128]{2,1,0:T(8,128)(2,1)S(1)} %get-tuple-element.53), channel_id=1, source_target_pairs={{0,16},{4,20},{8,24},{12,28},{16,0},{20,4},{24,8},{28,12},{1,17},{... | collective-permute-start | bytes 196616 | tf_op jit(solution)/shard_map/ppermute | solution.py:37
  21.7 7.2 %collective-permute-start.6 = (bf16[2,128,128]{2,1,0:T(8,128)(2,1)S(1)}, bf16[2,128,128]{2,1,0:T(8,128)(2,1)S(1)}, u32[]{:S(2)}, u32[]{:S(2)}) collective-permute-start(bf16[2,128,128]{2,1,0:T(8,128)(2,1)S(1)} %collective-permute-done.5.refs_4_), channel_id=1, source_target_pairs={{0,12},{4,8},{8,4},{12,0},{16,28},{20,24},{24,20},{28,16},{1,13},{... | collective-permute-start | bytes 196616 | tf_op jit(solution)/shard_map/ppermute | solution.py:37
  24.3 4.6 %collective-permute-start.7 = (bf16[2,128,128]{2,1,0:T(8,128)(2,1)S(1)}, bf16[2,128,128]{2,1,0:T(8,128)(2,1)S(1)}, u32[]{:S(2)}, u32[]{:S(2)}) collective-permute-start(bf16[2,128,128]{2,1,0:T(8,128)(2,1)S(1)} %collective-permute-done.5.refs_4_), channel_id=1, source_target_pairs={{0,4},{4,0},{8,12},{12,8},{16,20},{20,16},{24,28},{28,24},{1,5},{5... | collective-permute-start | bytes 196616 | tf_op jit(solution)/shard_map/ppermute | solution.py:37
  26.8 4.3 %collective-permute-start.8 = (bf16[2,128,128]{2,1,0:T(8,128)(2,1)S(1)}, bf16[2,128,128]{2,1,0:T(8,128)(2,1)S(1)}, u32[]{:S(2)}, u32[]{:S(2)}) collective-permute-start(bf16[2,128,128]{2,1,0:T(8,128)(2,1)S(1)} %collective-permute-done.5.refs_4_), channel_id=1, source_target_pairs={{0,8},{4,12},{8,0},{12,4},{16,24},{20,28},{24,16},{28,20},{1,9},{5... | collective-permute-start | bytes 196616 | tf_op jit(solution)/shard_map/ppermute | solution.py:37
  31.4 1.2 %collective-permute-start.9 = (f32[1,512]{1,0:T(1,128)S(1)}, f32[1,512]{1,0:T(1,128)S(1)}, u32[]{:S(2)}, u32[]{:S(2)}) collective-permute-start(f32[1,512]{1,0:T(1,128)S(1)} %get-tuple-element.51), channel_id=1, source_target_pairs={{0,1},{1,0},{2,3},{3,2},{4,5},{5,4},{6,7},{7,6},{8,9},{9,8},{10,11... | collective-permute-start | bytes 6152 | tf_op jit(solution)/shard_map/ppermute | solution.py:37
  32.7 3.6 %collective-permute-start.10 = (f32[1,512]{1,0:T(1,128)S(1)}, f32[1,512]{1,0:T(1,128)S(1)}, u32[]{:S(2)}, u32[]{:S(2)}) collective-permute-start(f32[1,512]{1,0:T(1,128)S(1)} %add.26), channel_id=1, source_target_pairs={{0,2},{1,3},{2,0},{3,1},{4,6},{5,7},{6,4},{7,5},{8,10},{9,11},{10,... | collective-permute-start | bytes 6152 | tf_op jit(solution)/shard_map/ppermute | solution.py:37

commit v4 on v3

--- a/solution.py
+++ b/solution.py
@@ -32,9 +32,9 @@
     return pl.CostEstimate(flops=flops, bytes_accessed=moved, transcendentals=0)
 
 
-def exchanged(block, axis, mask):
+def exchanged(block, axis, mask, lowest=0):
     count = lax.axis_size(axis)
-    return lax.ppermute(block, axis, [(i, i ^ mask) for i in range(count)])
+    return lax.ppermute(block, axis, [(i, i ^ mask) for i in range(lowest, count)])
 
 
 def nt(a, b):
@@ -230,14 +230,10 @@
         upper.append(came)
         running = running + came.astype(F32)
     top = jnp.concatenate(upper, axis=0) if len(upper) > 1 else upper[0]
-    tops = {0: top} | {r: exchanged(top, "seq", r) for r in (3, 1, 2)}
-
-    sums = [
-        three.astype(F32) + near[2 * group :].astype(F32),
-        pair,
-        one.astype(F32) + near[:group].astype(F32),
-    ]
-    middle = exchanged(jnp.concatenate(sums, axis=0).astype(BF16), "seq", 2)
+    tops = {0: top} | {r: exchanged(top, "seq", r, QUAD) for r in (3, 1, 2)}
+
+    left_pair = jnp.where(position >> 1 & 1 == 1, other, pair).astype(BF16)
+    middle = {0: left_pair} | {r: exchanged(left_pair, "seq", r) for r in (3, 1, 2)}
 
     def top_reads(ref):
         return tuple((bit, ref, (bit - 2) * group) for bit in range(2, seq_bits))
@@ -258,9 +254,9 @@
         totals.update({r: out for (r, _, _), out in zip(work, outs)})
         return outs[n]
 
-    below = {0: ((0, 0, 0), (1, 2, 0))} | {r: ((0, 1, (r - 1) * group), (1, 3, (r - 1) * group)) for r in (1, 2, 3)}
-    work = tuple((r, r == 0, below[r] + (top_reads(4) if r == 0 else ())) for r in (3, 1, 2, 0))
-    squares = readout(work, (got1, near, other.astype(BF16), middle, top), None)
+    below = {0: ((0, 0, 0), (1, 2, 0))} | {r: ((0, 1, (r - 1) * group), (1, 2 + r, 0)) for r in (1, 2, 3)}
+    work = tuple((r, r == 0, below[r] + (top_reads(6) if r == 0 else ())) for r in (3, 1, 2, 0))
+    squares = readout(work, (got1, near, *(middle[r] for r in range(QUAD)), top), None)
     squares = readout(((3, True, top_reads(0)), (1, True, top_reads(1))), (tops[3], tops[1]), squares)
     squares = readout(((2, True, top_reads(0)),), (tops[2],), squares, finish=True)
 

time: 37.8 us -> 38.1 us (level)
  the two profiles are of different devices: /device:TPU:0 before, /device:TPU:24 now
where the time goes in v4:
time: 38.1 us; the launch traced here: 37.5 us
  starting transfers between devices  19.8 us (52%)
  Pallas kernels  10.6 us (28%)
  waiting for transfers between devices  5.99 us (16%)
  other arithmetic  0.96 us (3%)
    ppermute x13, starting transfers between devices, exchanged(): lax.ppermute(block, axis, [(i, i ^ mask) for i in range(lowest, count)])  19.8 us
    ppermute x13, waiting for transfers between devices, exchanged(): lax.ppermute(block, axis, [(i, i ^ mask) for i in range(lowest, count)])  5.99 us
    pallas_call x1, Pallas kernels, local(): pl.pallas_call(functools.partial(own_kernel, group), out_shape=(sds((1,)...  2.98 us
    pallas_call x1, Pallas kernels, local(): pl.pallas_call(functools.partial(sent_kernel, group, groups), out_shape=(...  2.54 us
    pallas_call x2, Pallas kernels, local(): pl.pallas_call(functools.partial(intra_kernel, group, work), out_shape=(p...  2.23 us
    pallas_call x3, Pallas kernels, readout(): pl.pallas_call(kernel, out_shape=tuple(shapes), in_specs=[SMEM] + [VMEM]...  1.45 us
    pallas_call x1, Pallas kernels, local(): pl.pallas_call(functools.partial(norm_kernel, group, full_width), out_sha...  1.36 us
    convert_element_type x1, other arithmetic, local(): came = exchanged(running.astype(BF16), 'seq', 1 << bit)  0.95 us
  transfers between devices with their start and end apart: 13, of which 4 were waited for; matrix products, arithmetic and copies ran while one was open for 3% of the time, Pallas kernels for 17%

profile of v4, /device:TPU:24, one launch (start us, length us, event | category | flops | bytes accessed | tf_op | source)
XLA Modules:
  0.0 37.5 jit_solution(7784932136993411452)
XLA Ops:
  0.0 2.5 %sent.1 = (bf16[3,512,256]{2,1,0:T(8,128)(2,1)S(1)}, bf16[3,512,256]{2,1,0:T(8,128)(2,1)S(1)}, bf16[2,128,128]{2,1,0:T(8,128)(2,1)}, bf16[2,128,128]{2,1,0:T(8,128)(2,1)}, bf16[2,128,128]{2,1,0:T(8,128)(2,1)}) custom-call(s32[1]{0:T(128)} %bitcast.place_ref, bf16[512,1024]{1,0:T(8,128)(2,1)} %k_hbm.3, bf16[512,1024]{1,0:T(8,128)(2,1)} %v_hbm.3), custom_call_target="tpu_custom_call" | custom-call | flops 100663296 | bytes 1572864 | tf_op jit(solution)/shard_map/sent/pallas_call | solution.py:181
  2.5 0.0 copy-start.2
  2.6 1.6 %collective-permute-start = (bf16[2,128,128]{2,1,0:T(8,128)(2,1)}, bf16[2,128,128]{2,1,0:T(8,128)(2,1)S(1)}, u32[]{:S(2)}, u32[]{:S(2)}) collective-permute-start(bf16[2,128,128]{2,1,0:T(8,128)(2,1)} %get-tuple-element.29), channel_id=1, source_target_pairs={{0,4},{4,0},{8,12},{12,8},{16,20},{20,16},{24,28},{28,24},{1,5},{5... | collective-permute-start | bytes 196616 | tf_op jit(solution)/shard_map/ppermute | solution.py:37
  4.1 0.4 %collective-permute-start.2 = (bf16[2,128,128]{2,1,0:T(8,128)(2,1)}, bf16[2,128,128]{2,1,0:T(8,128)(2,1)}, u32[]{:S(2)}, u32[]{:S(2)}) collective-permute-start(bf16[2,128,128]{2,1,0:T(8,128)(2,1)} %get-tuple-element.31.two_ref), channel_id=1, source_target_pairs={{0,8},{4,12},{8,0},{12,4},{16,24},{20,28},{24,16},{28,20},{1,9},{5... | collective-permute-start | bytes 196616 | tf_op jit(solution)/shard_map/ppermute | solution.py:37
  4.6 1.5 %collective-permute-start.3 = (bf16[2,128,128]{2,1,0:T(8,128)(2,1)}, bf16[2,128,128]{2,1,0:T(8,128)(2,1)}, u32[]{:S(2)}, u32[]{:S(2)}) collective-permute-start(bf16[2,128,128]{2,1,0:T(8,128)(2,1)} %get-tuple-element.30.three_ref), channel_id=1, source_target_pairs={{0,12},{4,8},{8,4},{12,0},{16,28},{20,24},{24,20},{28,16},{1,13},{... | collective-permute-start | bytes 196616 | tf_op jit(solution)/shard_map/ppermute | solution.py:37
  6.1 0.0 copy-done.2
  6.1 0.0 copy-start
  6.1 3.0 %own.1 = (bf16[1,512,256]{2,1,0:T(8,128)(2,1)S(1)}, bf16[1,512,256]{2,1,0:T(8,128)(2,1)S(1)}, f32[1,1024]{1,0:T(1,128)S(1)}, f32[2,128,128]{2,1,0:T(8,128)S(1)}, bf16[6,128,128]{2,1,0:T(8,128)(2,1)}) custom-call(s32[1]{0:T(128)} %bitcast.place_ref, bf16[512,1024]{1,0:T(8,128)(2,1)} %k_hbm.3, bf16[512,1024]{1,0:T(8,128)(2,1)} %v_hbm.3, ...), custom_call_target="tpu_custom_call" | custom-call | flops 33554432 | bytes 524288 | tf_op jit(solution)/shard_map/own/pallas_call | solution.py:196
  9.1 1.6 %collective-permute-start.1 = (bf16[6,128,128]{2,1,0:T(8,128)(2,1)}, bf16[6,128,128]{2,1,0:T(8,128)(2,1)S(1)}, u32[]{:S(2)}, u32[]{:S(2)}) collective-permute-start(bf16[6,128,128]{2,1,0:T(8,128)(2,1)} %get-tuple-element.32), channel_id=1, source_target_pairs={{0,4},{4,0},{8,12},{12,8},{16,20},{20,16},{24,28},{28,24},{1,5},{5... | collective-permute-start | bytes 589832 | tf_op jit(solution)/shard_map/ppermute | solution.py:37
  10.7 0.0 collective-permute-done.refs_0_
  10.7 0.0 collective-permute-done.2
  10.7 0.0 collective-permute-done.3
  10.7 0.0 copy-start.1
  10.7 0.9 %add_convert_fusion = (bf16[2,128,128]{2,1,0:T(8,128)(2,1)S(1)}, bf16[2,128,128]{2,1,0:T(8,128)(2,1)S(1)}) fusion(bf16[2,128,128]{2,1,0:T(8,128)(2,1)} %collective-permute-done.3, bf16[2,128,128]{2,1,0:T(8,128)(2,1)} %collective-permute-done.2, f32[2,128,128]{2,1,0:T(8,128)S(1)} %get-tuple-element.33, bf16[2,128,128]{2,1,0:T(8,128)(2,1)S(1)} %collective-permute-done.refs_0_, ...), kind=kLoop, calls=%fused_computation | loop fusion | flops 294912 | bytes 458753 | tf_op jit(solution)/shard_map/convert_element_type | solution.py:229
  11.7 0.4 %collective-permute-start.7 = (bf16[2,128,128]{2,1,0:T(8,128)(2,1)S(1)}, bf16[2,128,128]{2,1,0:T(8,128)(2,1)S(1)}, u32[]{:S(2)}, u32[]{:S(2)}) collective-permute-start(bf16[2,128,128]{2,1,0:T(8,128)(2,1)S(1)} %get-tuple-element.53), channel_id=1, source_target_pairs={{0,16},{4,20},{8,24},{12,28},{16,0},{20,4},{24,8},{28,12},{1,17},{... | collective-permute-start | bytes 196616 | tf_op jit(solution)/shard_map/ppermute | solution.py:37
  12.1 0.5 %collective-permute-start.4 = (bf16[2,128,128]{2,1,0:T(8,128)(2,1)S(1)}, bf16[2,128,128]{2,1,0:T(8,128)(2,1)S(1)}, u32[]{:S(2)}, u32[]{:S(2)}) collective-permute-start(bf16[2,128,128]{2,1,0:T(8,128)(2,1)S(1)} %get-tuple-element.54.refs_2_), channel_id=1, source_target_pairs={{0,4},{4,0},{8,12},{12,8},{16,20},{20,16},{24,28},{28,24},{1,5},{5... | collective-permute-start | bytes 196616 | tf_op jit(solution)/shard_map/ppermute | solution.py:37
  12.6 0.9 %collective-permute-start.5 = (bf16[2,128,128]{2,1,0:T(8,128)(2,1)S(1)}, bf16[2,128,128]{2,1,0:T(8,128)(2,1)S(1)}, u32[]{:S(2)}, u32[]{:S(2)}) collective-permute-start(bf16[2,128,128]{2,1,0:T(8,128)(2,1)S(1)} %get-tuple-element.54.refs_2_), channel_id=1, source_target_pairs={{0,8},{4,12},{8,0},{12,4},{16,24},{20,28},{24,16},{28,20},{1,9},{5... | collective-permute-start | bytes 196616 | tf_op jit(solution)/shard_map/ppermute | solution.py:37
  13.5 2.0 %collective-permute-start.6 = (bf16[2,128,128]{2,1,0:T(8,128)(2,1)S(1)}, bf16[2,128,128]{2,1,0:T(8,128)(2,1)S(1)}, u32[]{:S(2)}, u32[]{:S(2)}) collective-permute-start(bf16[2,128,128]{2,1,0:T(8,128)(2,1)S(1)} %get-tuple-element.54.refs_2_), channel_id=1, source_target_pairs={{0,12},{4,8},{8,4},{12,0},{16,28},{20,24},{24,20},{28,16},{1,13},{... | collective-permute-start | bytes 196616 | tf_op jit(solution)/shard_map/ppermute | solution.py:37
  15.6 1.6 %collective-permute-done.7.refs_6_ = bf16[2,128,128]{2,1,0:T(8,128)(2,1)S(1)} collective-permute-done((bf16[2,128,128]{2,1,0:T(8,128)(2,1)S(1)}, bf16[2,128,128]{2,1,0:T(8,128)(2,1)S(1)}, u32[]{:S(2)}, u32[]{:S(2)}) %collective-permute-start.7) | collective-permute-done | bytes 65568 | tf_op jit(solution)/shard_map/ppermute | solution.py:37
  17.2 3.2 %collective-permute-start.8 = (bf16[2,128,128]{2,1,0:T(8,128)(2,1)S(1)}, bf16[2,128,128]{2,1,0:T(8,128)(2,1)S(1)}, u32[]{:S(2)}, u32[]{:S(2)}) collective-permute-start(bf16[2,128,128]{2,1,0:T(8,128)(2,1)S(1)} %collective-permute-done.7.refs_6_), channel_id=1, source_target_pairs={{16,28},{20,24},{24,20},{28,16},{17,29},{21,25},{25,21},{29,17},{1... | collective-permute-start | bytes 196616 | tf_op jit(solution)/shard_map/ppermute | solution.py:37
  20.4 0.0 collective-permute-done.4.refs_3_
  20.4 3.3 %collective-permute-start.9 = (bf16[2,128,128]{2,1,0:T(8,128)(2,1)S(1)}, bf16[2,128,128]{2,1,0:T(8,128)(2,1)S(1)}, u32[]{:S(2)}, u32[]{:S(2)}) collective-permute-start(bf16[2,128,128]{2,1,0:T(8,128)(2,1)S(1)} %collective-permute-done.7.refs_6_), channel_id=1, source_target_pairs={{16,20},{20,16},{24,28},{28,24},{17,21},{21,17},{25,29},{29,25},{1... | collective-permute-start | bytes 196616 | tf_op jit(solution)/shard_map/ppermute | solution.py:37
  23.7 0.0 copy-done
  23.7 0.0 copy-done.1
  23.8 1.1 %intra.2 = (f32[256,512]{1,0:T(8,128)S(1)}, f32[256,512]{1,0:T(8,128)S(1)}) custom-call(s32[1]{0:T(128)} %bitcast.place_ref, bf16[512,1024]{1,0:T(8,128)(2,1)S(1)} %copy-done, f32[5,8,512]{2,1,0:T(8,128)S(1)} %copy-done.1, bf16[3,512,256]{2,1,0:T(8,128)(2,1)S(1)} %get-tuple-element.34.refs_0_, bf16[3,512,256]{2,1,0:T(8,128)(2,1)S(1)} %get-tuple-element.35.refs_1_), custom_call_target="tpu_custom_call" | custom-call | flops 402653184 | bytes 1048576 | tf_op jit(solution)/shard_map/intra/pallas_call | solution.py:213
  24.9 0.0 collective-permute-done.5.refs_4_
  24.9 2.7 %collective-permute-start.10 = (bf16[2,128,128]{2,1,0:T(8,128)(2,1)S(1)}, bf16[2,128,128]{2,1,0:T(8,128)(2,1)S(1)}, u32[]{:S(2)}, u32[]{:S(2)}) collective-permute-start(bf16[2,128,128]{2,1,0:T(8,128)(2,1)S(1)} %collective-permute-done.7.refs_6_), channel_id=1, source_target_pairs={{16,24},{20,28},{24,16},{28,20},{17,25},{21,29},{25,17},{29,21},{1... | collective-permute-start | bytes 196616 | tf_op jit(solution)/shard_map/ppermute | solution.py:37
  27.6 1.1 %intra.3 = (f32[256,512]{1,0:T(8,128)S(1)}, f32[256,512]{1,0:T(8,128)S(1)}) custom-call(s32[1]{0:T(128)} %bitcast.place_ref, bf16[512,1024]{1,0:T(8,128)(2,1)S(1)} %copy-done, f32[5,8,512]{2,1,0:T(8,128)S(1)} %copy-done.1, bf16[3,512,256]{2,1,0:T(8,128)(2,1)S(1)} %get-tuple-element.34.refs_0_, bf16[3,512,256]{2,1,0:T(8,128)(2,1)S(1)} %get-tuple-element.35.refs_1_, ...), custom_call_target="tpu_custom_call" | custom-call | flops 402653184 | bytes 1048576 | tf_op jit(solution)/shard_map/intra/pallas_call | solution.py:213
  28.7 0.0 collective-permute-done.6.refs_5_
  28.7 0.0 collective-permute-done.1.refs_1_
  28.7 0.9 %shard_map.55 = (f32[256,512]{1,0:T(8,128)S(1)}, f32[256,512]{1,0:T(8,128)S(1)}, f32[256,512]{1,0:T(8,128)S(1)}, f32[256,512]{1,0:T(8,128)S(1)}, f32[8,512]{1,0:T(8,128)S(1)}) custom-call(s32[1]{0:T(128)} %bitcast.place_ref, bf16[512,1024]{1,0:T(8,128)(2,1)S(1)} %copy-done, f32[5,8,512]{2,1,0:T(8,128)S(1)} %copy-done.1, ...), custom_call_target="tpu_custom_call" | custom-call | flops 268435456 | bytes 4194304 | tf_op jit(solution)/shard_map/pallas_call | solution.py:246
  29.6 0.0 collective-permute-done.8.refs_0_
  29.6 0.0 collective-permute-done.9.refs_1_
  29.6 0.3 shard_map.56
  30.0 1.1 %collective-permute-done.10.refs_0_ = bf16[2,128,128]{2,1,0:T(8,128)(2,1)S(1)} collective-permute-done((bf16[2,128,128]{2,1,0:T(8,128)(2,1)S(1)}, bf16[2,128,128]{2,1,0:T(8,128)(2,1)S(1)}, u32[]{:S(2)}, u32[]{:S(2)}) %collective-permute-start.10) | collective-permute-done | bytes 65568 | tf_op jit(solution)/shard_map/ppermute | solution.py:37
  31.0 0.3 shard_map.57
  31.3 0.1 collective-permute-start.11
  31.4 1.1 %collective-permute-done.11 = f32[1,512]{1,0:T(1,128)S(1)} collective-permute-done((f32[1,512]{1,0:T(1,128)S(1)}, f32[1,512]{1,0:T(1,128)S(1)}, u32[]{:S(2)}, u32[]{:S(2)}) %collective-permute-start.11) | collective-permute-done | bytes 2080 | tf_op jit(solution)/shard_map/ppermute | solution.py:37
  32.5 1.5 %collective-permute-start.12 = (f32[1,512]{1,0:T(1,128)S(1)}, f32[1,512]{1,0:T(1,128)S(1)}, u32[]{:S(2)}, u32[]{:S(2)}) collective-permute-start(f32[1,512]{1,0:T(1,128)S(1)} %add.18), channel_id=1, source_target_pairs={{0,2},{1,3},{2,0},{3,1},{4,6},{5,7},{6,4},{7,5},{8,10},{9,11},{10,... | collective-permute-start | bytes 6152 | tf_op jit(solution)/shard_map/ppermute | solution.py:37
  34.0 2.1 %collective-permute-done.12 = f32[1,512]{1,0:T(1,128)S(1)} collective-permute-done((f32[1,512]{1,0:T(1,128)S(1)}, f32[1,512]{1,0:T(1,128)S(1)}, u32[]{:S(2)}, u32[]{:S(2)}) %collective-permute-start.12) | collective-permute-done | bytes 2080 | tf_op jit(solution)/shard_map/ppermute | solution.py:37
  36.1 1.4 %norm.1 = bf16[512,1024]{1,0:T(8,128)(2,1)} custom-call(s32[1]{0:T(128)} %bitcast.place_ref, f32[256,512]{1,0:T(8,128)S(1)} %get-tuple-element.42.refs_0_, f32[256,512]{1,0:T(8,128)S(1)} %get-tuple-element.46.refs_1_, f32[256,512]{1,0:T(8,128)S(1)} %get-tuple-element.49.refs_2_, f32[256,512]{1,0:T(8,128)S(1)} %get-tuple-element.50.refs_3_, ...), custom_call_target="tpu_custom_call" | custom-call | flops 1048576 | bytes 1048576 | tf_op jit(solution)/shard_map/norm/pallas_call | solution.py:268
  (2 shorter events, 0.0 us)
Async XLA Ops:
  2.5 3.6 %copy-start.2 = (f32[1024]{0:T(1024)S(1)}, f32[1024]{0:T(1024)}, u32[]{:S(2)}) copy-start(f32[1024]{0:T(1024)} %param.9) | copy-start | bytes 12292
  2.6 8.1 %collective-permute-start = (bf16[2,128,128]{2,1,0:T(8,128)(2,1)}, bf16[2,128,128]{2,1,0:T(8,128)(2,1)S(1)}, u32[]{:S(2)}, u32[]{:S(2)}) collective-permute-start(bf16[2,128,128]{2,1,0:T(8,128)(2,1)} %get-tuple-element.29), channel_id=1, source_target_pairs={{0,4},{4,0},{8,12},{12,8},{16,20},{20,16},{24,28},{28,24},{1,5},{5... | collective-permute-start | bytes 196616 | tf_op jit(solution)/shard_map/ppermute | solution.py:37
  4.1 6.5 %collective-permute-start.2 = (bf16[2,128,128]{2,1,0:T(8,128)(2,1)}, bf16[2,128,128]{2,1,0:T(8,128)(2,1)}, u32[]{:S(2)}, u32[]{:S(2)}) collective-permute-start(bf16[2,128,128]{2,1,0:T(8,128)(2,1)} %get-tuple-element.31.two_ref), channel_id=1, source_target_pairs={{0,8},{4,12},{8,0},{12,4},{16,24},{20,28},{24,16},{28,20},{1,9},{5... | collective-permute-start | bytes 196616 | tf_op jit(solution)/shard_map/ppermute | solution.py:37
  4.6 6.1 %collective-permute-start.3 = (bf16[2,128,128]{2,1,0:T(8,128)(2,1)}, bf16[2,128,128]{2,1,0:T(8,128)(2,1)}, u32[]{:S(2)}, u32[]{:S(2)}) collective-permute-start(bf16[2,128,128]{2,1,0:T(8,128)(2,1)} %get-tuple-element.30.three_ref), channel_id=1, source_target_pairs={{0,12},{4,8},{8,4},{12,0},{16,28},{20,24},{24,20},{28,16},{1,13},{... | collective-permute-start | bytes 196616 | tf_op jit(solution)/shard_map/ppermute | solution.py:37
  6.1 17.6 %copy-start = (bf16[512,1024]{1,0:T(8,128)(2,1)S(1)}, bf16[512,1024]{1,0:T(8,128)(2,1)}, u32[]{:S(2)}) copy-start(bf16[512,1024]{1,0:T(8,128)(2,1)} %q_ref.9) | copy-start | bytes 3145732
  9.1 19.6 %collective-permute-start.1 = (bf16[6,128,128]{2,1,0:T(8,128)(2,1)}, bf16[6,128,128]{2,1,0:T(8,128)(2,1)S(1)}, u32[]{:S(2)}, u32[]{:S(2)}) collective-permute-start(bf16[6,128,128]{2,1,0:T(8,128)(2,1)} %get-tuple-element.32), channel_id=1, source_target_pairs={{0,4},{4,0},{8,12},{12,8},{16,20},{20,16},{24,28},{28,24},{1,5},{5... | collective-permute-start | bytes 589832 | tf_op jit(solution)/shard_map/ppermute | solution.py:37
  10.7 13.0 %copy-start.1 = (f32[5,8,512]{2,1,0:T(8,128)S(1)}, f32[5,8,512]{2,1,0:T(8,128)}, u32[]{:S(2)}) copy-start(f32[5,8,512]{2,1,0:T(8,128)} %w_ref.9) | copy-start | bytes 245764
  11.7 5.5 %collective-permute-start.7 = (bf16[2,128,128]{2,1,0:T(8,128)(2,1)S(1)}, bf16[2,128,128]{2,1,0:T(8,128)(2,1)S(1)}, u32[]{:S(2)}, u32[]{:S(2)}) collective-permute-start(bf16[2,128,128]{2,1,0:T(8,128)(2,1)S(1)} %get-tuple-element.53), channel_id=1, source_target_pairs={{0,16},{4,20},{8,24},{12,28},{16,0},{20,4},{24,8},{28,12},{1,17},{... | collective-permute-start | bytes 196616 | tf_op jit(solution)/shard_map/ppermute | solution.py:37
  12.1 8.3 %collective-permute-start.4 = (bf16[2,128,128]{2,1,0:T(8,128)(2,1)S(1)}, bf16[2,128,128]{2,1,0:T(8,128)(2,1)S(1)}, u32[]{:S(2)}, u32[]{:S(2)}) collective-permute-start(bf16[2,128,128]{2,1,0:T(8,128)(2,1)S(1)} %get-tuple-element.54.refs_2_), channel_id=1, source_target_pairs={{0,4},{4,0},{8,12},{12,8},{16,20},{20,16},{24,28},{28,24},{1,5},{5... | collective-permute-start | bytes 196616 | tf_op jit(solution)/shard_map/ppermute | solution.py:37
  12.6 12.3 %collective-permute-start.5 = (bf16[2,128,128]{2,1,0:T(8,128)(2,1)S(1)}, bf16[2,128,128]{2,1,0:T(8,128)(2,1)S(1)}, u32[]{:S(2)}, u32[]{:S(2)}) collective-permute-start(bf16[2,128,128]{2,1,0:T(8,128)(2,1)S(1)} %get-tuple-element.54.refs_2_), channel_id=1, source_target_pairs={{0,8},{4,12},{8,0},{12,4},{16,24},{20,28},{24,16},{28,20},{1,9},{5... | collective-permute-start | bytes 196616 | tf_op jit(solution)/shard_map/ppermute | solution.py:37
  13.5 15.2 %collective-permute-start.6 = (bf16[2,128,128]{2,1,0:T(8,128)(2,1)S(1)}, bf16[2,128,128]{2,1,0:T(8,128)(2,1)S(1)}, u32[]{:S(2)}, u32[]{:S(2)}) collective-permute-start(bf16[2,128,128]{2,1,0:T(8,128)(2,1)S(1)} %get-tuple-element.54.refs_2_), channel_id=1, source_target_pairs={{0,12},{4,8},{8,4},{12,0},{16,28},{20,24},{24,20},{28,16},{1,13},{... | collective-permute-start | bytes 196616 | tf_op jit(solution)/shard_map/ppermute | solution.py:37
  17.2 12.4 %collective-permute-start.8 = (bf16[2,128,128]{2,1,0:T(8,128)(2,1)S(1)}, bf16[2,128,128]{2,1,0:T(8,128)(2,1)S(1)}, u32[]{:S(2)}, u32[]{:S(2)}) collective-permute-start(bf16[2,128,128]{2,1,0:T(8,128)(2,1)S(1)} %collective-permute-done.7.refs_6_), channel_id=1, source_target_pairs={{16,28},{20,24},{24,20},{28,16},{17,29},{21,25},{25,21},{29,17},{1... | collective-permute-start | bytes 196616 | tf_op jit(solution)/shard_map/ppermute | solution.py:37
  20.4 9.2 %collective-permute-start.9 = (bf16[2,128,128]{2,1,0:T(8,128)(2,1)S(1)}, bf16[2,128,128]{2,1,0:T(8,128)(2,1)S(1)}, u32[]{:S(2)}, u32[]{:S(2)}) collective-permute-start(bf16[2,128,128]{2,1,0:T(8,128)(2,1)S(1)} %collective-permute-done.7.refs_6_), channel_id=1, source_target_pairs={{16,20},{20,16},{24,28},{28,24},{17,21},{21,17},{25,29},{29,25},{1... | collective-permute-start | bytes 196616 | tf_op jit(solution)/shard_map/ppermute | solution.py:37
  24.9 6.2 %collective-permute-start.10 = (bf16[2,128,128]{2,1,0:T(8,128)(2,1)S(1)}, bf16[2,128,128]{2,1,0:T(8,128)(2,1)S(1)}, u32[]{:S(2)}, u32[]{:S(2)}) collective-permute-start(bf16[2,128,128]{2,1,0:T(8,128)(2,1)S(1)} %collective-permute-done.7.refs_6_), channel_id=1, source_target_pairs={{16,24},{20,28},{24,16},{28,20},{17,25},{21,29},{25,17},{29,21},{1... | collective-permute-start | bytes 196616 | tf_op jit(solution)/shard_map/ppermute | solution.py:37
  31.3 1.2 %collective-permute-start.11 = (f32[1,512]{1,0:T(1,128)S(1)}, f32[1,512]{1,0:T(1,128)S(1)}, u32[]{:S(2)}, u32[]{:S(2)}) collective-permute-start(f32[1,512]{1,0:T(1,128)S(1)} %get-tuple-element.51), channel_id=1, source_target_pairs={{0,1},{1,0},{2,3},{3,2},{4,5},{5,4},{6,7},{7,6},{8,9},{9,8},{10,11... | collective-permute-start | bytes 6152 | tf_op jit(solution)/shard_map/ppermute | solution.py:37
  32.5 3.6 %collective-permute-start.12 = (f32[1,512]{1,0:T(1,128)S(1)}, f32[1,512]{1,0:T(1,128)S(1)}, u32[]{:S(2)}, u32[]{:S(2)}) collective-permute-start(f32[1,512]{1,0:T(1,128)S(1)} %add.18), channel_id=1, source_target_pairs={{0,2},{1,3},{2,0},{3,1},{4,6},{5,7},{6,4},{7,5},{8,10},{9,11},{10,... | collective-permute-start | bytes 6152 | tf_op jit(solution)/shard_map/ppermute | solution.py:37

commit v5 on v4

--- a/solution.py
+++ b/solution.py
@@ -32,9 +32,19 @@
     return pl.CostEstimate(flops=flops, bytes_accessed=moved, transcendentals=0)
 
 
-def exchanged(block, axis, mask, lowest=0):
+def exchanged(block, axis, mask):
     count = lax.axis_size(axis)
-    return lax.ppermute(block, axis, [(i, i ^ mask) for i in range(lowest, count)])
+    return lax.ppermute(block, axis, [(i, i ^ mask) for i in range(count)])
+
+
+def exchanged_above(block, mask):
+    seq, head = lax.axis_size("seq"), lax.axis_size("head")
+    route = []
+    for s in range(seq):
+        for h in range(head):
+            to = (s ^ mask, h) if s >= QUAD else (s, h ^ 1)
+            route.append((s * head + h, to[0] * head + to[1]))
+    return lax.ppermute(block, ("seq", "head"), route)
 
 
 def nt(a, b):
@@ -90,6 +100,16 @@
 
     states_of(group, (0,), place_ref[0] & (QUAD - 1), k_hbm, v_hbm, k_ref, v_ref, sems, use)
     gain.wait()
+
+
+def sums_kernel(place_ref, own_ref, one_ref, two_ref, three_ref, sent_ref, left_ref, *total_refs):
+    pair = own_ref[...] + one_ref[...].astype(F32)
+    other = two_ref[...].astype(F32) + three_ref[...].astype(F32)
+    total = pair + other
+    for total_ref in total_refs:
+        total_ref[...] = total
+    sent_ref[...] = total.astype(BF16)
+    left_ref[...] = jnp.where(place_ref[0] >> 1 & 1 == 1, other, pair).astype(BF16)
 
 
 def intra_kernel(group, work, place_ref, q_ref, w_ref, *refs):
@@ -221,18 +241,24 @@
         )(place, queries, level_weights, *sources)
         totals |= {r: out for (r, _, _), out in zip(work, outs)}
 
-    pair = own + got1.astype(F32)
-    other = got2.astype(F32) + got3.astype(F32)
-    running = pair + other
+    sums, left_pair, *running = pl.pallas_call(
+        sums_kernel,
+        out_shape=(sds(block, BF16), sds(block, BF16)) + (sds(block, F32),) * (seq_bits > 3),
+        in_specs=[SMEM] + [VMEM] * 4,
+        out_specs=(VMEM,) * (2 + (seq_bits > 3)),
+        compiler_params=params(),
+        cost_estimate=cost(4 * group * HEAD_DIM**2, 16 * group * HEAD_DIM**2),
+        name="sums",
+    )(place, own, got1, got2, got3)
     upper = []
     for bit in range(2, seq_bits):
-        came = exchanged(running.astype(BF16), "seq", 1 << bit)
-        upper.append(came)
-        running = running + came.astype(F32)
+        if bit > 2:
+            running = [running[0] + upper[-1].astype(F32)]
+            sums = running[0].astype(BF16)
+        upper.append(exchanged(sums, "seq", 1 << bit))
     top = jnp.concatenate(upper, axis=0) if len(upper) > 1 else upper[0]
-    tops = {0: top} | {r: exchanged(top, "seq", r, QUAD) for r in (3, 1, 2)}
-
-    left_pair = jnp.where(position >> 1 & 1 == 1, other, pair).astype(BF16)
+    tops = {0: top} | {r: exchanged_above(top, r) for r in (3, 1, 2)}
+
     middle = {0: left_pair} | {r: exchanged(left_pair, "seq", r) for r in (3, 1, 2)}
 
     def top_reads(ref):

time: 38.1 us -> 30 us (0.79); the launches traced: 37.5 us -> 29.9 us
  starting transfers between devices: 19.8 us -> 14.2 us
  Pallas kernels: 10.6 us -> 8.4 us
  waiting for transfers between devices: 5.99 us -> 7.17 us
  other arithmetic: 0.96 us -> 0.01 us
    ppermute x13, starting transfers between devices: 19.8 us -> 14.2 us  [the longest x10 10.6 us: exchanged(): return lax.ppermute(block, axis, [(i, i ^ mask) for i in range(count)])]
    pallas_call x1, Pallas kernels: 2.98 us -> 1.43 us  [local(): pl.pallas_call(functools.partial(own_kernel, group), out_shape=(sds((1,)...]
    ppermute x13, waiting for transfers between devices: 5.99 us -> 7.17 us  [the longest x10 5.31 us: exchanged(): return lax.ppermute(block, axis, [(i, i ^ mask) for i in range(count)])]
    convert_element_type x1 -> x0, other arithmetic: 0.95 us -> none  [local(): came = exchanged(running.astype(BF16), 'seq', 1 << bit)]
    pallas_call x1, Pallas kernels: 2.54 us -> 1.92 us  [local(): pl.pallas_call(functools.partial(sent_kernel, group, groups), out_shape=(...]
  transfers between devices with their start and end apart: 13 -> 13, of which waited for: 4 -> 5; matrix products, arithmetic and copies ran while one was open for 3% -> 0% of each run, Pallas kernels for 17% -> 16%
where the time goes in v5:
time: 30 us; the launch traced here: 29.9 us
  starting transfers between devices  14.2 us (47%)
  Pallas kernels  8.4 us (28%)
  waiting for transfers between devices  7.17 us (24%)
    ppermute x10, starting transfers between devices, exchanged(): return lax.ppermute(block, axis, [(i, i ^ mask) for i in range(count)])  10.6 us
    ppermute x10, waiting for transfers between devices, exchanged(): return lax.ppermute(block, axis, [(i, i ^ mask) for i in range(count)])  5.31 us
    ppermute x3, starting transfers between devices, exchanged_above(): return lax.ppermute(block, ('seq', 'head'), route)  3.57 us
    pallas_call x2, Pallas kernels, local(): pl.pallas_call(functools.partial(intra_kernel, group, work), out_shape=(p...  2.21 us
    pallas_call x1, Pallas kernels, local(): pl.pallas_call(functools.partial(sent_kernel, group, groups), out_shape=(...  1.92 us
    ppermute x3, waiting for transfers between devices, exchanged_above(): return lax.ppermute(block, ('seq', 'head'), route)  1.86 us
    pallas_call x3, Pallas kernels, readout(): pl.pallas_call(kernel, out_shape=tuple(shapes), in_specs=[SMEM] + [VMEM]...  1.45 us
    pallas_call x1, Pallas kernels, local(): pl.pallas_call(functools.partial(own_kernel, group), out_shape=(sds((1,)...  1.43 us
  transfers between devices with their start and end apart: 13, of which 5 were waited for; matrix products, arithmetic and copies ran while one was open for 0% of the time, Pallas kernels for 16%

profile of v5, /device:TPU:24, one launch (start us, length us, event | category | flops | bytes accessed | tf_op | source)
XLA Modules:
  0.0 29.9 jit_solution(7313424715717911519)
XLA Ops:
  0.0 1.9 %sent.1 = (bf16[3,512,256]{2,1,0:T(8,128)(2,1)S(1)}, bf16[3,512,256]{2,1,0:T(8,128)(2,1)S(1)}, bf16[2,128,128]{2,1,0:T(8,128)(2,1)S(1)}, bf16[2,128,128]{2,1,0:T(8,128)(2,1)S(1)}, bf16[2,128,128]{2,1,0:T(8,128)(2,1)S(1)}) custom-call(s32[1]{0:T(128)} %bitcast.place_ref, bf16[512,1024]{1,0:T(8,128)(2,1)} %k_hbm.3, bf16[512,1024]{1,0:T(8,128)(2,1)} %v_hbm.3), custom_call_target="tpu_custom_call" | custom-call | flops 100663296 | bytes 1572864 | tf_op jit(solution)/shard_map/sent/pallas_call | solution.py:201
  1.9 0.0 copy-start.2
  1.9 1.6 %collective-permute-start = (bf16[2,128,128]{2,1,0:T(8,128)(2,1)S(1)}, bf16[2,128,128]{2,1,0:T(8,128)(2,1)S(1)}, u32[]{:S(2)}, u32[]{:S(2)}) collective-permute-start(bf16[2,128,128]{2,1,0:T(8,128)(2,1)S(1)} %get-tuple-element.31), channel_id=1, source_target_pairs={{0,4},{4,0},{8,12},{12,8},{16,20},{20,16},{24,28},{28,24},{1,5},{5... | collective-permute-start | bytes 196616 | tf_op jit(solution)/shard_map/ppermute | solution.py:37
  3.5 0.4 %collective-permute-start.2 = (bf16[2,128,128]{2,1,0:T(8,128)(2,1)S(1)}, bf16[2,128,128]{2,1,0:T(8,128)(2,1)S(1)}, u32[]{:S(2)}, u32[]{:S(2)}) collective-permute-start(bf16[2,128,128]{2,1,0:T(8,128)(2,1)S(1)} %get-tuple-element.33.two_ref), channel_id=1, source_target_pairs={{0,8},{4,12},{8,0},{12,4},{16,24},{20,28},{24,16},{28,20},{1,9},{5... | collective-permute-start | bytes 196616 | tf_op jit(solution)/shard_map/ppermute | solution.py:37
  4.0 1.5 %collective-permute-start.3 = (bf16[2,128,128]{2,1,0:T(8,128)(2,1)S(1)}, bf16[2,128,128]{2,1,0:T(8,128)(2,1)S(1)}, u32[]{:S(2)}, u32[]{:S(2)}) collective-permute-start(bf16[2,128,128]{2,1,0:T(8,128)(2,1)S(1)} %get-tuple-element.32.three_ref), channel_id=1, source_target_pairs={{0,12},{4,8},{8,4},{12,0},{16,28},{20,24},{24,20},{28,16},{1,13},{... | collective-permute-start | bytes 196616 | tf_op jit(solution)/shard_map/ppermute | solution.py:37
  5.5 0.0 copy-done.2
  5.5 0.0 copy-start
  5.5 1.4 %own.1 = (bf16[1,512,256]{2,1,0:T(8,128)(2,1)S(1)}, bf16[1,512,256]{2,1,0:T(8,128)(2,1)S(1)}, f32[1,1024]{1,0:T(1,128)S(1)}, f32[2,128,128]{2,1,0:T(8,128)S(1)}, bf16[6,128,128]{2,1,0:T(8,128)(2,1)S(1)}) custom-call(s32[1]{0:T(128)} %bitcast.place_ref, bf16[512,1024]{1,0:T(8,128)(2,1)} %k_hbm.3, bf16[512,1024]{1,0:T(8,128)(2,1)} %v_hbm.3, ...), custom_call_target="tpu_custom_call" | custom-call | flops 33554432 | bytes 524288 | tf_op jit(solution)/shard_map/own/pallas_call | solution.py:216
  6.9 1.6 %collective-permute-start.1 = (bf16[6,128,128]{2,1,0:T(8,128)(2,1)S(1)}, bf16[6,128,128]{2,1,0:T(8,128)(2,1)S(1)}, u32[]{:S(2)}, u32[]{:S(2)}) collective-permute-start(bf16[6,128,128]{2,1,0:T(8,128)(2,1)S(1)} %get-tuple-element.34), channel_id=1, source_target_pairs={{0,4},{4,0},{8,12},{12,8},{16,20},{20,16},{24,28},{28,24},{1,5},{5... | collective-permute-start | bytes 589832 | tf_op jit(solution)/shard_map/ppermute | solution.py:37
  8.5 0.0 collective-permute-done.one_ref.refs_0_
  8.5 0.0 collective-permute-done.2.two_ref
  8.5 0.7 %collective-permute-done.3.three_ref = bf16[2,128,128]{2,1,0:T(8,128)(2,1)S(1)} collective-permute-done((bf16[2,128,128]{2,1,0:T(8,128)(2,1)S(1)}, bf16[2,128,128]{2,1,0:T(8,128)(2,1)S(1)}, u32[]{:S(2)}, u32[]{:S(2)}) %collective-permute-start.3) | collective-permute-done | bytes 65568 | tf_op jit(solution)/shard_map/ppermute | solution.py:37
  9.2 0.0 copy-start.1
  9.2 0.4 %collective-permute-start.7 = (bf16[2,128,128]{2,1,0:T(8,128)(2,1)S(1)}, bf16[2,128,128]{2,1,0:T(8,128)(2,1)S(1)}, u32[]{:S(2)}, u32[]{:S(2)}) collective-permute-start(bf16[2,128,128]{2,1,0:T(8,128)(2,1)S(1)} %get-tuple-element.37), channel_id=1, source_target_pairs={{0,16},{4,20},{8,24},{12,28},{16,0},{20,4},{24,8},{28,12},{1,17},{... | collective-permute-start | bytes 196616 | tf_op jit(solution)/shard_map/ppermute | solution.py:37
  9.6 0.8 %collective-permute-start.4 = (bf16[2,128,128]{2,1,0:T(8,128)(2,1)S(1)}, bf16[2,128,128]{2,1,0:T(8,128)(2,1)S(1)}, u32[]{:S(2)}, u32[]{:S(2)}) collective-permute-start(bf16[2,128,128]{2,1,0:T(8,128)(2,1)S(1)} %get-tuple-element.36.refs_2_), channel_id=1, source_target_pairs={{0,4},{4,0},{8,12},{12,8},{16,20},{20,16},{24,28},{28,24},{1,5},{5... | collective-permute-start | bytes 196616 | tf_op jit(solution)/shard_map/ppermute | solution.py:37
  10.4 1.3 %collective-permute-start.5 = (bf16[2,128,128]{2,1,0:T(8,128)(2,1)S(1)}, bf16[2,128,128]{2,1,0:T(8,128)(2,1)S(1)}, u32[]{:S(2)}, u32[]{:S(2)}) collective-permute-start(bf16[2,128,128]{2,1,0:T(8,128)(2,1)S(1)} %get-tuple-element.36.refs_2_), channel_id=1, source_target_pairs={{0,8},{4,12},{8,0},{12,4},{16,24},{20,28},{24,16},{28,20},{1,9},{5... | collective-permute-start | bytes 196616 | tf_op jit(solution)/shard_map/ppermute | solution.py:37
  11.7 1.4 %collective-permute-start.6 = (bf16[2,128,128]{2,1,0:T(8,128)(2,1)S(1)}, bf16[2,128,128]{2,1,0:T(8,128)(2,1)S(1)}, u32[]{:S(2)}, u32[]{:S(2)}) collective-permute-start(bf16[2,128,128]{2,1,0:T(8,128)(2,1)S(1)} %get-tuple-element.36.refs_2_), channel_id=1, source_target_pairs={{0,12},{4,8},{8,4},{12,0},{16,28},{20,24},{24,20},{28,16},{1,13},{... | collective-permute-start | bytes 196616 | tf_op jit(solution)/shard_map/ppermute | solution.py:37
  13.1 1.4 %collective-permute-done.7.refs_6_ = bf16[2,128,128]{2,1,0:T(8,128)(2,1)S(1)} collective-permute-done((bf16[2,128,128]{2,1,0:T(8,128)(2,1)S(1)}, bf16[2,128,128]{2,1,0:T(8,128)(2,1)S(1)}, u32[]{:S(2)}, u32[]{:S(2)}) %collective-permute-start.7) | collective-permute-done | bytes 65568 | tf_op jit(solution)/shard_map/ppermute | solution.py:37
  14.5 1.9 %collective-permute-start.8 = (bf16[2,128,128]{2,1,0:T(8,128)(2,1)S(1)}, bf16[2,128,128]{2,1,0:T(8,128)(2,1)S(1)}, u32[]{:S(2)}, u32[]{:S(2)}) collective-permute-start(bf16[2,128,128]{2,1,0:T(8,128)(2,1)S(1)} %collective-permute-done.7.refs_6_), channel_id=1, source_target_pairs={{0,1},{1,0},{2,3},{3,2},{4,5},{5,4},{6,7},{7,6},{8,9},{9,8},{10,11... | collective-permute-start | bytes 196616 | tf_op jit(solution)/shard_map/ppermute | solution.py:47
  16.4 0.0 collective-permute-done.4.refs_3_
  16.4 1.5 %collective-permute-start.9 = (bf16[2,128,128]{2,1,0:T(8,128)(2,1)S(1)}, bf16[2,128,128]{2,1,0:T(8,128)(2,1)S(1)}, u32[]{:S(2)}, u32[]{:S(2)}) collective-permute-start(bf16[2,128,128]{2,1,0:T(8,128)(2,1)S(1)} %collective-permute-done.7.refs_6_), channel_id=1, source_target_pairs={{0,1},{1,0},{2,3},{3,2},{4,5},{5,4},{6,7},{7,6},{8,9},{9,8},{10,11... | collective-permute-start | bytes 196616 | tf_op jit(solution)/shard_map/ppermute | solution.py:47
  18.0 0.0 copy-done
  18.0 0.0 copy-done.1
  18.0 1.1 %intra.2 = (f32[256,512]{1,0:T(8,128)S(1)}, f32[256,512]{1,0:T(8,128)S(1)}) custom-call(s32[1]{0:T(128)} %bitcast.place_ref, bf16[512,1024]{1,0:T(8,128)(2,1)S(1)} %copy-done, f32[5,8,512]{2,1,0:T(8,128)S(1)} %copy-done.1, bf16[3,512,256]{2,1,0:T(8,128)(2,1)S(1)} %get-tuple-element.38.refs_0_, bf16[3,512,256]{2,1,0:T(8,128)(2,1)S(1)} %get-tuple-element.39.refs_1_), custom_call_target="tpu_custom_call" | custom-call | flops 402653184 | bytes 1048576 | tf_op jit(solution)/shard_map/intra/pallas_call | solution.py:233
  19.1 0.0 collective-permute-done.5.refs_4_
  19.1 0.1 collective-permute-start.10
  19.2 1.1 %intra.3 = (f32[256,512]{1,0:T(8,128)S(1)}, f32[256,512]{1,0:T(8,128)S(1)}) custom-call(s32[1]{0:T(128)} %bitcast.place_ref, bf16[512,1024]{1,0:T(8,128)(2,1)S(1)} %copy-done, f32[5,8,512]{2,1,0:T(8,128)S(1)} %copy-done.1, bf16[3,512,256]{2,1,0:T(8,128)(2,1)S(1)} %get-tuple-element.38.refs_0_, bf16[3,512,256]{2,1,0:T(8,128)(2,1)S(1)} %get-tuple-element.39.refs_1_, ...), custom_call_target="tpu_custom_call" | custom-call | flops 402653184 | bytes 1048576 | tf_op jit(solution)/shard_map/intra/pallas_call | solution.py:233
  20.3 0.0 collective-permute-done.6.refs_5_
  20.3 0.0 collective-permute-done.1.refs_1_
  20.4 0.8 %shard_map.55 = (f32[256,512]{1,0:T(8,128)S(1)}, f32[256,512]{1,0:T(8,128)S(1)}, f32[256,512]{1,0:T(8,128)S(1)}, f32[256,512]{1,0:T(8,128)S(1)}, f32[8,512]{1,0:T(8,128)S(1)}) custom-call(s32[1]{0:T(128)} %bitcast.place_ref, bf16[512,1024]{1,0:T(8,128)(2,1)S(1)} %copy-done, f32[5,8,512]{2,1,0:T(8,128)S(1)} %copy-done.1, ...), custom_call_target="tpu_custom_call" | custom-call | flops 268435456 | bytes 4194304 | tf_op jit(solution)/shard_map/pallas_call | solution.py:272
  21.2 0.0 collective-permute-done.8.refs_0_
  21.2 0.0 collective-permute-done.9.refs_1_
  21.2 0.3 %shard_map.56 = (f32[256,512]{1,0:T(8,128)S(1)}, f32[256,512]{1,0:T(8,128)S(1)}, f32[8,512]{1,0:T(8,128)S(1)}) custom-call(s32[1]{0:T(128)} %bitcast.place_ref, bf16[512,1024]{1,0:T(8,128)(2,1)S(1)} %copy-done, f32[5,8,512]{2,1,0:T(8,128)S(1)} %copy-done.1, bf16[2,128,128]{2,1,0:T(8,128)(2,1)S(1)} %collective-permute-done.8.refs_0_, ...), custom_call_target="tpu_custom_call" | custom-call | flops 134217728 | bytes 2097152 | tf_op jit(solution)/shard_map/pallas_call | solution.py:272
  21.6 1.9 %collective-permute-done.10.refs_0_ = bf16[2,128,128]{2,1,0:T(8,128)(2,1)S(1)} collective-permute-done((bf16[2,128,128]{2,1,0:T(8,128)(2,1)S(1)}, bf16[2,128,128]{2,1,0:T(8,128)(2,1)S(1)}, u32[]{:S(2)}, u32[]{:S(2)}) %collective-permute-start.10) | collective-permute-done | bytes 65568 | tf_op jit(solution)/shard_map/ppermute | solution.py:47
  23.4 0.3 shard_map.57
  23.7 0.1 collective-permute-start.11
  23.8 1.1 %collective-permute-done.11 = f32[1,512]{1,0:T(1,128)S(1)} collective-permute-done((f32[1,512]{1,0:T(1,128)S(1)}, f32[1,512]{1,0:T(1,128)S(1)}, u32[]{:S(2)}, u32[]{:S(2)}) %collective-permute-start.11) | collective-permute-done | bytes 2080 | tf_op jit(solution)/shard_map/ppermute | solution.py:37
  24.9 1.5 %collective-permute-start.12 = (f32[1,512]{1,0:T(1,128)S(1)}, f32[1,512]{1,0:T(1,128)S(1)}, u32[]{:S(2)}, u32[]{:S(2)}) collective-permute-start(f32[1,512]{1,0:T(1,128)S(1)} %add.6), channel_id=1, source_target_pairs={{0,2},{1,3},{2,0},{3,1},{4,6},{5,7},{6,4},{7,5},{8,10},{9,11},{10,... | collective-permute-start | bytes 6152 | tf_op jit(solution)/shard_map/ppermute | solution.py:37
  26.4 2.1 %collective-permute-done.12 = f32[1,512]{1,0:T(1,128)S(1)} collective-permute-done((f32[1,512]{1,0:T(1,128)S(1)}, f32[1,512]{1,0:T(1,128)S(1)}, u32[]{:S(2)}, u32[]{:S(2)}) %collective-permute-start.12) | collective-permute-done | bytes 2080 | tf_op jit(solution)/shard_map/ppermute | solution.py:37
  28.5 1.4 %norm.1 = bf16[512,1024]{1,0:T(8,128)(2,1)} custom-call(s32[1]{0:T(128)} %bitcast.place_ref, f32[256,512]{1,0:T(8,128)S(1)} %get-tuple-element.46.refs_0_, f32[256,512]{1,0:T(8,128)S(1)} %get-tuple-element.50.refs_1_, f32[256,512]{1,0:T(8,128)S(1)} %get-tuple-element.53.refs_2_, f32[256,512]{1,0:T(8,128)S(1)} %get-tuple-element.54.refs_3_, ...), custom_call_target="tpu_custom_call" | custom-call | flops 1048576 | bytes 1048576 | tf_op jit(solution)/shard_map/norm/pallas_call | solution.py:294
  (3 shorter events, 0.1 us)
Async XLA Ops:
  1.9 3.6 %copy-start.2 = (f32[1024]{0:T(1024)S(1)}, f32[1024]{0:T(1024)}, u32[]{:S(2)}) copy-start(f32[1024]{0:T(1024)} %param.9) | copy-start | bytes 12292
  1.9 6.6 %collective-permute-start = (bf16[2,128,128]{2,1,0:T(8,128)(2,1)S(1)}, bf16[2,128,128]{2,1,0:T(8,128)(2,1)S(1)}, u32[]{:S(2)}, u32[]{:S(2)}) collective-permute-start(bf16[2,128,128]{2,1,0:T(8,128)(2,1)S(1)} %get-tuple-element.31), channel_id=1, source_target_pairs={{0,4},{4,0},{8,12},{12,8},{16,20},{20,16},{24,28},{28,24},{1,5},{5... | collective-permute-start | bytes 196616 | tf_op jit(solution)/shard_map/ppermute | solution.py:37
  3.5 5.0 %collective-permute-start.2 = (bf16[2,128,128]{2,1,0:T(8,128)(2,1)S(1)}, bf16[2,128,128]{2,1,0:T(8,128)(2,1)S(1)}, u32[]{:S(2)}, u32[]{:S(2)}) collective-permute-start(bf16[2,128,128]{2,1,0:T(8,128)(2,1)S(1)} %get-tuple-element.33.two_ref), channel_id=1, source_target_pairs={{0,8},{4,12},{8,0},{12,4},{16,24},{20,28},{24,16},{28,20},{1,9},{5... | collective-permute-start | bytes 196616 | tf_op jit(solution)/shard_map/ppermute | solution.py:37
  4.0 5.2 %collective-permute-start.3 = (bf16[2,128,128]{2,1,0:T(8,128)(2,1)S(1)}, bf16[2,128,128]{2,1,0:T(8,128)(2,1)S(1)}, u32[]{:S(2)}, u32[]{:S(2)}) collective-permute-start(bf16[2,128,128]{2,1,0:T(8,128)(2,1)S(1)} %get-tuple-element.32.three_ref), channel_id=1, source_target_pairs={{0,12},{4,8},{8,4},{12,0},{16,28},{20,24},{24,20},{28,16},{1,13},{... | collective-permute-start | bytes 196616 | tf_op jit(solution)/shard_map/ppermute | solution.py:37
  5.5 12.5 %copy-start = (bf16[512,1024]{1,0:T(8,128)(2,1)S(1)}, bf16[512,1024]{1,0:T(8,128)(2,1)}, u32[]{:S(2)}) copy-start(bf16[512,1024]{1,0:T(8,128)(2,1)} %q_ref.9) | copy-start | bytes 3145732
  6.9 13.4 %collective-permute-start.1 = (bf16[6,128,128]{2,1,0:T(8,128)(2,1)S(1)}, bf16[6,128,128]{2,1,0:T(8,128)(2,1)S(1)}, u32[]{:S(2)}, u32[]{:S(2)}) collective-permute-start(bf16[6,128,128]{2,1,0:T(8,128)(2,1)S(1)} %get-tuple-element.34), channel_id=1, source_target_pairs={{0,4},{4,0},{8,12},{12,8},{16,20},{20,16},{24,28},{28,24},{1,5},{5... | collective-permute-start | bytes 589832 | tf_op jit(solution)/shard_map/ppermute | solution.py:37
  9.2 8.8 %copy-start.1 = (f32[5,8,512]{2,1,0:T(8,128)S(1)}, f32[5,8,512]{2,1,0:T(8,128)}, u32[]{:S(2)}) copy-start(f32[5,8,512]{2,1,0:T(8,128)} %w_ref.9) | copy-start | bytes 245764
  9.2 5.3 %collective-permute-start.7 = (bf16[2,128,128]{2,1,0:T(8,128)(2,1)S(1)}, bf16[2,128,128]{2,1,0:T(8,128)(2,1)S(1)}, u32[]{:S(2)}, u32[]{:S(2)}) collective-permute-start(bf16[2,128,128]{2,1,0:T(8,128)(2,1)S(1)} %get-tuple-element.37), channel_id=1, source_target_pairs={{0,16},{4,20},{8,24},{12,28},{16,0},{20,4},{24,8},{28,12},{1,17},{... | collective-permute-start | bytes 196616 | tf_op jit(solution)/shard_map/ppermute | solution.py:37
  9.6 6.8 %collective-permute-start.4 = (bf16[2,128,128]{2,1,0:T(8,128)(2,1)S(1)}, bf16[2,128,128]{2,1,0:T(8,128)(2,1)S(1)}, u32[]{:S(2)}, u32[]{:S(2)}) collective-permute-start(bf16[2,128,128]{2,1,0:T(8,128)(2,1)S(1)} %get-tuple-element.36.refs_2_), channel_id=1, source_target_pairs={{0,4},{4,0},{8,12},{12,8},{16,20},{20,16},{24,28},{28,24},{1,5},{5... | collective-permute-start | bytes 196616 | tf_op jit(solution)/shard_map/ppermute | solution.py:37
  10.4 8.7 %collective-permute-start.5 = (bf16[2,128,128]{2,1,0:T(8,128)(2,1)S(1)}, bf16[2,128,128]{2,1,0:T(8,128)(2,1)S(1)}, u32[]{:S(2)}, u32[]{:S(2)}) collective-permute-start(bf16[2,128,128]{2,1,0:T(8,128)(2,1)S(1)} %get-tuple-element.36.refs_2_), channel_id=1, source_target_pairs={{0,8},{4,12},{8,0},{12,4},{16,24},{20,28},{24,16},{28,20},{1,9},{5... | collective-permute-start | bytes 196616 | tf_op jit(solution)/shard_map/ppermute | solution.py:37
  11.7 8.6 %collective-permute-start.6 = (bf16[2,128,128]{2,1,0:T(8,128)(2,1)S(1)}, bf16[2,128,128]{2,1,0:T(8,128)(2,1)S(1)}, u32[]{:S(2)}, u32[]{:S(2)}) collective-permute-start(bf16[2,128,128]{2,1,0:T(8,128)(2,1)S(1)} %get-tuple-element.36.refs_2_), channel_id=1, source_target_pairs={{0,12},{4,8},{8,4},{12,0},{16,28},{20,24},{24,20},{28,16},{1,13},{... | collective-permute-start | bytes 196616 | tf_op jit(solution)/shard_map/ppermute | solution.py:37
  14.5 6.7 %collective-permute-start.8 = (bf16[2,128,128]{2,1,0:T(8,128)(2,1)S(1)}, bf16[2,128,128]{2,1,0:T(8,128)(2,1)S(1)}, u32[]{:S(2)}, u32[]{:S(2)}) collective-permute-start(bf16[2,128,128]{2,1,0:T(8,128)(2,1)S(1)} %collective-permute-done.7.refs_6_), channel_id=1, source_target_pairs={{0,1},{1,0},{2,3},{3,2},{4,5},{5,4},{6,7},{7,6},{8,9},{9,8},{10,11... | collective-permute-start | bytes 196616 | tf_op jit(solution)/shard_map/ppermute | solution.py:47
  16.4 4.8 %collective-permute-start.9 = (bf16[2,128,128]{2,1,0:T(8,128)(2,1)S(1)}, bf16[2,128,128]{2,1,0:T(8,128)(2,1)S(1)}, u32[]{:S(2)}, u32[]{:S(2)}) collective-permute-start(bf16[2,128,128]{2,1,0:T(8,128)(2,1)S(1)} %collective-permute-done.7.refs_6_), channel_id=1, source_target_pairs={{0,1},{1,0},{2,3},{3,2},{4,5},{5,4},{6,7},{7,6},{8,9},{9,8},{10,11... | collective-permute-start | bytes 196616 | tf_op jit(solution)/shard_map/ppermute | solution.py:47
  19.1 4.3 %collective-permute-start.10 = (bf16[2,128,128]{2,1,0:T(8,128)(2,1)S(1)}, bf16[2,128,128]{2,1,0:T(8,128)(2,1)S(1)}, u32[]{:S(2)}, u32[]{:S(2)}) collective-permute-start(bf16[2,128,128]{2,1,0:T(8,128)(2,1)S(1)} %collective-permute-done.7.refs_6_), channel_id=1, source_target_pairs={{0,1},{1,0},{2,3},{3,2},{4,5},{5,4},{6,7},{7,6},{8,9},{9,8},{10,11... | collective-permute-start | bytes 196616 | tf_op jit(solution)/shard_map/ppermute | solution.py:47
  23.7 1.2 %collective-permute-start.11 = (f32[1,512]{1,0:T(1,128)S(1)}, f32[1,512]{1,0:T(1,128)S(1)}, u32[]{:S(2)}, u32[]{:S(2)}) collective-permute-start(f32[1,512]{1,0:T(1,128)S(1)} %get-tuple-element.55), channel_id=1, source_target_pairs={{0,1},{1,0},{2,3},{3,2},{4,5},{5,4},{6,7},{7,6},{8,9},{9,8},{10,11... | collective-permute-start | bytes 6152 | tf_op jit(solution)/shard_map/ppermute | solution.py:37
  24.9 3.6 %collective-permute-start.12 = (f32[1,512]{1,0:T(1,128)S(1)}, f32[1,512]{1,0:T(1,128)S(1)}, u32[]{:S(2)}, u32[]{:S(2)}) collective-permute-start(f32[1,512]{1,0:T(1,128)S(1)} %add.6), channel_id=1, source_target_pairs={{0,2},{1,3},{2,0},{3,1},{4,6},{5,7},{6,4},{7,5},{8,10},{9,11},{10,... | collective-permute-start | bytes 6152 | tf_op jit(solution)/shard_map/ppermute | solution.py:37

commit v6 on v5

--- a/solution.py
+++ b/solution.py
@@ -20,8 +20,7 @@
 HBM = pl.BlockSpec(memory_space=pltpu.HBM)
 GRANT = 24 << 20
 TILE = 256
-STATES_GRANT = 52992 << 10
-OWN_GRANT = 53248 << 10
+STATES_GRANT = 51968 << 10
 
 
 def params(grant=GRANT):
@@ -37,12 +36,12 @@
     return lax.ppermute(block, axis, [(i, i ^ mask) for i in range(count)])
 
 
-def exchanged_above(block, mask):
+def exchanged_in(block, mask, real):
     seq, head = lax.axis_size("seq"), lax.axis_size("head")
     route = []
     for s in range(seq):
         for h in range(head):
-            to = (s ^ mask, h) if s >= QUAD else (s, h ^ 1)
+            to = (s ^ mask, h) if real(s // QUAD, seq // QUAD) else (s, h ^ 1)
             route.append((s * head + h, to[0] * head + to[1]))
     return lax.ppermute(block, ("seq", "head"), route)
 
@@ -59,77 +58,70 @@
     return pl.ds(head * HEAD_DIM, HEAD_DIM)
 
 
-def states_of(group, groups, place, k_hbm, v_hbm, k_ref, v_ref, sems, use):
+def states_kernel(group, place_ref, k_hbm, v_hbm, k_ref, v_ref, own_ref, one_ref, two_ref, three_ref, rest_ref, sems):
     width = group * HEAD_DIM
-    copies = []
-    for at, r in enumerate(groups):
+    place = place_ref[0] & (QUAD - 1)
+    order = (3, 1, 2, 0)
+    copies = {}
+    for r in order:
         cols = pl.ds(pl.multiple_of((place ^ r) * width, width), width)
-        copies.append(
-            (
-                pltpu.make_async_copy(k_hbm.at[:, cols], k_ref.at[at], sems.at[0, at]),
-                pltpu.make_async_copy(v_hbm.at[:, cols], v_ref.at[at], sems.at[1, at]),
-            )
+        copies[r] = (
+            pltpu.make_async_copy(k_hbm.at[:, cols], k_ref.at[r], sems.at[0, r]),
+            pltpu.make_async_copy(v_hbm.at[:, cols], v_ref.at[r], sems.at[1, r]),
         )
-        for copy in copies[-1]:
+        for copy in copies[r]:
             copy.start()
-    for at, r in enumerate(groups):
-        for copy in copies[at]:
+    sent = {1: one_ref, 2: two_ref, 3: three_ref}
+    spot = {0: 0, 3: 1, 2: 2}
+    for r in order:
+        for copy in copies[r]:
             copy.wait()
         for j in range(group):
-            use(r, j, tn(v_ref[at, :, column(j)], k_ref[at, :, column(j)]))
-
-
-def sent_kernel(group, groups, place_ref, k_hbm, v_hbm, k_ref, v_ref, *refs):
-    sent = dict(zip(groups, refs))
-
-    def use(r, j, state):
-        sent[r][j] = state.astype(BF16)
-
-    states_of(group, groups, place_ref[0] & (QUAD - 1), k_hbm, v_hbm, k_ref, v_ref, refs[-1], use)
-
-
-def own_kernel(group, place_ref, k_hbm, v_hbm, gain_hbm, three_ref, two_ref, k_ref, v_ref, gain_ref, own_ref, rest_ref, sems, gain_sem):
-    gain = pltpu.make_async_copy(gain_hbm, gain_ref, gain_sem)
-    gain.start()
-    rest_ref[group : 2 * group] = three_ref[...]
-    rest_ref[2 * group :] = two_ref[...]
-
-    def use(r, j, state):
-        own_ref[j] = state
-        rest_ref[j] = state.astype(BF16)
-
-    states_of(group, (0,), place_ref[0] & (QUAD - 1), k_hbm, v_hbm, k_ref, v_ref, sems, use)
-    gain.wait()
-
-
-def sums_kernel(place_ref, own_ref, one_ref, two_ref, three_ref, sent_ref, left_ref, *total_refs):
-    pair = own_ref[...] + one_ref[...].astype(F32)
-    other = two_ref[...].astype(F32) + three_ref[...].astype(F32)
-    total = pair + other
+            state = tn(v_ref[r, :, column(j)], k_ref[r, :, column(j)])
+            if r == 0:
+                own_ref[j] = state
+            else:
+                sent[r][j] = state.astype(BF16)
+            if r in spot:
+                rest_ref[spot[r] * group + j] = state.astype(BF16)
+
+
+def sums_kernel(own_ref, one_ref, two_ref, three_ref, sent_ref, *total_refs):
+    total = own_ref[...] + one_ref[...].astype(F32) + two_ref[...].astype(F32) + three_ref[...].astype(F32)
     for total_ref in total_refs:
         total_ref[...] = total
     sent_ref[...] = total.astype(BF16)
+
+
+def left_kernel(seq, place_ref, own_ref, *refs):
+    left_ref, neighbour_ref = refs[6:]
+    last_quad = place_ref[0] >= seq - QUAD
+    one, two, three = (jnp.where(last_quad, refs[3 + i][...], refs[i][...]) for i in range(3))
+    pair = own_ref[...] + one.astype(F32)
+    other = two.astype(F32) + three.astype(F32)
     left_ref[...] = jnp.where(place_ref[0] >> 1 & 1 == 1, other, pair).astype(BF16)
-
-
-def intra_kernel(group, work, place_ref, q_ref, w_ref, *refs):
-    n = len(work)
-    sources, out_refs = refs[:-n], refs[-n:]
+    neighbour_ref[...] = one
+
+
+def intra_kernel(group, groups, place_ref, q_ref, w_ref, k_all, v_all, *refs):
+    out_refs = refs[-len(groups) :]
+    if len(refs) > len(groups):
+        gain_ref, kept_ref = refs[:2]
+        kept_ref[...] = gain_ref[...]
     count = q_ref.shape[0] // STRETCH
     local_bits = count.bit_length() - 1
     place = place_ref[0] & (QUAD - 1)
     causal = lax.broadcasted_iota(jnp.int32, (STRETCH, STRETCH), 0) <= lax.broadcasted_iota(
         jnp.int32, (STRETCH, STRETCH), 1
     )
-    for (r, source, slot), out_ref in zip(work, out_refs):
-        k_ref, v_ref = sources[2 * source : 2 * source + 2]
+    for r, out_ref in zip(groups, out_refs):
         for j in range(group):
             head = (place ^ r) * group + j
             cols = pl.ds(pl.multiple_of(head * HEAD_DIM, HEAD_DIM), HEAD_DIM)
             states = []
             for c in range(count):
                 here = slice(c * STRETCH, (c + 1) * STRETCH)
-                q, k, v = q_ref[here, cols], k_ref[slot, here, column(j)], v_ref[slot, here, column(j)]
+                q, k, v = q_ref[here, cols], k_all[r, here, column(j)], v_all[r, here, column(j)]
                 probs = jnp.where(causal, nt(k, q), 0.0).astype(BF16)
                 total = w_ref[0, pl.ds(head, 1), here] * tn(v, probs)
                 for bit in range(local_bits):
@@ -195,69 +187,66 @@
     block = (group, HEAD_DIM, HEAD_DIM)
     others = (3 * group, HEAD_DIM, HEAD_DIM)
     panel = (rows, group * HEAD_DIM)
-    part = sds((group * HEAD_DIM, rows), F32)
-
-    groups = (3, 1, 2)
-    k_sent, v_sent, three, one, two = pl.pallas_call(
-        functools.partial(sent_kernel, group, groups),
-        out_shape=(sds((3,) + panel, BF16),) * 2 + (sds(block, BF16),) * 3,
+    part_shape = sds((group * HEAD_DIM, rows), F32)
+
+    k_all, v_all, own, one, two, three, rest = pl.pallas_call(
+        functools.partial(states_kernel, group),
+        out_shape=(sds((QUAD,) + panel, BF16),) * 2 + (sds(block, F32),) + (sds(block, BF16),) * 3 + (sds(others, BF16),),
         in_specs=[SMEM, HBM, HBM],
-        out_specs=(VMEM,) * 5,
-        scratch_shapes=[pltpu.SemaphoreType.DMA((2, 3))],
+        out_specs=(VMEM,) * 7,
+        scratch_shapes=[pltpu.SemaphoreType.DMA((2, QUAD))],
         compiler_params=params(STATES_GRANT),
-        cost_estimate=cost(3 * rows * width * HEAD_DIM // 2, 3 * rows * width),
-        name="sent",
+        cost_estimate=cost(2 * rows * width * HEAD_DIM, 4 * rows * width),
+        name="states",
     )(place, keys, values)
 
-    got3 = exchanged(three, "seq", 3)
-    got1 = exchanged(one, "seq", 1)
-    got2 = exchanged(two, "seq", 2)
-
-    k_own, v_own, gain, own, rest = pl.pallas_call(
-        functools.partial(own_kernel, group),
-        out_shape=(sds((1,) + panel, BF16),) * 2 + (sds((1, width), F32), sds(block, F32), sds(others, BF16)),
-        in_specs=[SMEM, HBM, HBM, HBM, VMEM, VMEM],
-        out_specs=(VMEM,) * 5,
-        scratch_shapes=[pltpu.SemaphoreType.DMA((2, 1)), pltpu.SemaphoreType.DMA],
-        compiler_params=params(OWN_GRANT),
-        cost_estimate=cost(rows * width * HEAD_DIM // 2, rows * width),
-        name="own",
-    )(place, keys, values, norm_gain.reshape(1, width), three, two)
+    parts = ((3, three), (1, one), (2, two))
+    early = {r: exchanged_in(part, r, lambda quad, quads: quad < quads - 1) for r, part in parts}
+    late = {r: exchanged_in(part, r, lambda quad, quads: quad == quads - 1) for r, part in parts}
     near = exchanged(rest, "seq", 1)
 
     totals = {}
-    for work, sources in (
-        (((3, 0, 0), (1, 0, 1)), (k_sent, v_sent)),
-        (((2, 0, 2), (0, 1, 0)), (k_sent, v_sent, k_own, v_own)),
-    ):
+    for number, groups in enumerate(((3, 1), (2, 0))):
+        extra = [norm_gain.reshape(1, width)] if number == 0 else []
         outs = pl.pallas_call(
-            functools.partial(intra_kernel, group, work),
-            out_shape=(part,) * len(work),
-            in_specs=[SMEM] + [VMEM] * (2 + len(sources)),
-            out_specs=(VMEM,) * len(work),
+            functools.partial(intra_kernel, group, groups),
+            out_shape=(sds((1, width), F32),) * len(extra) + (part_shape,) * len(groups),
+            in_specs=[SMEM] + [VMEM] * (4 + len(extra)),
+            out_specs=(VMEM,) * (len(extra) + len(groups)),
             compiler_params=params(),
             cost_estimate=cost(3 * rows * STRETCH * width, 2 * rows * width),
             name="intra",
-        )(place, queries, level_weights, *sources)
-        totals |= {r: out for (r, _, _), out in zip(work, outs)}
-
-    sums, left_pair, *running = pl.pallas_call(
+        )(place, queries, level_weights, k_all, v_all, *extra)
+        if extra:
+            gain, *outs = outs
+        totals |= dict(zip(groups, outs))
+
+    sums, *running = pl.pallas_call(
         sums_kernel,
-        out_shape=(sds(block, BF16), sds(block, BF16)) + (sds(block, F32),) * (seq_bits > 3),
-        in_specs=[SMEM] + [VMEM] * 4,
-        out_specs=(VMEM,) * (2 + (seq_bits > 3)),
+        out_shape=(sds(block, BF16),) + (sds(block, F32),) * (seq_bits > 3),
+        in_specs=[VMEM] * 4,
+        out_specs=(VMEM,) * (1 + (seq_bits > 3)),
         compiler_params=params(),
         cost_estimate=cost(4 * group * HEAD_DIM**2, 16 * group * HEAD_DIM**2),
         name="sums",
-    )(place, own, got1, got2, got3)
+    )(own, early[1], early[2], early[3])
     upper = []
     for bit in range(2, seq_bits):
         if bit > 2:
             running = [running[0] + upper[-1].astype(F32)]
             sums = running[0].astype(BF16)
         upper.append(exchanged(sums, "seq", 1 << bit))
+    left_pair, neighbour = pl.pallas_call(
+        functools.partial(left_kernel, lax.axis_size("seq")),
+        out_shape=(sds(block, BF16), sds(block, BF16)),
+        in_specs=[SMEM] + [VMEM] * 7,
+        out_specs=(VMEM,) * 2,
+        compiler_params=params(),
+        cost_estimate=cost(4 * group * HEAD_DIM**2, 16 * group * HEAD_DIM**2),
+        name="left",
+    )(place, own, early[1], early[2], early[3], late[1], late[2], late[3])
     top = jnp.concatenate(upper, axis=0) if len(upper) > 1 else upper[0]
-    tops = {0: top} | {r: exchanged_above(top, r) for r in (3, 1, 2)}
+    tops = {0: top} | {r: exchanged_in(top, r, lambda quad, quads: quad > 0) for r in (3, 1, 2)}
 
     middle = {0: left_pair} | {r: exchanged(left_pair, "seq", r) for r in (3, 1, 2)}
 
@@ -268,7 +257,7 @@
         n, carry = len(work), squares is not None
         kernel = functools.partial(readout_kernel, group, 1 + local_bits, work, len(states), carry, finish)
         ins = [place, queries, level_weights, *states, *(totals[r] for r, _, _ in work)] + [squares] * carry
-        shapes = [part] * n + [sds((1 if finish else 8, rows), F32)]
+        shapes = [part_shape] * n + [sds((1 if finish else 8, rows), F32)]
         outs = pl.pallas_call(
             kernel,
             out_shape=tuple(shapes),
@@ -282,7 +271,7 @@
 
     below = {0: ((0, 0, 0), (1, 2, 0))} | {r: ((0, 1, (r - 1) * group), (1, 2 + r, 0)) for r in (1, 2, 3)}
     work = tuple((r, r == 0, below[r] + (top_reads(6) if r == 0 else ())) for r in (3, 1, 2, 0))
-    squares = readout(work, (got1, near, *(middle[r] for r in range(QUAD)), top), None)
+    squares = readout(work, (neighbour, near, *(middle[r] for r in range(QUAD)), top), None)
     squares = readout(((3, True, top_reads(0)), (1, True, top_reads(1))), (tops[3], tops[1]), squares)
     squares = readout(((2, True, top_reads(0)),), (tops[2],), squares, finish=True)
 

time: 30 us -> 31.3 us (1.043)
  the two profiles are of different devices: /device:TPU:24 before, /device:TPU:16 now
where the time goes in v6:
time: 31.3 us; the launch traced here: 31.1 us
  starting transfers between devices  17.7 us (57%)
  Pallas kernels  7.42 us (24%)
  waiting for transfers between devices  5.88 us (19%)
    ppermute x7, starting transfers between devices, exchanged(): return lax.ppermute(block, axis, [(i, i ^ mask) for i in range(count)])  9.79 us
    ppermute x9, starting transfers between devices, exchanged_in(): return lax.ppermute(block, ('seq', 'head'), route)  7.88 us
    ppermute x7, waiting for transfers between devices, exchanged(): return lax.ppermute(block, axis, [(i, i ^ mask) for i in range(count)])  4.13 us
    pallas_call x1, Pallas kernels, local(): pl.pallas_call(functools.partial(states_kernel, group), out_shape=(sds((Q...  2.3 us
    pallas_call x2, Pallas kernels, local(): pl.pallas_call(functools.partial(intra_kernel, group, groups), out_shape=...  2.24 us
    ppermute x9, waiting for transfers between devices, exchanged_in(): return lax.ppermute(block, ('seq', 'head'), route)  1.75 us
    pallas_call x3, Pallas kernels, readout(): pl.pallas_call(kernel, out_shape=tuple(shapes), in_specs=[SMEM] + [VMEM]...  1.44 us
    pallas_call x1, Pallas kernels, local(): pl.pallas_call(functools.partial(norm_kernel, group, full_width), out_sha...  1.36 us
  transfers between devices with their start and end apart: 16, of which 5 were waited for; matrix products, arithmetic and copies ran while one was open for 0% of the time, Pallas kernels for 11%

profile of v6, /device:TPU:16, one launch (start us, length us, event | category | flops | bytes accessed | tf_op | source)
XLA Modules:
  0.0 31.1 jit_solution(12177513434149150604)
XLA Ops:
  0.0 0.0 copy-start
  0.0 2.3 %states.1 = (bf16[4,512,256]{2,1,0:T(8,128)(2,1)S(1)}, bf16[4,512,256]{2,1,0:T(8,128)(2,1)S(1)}, f32[2,128,128]{2,1,0:T(8,128)S(1)}, bf16[2,128,128]{2,1,0:T(8,1...) custom-call(s32[1]{0:T(128)} %bitcast.place_ref, ...), custom_call_target="tpu_custom_call" | custom-call | flops 134217728 | bytes 2097152 | tf_op jit(solution)/shard_map/states/pallas_call | solution.py:192
  2.3 0.1 collective-permute-start
  2.4 0.5 %collective-permute-start.1 = (bf16[2,128,128]{2,1,0:T(8,128)(2,1)S(1)}, bf16[2,128,128]{2,1,0:T(8,128)(2,1)S(1)}, u32[]{:S(2)}, u32[]{:S(2)}) collective-permute-start(bf16[2,128,128]{2,1,0:T(8,128)(2,1)S(1)} %get-tuple-element.31), channel_id=1, source_target_pairs={{0,8},{1,9},{2,10},{3,11},{4,12},{5,13},{6,14},{7,15},{8,0},{9,1},... | collective-permute-start | bytes 196616 | tf_op jit(solution)/shard_map/ppermute | solution.py:46
  2.9 0.1 collective-permute-start.2
  3.0 1.5 %collective-permute-start.3 = (bf16[2,128,128]{2,1,0:T(8,128)(2,1)S(1)}, bf16[2,128,128]{2,1,0:T(8,128)(2,1)S(1)}, u32[]{:S(2)}, u32[]{:S(2)}) collective-permute-start(bf16[2,128,128]{2,1,0:T(8,128)(2,1)S(1)} %get-tuple-element.30), channel_id=1, source_target_pairs={{0,1},{1,0},{2,3},{3,2},{4,5},{5,4},{6,7},{7,6},{8,9},{9,8},{10,11... | collective-permute-start | bytes 196616 | tf_op jit(solution)/shard_map/ppermute | solution.py:46
  4.5 1.6 %collective-permute-start.4 = (bf16[2,128,128]{2,1,0:T(8,128)(2,1)S(1)}, bf16[2,128,128]{2,1,0:T(8,128)(2,1)S(1)}, u32[]{:S(2)}, u32[]{:S(2)}) collective-permute-start(bf16[2,128,128]{2,1,0:T(8,128)(2,1)S(1)} %get-tuple-element.31), channel_id=1, source_target_pairs={{0,1},{1,0},{2,3},{3,2},{4,5},{5,4},{6,7},{7,6},{8,9},{9,8},{10,11... | collective-permute-start | bytes 196616 | tf_op jit(solution)/shard_map/ppermute | solution.py:46
  6.1 0.0 collective-permute-done.refs_0_.one_ref
  6.1 0.4 %collective-permute-start.5 = (bf16[2,128,128]{2,1,0:T(8,128)(2,1)S(1)}, bf16[2,128,128]{2,1,0:T(8,128)(2,1)S(1)}, u32[]{:S(2)}, u32[]{:S(2)}) collective-permute-start(bf16[2,128,128]{2,1,0:T(8,128)(2,1)S(1)} %get-tuple-element.32), channel_id=1, source_target_pairs={{0,1},{1,0},{2,3},{3,2},{4,5},{5,4},{6,7},{7,6},{8,9},{9,8},{10,11... | collective-permute-start | bytes 196616 | tf_op jit(solution)/shard_map/ppermute | solution.py:46
  6.5 0.0 collective-permute-done.1.refs_1_.two_ref
  6.5 1.5 %collective-permute-start.6 = (bf16[6,128,128]{2,1,0:T(8,128)(2,1)S(1)}, bf16[6,128,128]{2,1,0:T(8,128)(2,1)S(1)}, u32[]{:S(2)}, u32[]{:S(2)}) collective-permute-start(bf16[6,128,128]{2,1,0:T(8,128)(2,1)S(1)} %get-tuple-element.34), channel_id=1, source_target_pairs={{0,4},{4,0},{8,12},{12,8},{16,20},{20,16},{24,28},{28,24},{1,5},{5... | collective-permute-start | bytes 589832 | tf_op jit(solution)/shard_map/ppermute | solution.py:36
  8.0 0.0 collective-permute-done.2.refs_2_.three_ref
  8.0 0.0 copy-start.1
  8.0 3.2 %collective-permute-start.10 = (bf16[2,128,128]{2,1,0:T(8,128)(2,1)S(1)}, bf16[2,128,128]{2,1,0:T(8,128)(2,1)S(1)}, u32[]{:S(2)}, u32[]{:S(2)}) collective-permute-start(bf16[2,128,128]{2,1,0:T(8,128)(2,1)S(1)} %sums.1), channel_id=1, source_target_pairs={{0,16},{4,20},{8,24},{12,28},{16,0},{20,4},{24,8},{28,12},{1,17},{... | collective-permute-start | bytes 196616 | tf_op jit(solution)/shard_map/ppermute | solution.py:36
  11.2 0.0 collective-permute-done.3.refs_3_
  11.2 0.0 collective-permute-done.4.refs_4_
  11.2 0.3 %collective-permute-done.5.refs_5_ = bf16[2,128,128]{2,1,0:T(8,128)(2,1)S(1)} collective-permute-done((bf16[2,128,128]{2,1,0:T(8,128)(2,1)S(1)}, bf16[2,128,128]{2,1,0:T(8,128)(2,1)S(1)}, u32[]{:S(2)}, u32[]{:S(2)}) %collective-permute-start.5) | collective-permute-done | bytes 65568 | tf_op jit(solution)/shard_map/ppermute | solution.py:46
  11.5 0.1 left.1
  11.6 0.3 collective-permute-start.7
  11.9 1.4 %collective-permute-start.8 = (bf16[2,128,128]{2,1,0:T(8,128)(2,1)S(1)}, bf16[2,128,128]{2,1,0:T(8,128)(2,1)S(1)}, u32[]{:S(2)}, u32[]{:S(2)}) collective-permute-start(bf16[2,128,128]{2,1,0:T(8,128)(2,1)S(1)} %get-tuple-element.35.refs_2_), channel_id=1, source_target_pairs={{0,8},{4,12},{8,0},{12,4},{16,24},{20,28},{24,16},{28,20},{1,9},{5... | collective-permute-start | bytes 196616 | tf_op jit(solution)/shard_map/ppermute | solution.py:36
  13.3 1.8 %collective-permute-start.9 = (bf16[2,128,128]{2,1,0:T(8,128)(2,1)S(1)}, bf16[2,128,128]{2,1,0:T(8,128)(2,1)S(1)}, u32[]{:S(2)}, u32[]{:S(2)}) collective-permute-start(bf16[2,128,128]{2,1,0:T(8,128)(2,1)S(1)} %get-tuple-element.35.refs_2_), channel_id=1, source_target_pairs={{0,12},{4,8},{8,4},{12,0},{16,28},{20,24},{24,20},{28,16},{1,13},{... | collective-permute-start | bytes 196616 | tf_op jit(solution)/shard_map/ppermute | solution.py:36
  15.1 0.0 collective-permute-done.10.refs_6_
  15.1 1.1 %collective-permute-start.11 = (bf16[2,128,128]{2,1,0:T(8,128)(2,1)S(1)}, bf16[2,128,128]{2,1,0:T(8,128)(2,1)S(1)}, u32[]{:S(2)}, u32[]{:S(2)}) collective-permute-start(bf16[2,128,128]{2,1,0:T(8,128)(2,1)S(1)} %collective-permute-done.10.refs_6_), channel_id=1, source_target_pairs={{0,1},{1,0},{2,3},{3,2},{4,5},{5,4},{6,7},{7,6},{8,9},{9,8},{10,11... | collective-permute-start | bytes 196616 | tf_op jit(solution)/shard_map/ppermute | solution.py:46
  16.2 0.9 %collective-permute-done.7.refs_3_ = bf16[2,128,128]{2,1,0:T(8,128)(2,1)S(1)} collective-permute-done((bf16[2,128,128]{2,1,0:T(8,128)(2,1)S(1)}, bf16[2,128,128]{2,1,0:T(8,128)(2,1)S(1)}, u32[]{:S(2)}, u32[]{:S(2)}) %collective-permute-start.7) | collective-permute-done | bytes 65568 | tf_op jit(solution)/shard_map/ppermute | solution.py:36
  17.1 2.1 %collective-permute-start.12 = (bf16[2,128,128]{2,1,0:T(8,128)(2,1)S(1)}, bf16[2,128,128]{2,1,0:T(8,128)(2,1)S(1)}, u32[]{:S(2)}, u32[]{:S(2)}) collective-permute-start(bf16[2,128,128]{2,1,0:T(8,128)(2,1)S(1)} %collective-permute-done.10.refs_6_), channel_id=1, source_target_pairs={{0,1},{1,0},{2,3},{3,2},{4,5},{5,4},{6,7},{7,6},{8,9},{9,8},{10,11... | collective-permute-start | bytes 196616 | tf_op jit(solution)/shard_map/ppermute | solution.py:46
  19.2 0.0 copy-done
  19.2 0.0 copy-done.1
  19.2 0.0 copy-start.2
  19.2 1.1 %intra.3 = (f32[256,512]{1,0:T(8,128)S(1)}, f32[256,512]{1,0:T(8,128)S(1)}) custom-call(s32[1]{0:T(128)} %bitcast.place_ref, bf16[512,1024]{1,0:T(8,128)(2,1)S(1)} %copy-done, f32[5,8,512]{2,1,0:T(8,128)S(1)} %copy-done.1, bf16[4,512,256]{2,1,0:T(8,128)(2,1)S(1)} %get-tuple-element.36.k_all, bf16[4,512,256]{2,1,0:T(8,128)(2,1)S(1)} %get-tuple-element.37.v_all), custom_call_target="tpu_custom_call" | custom-call | flops 402653184 | bytes 1048576 | tf_op jit(solution)/shard_map/intra/pallas_call | solution.py:211
  20.3 0.0 collective-permute-done.8.refs_4_
  20.3 0.6 %collective-permute-start.13 = (bf16[2,128,128]{2,1,0:T(8,128)(2,1)S(1)}, bf16[2,128,128]{2,1,0:T(8,128)(2,1)S(1)}, u32[]{:S(2)}, u32[]{:S(2)}) collective-permute-start(bf16[2,128,128]{2,1,0:T(8,128)(2,1)S(1)} %collective-permute-done.10.refs_6_), channel_id=1, source_target_pairs={{0,1},{1,0},{2,3},{3,2},{4,5},{5,4},{6,7},{7,6},{8,9},{9,8},{10,11... | collective-permute-start | bytes 196616 | tf_op jit(solution)/shard_map/ppermute | solution.py:46
  20.9 0.0 copy-done.2
  20.9 1.1 %intra.2 = (f32[1,1024]{1,0:T(1,128)S(1)}, f32[256,512]{1,0:T(8,128)S(1)}, f32[256,512]{1,0:T(8,128)S(1)}) custom-call(s32[1]{0:T(128)} %bitcast.place_ref, bf16[512,1024]{1,0:T(8,128)(2,1)S(1)} %copy-done, f32[5,8,512]{2,1,0:T(8,128)S(1)} %copy-done.1, bf16[4,512,256]{2,1,0:T(8,128)(2,1)S(1)} %get-tuple-element.36.k_all, ...), custom_call_target="tpu_custom_call" | custom-call | flops 402653184 | bytes 1048576 | tf_op jit(solution)/shard_map/intra/pallas_call | solution.py:211
  22.0 0.0 collective-permute-done.9.refs_5_
  22.0 0.0 collective-permute-done.6.refs_1_
  22.0 0.8 %shard_map.55 = (f32[256,512]{1,0:T(8,128)S(1)}, f32[256,512]{1,0:T(8,128)S(1)}, f32[256,512]{1,0:T(8,128)S(1)}, f32[256,512]{1,0:T(8,128)S(1)}, f32[8,512]{1,0:T(8,128)S(1)}) custom-call(s32[1]{0:T(128)} %bitcast.place_ref, bf16[512,1024]{1,0:T(8,128)(2,1)S(1)} %copy-done, f32[5,8,512]{2,1,0:T(8,128)S(1)} %copy-done.1, ...), custom_call_target="tpu_custom_call" | custom-call | flops 268435456 | bytes 4194304 | tf_op jit(solution)/shard_map/pallas_call | solution.py:261
  22.9 0.0 collective-permute-done.11.refs_0_
  22.9 0.0 collective-permute-done.12.refs_1_
  22.9 0.3 %shard_map.56 = (f32[256,512]{1,0:T(8,128)S(1)}, f32[256,512]{1,0:T(8,128)S(1)}, f32[8,512]{1,0:T(8,128)S(1)}) custom-call(s32[1]{0:T(128)} %bitcast.place_ref, bf16[512,1024]{1,0:T(8,128)(2,1)S(1)} %copy-done, f32[5,8,512]{2,1,0:T(8,128)S(1)} %copy-done.1, bf16[2,128,128]{2,1,0:T(8,128)(2,1)S(1)} %collective-permute-done.11.refs_0_, ...), custom_call_target="tpu_custom_call" | custom-call | flops 134217728 | bytes 2097152 | tf_op jit(solution)/shard_map/pallas_call | solution.py:261
  23.3 1.4 %collective-permute-done.13.refs_0_ = bf16[2,128,128]{2,1,0:T(8,128)(2,1)S(1)} collective-permute-done((bf16[2,128,128]{2,1,0:T(8,128)(2,1)S(1)}, bf16[2,128,128]{2,1,0:T(8,128)(2,1)S(1)}, u32[]{:S(2)}, u32[]{:S(2)}) %collective-permute-start.13) | collective-permute-done | bytes 65568 | tf_op jit(solution)/shard_map/ppermute | solution.py:46
  24.7 0.3 shard_map.57
  24.9 0.1 collective-permute-start.14
  25.0 1.1 %collective-permute-done.14 = f32[1,512]{1,0:T(1,128)S(1)} collective-permute-done((f32[1,512]{1,0:T(1,128)S(1)}, f32[1,512]{1,0:T(1,128)S(1)}, u32[]{:S(2)}, u32[]{:S(2)}) %collective-permute-start.14) | collective-permute-done | bytes 2080 | tf_op jit(solution)/shard_map/ppermute | solution.py:36
  26.2 1.5 %collective-permute-start.15 = (f32[1,512]{1,0:T(1,128)S(1)}, f32[1,512]{1,0:T(1,128)S(1)}, u32[]{:S(2)}, u32[]{:S(2)}) collective-permute-start(f32[1,512]{1,0:T(1,128)S(1)} %add.6), channel_id=1, source_target_pairs={{0,2},{1,3},{2,0},{3,1},{4,6},{5,7},{6,4},{7,5},{8,10},{9,11},{10,... | collective-permute-start | bytes 6152 | tf_op jit(solution)/shard_map/ppermute | solution.py:36
  27.7 2.1 %collective-permute-done.15 = f32[1,512]{1,0:T(1,128)S(1)} collective-permute-done((f32[1,512]{1,0:T(1,128)S(1)}, f32[1,512]{1,0:T(1,128)S(1)}, u32[]{:S(2)}, u32[]{:S(2)}) %collective-permute-start.15) | collective-permute-done | bytes 2080 | tf_op jit(solution)/shard_map/ppermute | solution.py:36
  29.8 1.4 %norm.1 = bf16[512,1024]{1,0:T(8,128)(2,1)} custom-call(s32[1]{0:T(128)} %bitcast.place_ref, f32[256,512]{1,0:T(8,128)S(1)} %get-tuple-element.42.refs_0_, f32[256,512]{1,0:T(8,128)S(1)} %get-tuple-element.46.refs_1_, f32[256,512]{1,0:T(8,128)S(1)} %get-tuple-element.49.refs_2_, f32[256,512]{1,0:T(8,128)S(1)} %get-tuple-element.50.refs_3_, ...), custom_call_target="tpu_custom_call" | custom-call | flops 1048576 | bytes 1048576 | tf_op jit(solution)/shard_map/norm/pallas_call | solution.py:283
  (3 shorter events, 0.0 us)
Async XLA Ops:
  0.0 19.2 %copy-start = (bf16[512,1024]{1,0:T(8,128)(2,1)S(1)}, bf16[512,1024]{1,0:T(8,128)(2,1)}, u32[]{:S(2)}) copy-start(bf16[512,1024]{1,0:T(8,128)(2,1)} %q_ref.9) | copy-start | bytes 3145732
  2.3 3.8 %collective-permute-start = (bf16[2,128,128]{2,1,0:T(8,128)(2,1)S(1)}, bf16[2,128,128]{2,1,0:T(8,128)(2,1)S(1)}, u32[]{:S(2)}, u32[]{:S(2)}) collective-permute-start(bf16[2,128,128]{2,1,0:T(8,128)(2,1)S(1)} %get-tuple-element.30), channel_id=1, source_target_pairs={{0,4},{1,5},{2,6},{3,7},{4,0},{5,1},{6,2},{7,3},{8,12},{9,13},{10,... | collective-permute-start | bytes 196616 | tf_op jit(solution)/shard_map/ppermute | solution.py:46
  2.4 4.1 %collective-permute-start.1 = (bf16[2,128,128]{2,1,0:T(8,128)(2,1)S(1)}, bf16[2,128,128]{2,1,0:T(8,128)(2,1)S(1)}, u32[]{:S(2)}, u32[]{:S(2)}) collective-permute-start(bf16[2,128,128]{2,1,0:T(8,128)(2,1)S(1)} %get-tuple-element.31), channel_id=1, source_target_pairs={{0,8},{1,9},{2,10},{3,11},{4,12},{5,13},{6,14},{7,15},{8,0},{9,1},... | collective-permute-start | bytes 196616 | tf_op jit(solution)/shard_map/ppermute | solution.py:46
  2.9 5.1 %collective-permute-start.2 = (bf16[2,128,128]{2,1,0:T(8,128)(2,1)S(1)}, bf16[2,128,128]{2,1,0:T(8,128)(2,1)S(1)}, u32[]{:S(2)}, u32[]{:S(2)}) collective-permute-start(bf16[2,128,128]{2,1,0:T(8,128)(2,1)S(1)} %get-tuple-element.32), channel_id=1, source_target_pairs={{0,12},{1,13},{2,14},{3,15},{4,8},{5,9},{6,10},{7,11},{8,4},{9,5},... | collective-permute-start | bytes 196616 | tf_op jit(solution)/shard_map/ppermute | solution.py:46
  3.0 8.2 %collective-permute-start.3 = (bf16[2,128,128]{2,1,0:T(8,128)(2,1)S(1)}, bf16[2,128,128]{2,1,0:T(8,128)(2,1)S(1)}, u32[]{:S(2)}, u32[]{:S(2)}) collective-permute-start(bf16[2,128,128]{2,1,0:T(8,128)(2,1)S(1)} %get-tuple-element.30), channel_id=1, source_target_pairs={{0,1},{1,0},{2,3},{3,2},{4,5},{5,4},{6,7},{7,6},{8,9},{9,8},{10,11... | collective-permute-start | bytes 196616 | tf_op jit(solution)/shard_map/ppermute | solution.py:46
  4.5 6.7 %collective-permute-start.4 = (bf16[2,128,128]{2,1,0:T(8,128)(2,1)S(1)}, bf16[2,128,128]{2,1,0:T(8,128)(2,1)S(1)}, u32[]{:S(2)}, u32[]{:S(2)}) collective-permute-start(bf16[2,128,128]{2,1,0:T(8,128)(2,1)S(1)} %get-tuple-element.31), channel_id=1, source_target_pairs={{0,1},{1,0},{2,3},{3,2},{4,5},{5,4},{6,7},{7,6},{8,9},{9,8},{10,11... | collective-permute-start | bytes 196616 | tf_op jit(solution)/shard_map/ppermute | solution.py:46
  6.1 5.5 %collective-permute-start.5 = (bf16[2,128,128]{2,1,0:T(8,128)(2,1)S(1)}, bf16[2,128,128]{2,1,0:T(8,128)(2,1)S(1)}, u32[]{:S(2)}, u32[]{:S(2)}) collective-permute-start(bf16[2,128,128]{2,1,0:T(8,128)(2,1)S(1)} %get-tuple-element.32), channel_id=1, source_target_pairs={{0,1},{1,0},{2,3},{3,2},{4,5},{5,4},{6,7},{7,6},{8,9},{9,8},{10,11... | collective-permute-start | bytes 196616 | tf_op jit(solution)/shard_map/ppermute | solution.py:46
  6.5 15.6 %collective-permute-start.6 = (bf16[6,128,128]{2,1,0:T(8,128)(2,1)S(1)}, bf16[6,128,128]{2,1,0:T(8,128)(2,1)S(1)}, u32[]{:S(2)}, u32[]{:S(2)}) collective-permute-start(bf16[6,128,128]{2,1,0:T(8,128)(2,1)S(1)} %get-tuple-element.34), channel_id=1, source_target_pairs={{0,4},{4,0},{8,12},{12,8},{16,20},{20,16},{24,28},{28,24},{1,5},{5... | collective-permute-start | bytes 589832 | tf_op jit(solution)/shard_map/ppermute | solution.py:36
  8.0 11.2 %copy-start.1 = (f32[5,8,512]{2,1,0:T(8,128)S(1)}, f32[5,8,512]{2,1,0:T(8,128)}, u32[]{:S(2)}) copy-start(f32[5,8,512]{2,1,0:T(8,128)} %w_ref.9) | copy-start | bytes 245764
  8.0 7.1 %collective-permute-start.10 = (bf16[2,128,128]{2,1,0:T(8,128)(2,1)S(1)}, bf16[2,128,128]{2,1,0:T(8,128)(2,1)S(1)}, u32[]{:S(2)}, u32[]{:S(2)}) collective-permute-start(bf16[2,128,128]{2,1,0:T(8,128)(2,1)S(1)} %sums.1), channel_id=1, source_target_pairs={{0,16},{4,20},{8,24},{12,28},{16,0},{20,4},{24,8},{28,12},{1,17},{... | collective-permute-start | bytes 196616 | tf_op jit(solution)/shard_map/ppermute | solution.py:36
  11.6 5.5 %collective-permute-start.7 = (bf16[2,128,128]{2,1,0:T(8,128)(2,1)S(1)}, bf16[2,128,128]{2,1,0:T(8,128)(2,1)S(1)}, u32[]{:S(2)}, u32[]{:S(2)}) collective-permute-start(bf16[2,128,128]{2,1,0:T(8,128)(2,1)S(1)} %get-tuple-element.35.refs_2_), channel_id=1, source_target_pairs={{0,4},{4,0},{8,12},{12,8},{16,20},{20,16},{24,28},{28,24},{1,5},{5... | collective-permute-start | bytes 196616 | tf_op jit(solution)/shard_map/ppermute | solution.py:36
  11.9 8.5 %collective-permute-start.8 = (bf16[2,128,128]{2,1,0:T(8,128)(2,1)S(1)}, bf16[2,128,128]{2,1,0:T(8,128)(2,1)S(1)}, u32[]{:S(2)}, u32[]{:S(2)}) collective-permute-start(bf16[2,128,128]{2,1,0:T(8,128)(2,1)S(1)} %get-tuple-element.35.refs_2_), channel_id=1, source_target_pairs={{0,8},{4,12},{8,0},{12,4},{16,24},{20,28},{24,16},{28,20},{1,9},{5... | collective-permute-start | bytes 196616 | tf_op jit(solution)/shard_map/ppermute | solution.py:36
  13.3 8.7 %collective-permute-start.9 = (bf16[2,128,128]{2,1,0:T(8,128)(2,1)S(1)}, bf16[2,128,128]{2,1,0:T(8,128)(2,1)S(1)}, u32[]{:S(2)}, u32[]{:S(2)}) collective-permute-start(bf16[2,128,128]{2,1,0:T(8,128)(2,1)S(1)} %get-tuple-element.35.refs_2_), channel_id=1, source_target_pairs={{0,12},{4,8},{8,4},{12,0},{16,28},{20,24},{24,20},{28,16},{1,13},{... | collective-permute-start | bytes 196616 | tf_op jit(solution)/shard_map/ppermute | solution.py:36
  15.1 7.8 %collective-permute-start.11 = (bf16[2,128,128]{2,1,0:T(8,128)(2,1)S(1)}, bf16[2,128,128]{2,1,0:T(8,128)(2,1)S(1)}, u32[]{:S(2)}, u32[]{:S(2)}) collective-permute-start(bf16[2,128,128]{2,1,0:T(8,128)(2,1)S(1)} %collective-permute-done.10.refs_6_), channel_id=1, source_target_pairs={{0,1},{1,0},{2,3},{3,2},{4,5},{5,4},{6,7},{7,6},{8,9},{9,8},{10,11... | collective-permute-start | bytes 196616 | tf_op jit(solution)/shard_map/ppermute | solution.py:46
  17.1 5.8 %collective-permute-start.12 = (bf16[2,128,128]{2,1,0:T(8,128)(2,1)S(1)}, bf16[2,128,128]{2,1,0:T(8,128)(2,1)S(1)}, u32[]{:S(2)}, u32[]{:S(2)}) collective-permute-start(bf16[2,128,128]{2,1,0:T(8,128)(2,1)S(1)} %collective-permute-done.10.refs_6_), channel_id=1, source_target_pairs={{0,1},{1,0},{2,3},{3,2},{4,5},{5,4},{6,7},{7,6},{8,9},{9,8},{10,11... | collective-permute-start | bytes 196616 | tf_op jit(solution)/shard_map/ppermute | solution.py:46
  19.2 1.7 %copy-start.2 = (f32[1024]{0:T(1024)S(1)}, f32[1024]{0:T(1024)}, u32[]{:S(2)}) copy-start(f32[1024]{0:T(1024)} %param.9) | copy-start | bytes 12292
  20.3 4.3 %collective-permute-start.13 = (bf16[2,128,128]{2,1,0:T(8,128)(2,1)S(1)}, bf16[2,128,128]{2,1,0:T(8,128)(2,1)S(1)}, u32[]{:S(2)}, u32[]{:S(2)}) collective-permute-start(bf16[2,128,128]{2,1,0:T(8,128)(2,1)S(1)} %collective-permute-done.10.refs_6_), channel_id=1, source_target_pairs={{0,1},{1,0},{2,3},{3,2},{4,5},{5,4},{6,7},{7,6},{8,9},{9,8},{10,11... | collective-permute-start | bytes 196616 | tf_op jit(solution)/shard_map/ppermute | solution.py:46
  24.9 1.2 %collective-permute-start.14 = (f32[1,512]{1,0:T(1,128)S(1)}, f32[1,512]{1,0:T(1,128)S(1)}, u32[]{:S(2)}, u32[]{:S(2)}) collective-permute-start(f32[1,512]{1,0:T(1,128)S(1)} %get-tuple-element.51), channel_id=1, source_target_pairs={{0,1},{1,0},{2,3},{3,2},{4,5},{5,4},{6,7},{7,6},{8,9},{9,8},{10,11... | collective-permute-start | bytes 6152 | tf_op jit(solution)/shard_map/ppermute | solution.py:36
  26.2 3.6 %collective-permute-start.15 = (f32[1,512]{1,0:T(1,128)S(1)}, f32[1,512]{1,0:T(1,128)S(1)}, u32[]{:S(2)}, u32[]{:S(2)}) collective-permute-start(f32[1,512]{1,0:T(1,128)S(1)} %add.6), channel_id=1, source_target_pairs={{0,2},{1,3},{2,0},{3,1},{4,6},{5,7},{6,4},{7,5},{8,10},{9,11},{10,... | collective-permute-start | bytes 6152 | tf_op jit(solution)/shard_map/ppermute | solution.py:36

commit v7 on v6

--- a/solution.py
+++ b/solution.py
@@ -160,10 +160,10 @@
 
 
 def norm_kernel(group, full_width, place_ref, *refs):
-    total_refs, (sq_ref, gain_ref, out_hbm, buf, sems) = refs[:QUAD], refs[QUAD:]
+    total_refs, share_refs, (gain_ref, out_hbm, buf, sems) = refs[:QUAD], refs[QUAD:-4], refs[-4:]
     width = group * HEAD_DIM
     place = place_ref[0] & (QUAD - 1)
-    scale = lax.rsqrt(sq_ref[...] / full_width + EPSILON)
+    scale = lax.rsqrt(functools.reduce(jnp.add, (ref[...] for ref in share_refs)) / full_width + EPSILON)
     copies = []
     for r in range(QUAD):
         cols = pl.ds(pl.multiple_of((place ^ r) * width, width), width)
@@ -275,21 +275,18 @@
     squares = readout(((3, True, top_reads(0)), (1, True, top_reads(1))), (tops[3], tops[1]), squares)
     squares = readout(((2, True, top_reads(0)),), (tops[2],), squares, finish=True)
 
-    mask = 1
-    while mask < lax.axis_size("head"):
-        squares = squares + exchanged(squares, "head", mask)
-        mask *= 2
+    shares = [squares] + [exchanged(squares, "head", mask) for mask in range(1, lax.axis_size("head"))]
 
     return pl.pallas_call(
         functools.partial(norm_kernel, group, full_width),
         out_shape=sds((rows, width), BF16),
-        in_specs=[SMEM] + [VMEM] * (QUAD + 2),
+        in_specs=[SMEM] + [VMEM] * (QUAD + len(shares) + 1),
         out_specs=ANY,
         scratch_shapes=[pltpu.VMEM((QUAD,) + panel, BF16), pltpu.SemaphoreType.DMA((QUAD,))],
         compiler_params=params(),
         cost_estimate=cost(2 * rows * width, 2 * rows * width),
         name="norm",
-    )(place, *(totals[r] for r in range(QUAD)), squares, gain)
+    )(place, *(totals[r] for r in range(QUAD)), *shares, gain)
 
 
 def solution(mesh):

time: 31.3 us -> 31.4 us (level)
  the two profiles are of different devices: /device:TPU:16 before, /device:TPU:17 now
where the time goes in v7:
time: 31.4 us; the launch traced here: 31.2 us
  starting transfers between devices  18.9 us (60%)
  Pallas kernels  7.42 us (24%)
  waiting for transfers between devices  4.82 us (15%)
    ppermute x8, starting transfers between devices, exchanged(): return lax.ppermute(block, axis, [(i, i ^ mask) for i in range(count)])  10.5 us
    ppermute x9, starting transfers between devices, exchanged_in(): return lax.ppermute(block, ('seq', 'head'), route)  8.43 us
    ppermute x8, waiting for transfers between devices, exchanged(): return lax.ppermute(block, axis, [(i, i ^ mask) for i in range(count)])  3.52 us
    pallas_call x1, Pallas kernels, local(): pl.pallas_call(functools.partial(states_kernel, group), out_shape=(sds((Q...  2.3 us
    pallas_call x2, Pallas kernels, local(): pl.pallas_call(functools.partial(intra_kernel, group, groups), out_shape=...  2.24 us
    pallas_call x3, Pallas kernels, readout(): pl.pallas_call(kernel, out_shape=tuple(shapes), in_specs=[SMEM] + [VMEM]...  1.44 us
    pallas_call x1, Pallas kernels, local(): pl.pallas_call(functools.partial(norm_kernel, group, full_width), out_sha...  1.36 us
    ppermute x9, waiting for transfers between devices, exchanged_in(): return lax.ppermute(block, ('seq', 'head'), route)  1.3 us
  transfers between devices with their start and end apart: 17, of which 5 were waited for; matrix products, arithmetic and copies ran while one was open for 0% of the time, Pallas kernels for 11%

profile of v7, /device:TPU:17, one launch (start us, length us, event | category | flops | bytes accessed | tf_op | source)
XLA Modules:
  0.0 31.2 jit_solution(13337488349076715113)
XLA Ops:
  0.0 0.0 copy-start
  0.0 2.3 %states.1 = (bf16[4,512,256]{2,1,0:T(8,128)(2,1)S(1)}, bf16[4,512,256]{2,1,0:T(8,128)(2,1)S(1)}, f32[2,128,128]{2,1,0:T(8,128)S(1)}, bf16[2,128,128]{2,1,0:T(8,1...) custom-call(s32[1]{0:T(128)} %bitcast.place_ref, ...), custom_call_target="tpu_custom_call" | custom-call | flops 134217728 | bytes 2097152 | tf_op jit(solution)/shard_map/states/pallas_call | solution.py:192
  2.3 0.7 %collective-permute-start = (bf16[2,128,128]{2,1,0:T(8,128)(2,1)S(1)}, bf16[2,128,128]{2,1,0:T(8,128)(2,1)S(1)}, u32[]{:S(2)}, u32[]{:S(2)}) collective-permute-start(bf16[2,128,128]{2,1,0:T(8,128)(2,1)S(1)} %get-tuple-element.30), channel_id=1, source_target_pairs={{0,4},{1,5},{2,6},{3,7},{4,0},{5,1},{6,2},{7,3},{8,12},{9,13},{10,... | collective-permute-start | bytes 196616 | tf_op jit(solution)/shard_map/ppermute | solution.py:46
  3.1 0.1 collective-permute-start.1
  3.1 0.4 %collective-permute-start.2 = (bf16[2,128,128]{2,1,0:T(8,128)(2,1)S(1)}, bf16[2,128,128]{2,1,0:T(8,128)(2,1)S(1)}, u32[]{:S(2)}, u32[]{:S(2)}) collective-permute-start(bf16[2,128,128]{2,1,0:T(8,128)(2,1)S(1)} %get-tuple-element.32), channel_id=1, source_target_pairs={{0,12},{1,13},{2,14},{3,15},{4,8},{5,9},{6,10},{7,11},{8,4},{9,5},... | collective-permute-start | bytes 196616 | tf_op jit(solution)/shard_map/ppermute | solution.py:46
  3.6 1.2 %collective-permute-start.3 = (bf16[2,128,128]{2,1,0:T(8,128)(2,1)S(1)}, bf16[2,128,128]{2,1,0:T(8,128)(2,1)S(1)}, u32[]{:S(2)}, u32[]{:S(2)}) collective-permute-start(bf16[2,128,128]{2,1,0:T(8,128)(2,1)S(1)} %get-tuple-element.30), channel_id=1, source_target_pairs={{0,1},{1,0},{2,3},{3,2},{4,5},{5,4},{6,7},{7,6},{8,9},{9,8},{10,11... | collective-permute-start | bytes 196616 | tf_op jit(solution)/shard_map/ppermute | solution.py:46
  4.8 1.3 %collective-permute-start.4 = (bf16[2,128,128]{2,1,0:T(8,128)(2,1)S(1)}, bf16[2,128,128]{2,1,0:T(8,128)(2,1)S(1)}, u32[]{:S(2)}, u32[]{:S(2)}) collective-permute-start(bf16[2,128,128]{2,1,0:T(8,128)(2,1)S(1)} %get-tuple-element.31), channel_id=1, source_target_pairs={{0,1},{1,0},{2,3},{3,2},{4,5},{5,4},{6,7},{7,6},{8,9},{9,8},{10,11... | collective-permute-start | bytes 196616 | tf_op jit(solution)/shard_map/ppermute | solution.py:46
  6.1 0.0 collective-permute-done.refs_0_.one_ref
  6.1 0.1 collective-permute-start.5
  6.2 0.0 collective-permute-done.1.refs_1_.two_ref
  6.2 1.2 %collective-permute-start.6 = (bf16[6,128,128]{2,1,0:T(8,128)(2,1)S(1)}, bf16[6,128,128]{2,1,0:T(8,128)(2,1)S(1)}, u32[]{:S(2)}, u32[]{:S(2)}) collective-permute-start(bf16[6,128,128]{2,1,0:T(8,128)(2,1)S(1)} %get-tuple-element.34), channel_id=1, source_target_pairs={{0,4},{4,0},{8,12},{12,8},{16,20},{20,16},{24,28},{28,24},{1,5},{5... | collective-permute-start | bytes 589832 | tf_op jit(solution)/shard_map/ppermute | solution.py:36
  7.5 0.0 collective-permute-done.2.refs_2_.three_ref
  7.5 0.0 copy-start.1
  7.5 1.6 %collective-permute-start.10 = (bf16[2,128,128]{2,1,0:T(8,128)(2,1)S(1)}, bf16[2,128,128]{2,1,0:T(8,128)(2,1)S(1)}, u32[]{:S(2)}, u32[]{:S(2)}) collective-permute-start(bf16[2,128,128]{2,1,0:T(8,128)(2,1)S(1)} %sums.1), channel_id=1, source_target_pairs={{0,16},{4,20},{8,24},{12,28},{16,0},{20,4},{24,8},{28,12},{1,17},{... | collective-permute-start | bytes 196616 | tf_op jit(solution)/shard_map/ppermute | solution.py:36
  9.1 0.0 collective-permute-done.3.refs_3_
  9.1 0.0 collective-permute-done.4.refs_4_
  9.1 1.1 %collective-permute-done.5.refs_5_ = bf16[2,128,128]{2,1,0:T(8,128)(2,1)S(1)} collective-permute-done((bf16[2,128,128]{2,1,0:T(8,128)(2,1)S(1)}, bf16[2,128,128]{2,1,0:T(8,128)(2,1)S(1)}, u32[]{:S(2)}, u32[]{:S(2)}) %collective-permute-start.5) | collective-permute-done | bytes 65568 | tf_op jit(solution)/shard_map/ppermute | solution.py:46
  10.2 0.1 left.1
  10.3 0.6 %collective-permute-start.7 = (bf16[2,128,128]{2,1,0:T(8,128)(2,1)S(1)}, bf16[2,128,128]{2,1,0:T(8,128)(2,1)S(1)}, u32[]{:S(2)}, u32[]{:S(2)}) collective-permute-start(bf16[2,128,128]{2,1,0:T(8,128)(2,1)S(1)} %get-tuple-element.35.refs_2_), channel_id=1, source_target_pairs={{0,4},{4,0},{8,12},{12,8},{16,20},{20,16},{24,28},{28,24},{1,5},{5... | collective-permute-start | bytes 196616 | tf_op jit(solution)/shard_map/ppermute | solution.py:36
  10.8 1.0 %collective-permute-start.8 = (bf16[2,128,128]{2,1,0:T(8,128)(2,1)S(1)}, bf16[2,128,128]{2,1,0:T(8,128)(2,1)S(1)}, u32[]{:S(2)}, u32[]{:S(2)}) collective-permute-start(bf16[2,128,128]{2,1,0:T(8,128)(2,1)S(1)} %get-tuple-element.35.refs_2_), channel_id=1, source_target_pairs={{0,8},{4,12},{8,0},{12,4},{16,24},{20,28},{24,16},{28,20},{1,9},{5... | collective-permute-start | bytes 196616 | tf_op jit(solution)/shard_map/ppermute | solution.py:36
  11.8 1.2 %collective-permute-start.9 = (bf16[2,128,128]{2,1,0:T(8,128)(2,1)S(1)}, bf16[2,128,128]{2,1,0:T(8,128)(2,1)S(1)}, u32[]{:S(2)}, u32[]{:S(2)}) collective-permute-start(bf16[2,128,128]{2,1,0:T(8,128)(2,1)S(1)} %get-tuple-element.35.refs_2_), channel_id=1, source_target_pairs={{0,12},{4,8},{8,4},{12,0},{16,28},{20,24},{24,20},{28,16},{1,13},{... | collective-permute-start | bytes 196616 | tf_op jit(solution)/shard_map/ppermute | solution.py:36
  13.0 0.0 collective-permute-done.10.refs_6_
  13.0 1.2 %collective-permute-start.11 = (bf16[2,128,128]{2,1,0:T(8,128)(2,1)S(1)}, bf16[2,128,128]{2,1,0:T(8,128)(2,1)S(1)}, u32[]{:S(2)}, u32[]{:S(2)}) collective-permute-start(bf16[2,128,128]{2,1,0:T(8,128)(2,1)S(1)} %collective-permute-done.10.refs_6_), channel_id=1, source_target_pairs={{0,1},{1,0},{2,3},{3,2},{4,5},{5,4},{6,7},{7,6},{8,9},{9,8},{10,11... | collective-permute-start | bytes 196616 | tf_op jit(solution)/shard_map/ppermute | solution.py:46
  14.2 1.0 %collective-permute-done.7.refs_3_ = bf16[2,128,128]{2,1,0:T(8,128)(2,1)S(1)} collective-permute-done((bf16[2,128,128]{2,1,0:T(8,128)(2,1)S(1)}, bf16[2,128,128]{2,1,0:T(8,128)(2,1)S(1)}, u32[]{:S(2)}, u32[]{:S(2)}) %collective-permute-start.7) | collective-permute-done | bytes 65568 | tf_op jit(solution)/shard_map/ppermute | solution.py:36
  15.2 2.7 %collective-permute-start.12 = (bf16[2,128,128]{2,1,0:T(8,128)(2,1)S(1)}, bf16[2,128,128]{2,1,0:T(8,128)(2,1)S(1)}, u32[]{:S(2)}, u32[]{:S(2)}) collective-permute-start(bf16[2,128,128]{2,1,0:T(8,128)(2,1)S(1)} %collective-permute-done.10.refs_6_), channel_id=1, source_target_pairs={{0,1},{1,0},{2,3},{3,2},{4,5},{5,4},{6,7},{7,6},{8,9},{9,8},{10,11... | collective-permute-start | bytes 196616 | tf_op jit(solution)/shard_map/ppermute | solution.py:46
  17.9 0.0 copy-done
  17.9 0.0 copy-done.1
  17.9 0.0 copy-start.2
  17.9 1.1 %intra.3 = (f32[256,512]{1,0:T(8,128)S(1)}, f32[256,512]{1,0:T(8,128)S(1)}) custom-call(s32[1]{0:T(128)} %bitcast.place_ref, bf16[512,1024]{1,0:T(8,128)(2,1)S(1)} %copy-done, f32[5,8,512]{2,1,0:T(8,128)S(1)} %copy-done.1, bf16[4,512,256]{2,1,0:T(8,128)(2,1)S(1)} %get-tuple-element.36.k_all, bf16[4,512,256]{2,1,0:T(8,128)(2,1)S(1)} %get-tuple-element.37.v_all), custom_call_target="tpu_custom_call" | custom-call | flops 402653184 | bytes 1048576 | tf_op jit(solution)/shard_map/intra/pallas_call | solution.py:211
  19.0 0.0 collective-permute-done.8.refs_4_
  19.0 0.7 %collective-permute-start.13 = (bf16[2,128,128]{2,1,0:T(8,128)(2,1)S(1)}, bf16[2,128,128]{2,1,0:T(8,128)(2,1)S(1)}, u32[]{:S(2)}, u32[]{:S(2)}) collective-permute-start(bf16[2,128,128]{2,1,0:T(8,128)(2,1)S(1)} %collective-permute-done.10.refs_6_), channel_id=1, source_target_pairs={{0,1},{1,0},{2,3},{3,2},{4,5},{5,4},{6,7},{7,6},{8,9},{9,8},{10,11... | collective-permute-start | bytes 196616 | tf_op jit(solution)/shard_map/ppermute | solution.py:46
  19.7 0.0 copy-done.2
  19.7 1.1 %intra.2 = (f32[1,1024]{1,0:T(1,128)S(1)}, f32[256,512]{1,0:T(8,128)S(1)}, f32[256,512]{1,0:T(8,128)S(1)}) custom-call(s32[1]{0:T(128)} %bitcast.place_ref, bf16[512,1024]{1,0:T(8,128)(2,1)S(1)} %copy-done, f32[5,8,512]{2,1,0:T(8,128)S(1)} %copy-done.1, bf16[4,512,256]{2,1,0:T(8,128)(2,1)S(1)} %get-tuple-element.36.k_all, ...), custom_call_target="tpu_custom_call" | custom-call | flops 402653184 | bytes 1048576 | tf_op jit(solution)/shard_map/intra/pallas_call | solution.py:211
  20.8 0.0 collective-permute-done.9.refs_5_
  20.8 0.0 collective-permute-done.6.refs_1_
  20.8 0.8 %shard_map.55 = (f32[256,512]{1,0:T(8,128)S(1)}, f32[256,512]{1,0:T(8,128)S(1)}, f32[256,512]{1,0:T(8,128)S(1)}, f32[256,512]{1,0:T(8,128)S(1)}, f32[8,512]{1,0:T(8,128)S(1)}) custom-call(s32[1]{0:T(128)} %bitcast.place_ref, bf16[512,1024]{1,0:T(8,128)(2,1)S(1)} %copy-done, f32[5,8,512]{2,1,0:T(8,128)S(1)} %copy-done.1, ...), custom_call_target="tpu_custom_call" | custom-call | flops 268435456 | bytes 4194304 | tf_op jit(solution)/shard_map/pallas_call | solution.py:261
  21.7 0.0 collective-permute-done.11.refs_0_
  21.7 0.0 collective-permute-done.12.refs_1_
  21.7 0.3 %shard_map.56 = (f32[256,512]{1,0:T(8,128)S(1)}, f32[256,512]{1,0:T(8,128)S(1)}, f32[8,512]{1,0:T(8,128)S(1)}) custom-call(s32[1]{0:T(128)} %bitcast.place_ref, bf16[512,1024]{1,0:T(8,128)(2,1)S(1)} %copy-done, f32[5,8,512]{2,1,0:T(8,128)S(1)} %copy-done.1, bf16[2,128,128]{2,1,0:T(8,128)(2,1)S(1)} %collective-permute-done.11.refs_0_, ...), custom_call_target="tpu_custom_call" | custom-call | flops 134217728 | bytes 2097152 | tf_op jit(solution)/shard_map/pallas_call | solution.py:261
  22.0 0.2 collective-permute-done.13.refs_0_
  22.2 0.3 shard_map.57
  22.5 3.2 %collective-permute-start.14 = (f32[1,512]{1,0:T(1,128)S(1)}, f32[1,512]{1,0:T(1,128)S(1)}, u32[]{:S(2)}, u32[]{:S(2)}) collective-permute-start(f32[1,512]{1,0:T(1,128)S(1)} %get-tuple-element.51.refs_4_), channel_id=1, source_target_pairs={{0,1},{1,0},{2,3},{3,2},{4,5},{5,4},{6,7},{7,6},{8,9},{9,8},{10,11... | collective-permute-start | bytes 6152 | tf_op jit(solution)/shard_map/ppermute | solution.py:36
  25.7 1.2 %collective-permute-start.15 = (f32[1,512]{1,0:T(1,128)S(1)}, f32[1,512]{1,0:T(1,128)S(1)}, u32[]{:S(2)}, u32[]{:S(2)}) collective-permute-start(f32[1,512]{1,0:T(1,128)S(1)} %get-tuple-element.51.refs_4_), channel_id=1, source_target_pairs={{0,2},{1,3},{2,0},{3,1},{4,6},{5,7},{6,4},{7,5},{8,10},{9,11},{10,... | collective-permute-start | bytes 6152 | tf_op jit(solution)/shard_map/ppermute | solution.py:36
  26.9 0.5 %collective-permute-start.16 = (f32[1,512]{1,0:T(1,128)S(1)}, f32[1,512]{1,0:T(1,128)S(1)}, u32[]{:S(2)}, u32[]{:S(2)}) collective-permute-start(f32[1,512]{1,0:T(1,128)S(1)} %get-tuple-element.51.refs_4_), channel_id=1, source_target_pairs={{0,3},{1,2},{2,1},{3,0},{4,7},{5,6},{6,5},{7,4},{8,11},{9,10},{10,... | collective-permute-start | bytes 6152 | tf_op jit(solution)/shard_map/ppermute | solution.py:36
  27.4 0.0 collective-permute-done.14.refs_5_
  27.4 0.7 %collective-permute-done.15.refs_6_ = f32[1,512]{1,0:T(1,128)S(1)} collective-permute-done((f32[1,512]{1,0:T(1,128)S(1)}, f32[1,512]{1,0:T(1,128)S(1)}, u32[]{:S(2)}, u32[]{:S(2)}) %collective-permute-start.15) | collective-permute-done | bytes 2080 | tf_op jit(solution)/shard_map/ppermute | solution.py:36
  28.1 1.8 %collective-permute-done.16.refs_7_ = f32[1,512]{1,0:T(1,128)S(1)} collective-permute-done((f32[1,512]{1,0:T(1,128)S(1)}, f32[1,512]{1,0:T(1,128)S(1)}, u32[]{:S(2)}, u32[]{:S(2)}) %collective-permute-start.16) | collective-permute-done | bytes 2080 | tf_op jit(solution)/shard_map/ppermute | solution.py:36
  29.9 1.4 %norm.1 = bf16[512,1024]{1,0:T(8,128)(2,1)} custom-call(s32[1]{0:T(128)} %bitcast.place_ref, f32[256,512]{1,0:T(8,128)S(1)} %get-tuple-element.42.refs_0_, f32[256,512]{1,0:T(8,128)S(1)} %get-tuple-element.46.refs_1_, f32[256,512]{1,0:T(8,128)S(1)} %get-tuple-element.49.refs_2_, f32[256,512]{1,0:T(8,128)S(1)} %get-tuple-element.50.refs_3_, ...), custom_call_target="tpu_custom_call" | custom-call | flops 1048576 | bytes 1048576 | tf_op jit(solution)/shard_map/norm/pallas_call | solution.py:280
  (1 shorter events, 0.0 us)
Async XLA Ops:
  0.0 17.9 %copy-start = (bf16[512,1024]{1,0:T(8,128)(2,1)S(1)}, bf16[512,1024]{1,0:T(8,128)(2,1)}, u32[]{:S(2)}) copy-start(bf16[512,1024]{1,0:T(8,128)(2,1)} %q_ref.9) | copy-start | bytes 3145732
  2.3 3.8 %collective-permute-start = (bf16[2,128,128]{2,1,0:T(8,128)(2,1)S(1)}, bf16[2,128,128]{2,1,0:T(8,128)(2,1)S(1)}, u32[]{:S(2)}, u32[]{:S(2)}) collective-permute-start(bf16[2,128,128]{2,1,0:T(8,128)(2,1)S(1)} %get-tuple-element.30), channel_id=1, source_target_pairs={{0,4},{1,5},{2,6},{3,7},{4,0},{5,1},{6,2},{7,3},{8,12},{9,13},{10,... | collective-permute-start | bytes 196616 | tf_op jit(solution)/shard_map/ppermute | solution.py:46
  3.1 3.2 %collective-permute-start.1 = (bf16[2,128,128]{2,1,0:T(8,128)(2,1)S(1)}, bf16[2,128,128]{2,1,0:T(8,128)(2,1)S(1)}, u32[]{:S(2)}, u32[]{:S(2)}) collective-permute-start(bf16[2,128,128]{2,1,0:T(8,128)(2,1)S(1)} %get-tuple-element.31), channel_id=1, source_target_pairs={{0,8},{1,9},{2,10},{3,11},{4,12},{5,13},{6,14},{7,15},{8,0},{9,1},... | collective-permute-start | bytes 196616 | tf_op jit(solution)/shard_map/ppermute | solution.py:46
  3.1 4.3 %collective-permute-start.2 = (bf16[2,128,128]{2,1,0:T(8,128)(2,1)S(1)}, bf16[2,128,128]{2,1,0:T(8,128)(2,1)S(1)}, u32[]{:S(2)}, u32[]{:S(2)}) collective-permute-start(bf16[2,128,128]{2,1,0:T(8,128)(2,1)S(1)} %get-tuple-element.32), channel_id=1, source_target_pairs={{0,12},{1,13},{2,14},{3,15},{4,8},{5,9},{6,10},{7,11},{8,4},{9,5},... | collective-permute-start | bytes 196616 | tf_op jit(solution)/shard_map/ppermute | solution.py:46
  3.6 5.5 %collective-permute-start.3 = (bf16[2,128,128]{2,1,0:T(8,128)(2,1)S(1)}, bf16[2,128,128]{2,1,0:T(8,128)(2,1)S(1)}, u32[]{:S(2)}, u32[]{:S(2)}) collective-permute-start(bf16[2,128,128]{2,1,0:T(8,128)(2,1)S(1)} %get-tuple-element.30), channel_id=1, source_target_pairs={{0,1},{1,0},{2,3},{3,2},{4,5},{5,4},{6,7},{7,6},{8,9},{9,8},{10,11... | collective-permute-start | bytes 196616 | tf_op jit(solution)/shard_map/ppermute | solution.py:46
  4.8 4.3 %collective-permute-start.4 = (bf16[2,128,128]{2,1,0:T(8,128)(2,1)S(1)}, bf16[2,128,128]{2,1,0:T(8,128)(2,1)S(1)}, u32[]{:S(2)}, u32[]{:S(2)}) collective-permute-start(bf16[2,128,128]{2,1,0:T(8,128)(2,1)S(1)} %get-tuple-element.31), channel_id=1, source_target_pairs={{0,1},{1,0},{2,3},{3,2},{4,5},{5,4},{6,7},{7,6},{8,9},{9,8},{10,11... | collective-permute-start | bytes 196616 | tf_op jit(solution)/shard_map/ppermute | solution.py:46
  6.1 4.1 %collective-permute-start.5 = (bf16[2,128,128]{2,1,0:T(8,128)(2,1)S(1)}, bf16[2,128,128]{2,1,0:T(8,128)(2,1)S(1)}, u32[]{:S(2)}, u32[]{:S(2)}) collective-permute-start(bf16[2,128,128]{2,1,0:T(8,128)(2,1)S(1)} %get-tuple-element.32), channel_id=1, source_target_pairs={{0,1},{1,0},{2,3},{3,2},{4,5},{5,4},{6,7},{7,6},{8,9},{9,8},{10,11... | collective-permute-start | bytes 196616 | tf_op jit(solution)/shard_map/ppermute | solution.py:46
  6.2 14.6 %collective-permute-start.6 = (bf16[6,128,128]{2,1,0:T(8,128)(2,1)S(1)}, bf16[6,128,128]{2,1,0:T(8,128)(2,1)S(1)}, u32[]{:S(2)}, u32[]{:S(2)}) collective-permute-start(bf16[6,128,128]{2,1,0:T(8,128)(2,1)S(1)} %get-tuple-element.34), channel_id=1, source_target_pairs={{0,4},{4,0},{8,12},{12,8},{16,20},{20,16},{24,28},{28,24},{1,5},{5... | collective-permute-start | bytes 589832 | tf_op jit(solution)/shard_map/ppermute | solution.py:36
  7.5 10.4 %copy-start.1 = (f32[5,8,512]{2,1,0:T(8,128)S(1)}, f32[5,8,512]{2,1,0:T(8,128)}, u32[]{:S(2)}) copy-start(f32[5,8,512]{2,1,0:T(8,128)} %w_ref.9) | copy-start | bytes 245764
  7.5 5.5 %collective-permute-start.10 = (bf16[2,128,128]{2,1,0:T(8,128)(2,1)S(1)}, bf16[2,128,128]{2,1,0:T(8,128)(2,1)S(1)}, u32[]{:S(2)}, u32[]{:S(2)}) collective-permute-start(bf16[2,128,128]{2,1,0:T(8,128)(2,1)S(1)} %sums.1), channel_id=1, source_target_pairs={{0,16},{4,20},{8,24},{12,28},{16,0},{20,4},{24,8},{28,12},{1,17},{... | collective-permute-start | bytes 196616 | tf_op jit(solution)/shard_map/ppermute | solution.py:36
  10.3 4.9 %collective-permute-start.7 = (bf16[2,128,128]{2,1,0:T(8,128)(2,1)S(1)}, bf16[2,128,128]{2,1,0:T(8,128)(2,1)S(1)}, u32[]{:S(2)}, u32[]{:S(2)}) collective-permute-start(bf16[2,128,128]{2,1,0:T(8,128)(2,1)S(1)} %get-tuple-element.35.refs_2_), channel_id=1, source_target_pairs={{0,4},{4,0},{8,12},{12,8},{16,20},{20,16},{24,28},{28,24},{1,5},{5... | collective-permute-start | bytes 196616 | tf_op jit(solution)/shard_map/ppermute | solution.py:36
  10.8 8.2 %collective-permute-start.8 = (bf16[2,128,128]{2,1,0:T(8,128)(2,1)S(1)}, bf16[2,128,128]{2,1,0:T(8,128)(2,1)S(1)}, u32[]{:S(2)}, u32[]{:S(2)}) collective-permute-start(bf16[2,128,128]{2,1,0:T(8,128)(2,1)S(1)} %get-tuple-element.35.refs_2_), channel_id=1, source_target_pairs={{0,8},{4,12},{8,0},{12,4},{16,24},{20,28},{24,16},{28,20},{1,9},{5... | collective-permute-start | bytes 196616 | tf_op jit(solution)/shard_map/ppermute | solution.py:36
  11.8 9.0 %collective-permute-start.9 = (bf16[2,128,128]{2,1,0:T(8,128)(2,1)S(1)}, bf16[2,128,128]{2,1,0:T(8,128)(2,1)S(1)}, u32[]{:S(2)}, u32[]{:S(2)}) collective-permute-start(bf16[2,128,128]{2,1,0:T(8,128)(2,1)S(1)} %get-tuple-element.35.refs_2_), channel_id=1, source_target_pairs={{0,12},{4,8},{8,4},{12,0},{16,28},{20,24},{24,20},{28,16},{1,13},{... | collective-permute-start | bytes 196616 | tf_op jit(solution)/shard_map/ppermute | solution.py:36
  13.0 8.7 %collective-permute-start.11 = (bf16[2,128,128]{2,1,0:T(8,128)(2,1)S(1)}, bf16[2,128,128]{2,1,0:T(8,128)(2,1)S(1)}, u32[]{:S(2)}, u32[]{:S(2)}) collective-permute-start(bf16[2,128,128]{2,1,0:T(8,128)(2,1)S(1)} %collective-permute-done.10.refs_6_), channel_id=1, source_target_pairs={{0,1},{1,0},{2,3},{3,2},{4,5},{5,4},{6,7},{7,6},{8,9},{9,8},{10,11... | collective-permute-start | bytes 196616 | tf_op jit(solution)/shard_map/ppermute | solution.py:46
  15.2 6.5 %collective-permute-start.12 = (bf16[2,128,128]{2,1,0:T(8,128)(2,1)S(1)}, bf16[2,128,128]{2,1,0:T(8,128)(2,1)S(1)}, u32[]{:S(2)}, u32[]{:S(2)}) collective-permute-start(bf16[2,128,128]{2,1,0:T(8,128)(2,1)S(1)} %collective-permute-done.10.refs_6_), channel_id=1, source_target_pairs={{0,1},{1,0},{2,3},{3,2},{4,5},{5,4},{6,7},{7,6},{8,9},{9,8},{10,11... | collective-permute-start | bytes 196616 | tf_op jit(solution)/shard_map/ppermute | solution.py:46
  17.9 1.8 %copy-start.2 = (f32[1024]{0:T(1024)S(1)}, f32[1024]{0:T(1024)}, u32[]{:S(2)}) copy-start(f32[1024]{0:T(1024)} %param.9) | copy-start | bytes 12292
  19.0 3.2 %collective-permute-start.13 = (bf16[2,128,128]{2,1,0:T(8,128)(2,1)S(1)}, bf16[2,128,128]{2,1,0:T(8,128)(2,1)S(1)}, u32[]{:S(2)}, u32[]{:S(2)}) collective-permute-start(bf16[2,128,128]{2,1,0:T(8,128)(2,1)S(1)} %collective-permute-done.10.refs_6_), channel_id=1, source_target_pairs={{0,1},{1,0},{2,3},{3,2},{4,5},{5,4},{6,7},{7,6},{8,9},{9,8},{10,11... | collective-permute-start | bytes 196616 | tf_op jit(solution)/shard_map/ppermute | solution.py:46
  22.5 4.9 %collective-permute-start.14 = (f32[1,512]{1,0:T(1,128)S(1)}, f32[1,512]{1,0:T(1,128)S(1)}, u32[]{:S(2)}, u32[]{:S(2)}) collective-permute-start(f32[1,512]{1,0:T(1,128)S(1)} %get-tuple-element.51.refs_4_), channel_id=1, source_target_pairs={{0,1},{1,0},{2,3},{3,2},{4,5},{5,4},{6,7},{7,6},{8,9},{9,8},{10,11... | collective-permute-start | bytes 6152 | tf_op jit(solution)/shard_map/ppermute | solution.py:36
  25.7 2.4 %collective-permute-start.15 = (f32[1,512]{1,0:T(1,128)S(1)}, f32[1,512]{1,0:T(1,128)S(1)}, u32[]{:S(2)}, u32[]{:S(2)}) collective-permute-start(f32[1,512]{1,0:T(1,128)S(1)} %get-tuple-element.51.refs_4_), channel_id=1, source_target_pairs={{0,2},{1,3},{2,0},{3,1},{4,6},{5,7},{6,4},{7,5},{8,10},{9,11},{10,... | collective-permute-start | bytes 6152 | tf_op jit(solution)/shard_map/ppermute | solution.py:36
  26.9 3.0 %collective-permute-start.16 = (f32[1,512]{1,0:T(1,128)S(1)}, f32[1,512]{1,0:T(1,128)S(1)}, u32[]{:S(2)}, u32[]{:S(2)}) collective-permute-start(f32[1,512]{1,0:T(1,128)S(1)} %get-tuple-element.51.refs_4_), channel_id=1, source_target_pairs={{0,3},{1,2},{2,1},{3,0},{4,7},{5,6},{6,5},{7,4},{8,11},{9,10},{10,... | collective-permute-start | bytes 6152 | tf_op jit(solution)/shard_map/ppermute | solution.py:36

commit v8 on v7

--- a/solution.py
+++ b/solution.py
@@ -58,7 +58,7 @@
     return pl.ds(head * HEAD_DIM, HEAD_DIM)
 
 
-def states_kernel(group, place_ref, k_hbm, v_hbm, k_ref, v_ref, own_ref, one_ref, two_ref, three_ref, rest_ref, sems):
+def states_kernel(group, place_ref, k_hbm, v_hbm, k_ref, v_ref, even_ref, one_ref, two_ref, three_ref, odd_sent_ref, even_sent_ref, sems):
     width = group * HEAD_DIM
     place = place_ref[0] & (QUAD - 1)
     order = (3, 1, 2, 0)
@@ -72,35 +72,28 @@
         for copy in copies[r]:
             copy.start()
     sent = {1: one_ref, 2: two_ref, 3: three_ref}
-    spot = {0: 0, 3: 1, 2: 2}
     for r in order:
         for copy in copies[r]:
             copy.wait()
         for j in range(group):
             state = tn(v_ref[r, :, column(j)], k_ref[r, :, column(j)])
-            if r == 0:
-                own_ref[j] = state
-            else:
+            spot = r // 2 * group + j
+            if r % 2 == 0:
+                even_ref[spot] = state
+            (odd_sent_ref if r % 2 else even_sent_ref)[spot] = state.astype(BF16)
+            if r in sent:
                 sent[r][j] = state.astype(BF16)
-            if r in spot:
-                rest_ref[spot[r] * group + j] = state.astype(BF16)
-
-
-def sums_kernel(own_ref, one_ref, two_ref, three_ref, sent_ref, *total_refs):
-    total = own_ref[...] + one_ref[...].astype(F32) + two_ref[...].astype(F32) + three_ref[...].astype(F32)
+
+
+def sums_kernel(group, even_ref, one_ref, two_ref, three_ref, sent_ref, *total_refs):
+    total = even_ref[:group] + one_ref[...].astype(F32) + two_ref[...].astype(F32) + three_ref[...].astype(F32)
     for total_ref in total_refs:
         total_ref[...] = total
     sent_ref[...] = total.astype(BF16)
 
 
-def left_kernel(seq, place_ref, own_ref, *refs):
-    left_ref, neighbour_ref = refs[6:]
-    last_quad = place_ref[0] >= seq - QUAD
-    one, two, three = (jnp.where(last_quad, refs[3 + i][...], refs[i][...]) for i in range(3))
-    pair = own_ref[...] + one.astype(F32)
-    other = two.astype(F32) + three.astype(F32)
-    left_ref[...] = jnp.where(place_ref[0] >> 1 & 1 == 1, other, pair).astype(BF16)
-    neighbour_ref[...] = one
+def pair_kernel(even_ref, near_ref, pair_ref):
+    pair_ref[...] = (even_ref[...] + near_ref[...].astype(F32)).astype(BF16)
 
 
 def intra_kernel(group, groups, place_ref, q_ref, w_ref, k_all, v_all, *refs):
@@ -185,15 +178,15 @@
     place = position.reshape(1)
     sds = jax.ShapeDtypeStruct
     block = (group, HEAD_DIM, HEAD_DIM)
-    others = (3 * group, HEAD_DIM, HEAD_DIM)
+    half = (2 * group, HEAD_DIM, HEAD_DIM)
     panel = (rows, group * HEAD_DIM)
     part_shape = sds((group * HEAD_DIM, rows), F32)
 
-    k_all, v_all, own, one, two, three, rest = pl.pallas_call(
+    k_all, v_all, even, one, two, three, odd_sent, even_sent = pl.pallas_call(
         functools.partial(states_kernel, group),
-        out_shape=(sds((QUAD,) + panel, BF16),) * 2 + (sds(block, F32),) + (sds(block, BF16),) * 3 + (sds(others, BF16),),
+        out_shape=(sds((QUAD,) + panel, BF16),) * 2 + (sds(half, F32),) + (sds(block, BF16),) * 3 + (sds(half, BF16),) * 2,
         in_specs=[SMEM, HBM, HBM],
-        out_specs=(VMEM,) * 7,
+        out_specs=(VMEM,) * 8,
         scratch_shapes=[pltpu.SemaphoreType.DMA((2, QUAD))],
         compiler_params=params(STATES_GRANT),
         cost_estimate=cost(2 * rows * width * HEAD_DIM, 4 * rows * width),
@@ -201,9 +194,8 @@
     )(place, keys, values)
 
     parts = ((3, three), (1, one), (2, two))
-    early = {r: exchanged_in(part, r, lambda quad, quads: quad < quads - 1) for r, part in parts}
-    late = {r: exchanged_in(part, r, lambda quad, quads: quad == quads - 1) for r, part in parts}
-    near = exchanged(rest, "seq", 1)
+    taken = {r: exchanged_in(part, r, lambda quad, quads: quad < quads - 1) for r, part in parts}
+    near = exchanged(odd_sent, "seq", 1), exchanged(even_sent, "seq", 1)
 
     totals = {}
     for number, groups in enumerate(((3, 1), (2, 0))):
@@ -222,33 +214,32 @@
         totals |= dict(zip(groups, outs))
 
     sums, *running = pl.pallas_call(
-        sums_kernel,
+        functools.partial(sums_kernel, group),
         out_shape=(sds(block, BF16),) + (sds(block, F32),) * (seq_bits > 3),
         in_specs=[VMEM] * 4,
         out_specs=(VMEM,) * (1 + (seq_bits > 3)),
         compiler_params=params(),
         cost_estimate=cost(4 * group * HEAD_DIM**2, 16 * group * HEAD_DIM**2),
         name="sums",
-    )(own, early[1], early[2], early[3])
+    )(even, taken[1], taken[2], taken[3])
     upper = []
     for bit in range(2, seq_bits):
         if bit > 2:
             running = [running[0] + upper[-1].astype(F32)]
             sums = running[0].astype(BF16)
         upper.append(exchanged(sums, "seq", 1 << bit))
-    left_pair, neighbour = pl.pallas_call(
-        functools.partial(left_kernel, lax.axis_size("seq")),
-        out_shape=(sds(block, BF16), sds(block, BF16)),
-        in_specs=[SMEM] + [VMEM] * 7,
-        out_specs=(VMEM,) * 2,
+    pair = pl.pallas_call(
+        pair_kernel,
+        out_shape=sds(half, BF16),
+        in_specs=[VMEM] * 2,
+        out_specs=VMEM,
         compiler_params=params(),
-        cost_estimate=cost(4 * group * HEAD_DIM**2, 16 * group * HEAD_DIM**2),
-        name="left",
-    )(place, own, early[1], early[2], early[3], late[1], late[2], late[3])
+        cost_estimate=cost(2 * group * HEAD_DIM**2, 16 * group * HEAD_DIM**2),
+        name="pair",
+    )(even, near[0])
+    middle = exchanged(pair, "seq", 2), exchanged(pair, "seq", 3)
     top = jnp.concatenate(upper, axis=0) if len(upper) > 1 else upper[0]
     tops = {0: top} | {r: exchanged_in(top, r, lambda quad, quads: quad > 0) for r in (3, 1, 2)}
-
-    middle = {0: left_pair} | {r: exchanged(left_pair, "seq", r) for r in (3, 1, 2)}
 
     def top_reads(ref):
         return tuple((bit, ref, (bit - 2) * group) for bit in range(2, seq_bits))
@@ -269,9 +260,9 @@
         totals.update({r: out for (r, _, _), out in zip(work, outs)})
         return outs[n]
 
-    below = {0: ((0, 0, 0), (1, 2, 0))} | {r: ((0, 1, (r - 1) * group), (1, 2 + r, 0)) for r in (1, 2, 3)}
-    work = tuple((r, r == 0, below[r] + (top_reads(6) if r == 0 else ())) for r in (3, 1, 2, 0))
-    squares = readout(work, (neighbour, near, *(middle[r] for r in range(QUAD)), top), None)
+    below = {r: ((0, r % 2, r // 2 * group), (1, 2 + r % 2, (1 - r // 2) * group)) for r in range(QUAD)}
+    work = tuple((r, r == 0, below[r] + (top_reads(4) if r == 0 else ())) for r in (3, 1, 2, 0))
+    squares = readout(work, (*near, *middle, top), None)
     squares = readout(((3, True, top_reads(0)), (1, True, top_reads(1))), (tops[3], tops[1]), squares)
     squares = readout(((2, True, top_reads(0)),), (tops[2],), squares, finish=True)
 

time: 31.4 us -> 30.3 us (0.965)
  starting transfers between devices: 18.9 us -> 18.3 us
  waiting for transfers between devices: 4.82 us -> 4.4 us
    ppermute x9 -> x6, starting transfers between devices: 8.43 us -> 4.17 us  [exchanged_in(): return lax.ppermute(block, ('seq', 'head'), route)]
    ppermute x8, starting transfers between devices: 10.5 us -> 14.1 us  [exchanged(): return lax.ppermute(block, axis, [(i, i ^ mask) for i in range(count)])]
    ppermute x8, waiting for transfers between devices: 3.52 us -> 2.53 us  [exchanged(): return lax.ppermute(block, axis, [(i, i ^ mask) for i in range(count)])]
    ppermute x9 -> x6, waiting for transfers between devices: 1.3 us -> 1.87 us  [exchanged_in(): return lax.ppermute(block, ('seq', 'head'), route)]
  transfers between devices with their start and end apart: 17 -> 14, of which waited for: 5 -> 6; matrix products, arithmetic and copies ran while one was open for 0% -> 0% of each run, Pallas kernels for 11% -> 12%
where the time goes in v8:
time: 30.3 us; the launch traced here: 30.2 us
  starting transfers between devices  18.3 us (60%)
  Pallas kernels  7.35 us (24%)
  waiting for transfers between devices  4.4 us (15%)
    ppermute x8, starting transfers between devices, exchanged(): return lax.ppermute(block, axis, [(i, i ^ mask) for i in range(count)])  14.1 us
    ppermute x6, starting transfers between devices, exchanged_in(): return lax.ppermute(block, ('seq', 'head'), route)  4.17 us
    ppermute x8, waiting for transfers between devices, exchanged(): return lax.ppermute(block, axis, [(i, i ^ mask) for i in range(count)])  2.53 us
    pallas_call x1, Pallas kernels, local(): pl.pallas_call(functools.partial(states_kernel, group), out_shape=(sds((Q...  2.25 us
    pallas_call x2, Pallas kernels, local(): pl.pallas_call(functools.partial(intra_kernel, group, groups), out_shape=...  2.24 us
    ppermute x6, waiting for transfers between devices, exchanged_in(): return lax.ppermute(block, ('seq', 'head'), route)  1.87 us
    pallas_call x3, Pallas kernels, readout(): pl.pallas_call(kernel, out_shape=tuple(shapes), in_specs=[SMEM] + [VMEM]...  1.45 us
    pallas_call x1, Pallas kernels, local(): pl.pallas_call(functools.partial(norm_kernel, group, full_width), out_sha...  1.36 us
  transfers between devices with their start and end apart: 14, of which 6 were waited for; matrix products, arithmetic and copies ran while one was open for 0% of the time, Pallas kernels for 12%

profile of v8, /device:TPU:17, one launch (start us, length us, event | category | flops | bytes accessed | tf_op | source)
XLA Modules:
  0.0 30.2 jit_solution(16862022142697987965)
XLA Ops:
  0.0 0.0 copy-start.1
  0.0 2.2 %states.1 = (bf16[4,512,256]{2,1,0:T(8,128)(2,1)S(1)}, bf16[4,512,256]{2,1,0:T(8,128)(2,1)S(1)}, f32[4,128,128]{2,1,0:T(8,128)S(1)}, bf16[2,128,128]{2,1,0:T(8,1...) custom-call(s32[1]{0:T(128)} %bitcast.place_ref, ...), custom_call_target="tpu_custom_call" | custom-call | flops 134217728 | bytes 2097152 | tf_op jit(solution)/shard_map/states/pallas_call | solution.py:185
  2.3 0.0 copy-start
  2.3 1.3 %collective-permute-start = (bf16[4,128,128]{2,1,0:T(8,128)(2,1)S(1)}, bf16[4,128,128]{2,1,0:T(8,128)(2,1)S(1)}, u32[]{:S(2)}, u32[]{:S(2)}) collective-permute-start(bf16[4,128,128]{2,1,0:T(8,128)(2,1)S(1)} %get-tuple-element.28), channel_id=1, source_target_pairs={{0,4},{4,0},{8,12},{12,8},{16,20},{20,16},{24,28},{28,24},{1,5},{5... | collective-permute-start | bytes 393224 | tf_op jit(solution)/shard_map/ppermute | solution.py:36
  3.6 1.0 %collective-permute-start.4 = (bf16[2,128,128]{2,1,0:T(8,128)(2,1)S(1)}, bf16[2,128,128]{2,1,0:T(8,128)(2,1)S(1)}, u32[]{:S(2)}, u32[]{:S(2)}) collective-permute-start(bf16[2,128,128]{2,1,0:T(8,128)(2,1)S(1)} %get-tuple-element.31), channel_id=1, source_target_pairs={{0,4},{1,5},{2,6},{3,7},{4,0},{5,1},{6,2},{7,3},{8,12},{9,13},{10,... | collective-permute-start | bytes 196616 | tf_op jit(solution)/shard_map/ppermute | solution.py:46
  4.5 0.0 collective-permute-start.5
  4.5 0.5 %collective-permute-start.6 = (bf16[2,128,128]{2,1,0:T(8,128)(2,1)S(1)}, bf16[2,128,128]{2,1,0:T(8,128)(2,1)S(1)}, u32[]{:S(2)}, u32[]{:S(2)}) collective-permute-start(bf16[2,128,128]{2,1,0:T(8,128)(2,1)S(1)} %get-tuple-element.33), channel_id=1, source_target_pairs={{0,12},{1,13},{2,14},{3,15},{4,8},{5,9},{6,10},{7,11},{8,4},{9,5},... | collective-permute-start | bytes 196616 | tf_op jit(solution)/shard_map/ppermute | solution.py:46
  5.0 0.2 collective-permute-start.1
  5.3 0.2 collective-permute-done.4.one_ref
  5.4 0.4 %collective-permute-done.5.two_ref = bf16[2,128,128]{2,1,0:T(8,128)(2,1)S(1)} collective-permute-done((bf16[2,128,128]{2,1,0:T(8,128)(2,1)S(1)}, bf16[2,128,128]{2,1,0:T(8,128)(2,1)S(1)}, u32[]{:S(2)}, u32[]{:S(2)}) %collective-permute-start.5) | collective-permute-done | bytes 65568 | tf_op jit(solution)/shard_map/ppermute | solution.py:46
  5.8 0.2 collective-permute-done.6.three_ref
  6.0 3.5 %collective-permute-start.7 = (bf16[2,128,128]{2,1,0:T(8,128)(2,1)S(1)}, bf16[2,128,128]{2,1,0:T(8,128)(2,1)S(1)}, u32[]{:S(2)}, u32[]{:S(2)}) collective-permute-start(bf16[2,128,128]{2,1,0:T(8,128)(2,1)S(1)} %sums.1), channel_id=1, source_target_pairs={{0,16},{4,20},{8,24},{12,28},{16,0},{20,4},{24,8},{28,12},{1,17},{... | collective-permute-start | bytes 196616 | tf_op jit(solution)/shard_map/ppermute | solution.py:36
  9.5 0.0 collective-permute-done.near_ref.refs_0_
  9.5 0.7 %collective-permute-start.2 = (bf16[4,128,128]{2,1,0:T(8,128)(2,1)S(1)}, bf16[4,128,128]{2,1,0:T(8,128)(2,1)S(1)}, u32[]{:S(2)}, u32[]{:S(2)}) collective-permute-start(bf16[4,128,128]{2,1,0:T(8,128)(2,1)S(1)} %pair.1), channel_id=1, source_target_pairs={{0,8},{4,12},{8,0},{12,4},{16,24},{20,28},{24,16},{28,20},{1,9},{5... | collective-permute-start | bytes 393224 | tf_op jit(solution)/shard_map/ppermute | solution.py:36
  10.2 1.7 %collective-permute-start.3 = (bf16[4,128,128]{2,1,0:T(8,128)(2,1)S(1)}, bf16[4,128,128]{2,1,0:T(8,128)(2,1)S(1)}, u32[]{:S(2)}, u32[]{:S(2)}) collective-permute-start(bf16[4,128,128]{2,1,0:T(8,128)(2,1)S(1)} %pair.1), channel_id=1, source_target_pairs={{0,12},{4,8},{8,4},{12,0},{16,28},{20,24},{24,20},{28,16},{1,13},{... | collective-permute-start | bytes 393224 | tf_op jit(solution)/shard_map/ppermute | solution.py:36
  11.9 0.0 collective-permute-done.7.refs_4_
  11.9 1.7 %collective-permute-start.8 = (bf16[2,128,128]{2,1,0:T(8,128)(2,1)S(1)}, bf16[2,128,128]{2,1,0:T(8,128)(2,1)S(1)}, u32[]{:S(2)}, u32[]{:S(2)}) collective-permute-start(bf16[2,128,128]{2,1,0:T(8,128)(2,1)S(1)} %collective-permute-done.7.refs_4_), channel_id=1, source_target_pairs={{0,1},{1,0},{2,3},{3,2},{4,5},{5,4},{6,7},{7,6},{8,9},{9,8},{10,11... | collective-permute-start | bytes 196616 | tf_op jit(solution)/shard_map/ppermute | solution.py:46
  13.6 0.4 %collective-permute-start.9 = (bf16[2,128,128]{2,1,0:T(8,128)(2,1)S(1)}, bf16[2,128,128]{2,1,0:T(8,128)(2,1)S(1)}, u32[]{:S(2)}, u32[]{:S(2)}) collective-permute-start(bf16[2,128,128]{2,1,0:T(8,128)(2,1)S(1)} %collective-permute-done.7.refs_4_), channel_id=1, source_target_pairs={{0,1},{1,0},{2,3},{3,2},{4,5},{5,4},{6,7},{7,6},{8,9},{9,8},{10,11... | collective-permute-start | bytes 196616 | tf_op jit(solution)/shard_map/ppermute | solution.py:46
  14.0 0.0 copy-done.1
  14.0 0.0 copy-done
  14.0 0.0 copy-start.2
  14.0 1.1 %intra.3 = (f32[256,512]{1,0:T(8,128)S(1)}, f32[256,512]{1,0:T(8,128)S(1)}) custom-call(s32[1]{0:T(128)} %bitcast.place_ref, bf16[512,1024]{1,0:T(8,128)(2,1)S(1)} %copy-done, f32[5,8,512]{2,1,0:T(8,128)S(1)} %copy-done.1, bf16[4,512,256]{2,1,0:T(8,128)(2,1)S(1)} %get-tuple-element.34.k_all, bf16[4,512,256]{2,1,0:T(8,128)(2,1)S(1)} %get-tuple-element.35.v_all), custom_call_target="tpu_custom_call" | custom-call | flops 402653184 | bytes 1048576 | tf_op jit(solution)/shard_map/intra/pallas_call | solution.py:203
  15.1 0.0 collective-permute-done.1.refs_1_
  15.1 0.6 %collective-permute-start.10 = (bf16[2,128,128]{2,1,0:T(8,128)(2,1)S(1)}, bf16[2,128,128]{2,1,0:T(8,128)(2,1)S(1)}, u32[]{:S(2)}, u32[]{:S(2)}) collective-permute-start(bf16[2,128,128]{2,1,0:T(8,128)(2,1)S(1)} %collective-permute-done.7.refs_4_), channel_id=1, source_target_pairs={{0,1},{1,0},{2,3},{3,2},{4,5},{5,4},{6,7},{7,6},{8,9},{9,8},{10,11... | collective-permute-start | bytes 196616 | tf_op jit(solution)/shard_map/ppermute | solution.py:46
  15.7 0.0 copy-done.2
  15.7 1.1 %intra.2 = (f32[1,1024]{1,0:T(1,128)S(1)}, f32[256,512]{1,0:T(8,128)S(1)}, f32[256,512]{1,0:T(8,128)S(1)}) custom-call(s32[1]{0:T(128)} %bitcast.place_ref, bf16[512,1024]{1,0:T(8,128)(2,1)S(1)} %copy-done, f32[5,8,512]{2,1,0:T(8,128)S(1)} %copy-done.1, bf16[4,512,256]{2,1,0:T(8,128)(2,1)S(1)} %get-tuple-element.34.k_all, ...), custom_call_target="tpu_custom_call" | custom-call | flops 402653184 | bytes 1048576 | tf_op jit(solution)/shard_map/intra/pallas_call | solution.py:203
  16.9 0.0 collective-permute-done.2.refs_2_
  16.9 0.0 collective-permute-done.3.refs_3_
  16.9 0.8 %shard_map.55 = (f32[256,512]{1,0:T(8,128)S(1)}, f32[256,512]{1,0:T(8,128)S(1)}, f32[256,512]{1,0:T(8,128)S(1)}, f32[256,512]{1,0:T(8,128)S(1)}, f32[8,512]{1,0:T(8,128)S(1)}) custom-call(s32[1]{0:T(128)} %bitcast.place_ref, bf16[512,1024]{1,0:T(8,128)(2,1)S(1)} %copy-done, f32[5,8,512]{2,1,0:T(8,128)S(1)} %copy-done.1, ...), custom_call_target="tpu_custom_call" | custom-call | flops 268435456 | bytes 4194304 | tf_op jit(solution)/shard_map/pallas_call | solution.py:252
  17.7 0.0 collective-permute-done.8.refs_0_
  17.8 0.0 collective-permute-done.9.refs_1_
  17.8 0.3 %shard_map.56 = (f32[256,512]{1,0:T(8,128)S(1)}, f32[256,512]{1,0:T(8,128)S(1)}, f32[8,512]{1,0:T(8,128)S(1)}) custom-call(s32[1]{0:T(128)} %bitcast.place_ref, bf16[512,1024]{1,0:T(8,128)(2,1)S(1)} %copy-done, f32[5,8,512]{2,1,0:T(8,128)S(1)} %copy-done.1, bf16[2,128,128]{2,1,0:T(8,128)(2,1)S(1)} %collective-permute-done.8.refs_0_, ...), custom_call_target="tpu_custom_call" | custom-call | flops 134217728 | bytes 2097152 | tf_op jit(solution)/shard_map/pallas_call | solution.py:252
  18.1 1.2 %collective-permute-done.10.refs_0_ = bf16[2,128,128]{2,1,0:T(8,128)(2,1)S(1)} collective-permute-done((bf16[2,128,128]{2,1,0:T(8,128)(2,1)S(1)}, bf16[2,128,128]{2,1,0:T(8,128)(2,1)S(1)}, u32[]{:S(2)}, u32[]{:S(2)}) %collective-permute-start.10) | collective-permute-done | bytes 65568 | tf_op jit(solution)/shard_map/ppermute | solution.py:46
  19.3 0.3 shard_map.57
  19.6 5.0 %collective-permute-start.11 = (f32[1,512]{1,0:T(1,128)S(1)}, f32[1,512]{1,0:T(1,128)S(1)}, u32[]{:S(2)}, u32[]{:S(2)}) collective-permute-start(f32[1,512]{1,0:T(1,128)S(1)} %get-tuple-element.49.refs_4_), channel_id=1, source_target_pairs={{0,1},{1,0},{2,3},{3,2},{4,5},{5,4},{6,7},{7,6},{8,9},{9,8},{10,11... | collective-permute-start | bytes 6152 | tf_op jit(solution)/shard_map/ppermute | solution.py:36
  24.6 1.2 %collective-permute-start.12 = (f32[1,512]{1,0:T(1,128)S(1)}, f32[1,512]{1,0:T(1,128)S(1)}, u32[]{:S(2)}, u32[]{:S(2)}) collective-permute-start(f32[1,512]{1,0:T(1,128)S(1)} %get-tuple-element.49.refs_4_), channel_id=1, source_target_pairs={{0,2},{1,3},{2,0},{3,1},{4,6},{5,7},{6,4},{7,5},{8,10},{9,11},{10,... | collective-permute-start | bytes 6152 | tf_op jit(solution)/shard_map/ppermute | solution.py:36
  25.8 0.5 %collective-permute-start.13 = (f32[1,512]{1,0:T(1,128)S(1)}, f32[1,512]{1,0:T(1,128)S(1)}, u32[]{:S(2)}, u32[]{:S(2)}) collective-permute-start(f32[1,512]{1,0:T(1,128)S(1)} %get-tuple-element.49.refs_4_), channel_id=1, source_target_pairs={{0,3},{1,2},{2,1},{3,0},{4,7},{5,6},{6,5},{7,4},{8,11},{9,10},{10,... | collective-permute-start | bytes 6152 | tf_op jit(solution)/shard_map/ppermute | solution.py:36
  26.3 0.0 collective-permute-done.11.refs_5_
  26.3 0.7 %collective-permute-done.12.refs_6_ = f32[1,512]{1,0:T(1,128)S(1)} collective-permute-done((f32[1,512]{1,0:T(1,128)S(1)}, f32[1,512]{1,0:T(1,128)S(1)}, u32[]{:S(2)}, u32[]{:S(2)}) %collective-permute-start.12) | collective-permute-done | bytes 2080 | tf_op jit(solution)/shard_map/ppermute | solution.py:36
  27.0 1.8 %collective-permute-done.13.refs_7_ = f32[1,512]{1,0:T(1,128)S(1)} collective-permute-done((f32[1,512]{1,0:T(1,128)S(1)}, f32[1,512]{1,0:T(1,128)S(1)}, u32[]{:S(2)}, u32[]{:S(2)}) %collective-permute-start.13) | collective-permute-done | bytes 2080 | tf_op jit(solution)/shard_map/ppermute | solution.py:36
  28.8 1.4 %norm.1 = bf16[512,1024]{1,0:T(8,128)(2,1)} custom-call(s32[1]{0:T(128)} %bitcast.place_ref, f32[256,512]{1,0:T(8,128)S(1)} %get-tuple-element.40.refs_0_, f32[256,512]{1,0:T(8,128)S(1)} %get-tuple-element.44.refs_1_, f32[256,512]{1,0:T(8,128)S(1)} %get-tuple-element.47.refs_2_, f32[256,512]{1,0:T(8,128)S(1)} %get-tuple-element.48.refs_3_, ...), custom_call_target="tpu_custom_call" | custom-call | flops 1048576 | bytes 1048576 | tf_op jit(solution)/shard_map/norm/pallas_call | solution.py:271
  (2 shorter events, 0.1 us)
Async XLA Ops:
  0.0 14.0 %copy-start.1 = (f32[5,8,512]{2,1,0:T(8,128)S(1)}, f32[5,8,512]{2,1,0:T(8,128)}, u32[]{:S(2)}) copy-start(f32[5,8,512]{2,1,0:T(8,128)} %w_ref.9) | copy-start | bytes 245764
  2.3 11.7 %copy-start = (bf16[512,1024]{1,0:T(8,128)(2,1)S(1)}, bf16[512,1024]{1,0:T(8,128)(2,1)}, u32[]{:S(2)}) copy-start(bf16[512,1024]{1,0:T(8,128)(2,1)} %q_ref.9) | copy-start | bytes 3145732
  2.3 7.3 %collective-permute-start = (bf16[4,128,128]{2,1,0:T(8,128)(2,1)S(1)}, bf16[4,128,128]{2,1,0:T(8,128)(2,1)S(1)}, u32[]{:S(2)}, u32[]{:S(2)}) collective-permute-start(bf16[4,128,128]{2,1,0:T(8,128)(2,1)S(1)} %get-tuple-element.28), channel_id=1, source_target_pairs={{0,4},{4,0},{8,12},{12,8},{16,20},{20,16},{24,28},{28,24},{1,5},{5... | collective-permute-start | bytes 393224 | tf_op jit(solution)/shard_map/ppermute | solution.py:36
  3.6 1.9 %collective-permute-start.4 = (bf16[2,128,128]{2,1,0:T(8,128)(2,1)S(1)}, bf16[2,128,128]{2,1,0:T(8,128)(2,1)S(1)}, u32[]{:S(2)}, u32[]{:S(2)}) collective-permute-start(bf16[2,128,128]{2,1,0:T(8,128)(2,1)S(1)} %get-tuple-element.31), channel_id=1, source_target_pairs={{0,4},{1,5},{2,6},{3,7},{4,0},{5,1},{6,2},{7,3},{8,12},{9,13},{10,... | collective-permute-start | bytes 196616 | tf_op jit(solution)/shard_map/ppermute | solution.py:46
  4.5 1.3 %collective-permute-start.5 = (bf16[2,128,128]{2,1,0:T(8,128)(2,1)S(1)}, bf16[2,128,128]{2,1,0:T(8,128)(2,1)S(1)}, u32[]{:S(2)}, u32[]{:S(2)}) collective-permute-start(bf16[2,128,128]{2,1,0:T(8,128)(2,1)S(1)} %get-tuple-element.32), channel_id=1, source_target_pairs={{0,8},{1,9},{2,10},{3,11},{4,12},{5,13},{6,14},{7,15},{8,0},{9,1},... | collective-permute-start | bytes 196616 | tf_op jit(solution)/shard_map/ppermute | solution.py:46
  4.5 1.4 %collective-permute-start.6 = (bf16[2,128,128]{2,1,0:T(8,128)(2,1)S(1)}, bf16[2,128,128]{2,1,0:T(8,128)(2,1)S(1)}, u32[]{:S(2)}, u32[]{:S(2)}) collective-permute-start(bf16[2,128,128]{2,1,0:T(8,128)(2,1)S(1)} %get-tuple-element.33), channel_id=1, source_target_pairs={{0,12},{1,13},{2,14},{3,15},{4,8},{5,9},{6,10},{7,11},{8,4},{9,5},... | collective-permute-start | bytes 196616 | tf_op jit(solution)/shard_map/ppermute | solution.py:46
  5.0 10.1 %collective-permute-start.1 = (bf16[4,128,128]{2,1,0:T(8,128)(2,1)S(1)}, bf16[4,128,128]{2,1,0:T(8,128)(2,1)S(1)}, u32[]{:S(2)}, u32[]{:S(2)}) collective-permute-start(bf16[4,128,128]{2,1,0:T(8,128)(2,1)S(1)} %get-tuple-element.29), channel_id=1, source_target_pairs={{0,4},{4,0},{8,12},{12,8},{16,20},{20,16},{24,28},{28,24},{1,5},{5... | collective-permute-start | bytes 393224 | tf_op jit(solution)/shard_map/ppermute | solution.py:36
  6.0 5.9 %collective-permute-start.7 = (bf16[2,128,128]{2,1,0:T(8,128)(2,1)S(1)}, bf16[2,128,128]{2,1,0:T(8,128)(2,1)S(1)}, u32[]{:S(2)}, u32[]{:S(2)}) collective-permute-start(bf16[2,128,128]{2,1,0:T(8,128)(2,1)S(1)} %sums.1), channel_id=1, source_target_pairs={{0,16},{4,20},{8,24},{12,28},{16,0},{20,4},{24,8},{28,12},{1,17},{... | collective-permute-start | bytes 196616 | tf_op jit(solution)/shard_map/ppermute | solution.py:36
  9.5 7.3 %collective-permute-start.2 = (bf16[4,128,128]{2,1,0:T(8,128)(2,1)S(1)}, bf16[4,128,128]{2,1,0:T(8,128)(2,1)S(1)}, u32[]{:S(2)}, u32[]{:S(2)}) collective-permute-start(bf16[4,128,128]{2,1,0:T(8,128)(2,1)S(1)} %pair.1), channel_id=1, source_target_pairs={{0,8},{4,12},{8,0},{12,4},{16,24},{20,28},{24,16},{28,20},{1,9},{5... | collective-permute-start | bytes 393224 | tf_op jit(solution)/shard_map/ppermute | solution.py:36
  10.2 6.7 %collective-permute-start.3 = (bf16[4,128,128]{2,1,0:T(8,128)(2,1)S(1)}, bf16[4,128,128]{2,1,0:T(8,128)(2,1)S(1)}, u32[]{:S(2)}, u32[]{:S(2)}) collective-permute-start(bf16[4,128,128]{2,1,0:T(8,128)(2,1)S(1)} %pair.1), channel_id=1, source_target_pairs={{0,12},{4,8},{8,4},{12,0},{16,28},{20,24},{24,20},{28,16},{1,13},{... | collective-permute-start | bytes 393224 | tf_op jit(solution)/shard_map/ppermute | solution.py:36
  11.9 5.9 %collective-permute-start.8 = (bf16[2,128,128]{2,1,0:T(8,128)(2,1)S(1)}, bf16[2,128,128]{2,1,0:T(8,128)(2,1)S(1)}, u32[]{:S(2)}, u32[]{:S(2)}) collective-permute-start(bf16[2,128,128]{2,1,0:T(8,128)(2,1)S(1)} %collective-permute-done.7.refs_4_), channel_id=1, source_target_pairs={{0,1},{1,0},{2,3},{3,2},{4,5},{5,4},{6,7},{7,6},{8,9},{9,8},{10,11... | collective-permute-start | bytes 196616 | tf_op jit(solution)/shard_map/ppermute | solution.py:46
  13.6 4.2 %collective-permute-start.9 = (bf16[2,128,128]{2,1,0:T(8,128)(2,1)S(1)}, bf16[2,128,128]{2,1,0:T(8,128)(2,1)S(1)}, u32[]{:S(2)}, u32[]{:S(2)}) collective-permute-start(bf16[2,128,128]{2,1,0:T(8,128)(2,1)S(1)} %collective-permute-done.7.refs_4_), channel_id=1, source_target_pairs={{0,1},{1,0},{2,3},{3,2},{4,5},{5,4},{6,7},{7,6},{8,9},{9,8},{10,11... | collective-permute-start | bytes 196616 | tf_op jit(solution)/shard_map/ppermute | solution.py:46
  14.0 1.7 %copy-start.2 = (f32[1024]{0:T(1024)S(1)}, f32[1024]{0:T(1024)}, u32[]{:S(2)}) copy-start(f32[1024]{0:T(1024)} %param.9) | copy-start | bytes 12292
  15.1 4.2 %collective-permute-start.10 = (bf16[2,128,128]{2,1,0:T(8,128)(2,1)S(1)}, bf16[2,128,128]{2,1,0:T(8,128)(2,1)S(1)}, u32[]{:S(2)}, u32[]{:S(2)}) collective-permute-start(bf16[2,128,128]{2,1,0:T(8,128)(2,1)S(1)} %collective-permute-done.7.refs_4_), channel_id=1, source_target_pairs={{0,1},{1,0},{2,3},{3,2},{4,5},{5,4},{6,7},{7,6},{8,9},{9,8},{10,11... | collective-permute-start | bytes 196616 | tf_op jit(solution)/shard_map/ppermute | solution.py:46
  19.6 6.7 %collective-permute-start.11 = (f32[1,512]{1,0:T(1,128)S(1)}, f32[1,512]{1,0:T(1,128)S(1)}, u32[]{:S(2)}, u32[]{:S(2)}) collective-permute-start(f32[1,512]{1,0:T(1,128)S(1)} %get-tuple-element.49.refs_4_), channel_id=1, source_target_pairs={{0,1},{1,0},{2,3},{3,2},{4,5},{5,4},{6,7},{7,6},{8,9},{9,8},{10,11... | collective-permute-start | bytes 6152 | tf_op jit(solution)/shard_map/ppermute | solution.py:36
  24.6 2.4 %collective-permute-start.12 = (f32[1,512]{1,0:T(1,128)S(1)}, f32[1,512]{1,0:T(1,128)S(1)}, u32[]{:S(2)}, u32[]{:S(2)}) collective-permute-start(f32[1,512]{1,0:T(1,128)S(1)} %get-tuple-element.49.refs_4_), channel_id=1, source_target_pairs={{0,2},{1,3},{2,0},{3,1},{4,6},{5,7},{6,4},{7,5},{8,10},{9,11},{10,... | collective-permute-start | bytes 6152 | tf_op jit(solution)/shard_map/ppermute | solution.py:36
  25.8 3.0 %collective-permute-start.13 = (f32[1,512]{1,0:T(1,128)S(1)}, f32[1,512]{1,0:T(1,128)S(1)}, u32[]{:S(2)}, u32[]{:S(2)}) collective-permute-start(f32[1,512]{1,0:T(1,128)S(1)} %get-tuple-element.49.refs_4_), channel_id=1, source_target_pairs={{0,3},{1,2},{2,1},{3,0},{4,7},{5,6},{6,5},{7,4},{8,11},{9,10},{10,... | collective-permute-start | bytes 6152 | tf_op jit(solution)/shard_map/ppermute | solution.py:36

commit v9 on v8

--- a/solution.py
+++ b/solution.py
@@ -58,7 +58,7 @@
     return pl.ds(head * HEAD_DIM, HEAD_DIM)
 
 
-def states_kernel(group, place_ref, k_hbm, v_hbm, k_ref, v_ref, even_ref, one_ref, two_ref, three_ref, odd_sent_ref, even_sent_ref, sems):
+def states_kernel(group, place_ref, k_hbm, v_hbm, k_ref, v_ref, even_ref, one_ref, two_ref, three_ref, even_sent_ref, sems):
     width = group * HEAD_DIM
     place = place_ref[0] & (QUAD - 1)
     order = (3, 1, 2, 0)
@@ -80,7 +80,7 @@
             spot = r // 2 * group + j
             if r % 2 == 0:
                 even_ref[spot] = state
-            (odd_sent_ref if r % 2 else even_sent_ref)[spot] = state.astype(BF16)
+                even_sent_ref[spot] = state.astype(BF16)
             if r in sent:
                 sent[r][j] = state.astype(BF16)
 
@@ -92,8 +92,9 @@
     sent_ref[...] = total.astype(BF16)
 
 
-def pair_kernel(even_ref, near_ref, pair_ref):
-    pair_ref[...] = (even_ref[...] + near_ref[...].astype(F32)).astype(BF16)
+def pair_kernel(group, even_ref, near0_ref, near2_ref, pair_ref):
+    pair_ref[:group] = (even_ref[:group] + near0_ref[...].astype(F32)).astype(BF16)
+    pair_ref[group:] = (even_ref[group:] + near2_ref[...].astype(F32)).astype(BF16)
 
 
 def intra_kernel(group, groups, place_ref, q_ref, w_ref, k_all, v_all, *refs):
@@ -182,20 +183,21 @@
     panel = (rows, group * HEAD_DIM)
     part_shape = sds((group * HEAD_DIM, rows), F32)
 
-    k_all, v_all, even, one, two, three, odd_sent, even_sent = pl.pallas_call(
+    k_all, v_all, even, one, two, three, even_sent = pl.pallas_call(
         functools.partial(states_kernel, group),
-        out_shape=(sds((QUAD,) + panel, BF16),) * 2 + (sds(half, F32),) + (sds(block, BF16),) * 3 + (sds(half, BF16),) * 2,
+        out_shape=(sds((QUAD,) + panel, BF16),) * 2 + (sds(half, F32),) + (sds(block, BF16),) * 3 + (sds(half, BF16),),
         in_specs=[SMEM, HBM, HBM],
-        out_specs=(VMEM,) * 8,
+        out_specs=(VMEM,) * 7,
         scratch_shapes=[pltpu.SemaphoreType.DMA((2, QUAD))],
         compiler_params=params(STATES_GRANT),
         cost_estimate=cost(2 * rows * width * HEAD_DIM, 4 * rows * width),
         name="states",
     )(place, keys, values)
 
-    parts = ((3, three), (1, one), (2, two))
-    taken = {r: exchanged_in(part, r, lambda quad, quads: quad < quads - 1) for r, part in parts}
-    near = exchanged(odd_sent, "seq", 1), exchanged(even_sent, "seq", 1)
+    taken3 = exchanged_in(three, 3, lambda quad, quads: quad < quads - 1)
+    taken1 = exchanged(one, "seq", 1)
+    taken2 = exchanged_in(two, 2, lambda quad, quads: quad < quads - 1)
+    near2, near_odd = exchanged(three, "seq", 1), exchanged(even_sent, "seq", 1)
 
     totals = {}
     for number, groups in enumerate(((3, 1), (2, 0))):
@@ -221,7 +223,7 @@
         compiler_params=params(),
         cost_estimate=cost(4 * group * HEAD_DIM**2, 16 * group * HEAD_DIM**2),
         name="sums",
-    )(even, taken[1], taken[2], taken[3])
+    )(even, taken1, taken2, taken3)
     upper = []
     for bit in range(2, seq_bits):
         if bit > 2:
@@ -229,14 +231,14 @@
             sums = running[0].astype(BF16)
         upper.append(exchanged(sums, "seq", 1 << bit))
     pair = pl.pallas_call(
-        pair_kernel,
+        functools.partial(pair_kernel, group),
         out_shape=sds(half, BF16),
-        in_specs=[VMEM] * 2,
+        in_specs=[VMEM] * 3,
         out_specs=VMEM,
         compiler_params=params(),
         cost_estimate=cost(2 * group * HEAD_DIM**2, 16 * group * HEAD_DIM**2),
         name="pair",
-    )(even, near[0])
+    )(even, taken1, near2)
     middle = exchanged(pair, "seq", 2), exchanged(pair, "seq", 3)
     top = jnp.concatenate(upper, axis=0) if len(upper) > 1 else upper[0]
     tops = {0: top} | {r: exchanged_in(top, r, lambda quad, quads: quad > 0) for r in (3, 1, 2)}
@@ -260,9 +262,10 @@
         totals.update({r: out for (r, _, _), out in zip(work, outs)})
         return outs[n]
 
-    below = {r: ((0, r % 2, r // 2 * group), (1, 2 + r % 2, (1 - r // 2) * group)) for r in range(QUAD)}
-    work = tuple((r, r == 0, below[r] + (top_reads(4) if r == 0 else ())) for r in (3, 1, 2, 0))
-    squares = readout(work, (*near, *middle, top), None)
+    bit0 = {0: (0, 0, 0), 2: (0, 1, 0), 1: (0, 2, 0), 3: (0, 2, group)}
+    bit1 = {r: (1, 3 + r % 2, (1 - r // 2) * group) for r in range(QUAD)}
+    work = tuple((r, r == 0, (bit0[r], bit1[r]) + (top_reads(5) if r == 0 else ())) for r in (3, 1, 2, 0))
+    squares = readout(work, (taken1, near2, near_odd, *middle, top), None)
     squares = readout(((3, True, top_reads(0)), (1, True, top_reads(1))), (tops[3], tops[1]), squares)
     squares = readout(((2, True, top_reads(0)),), (tops[2],), squares, finish=True)
 

time: 30.3 us -> 28.6 us (0.944)
  the two profiles are of different devices: /device:TPU:17 before, /device:TPU:0 now
where the time goes in v9:
time: 28.6 us; the launch traced here: 28.4 us
  starting transfers between devices  12.2 us (43%)
  waiting for transfers between devices  8.69 us (30%)
  Pallas kernels  7.35 us (26%)
    ppermute x9, starting transfers between devices, exchanged(): return lax.ppermute(block, axis, [(i, i ^ mask) for i in range(count)])  10.1 us
    ppermute x9, waiting for transfers between devices, exchanged(): return lax.ppermute(block, axis, [(i, i ^ mask) for i in range(count)])  6.44 us
    ppermute x5, waiting for transfers between devices, exchanged_in(): return lax.ppermute(block, ('seq', 'head'), route)  2.25 us
    pallas_call x1, Pallas kernels, local(): pl.pallas_call(functools.partial(states_kernel, group), out_shape=(sds((Q...  2.24 us
    pallas_call x2, Pallas kernels, local(): pl.pallas_call(functools.partial(intra_kernel, group, groups), out_shape=...  2.24 us
    ppermute x5, starting transfers between devices, exchanged_in(): return lax.ppermute(block, ('seq', 'head'), route)  2.18 us
    pallas_call x3, Pallas kernels, readout(): pl.pallas_call(kernel, out_shape=tuple(shapes), in_specs=[SMEM] + [VMEM]...  1.44 us
    pallas_call x1, Pallas kernels, local(): pl.pallas_call(functools.partial(norm_kernel, group, full_width), out_sha...  1.36 us
  transfers between devices with their start and end apart: 14, of which 6 were waited for; matrix products, arithmetic and copies ran while one was open for 0% of the time, Pallas kernels for 12%

profile of v9, /device:TPU:0, one launch (start us, length us, event | category | flops | bytes accessed | tf_op | source)
XLA Modules:
  0.0 28.4 jit_solution(4523100898818613130)
XLA Ops:
  0.0 0.0 copy-start.1
  0.0 2.2 %states.1 = (bf16[4,512,256]{2,1,0:T(8,128)(2,1)S(1)}, bf16[4,512,256]{2,1,0:T(8,128)(2,1)S(1)}, f32[4,128,128]{2,1,0:T(8,128)S(1)}, bf16[2,128,128]{2,1,0:T(8,1...) custom-call(s32[1]{0:T(128)} %bitcast.place_ref, ...), custom_call_target="tpu_custom_call" | custom-call | flops 134217728 | bytes 2097152 | tf_op jit(solution)/shard_map/states/pallas_call | solution.py:186
  2.3 0.0 copy-start
  2.3 3.1 %collective-permute-start = (bf16[2,128,128]{2,1,0:T(8,128)(2,1)S(1)}, bf16[2,128,128]{2,1,0:T(8,128)(2,1)S(1)}, u32[]{:S(2)}, u32[]{:S(2)}) collective-permute-start(bf16[2,128,128]{2,1,0:T(8,128)(2,1)S(1)} %get-tuple-element.27), channel_id=1, source_target_pairs={{0,4},{4,0},{8,12},{12,8},{16,20},{20,16},{24,28},{28,24},{1,5},{5... | collective-permute-start | bytes 196616 | tf_op jit(solution)/shard_map/ppermute | solution.py:36
  5.3 1.5 %collective-permute-start.6 = (bf16[2,128,128]{2,1,0:T(8,128)(2,1)S(1)}, bf16[2,128,128]{2,1,0:T(8,128)(2,1)S(1)}, u32[]{:S(2)}, u32[]{:S(2)}) collective-permute-start(bf16[2,128,128]{2,1,0:T(8,128)(2,1)S(1)} %get-tuple-element.28), channel_id=1, source_target_pairs={{0,12},{1,13},{2,14},{3,15},{4,8},{5,9},{6,10},{7,11},{8,4},{9,5},... | collective-permute-start | bytes 196616 | tf_op jit(solution)/shard_map/ppermute | solution.py:46
  6.8 0.1 collective-permute-start.5
  6.9 1.9 %collective-permute-start.1 = (bf16[2,128,128]{2,1,0:T(8,128)(2,1)S(1)}, bf16[2,128,128]{2,1,0:T(8,128)(2,1)S(1)}, u32[]{:S(2)}, u32[]{:S(2)}) collective-permute-start(bf16[2,128,128]{2,1,0:T(8,128)(2,1)S(1)} %get-tuple-element.28), channel_id=1, source_target_pairs={{0,4},{4,0},{8,12},{12,8},{16,20},{20,16},{24,28},{28,24},{1,5},{5... | collective-permute-start | bytes 196616 | tf_op jit(solution)/shard_map/ppermute | solution.py:36
  8.8 0.1 collective-permute-start.2
  8.9 0.0 collective-permute-done.near0_ref.one_ref.refs_0_
  8.9 2.2 %collective-permute-done.6.three_ref = bf16[2,128,128]{2,1,0:T(8,128)(2,1)S(1)} collective-permute-done((bf16[2,128,128]{2,1,0:T(8,128)(2,1)S(1)}, bf16[2,128,128]{2,1,0:T(8,128)(2,1)S(1)}, u32[]{:S(2)}, u32[]{:S(2)}) %collective-permute-start.6) | collective-permute-done | bytes 65568 | tf_op jit(solution)/shard_map/ppermute | solution.py:46
  11.2 0.0 collective-permute-done.5.two_ref
  11.2 0.1 collective-permute-start.7
  11.3 0.9 %collective-permute-done.1.near2_ref.refs_1_ = bf16[2,128,128]{2,1,0:T(8,128)(2,1)S(1)} collective-permute-done((bf16[2,128,128]{2,1,0:T(8,128)(2,1)S(1)}, bf16[2,128,128]{2,1,0:T(8,128)(2,1)S(1)}, u32[]{:S(2)}, u32[]{:S(2)}) %collective-permute-start.1) | collective-permute-done | bytes 65568 | tf_op jit(solution)/shard_map/ppermute | solution.py:36
  12.3 1.7 %collective-permute-start.3 = (bf16[4,128,128]{2,1,0:T(8,128)(2,1)S(1)}, bf16[4,128,128]{2,1,0:T(8,128)(2,1)S(1)}, u32[]{:S(2)}, u32[]{:S(2)}) collective-permute-start(bf16[4,128,128]{2,1,0:T(8,128)(2,1)S(1)} %pair.1), channel_id=1, source_target_pairs={{0,8},{4,12},{8,0},{12,4},{16,24},{20,28},{24,16},{28,20},{1,9},{5... | collective-permute-start | bytes 393224 | tf_op jit(solution)/shard_map/ppermute | solution.py:36
  13.9 1.3 %collective-permute-start.4 = (bf16[4,128,128]{2,1,0:T(8,128)(2,1)S(1)}, bf16[4,128,128]{2,1,0:T(8,128)(2,1)S(1)}, u32[]{:S(2)}, u32[]{:S(2)}) collective-permute-start(bf16[4,128,128]{2,1,0:T(8,128)(2,1)S(1)} %pair.1), channel_id=1, source_target_pairs={{0,12},{4,8},{8,4},{12,0},{16,28},{20,24},{24,20},{28,16},{1,13},{... | collective-permute-start | bytes 393224 | tf_op jit(solution)/shard_map/ppermute | solution.py:36
  15.2 1.5 %collective-permute-done.7.refs_5_ = bf16[2,128,128]{2,1,0:T(8,128)(2,1)S(1)} collective-permute-done((bf16[2,128,128]{2,1,0:T(8,128)(2,1)S(1)}, bf16[2,128,128]{2,1,0:T(8,128)(2,1)S(1)}, u32[]{:S(2)}, u32[]{:S(2)}) %collective-permute-start.7) | collective-permute-done | bytes 65568 | tf_op jit(solution)/shard_map/ppermute | solution.py:36
  16.8 0.0 collective-permute-start.8
  16.8 0.5 %collective-permute-start.9 = (bf16[2,128,128]{2,1,0:T(8,128)(2,1)S(1)}, bf16[2,128,128]{2,1,0:T(8,128)(2,1)S(1)}, u32[]{:S(2)}, u32[]{:S(2)}) collective-permute-start(bf16[2,128,128]{2,1,0:T(8,128)(2,1)S(1)} %collective-permute-done.7.refs_5_), channel_id=1, source_target_pairs={{0,1},{1,0},{2,3},{3,2},{4,5},{5,4},{6,7},{7,6},{8,9},{9,8},{10,11... | collective-permute-start | bytes 196616 | tf_op jit(solution)/shard_map/ppermute | solution.py:46
  17.3 0.0 copy-done.1
  17.3 0.0 copy-done
  17.3 0.0 copy-start.2
  17.3 1.1 %intra.3 = (f32[256,512]{1,0:T(8,128)S(1)}, f32[256,512]{1,0:T(8,128)S(1)}) custom-call(s32[1]{0:T(128)} %bitcast.place_ref, bf16[512,1024]{1,0:T(8,128)(2,1)S(1)} %copy-done, f32[5,8,512]{2,1,0:T(8,128)S(1)} %copy-done.1, bf16[4,512,256]{2,1,0:T(8,128)(2,1)S(1)} %get-tuple-element.32.k_all, bf16[4,512,256]{2,1,0:T(8,128)(2,1)S(1)} %get-tuple-element.33.v_all), custom_call_target="tpu_custom_call" | custom-call | flops 402653184 | bytes 1048576 | tf_op jit(solution)/shard_map/intra/pallas_call | solution.py:205
  18.4 0.0 collective-permute-done.2.refs_2_
  18.4 0.1 collective-permute-start.10
  18.5 0.0 copy-done.2
  18.5 1.1 %intra.2 = (f32[1,1024]{1,0:T(1,128)S(1)}, f32[256,512]{1,0:T(8,128)S(1)}, f32[256,512]{1,0:T(8,128)S(1)}) custom-call(s32[1]{0:T(128)} %bitcast.place_ref, bf16[512,1024]{1,0:T(8,128)(2,1)S(1)} %copy-done, f32[5,8,512]{2,1,0:T(8,128)S(1)} %copy-done.1, bf16[4,512,256]{2,1,0:T(8,128)(2,1)S(1)} %get-tuple-element.32.k_all, ...), custom_call_target="tpu_custom_call" | custom-call | flops 402653184 | bytes 1048576 | tf_op jit(solution)/shard_map/intra/pallas_call | solution.py:205
  19.6 0.0 collective-permute-done.3.refs_3_
  19.7 1.1 %collective-permute-done.4.refs_4_ = bf16[4,128,128]{2,1,0:T(8,128)(2,1)S(1)} collective-permute-done((bf16[4,128,128]{2,1,0:T(8,128)(2,1)S(1)}, bf16[4,128,128]{2,1,0:T(8,128)(2,1)S(1)}, u32[]{:S(2)}, u32[]{:S(2)}) %collective-permute-start.4) | collective-permute-done | bytes 131104 | tf_op jit(solution)/shard_map/ppermute | solution.py:36
  20.8 0.8 %shard_map.55 = (f32[256,512]{1,0:T(8,128)S(1)}, f32[256,512]{1,0:T(8,128)S(1)}, f32[256,512]{1,0:T(8,128)S(1)}, f32[256,512]{1,0:T(8,128)S(1)}, f32[8,512]{1,0:T(8,128)S(1)}) custom-call(s32[1]{0:T(128)} %bitcast.place_ref, bf16[512,1024]{1,0:T(8,128)(2,1)S(1)} %copy-done, f32[5,8,512]{2,1,0:T(8,128)S(1)} %copy-done.1, ...), custom_call_target="tpu_custom_call" | custom-call | flops 268435456 | bytes 4194304 | tf_op jit(solution)/shard_map/pallas_call | solution.py:254
  21.6 0.0 collective-permute-done.8.refs_0_
  21.6 0.0 collective-permute-done.9.refs_1_
  21.7 0.3 %shard_map.56 = (f32[256,512]{1,0:T(8,128)S(1)}, f32[256,512]{1,0:T(8,128)S(1)}, f32[8,512]{1,0:T(8,128)S(1)}) custom-call(s32[1]{0:T(128)} %bitcast.place_ref, bf16[512,1024]{1,0:T(8,128)(2,1)S(1)} %copy-done, f32[5,8,512]{2,1,0:T(8,128)S(1)} %copy-done.1, bf16[2,128,128]{2,1,0:T(8,128)(2,1)S(1)} %collective-permute-done.8.refs_0_, ...), custom_call_target="tpu_custom_call" | custom-call | flops 134217728 | bytes 2097152 | tf_op jit(solution)/shard_map/pallas_call | solution.py:254
  22.0 0.0 collective-permute-done.10.refs_0_
  22.0 0.3 shard_map.57
  22.3 0.1 collective-permute-start.11
  22.4 1.7 %collective-permute-start.12 = (f32[1,512]{1,0:T(1,128)S(1)}, f32[1,512]{1,0:T(1,128)S(1)}, u32[]{:S(2)}, u32[]{:S(2)}) collective-permute-start(f32[1,512]{1,0:T(1,128)S(1)} %get-tuple-element.47.refs_4_), channel_id=1, source_target_pairs={{0,2},{1,3},{2,0},{3,1},{4,6},{5,7},{6,4},{7,5},{8,10},{9,11},{10,... | collective-permute-start | bytes 6152 | tf_op jit(solution)/shard_map/ppermute | solution.py:36
  24.0 0.2 collective-permute-start.13
  24.2 0.0 collective-permute-done.11.refs_5_
  24.2 1.8 %collective-permute-done.12.refs_6_ = f32[1,512]{1,0:T(1,128)S(1)} collective-permute-done((f32[1,512]{1,0:T(1,128)S(1)}, f32[1,512]{1,0:T(1,128)S(1)}, u32[]{:S(2)}, u32[]{:S(2)}) %collective-permute-start.12) | collective-permute-done | bytes 2080 | tf_op jit(solution)/shard_map/ppermute | solution.py:36
  26.0 1.0 %collective-permute-done.13.refs_7_ = f32[1,512]{1,0:T(1,128)S(1)} collective-permute-done((f32[1,512]{1,0:T(1,128)S(1)}, f32[1,512]{1,0:T(1,128)S(1)}, u32[]{:S(2)}, u32[]{:S(2)}) %collective-permute-start.13) | collective-permute-done | bytes 2080 | tf_op jit(solution)/shard_map/ppermute | solution.py:36
  27.1 1.4 %norm.1 = bf16[512,1024]{1,0:T(8,128)(2,1)} custom-call(s32[1]{0:T(128)} %bitcast.place_ref, f32[256,512]{1,0:T(8,128)S(1)} %get-tuple-element.38.refs_0_, f32[256,512]{1,0:T(8,128)S(1)} %get-tuple-element.42.refs_1_, f32[256,512]{1,0:T(8,128)S(1)} %get-tuple-element.45.refs_2_, f32[256,512]{1,0:T(8,128)S(1)} %get-tuple-element.46.refs_3_, ...), custom_call_target="tpu_custom_call" | custom-call | flops 1048576 | bytes 1048576 | tf_op jit(solution)/shard_map/norm/pallas_call | solution.py:274
  (2 shorter events, 0.1 us)
Async XLA Ops:
  0.0 17.3 %copy-start.1 = (f32[5,8,512]{2,1,0:T(8,128)S(1)}, f32[5,8,512]{2,1,0:T(8,128)}, u32[]{:S(2)}) copy-start(f32[5,8,512]{2,1,0:T(8,128)} %w_ref.9) | copy-start | bytes 245764
  2.3 15.0 %copy-start = (bf16[512,1024]{1,0:T(8,128)(2,1)S(1)}, bf16[512,1024]{1,0:T(8,128)(2,1)}, u32[]{:S(2)}) copy-start(bf16[512,1024]{1,0:T(8,128)(2,1)} %q_ref.9) | copy-start | bytes 3145732
  2.3 6.7 %collective-permute-start = (bf16[2,128,128]{2,1,0:T(8,128)(2,1)S(1)}, bf16[2,128,128]{2,1,0:T(8,128)(2,1)S(1)}, u32[]{:S(2)}, u32[]{:S(2)}) collective-permute-start(bf16[2,128,128]{2,1,0:T(8,128)(2,1)S(1)} %get-tuple-element.27), channel_id=1, source_target_pairs={{0,4},{4,0},{8,12},{12,8},{16,20},{20,16},{24,28},{28,24},{1,5},{5... | collective-permute-start | bytes 196616 | tf_op jit(solution)/shard_map/ppermute | solution.py:36
  5.3 5.8 %collective-permute-start.6 = (bf16[2,128,128]{2,1,0:T(8,128)(2,1)S(1)}, bf16[2,128,128]{2,1,0:T(8,128)(2,1)S(1)}, u32[]{:S(2)}, u32[]{:S(2)}) collective-permute-start(bf16[2,128,128]{2,1,0:T(8,128)(2,1)S(1)} %get-tuple-element.28), channel_id=1, source_target_pairs={{0,12},{1,13},{2,14},{3,15},{4,8},{5,9},{6,10},{7,11},{8,4},{9,5},... | collective-permute-start | bytes 196616 | tf_op jit(solution)/shard_map/ppermute | solution.py:46
  6.8 4.3 %collective-permute-start.5 = (bf16[2,128,128]{2,1,0:T(8,128)(2,1)S(1)}, bf16[2,128,128]{2,1,0:T(8,128)(2,1)S(1)}, u32[]{:S(2)}, u32[]{:S(2)}) collective-permute-start(bf16[2,128,128]{2,1,0:T(8,128)(2,1)S(1)} %get-tuple-element.31), channel_id=1, source_target_pairs={{0,8},{1,9},{2,10},{3,11},{4,12},{5,13},{6,14},{7,15},{8,0},{9,1},... | collective-permute-start | bytes 196616 | tf_op jit(solution)/shard_map/ppermute | solution.py:46
  6.9 5.3 %collective-permute-start.1 = (bf16[2,128,128]{2,1,0:T(8,128)(2,1)S(1)}, bf16[2,128,128]{2,1,0:T(8,128)(2,1)S(1)}, u32[]{:S(2)}, u32[]{:S(2)}) collective-permute-start(bf16[2,128,128]{2,1,0:T(8,128)(2,1)S(1)} %get-tuple-element.28), channel_id=1, source_target_pairs={{0,4},{4,0},{8,12},{12,8},{16,20},{20,16},{24,28},{28,24},{1,5},{5... | collective-permute-start | bytes 196616 | tf_op jit(solution)/shard_map/ppermute | solution.py:36
  8.8 9.6 %collective-permute-start.2 = (bf16[4,128,128]{2,1,0:T(8,128)(2,1)S(1)}, bf16[4,128,128]{2,1,0:T(8,128)(2,1)S(1)}, u32[]{:S(2)}, u32[]{:S(2)}) collective-permute-start(bf16[4,128,128]{2,1,0:T(8,128)(2,1)S(1)} %get-tuple-element.29), channel_id=1, source_target_pairs={{0,4},{4,0},{8,12},{12,8},{16,20},{20,16},{24,28},{28,24},{1,5},{5... | collective-permute-start | bytes 393224 | tf_op jit(solution)/shard_map/ppermute | solution.py:36
  11.2 5.6 %collective-permute-start.7 = (bf16[2,128,128]{2,1,0:T(8,128)(2,1)S(1)}, bf16[2,128,128]{2,1,0:T(8,128)(2,1)S(1)}, u32[]{:S(2)}, u32[]{:S(2)}) collective-permute-start(bf16[2,128,128]{2,1,0:T(8,128)(2,1)S(1)} %sums.1), channel_id=1, source_target_pairs={{0,16},{4,20},{8,24},{12,28},{16,0},{20,4},{24,8},{28,12},{1,17},{... | collective-permute-start | bytes 196616 | tf_op jit(solution)/shard_map/ppermute | solution.py:36
  12.3 7.4 %collective-permute-start.3 = (bf16[4,128,128]{2,1,0:T(8,128)(2,1)S(1)}, bf16[4,128,128]{2,1,0:T(8,128)(2,1)S(1)}, u32[]{:S(2)}, u32[]{:S(2)}) collective-permute-start(bf16[4,128,128]{2,1,0:T(8,128)(2,1)S(1)} %pair.1), channel_id=1, source_target_pairs={{0,8},{4,12},{8,0},{12,4},{16,24},{20,28},{24,16},{28,20},{1,9},{5... | collective-permute-start | bytes 393224 | tf_op jit(solution)/shard_map/ppermute | solution.py:36
  13.9 6.9 %collective-permute-start.4 = (bf16[4,128,128]{2,1,0:T(8,128)(2,1)S(1)}, bf16[4,128,128]{2,1,0:T(8,128)(2,1)S(1)}, u32[]{:S(2)}, u32[]{:S(2)}) collective-permute-start(bf16[4,128,128]{2,1,0:T(8,128)(2,1)S(1)} %pair.1), channel_id=1, source_target_pairs={{0,12},{4,8},{8,4},{12,0},{16,28},{20,24},{24,20},{28,16},{1,13},{... | collective-permute-start | bytes 393224 | tf_op jit(solution)/shard_map/ppermute | solution.py:36
  16.8 4.9 %collective-permute-start.8 = (bf16[2,128,128]{2,1,0:T(8,128)(2,1)S(1)}, bf16[2,128,128]{2,1,0:T(8,128)(2,1)S(1)}, u32[]{:S(2)}, u32[]{:S(2)}) collective-permute-start(bf16[2,128,128]{2,1,0:T(8,128)(2,1)S(1)} %collective-permute-done.7.refs_5_), channel_id=1, source_target_pairs={{0,1},{1,0},{2,3},{3,2},{4,5},{5,4},{6,7},{7,6},{8,9},{9,8},{10,11... | collective-permute-start | bytes 196616 | tf_op jit(solution)/shard_map/ppermute | solution.py:46
  16.8 4.9 %collective-permute-start.9 = (bf16[2,128,128]{2,1,0:T(8,128)(2,1)S(1)}, bf16[2,128,128]{2,1,0:T(8,128)(2,1)S(1)}, u32[]{:S(2)}, u32[]{:S(2)}) collective-permute-start(bf16[2,128,128]{2,1,0:T(8,128)(2,1)S(1)} %collective-permute-done.7.refs_5_), channel_id=1, source_target_pairs={{0,1},{1,0},{2,3},{3,2},{4,5},{5,4},{6,7},{7,6},{8,9},{9,8},{10,11... | collective-permute-start | bytes 196616 | tf_op jit(solution)/shard_map/ppermute | solution.py:46
  17.3 1.2 %copy-start.2 = (f32[1024]{0:T(1024)S(1)}, f32[1024]{0:T(1024)}, u32[]{:S(2)}) copy-start(f32[1024]{0:T(1024)} %param.9) | copy-start | bytes 12292
  18.4 3.6 %collective-permute-start.10 = (bf16[2,128,128]{2,1,0:T(8,128)(2,1)S(1)}, bf16[2,128,128]{2,1,0:T(8,128)(2,1)S(1)}, u32[]{:S(2)}, u32[]{:S(2)}) collective-permute-start(bf16[2,128,128]{2,1,0:T(8,128)(2,1)S(1)} %collective-permute-done.7.refs_5_), channel_id=1, source_target_pairs={{0,1},{1,0},{2,3},{3,2},{4,5},{5,4},{6,7},{7,6},{8,9},{9,8},{10,11... | collective-permute-start | bytes 196616 | tf_op jit(solution)/shard_map/ppermute | solution.py:46
  22.3 1.9 %collective-permute-start.11 = (f32[1,512]{1,0:T(1,128)S(1)}, f32[1,512]{1,0:T(1,128)S(1)}, u32[]{:S(2)}, u32[]{:S(2)}) collective-permute-start(f32[1,512]{1,0:T(1,128)S(1)} %get-tuple-element.47.refs_4_), channel_id=1, source_target_pairs={{0,1},{1,0},{2,3},{3,2},{4,5},{5,4},{6,7},{7,6},{8,9},{9,8},{10,11... | collective-permute-start | bytes 6152 | tf_op jit(solution)/shard_map/ppermute | solution.py:36
  22.4 3.7 %collective-permute-start.12 = (f32[1,512]{1,0:T(1,128)S(1)}, f32[1,512]{1,0:T(1,128)S(1)}, u32[]{:S(2)}, u32[]{:S(2)}) collective-permute-start(f32[1,512]{1,0:T(1,128)S(1)} %get-tuple-element.47.refs_4_), channel_id=1, source_target_pairs={{0,2},{1,3},{2,0},{3,1},{4,6},{5,7},{6,4},{7,5},{8,10},{9,11},{10,... | collective-permute-start | bytes 6152 | tf_op jit(solution)/shard_map/ppermute | solution.py:36
  24.0 3.0 %collective-permute-start.13 = (f32[1,512]{1,0:T(1,128)S(1)}, f32[1,512]{1,0:T(1,128)S(1)}, u32[]{:S(2)}, u32[]{:S(2)}) collective-permute-start(f32[1,512]{1,0:T(1,128)S(1)} %get-tuple-element.47.refs_4_), channel_id=1, source_target_pairs={{0,3},{1,2},{2,1},{3,0},{4,7},{5,6},{6,5},{7,4},{8,11},{9,10},{10,... | collective-permute-start | bytes 6152 | tf_op jit(solution)/shard_map/ppermute | solution.py:36

commit v10 on v7

--- a/solution.py
+++ b/solution.py
@@ -41,7 +41,7 @@
     route = []
     for s in range(seq):
         for h in range(head):
-            to = (s ^ mask, h) if real(s // QUAD, seq // QUAD) else (s, h ^ 1)
+            to = (s ^ mask, h) if real(s, seq) else (s, h ^ 1)
             route.append((s * head + h, to[0] * head + to[1]))
     return lax.ppermute(block, ("seq", "head"), route)
 
@@ -93,14 +93,13 @@
     sent_ref[...] = total.astype(BF16)
 
 
-def left_kernel(seq, place_ref, own_ref, *refs):
-    left_ref, neighbour_ref = refs[6:]
+def left_kernel(seq, place_ref, own_ref, one_ref, early2_ref, early3_ref, late2_ref, late3_ref, left_ref):
     last_quad = place_ref[0] >= seq - QUAD
-    one, two, three = (jnp.where(last_quad, refs[3 + i][...], refs[i][...]) for i in range(3))
-    pair = own_ref[...] + one.astype(F32)
+    two = jnp.where(last_quad, late2_ref[...], early2_ref[...])
+    three = jnp.where(last_quad, late3_ref[...], early3_ref[...])
+    pair = own_ref[...] + one_ref[...].astype(F32)
     other = two.astype(F32) + three.astype(F32)
     left_ref[...] = jnp.where(place_ref[0] >> 1 & 1 == 1, other, pair).astype(BF16)
-    neighbour_ref[...] = one
 
 
 def intra_kernel(group, groups, place_ref, q_ref, w_ref, k_all, v_all, *refs):
@@ -200,9 +199,11 @@
         name="states",
     )(place, keys, values)
 
-    parts = ((3, three), (1, one), (2, two))
-    early = {r: exchanged_in(part, r, lambda quad, quads: quad < quads - 1) for r, part in parts}
-    late = {r: exchanged_in(part, r, lambda quad, quads: quad == quads - 1) for r, part in parts}
+    early3 = exchanged_in(three, 3, lambda s, seq: s < seq - QUAD)
+    taken1 = exchanged(one, "seq", 1)
+    early2 = exchanged_in(two, 2, lambda s, seq: s < seq - QUAD)
+    late3 = exchanged_in(three, 3, lambda s, seq: s >= seq - QUAD)
+    late2 = exchanged_in(two, 2, lambda s, seq: s >= seq - QUAD)
     near = exchanged(rest, "seq", 1)
 
     totals = {}
@@ -229,26 +230,27 @@
         compiler_params=params(),
         cost_estimate=cost(4 * group * HEAD_DIM**2, 16 * group * HEAD_DIM**2),
         name="sums",
-    )(own, early[1], early[2], early[3])
+    )(own, taken1, early2, early3)
     upper = []
     for bit in range(2, seq_bits):
         if bit > 2:
             running = [running[0] + upper[-1].astype(F32)]
             sums = running[0].astype(BF16)
         upper.append(exchanged(sums, "seq", 1 << bit))
-    left_pair, neighbour = pl.pallas_call(
+    left_pair = pl.pallas_call(
         functools.partial(left_kernel, lax.axis_size("seq")),
-        out_shape=(sds(block, BF16), sds(block, BF16)),
-        in_specs=[SMEM] + [VMEM] * 7,
-        out_specs=(VMEM,) * 2,
+        out_shape=sds(block, BF16),
+        in_specs=[SMEM] + [VMEM] * 6,
+        out_specs=VMEM,
         compiler_params=params(),
         cost_estimate=cost(4 * group * HEAD_DIM**2, 16 * group * HEAD_DIM**2),
         name="left",
-    )(place, own, early[1], early[2], early[3], late[1], late[2], late[3])
+    )(place, own, taken1, early2, early3, late2, late3)
     top = jnp.concatenate(upper, axis=0) if len(upper) > 1 else upper[0]
-    tops = {0: top} | {r: exchanged_in(top, r, lambda quad, quads: quad > 0) for r in (3, 1, 2)}
-
-    middle = {0: left_pair} | {r: exchanged(left_pair, "seq", r) for r in (3, 1, 2)}
+    tops = {0: top} | {r: exchanged_in(top, r, lambda s, seq: s >= QUAD) for r in (3, 1, 2)}
+
+    middle = {0: left_pair} | {r: exchanged(left_pair, "seq", r) for r in (3, 2)}
+    middle[1] = exchanged_in(left_pair, 1, lambda s, seq: s >> 1 & 1 == 1)
 
     def top_reads(ref):
         return tuple((bit, ref, (bit - 2) * group) for bit in range(2, seq_bits))
@@ -271,7 +273,7 @@
 
     below = {0: ((0, 0, 0), (1, 2, 0))} | {r: ((0, 1, (r - 1) * group), (1, 2 + r, 0)) for r in (1, 2, 3)}
     work = tuple((r, r == 0, below[r] + (top_reads(6) if r == 0 else ())) for r in (3, 1, 2, 0))
-    squares = readout(work, (neighbour, near, *(middle[r] for r in range(QUAD)), top), None)
+    squares = readout(work, (taken1, near, *(middle[r] for r in range(QUAD)), top), None)
     squares = readout(((3, True, top_reads(0)), (1, True, top_reads(1))), (tops[3], tops[1]), squares)
     squares = readout(((2, True, top_reads(0)),), (tops[2],), squares, finish=True)
 

time: 31.4 us -> 29.4 us (0.936)
  the two profiles are of different devices: /device:TPU:17 before, /device:TPU:24 now
where the time goes in v10:
time: 29.4 us; the launch traced here: 28.9 us
  starting transfers between devices  16.3 us (55%)
  Pallas kernels  7.39 us (25%)
  waiting for transfers between devices  5.09 us (17%)
    ppermute x8, starting transfers between devices, exchanged(): return lax.ppermute(block, axis, [(i, i ^ mask) for i in range(count)])  9.05 us
    ppermute x8, starting transfers between devices, exchanged_in(): return lax.ppermute(block, ('seq', 'head'), route)  7.21 us
    ppermute x8, waiting for transfers between devices, exchanged(): return lax.ppermute(block, axis, [(i, i ^ mask) for i in range(count)])  3.42 us
    pallas_call x1, Pallas kernels, local(): pl.pallas_call(functools.partial(states_kernel, group), out_shape=(sds((Q...  2.3 us
    pallas_call x2, Pallas kernels, local(): pl.pallas_call(functools.partial(intra_kernel, group, groups), out_shape=...  2.21 us
    ppermute x8, waiting for transfers between devices, exchanged_in(): return lax.ppermute(block, ('seq', 'head'), route)  1.67 us
    pallas_call x3, Pallas kernels, readout(): pl.pallas_call(kernel, out_shape=tuple(shapes), in_specs=[SMEM] + [VMEM]...  1.44 us
    pallas_call x1, Pallas kernels, local(): pl.pallas_call(functools.partial(norm_kernel, group, full_width), out_sha...  1.36 us
  transfers between devices with their start and end apart: 16, of which 7 were waited for; matrix products, arithmetic and copies ran while one was open for 0% of the time, Pallas kernels for 12%

profile of v10, /device:TPU:24, one launch (start us, length us, event | category | flops | bytes accessed | tf_op | source)
XLA Modules:
  0.0 28.9 jit_solution(2108511444309944299)
XLA Ops:
  0.0 0.0 copy-start
  0.0 2.3 %states.1 = (bf16[4,512,256]{2,1,0:T(8,128)(2,1)S(1)}, bf16[4,512,256]{2,1,0:T(8,128)(2,1)S(1)}, f32[2,128,128]{2,1,0:T(8,128)S(1)}, bf16[2,128,128]{2,1,0:T(8,1...) custom-call(s32[1]{0:T(128)} %bitcast.place_ref, ...), custom_call_target="tpu_custom_call" | custom-call | flops 134217728 | bytes 2097152 | tf_op jit(solution)/shard_map/states/pallas_call | solution.py:191
  2.3 1.6 %collective-permute-start = (bf16[2,128,128]{2,1,0:T(8,128)(2,1)S(1)}, bf16[2,128,128]{2,1,0:T(8,128)(2,1)S(1)}, u32[]{:S(2)}, u32[]{:S(2)}) collective-permute-start(bf16[2,128,128]{2,1,0:T(8,128)(2,1)S(1)} %get-tuple-element.27), channel_id=1, source_target_pairs={{0,4},{4,0},{8,12},{12,8},{16,20},{20,16},{24,28},{28,24},{1,5},{5... | collective-permute-start | bytes 196616 | tf_op jit(solution)/shard_map/ppermute | solution.py:36
  3.9 0.0 collective-permute-start.2
  3.9 0.5 %collective-permute-start.3 = (bf16[2,128,128]{2,1,0:T(8,128)(2,1)S(1)}, bf16[2,128,128]{2,1,0:T(8,128)(2,1)S(1)}, u32[]{:S(2)}, u32[]{:S(2)}) collective-permute-start(bf16[2,128,128]{2,1,0:T(8,128)(2,1)S(1)} %get-tuple-element.31), channel_id=1, source_target_pairs={{0,12},{1,13},{2,14},{3,15},{4,8},{5,9},{6,10},{7,11},{8,4},{9,5},... | collective-permute-start | bytes 196616 | tf_op jit(solution)/shard_map/ppermute | solution.py:46
  4.4 0.4 %collective-permute-start.4 = (bf16[2,128,128]{2,1,0:T(8,128)(2,1)S(1)}, bf16[2,128,128]{2,1,0:T(8,128)(2,1)S(1)}, u32[]{:S(2)}, u32[]{:S(2)}) collective-permute-start(bf16[2,128,128]{2,1,0:T(8,128)(2,1)S(1)} %get-tuple-element.30), channel_id=1, source_target_pairs={{0,1},{1,0},{2,3},{3,2},{4,5},{5,4},{6,7},{7,6},{8,9},{9,8},{10,11... | collective-permute-start | bytes 196616 | tf_op jit(solution)/shard_map/ppermute | solution.py:46
  4.9 1.5 %collective-permute-start.5 = (bf16[2,128,128]{2,1,0:T(8,128)(2,1)S(1)}, bf16[2,128,128]{2,1,0:T(8,128)(2,1)S(1)}, u32[]{:S(2)}, u32[]{:S(2)}) collective-permute-start(bf16[2,128,128]{2,1,0:T(8,128)(2,1)S(1)} %get-tuple-element.31), channel_id=1, source_target_pairs={{0,1},{1,0},{2,3},{3,2},{4,5},{5,4},{6,7},{7,6},{8,9},{9,8},{10,11... | collective-permute-start | bytes 196616 | tf_op jit(solution)/shard_map/ppermute | solution.py:46
  6.4 0.3 collective-permute-done.one_ref.refs_0_
  6.6 1.5 %collective-permute-start.1 = (bf16[6,128,128]{2,1,0:T(8,128)(2,1)S(1)}, bf16[6,128,128]{2,1,0:T(8,128)(2,1)S(1)}, u32[]{:S(2)}, u32[]{:S(2)}) collective-permute-start(bf16[6,128,128]{2,1,0:T(8,128)(2,1)S(1)} %get-tuple-element.28), channel_id=1, source_target_pairs={{0,4},{4,0},{8,12},{12,8},{16,20},{20,16},{24,28},{28,24},{1,5},{5... | collective-permute-start | bytes 589832 | tf_op jit(solution)/shard_map/ppermute | solution.py:36
  8.2 0.0 collective-permute-done.2.early2_ref.two_ref
  8.2 0.0 collective-permute-done.3.early3_ref.three_ref
  8.2 0.0 copy-start.1
  8.2 1.8 %collective-permute-start.9 = (bf16[2,128,128]{2,1,0:T(8,128)(2,1)S(1)}, bf16[2,128,128]{2,1,0:T(8,128)(2,1)S(1)}, u32[]{:S(2)}, u32[]{:S(2)}) collective-permute-start(bf16[2,128,128]{2,1,0:T(8,128)(2,1)S(1)} %sums.1), channel_id=1, source_target_pairs={{0,16},{4,20},{8,24},{12,28},{16,0},{20,4},{24,8},{28,12},{1,17},{... | collective-permute-start | bytes 196616 | tf_op jit(solution)/shard_map/ppermute | solution.py:36
  10.0 0.0 collective-permute-done.4.late2_ref
  10.0 0.1 collective-permute-done.5.late3_ref
  10.2 1.3 %collective-permute-start.6 = (bf16[2,128,128]{2,1,0:T(8,128)(2,1)S(1)}, bf16[2,128,128]{2,1,0:T(8,128)(2,1)S(1)}, u32[]{:S(2)}, u32[]{:S(2)}) collective-permute-start(bf16[2,128,128]{2,1,0:T(8,128)(2,1)S(1)} %left.1.refs_2_), channel_id=1, source_target_pairs={{0,1},{1,0},{2,3},{3,2},{4,5},{5,4},{6,7},{7,6},{8,12},{9,13},{10,... | collective-permute-start | bytes 196616 | tf_op jit(solution)/shard_map/ppermute | solution.py:46
  11.5 0.7 %collective-permute-start.7 = (bf16[2,128,128]{2,1,0:T(8,128)(2,1)S(1)}, bf16[2,128,128]{2,1,0:T(8,128)(2,1)S(1)}, u32[]{:S(2)}, u32[]{:S(2)}) collective-permute-start(bf16[2,128,128]{2,1,0:T(8,128)(2,1)S(1)} %left.1.refs_2_), channel_id=1, source_target_pairs={{0,8},{4,12},{8,0},{12,4},{16,24},{20,28},{24,16},{28,20},{1,9},{5... | collective-permute-start | bytes 196616 | tf_op jit(solution)/shard_map/ppermute | solution.py:36
  12.2 1.5 %collective-permute-start.8 = (bf16[2,128,128]{2,1,0:T(8,128)(2,1)S(1)}, bf16[2,128,128]{2,1,0:T(8,128)(2,1)S(1)}, u32[]{:S(2)}, u32[]{:S(2)}) collective-permute-start(bf16[2,128,128]{2,1,0:T(8,128)(2,1)S(1)} %left.1.refs_2_), channel_id=1, source_target_pairs={{0,12},{4,8},{8,4},{12,0},{16,28},{20,24},{24,20},{28,16},{1,13},{... | collective-permute-start | bytes 196616 | tf_op jit(solution)/shard_map/ppermute | solution.py:36
  13.7 0.4 %collective-permute-done.9.refs_6_ = bf16[2,128,128]{2,1,0:T(8,128)(2,1)S(1)} collective-permute-done((bf16[2,128,128]{2,1,0:T(8,128)(2,1)S(1)}, bf16[2,128,128]{2,1,0:T(8,128)(2,1)S(1)}, u32[]{:S(2)}, u32[]{:S(2)}) %collective-permute-start.9) | collective-permute-done | bytes 65568 | tf_op jit(solution)/shard_map/ppermute | solution.py:36
  14.2 1.0 %collective-permute-start.10 = (bf16[2,128,128]{2,1,0:T(8,128)(2,1)S(1)}, bf16[2,128,128]{2,1,0:T(8,128)(2,1)S(1)}, u32[]{:S(2)}, u32[]{:S(2)}) collective-permute-start(bf16[2,128,128]{2,1,0:T(8,128)(2,1)S(1)} %collective-permute-done.9.refs_6_), channel_id=1, source_target_pairs={{0,1},{1,0},{2,3},{3,2},{4,5},{5,4},{6,7},{7,6},{8,9},{9,8},{10,11... | collective-permute-start | bytes 196616 | tf_op jit(solution)/shard_map/ppermute | solution.py:46
  15.1 0.2 collective-permute-done.6.refs_3_
  15.3 1.9 %collective-permute-start.11 = (bf16[2,128,128]{2,1,0:T(8,128)(2,1)S(1)}, bf16[2,128,128]{2,1,0:T(8,128)(2,1)S(1)}, u32[]{:S(2)}, u32[]{:S(2)}) collective-permute-start(bf16[2,128,128]{2,1,0:T(8,128)(2,1)S(1)} %collective-permute-done.9.refs_6_), channel_id=1, source_target_pairs={{0,1},{1,0},{2,3},{3,2},{4,5},{5,4},{6,7},{7,6},{8,9},{9,8},{10,11... | collective-permute-start | bytes 196616 | tf_op jit(solution)/shard_map/ppermute | solution.py:46
  17.1 0.0 copy-done
  17.1 0.0 copy-done.1
  17.2 0.0 copy-start.2
  17.2 1.1 %intra.3 = (f32[256,512]{1,0:T(8,128)S(1)}, f32[256,512]{1,0:T(8,128)S(1)}) custom-call(s32[1]{0:T(128)} %bitcast.place_ref, bf16[512,1024]{1,0:T(8,128)(2,1)S(1)} %copy-done, f32[5,8,512]{2,1,0:T(8,128)S(1)} %copy-done.1, bf16[4,512,256]{2,1,0:T(8,128)(2,1)S(1)} %get-tuple-element.32.k_all, bf16[4,512,256]{2,1,0:T(8,128)(2,1)S(1)} %get-tuple-element.33.v_all), custom_call_target="tpu_custom_call" | custom-call | flops 402653184 | bytes 1048576 | tf_op jit(solution)/shard_map/intra/pallas_call | solution.py:212
  18.3 0.0 collective-permute-done.7.refs_4_
  18.3 0.6 %collective-permute-start.12 = (bf16[2,128,128]{2,1,0:T(8,128)(2,1)S(1)}, bf16[2,128,128]{2,1,0:T(8,128)(2,1)S(1)}, u32[]{:S(2)}, u32[]{:S(2)}) collective-permute-start(bf16[2,128,128]{2,1,0:T(8,128)(2,1)S(1)} %collective-permute-done.9.refs_6_), channel_id=1, source_target_pairs={{0,1},{1,0},{2,3},{3,2},{4,5},{5,4},{6,7},{7,6},{8,9},{9,8},{10,11... | collective-permute-start | bytes 196616 | tf_op jit(solution)/shard_map/ppermute | solution.py:46
  18.9 0.0 copy-done.2
  18.9 1.1 %intra.2 = (f32[1,1024]{1,0:T(1,128)S(1)}, f32[256,512]{1,0:T(8,128)S(1)}, f32[256,512]{1,0:T(8,128)S(1)}) custom-call(s32[1]{0:T(128)} %bitcast.place_ref, bf16[512,1024]{1,0:T(8,128)(2,1)S(1)} %copy-done, f32[5,8,512]{2,1,0:T(8,128)S(1)} %copy-done.1, bf16[4,512,256]{2,1,0:T(8,128)(2,1)S(1)} %get-tuple-element.32.k_all, ...), custom_call_target="tpu_custom_call" | custom-call | flops 402653184 | bytes 1048576 | tf_op jit(solution)/shard_map/intra/pallas_call | solution.py:212
  20.0 0.0 collective-permute-done.8.refs_5_
  20.0 0.0 collective-permute-done.1.refs_1_
  20.0 0.8 %shard_map.55 = (f32[256,512]{1,0:T(8,128)S(1)}, f32[256,512]{1,0:T(8,128)S(1)}, f32[256,512]{1,0:T(8,128)S(1)}, f32[256,512]{1,0:T(8,128)S(1)}, f32[8,512]{1,0:T(8,128)S(1)}) custom-call(s32[1]{0:T(128)} %bitcast.place_ref, bf16[512,1024]{1,0:T(8,128)(2,1)S(1)} %copy-done, f32[5,8,512]{2,1,0:T(8,128)S(1)} %copy-done.1, ...), custom_call_target="tpu_custom_call" | custom-call | flops 268435456 | bytes 4194304 | tf_op jit(solution)/shard_map/pallas_call | solution.py:263
  20.8 0.0 collective-permute-done.10.refs_0_
  20.9 0.0 collective-permute-done.11.refs_1_
  20.9 0.3 %shard_map.56 = (f32[256,512]{1,0:T(8,128)S(1)}, f32[256,512]{1,0:T(8,128)S(1)}, f32[8,512]{1,0:T(8,128)S(1)}) custom-call(s32[1]{0:T(128)} %bitcast.place_ref, bf16[512,1024]{1,0:T(8,128)(2,1)S(1)} %copy-done, f32[5,8,512]{2,1,0:T(8,128)S(1)} %copy-done.1, bf16[2,128,128]{2,1,0:T(8,128)(2,1)S(1)} %collective-permute-done.10.refs_0_, ...), custom_call_target="tpu_custom_call" | custom-call | flops 134217728 | bytes 2097152 | tf_op jit(solution)/shard_map/pallas_call | solution.py:263
  21.2 1.4 %collective-permute-done.12.refs_0_ = bf16[2,128,128]{2,1,0:T(8,128)(2,1)S(1)} collective-permute-done((bf16[2,128,128]{2,1,0:T(8,128)(2,1)S(1)}, bf16[2,128,128]{2,1,0:T(8,128)(2,1)S(1)}, u32[]{:S(2)}, u32[]{:S(2)}) %collective-permute-start.12) | collective-permute-done | bytes 65568 | tf_op jit(solution)/shard_map/ppermute | solution.py:46
  22.6 0.3 shard_map.57
  22.9 0.1 collective-permute-start.13
  23.0 1.6 %collective-permute-start.14 = (f32[1,512]{1,0:T(1,128)S(1)}, f32[1,512]{1,0:T(1,128)S(1)}, u32[]{:S(2)}, u32[]{:S(2)}) collective-permute-start(f32[1,512]{1,0:T(1,128)S(1)} %get-tuple-element.47.refs_4_), channel_id=1, source_target_pairs={{0,2},{1,3},{2,0},{3,1},{4,6},{5,7},{6,4},{7,5},{8,10},{9,11},{10,... | collective-permute-start | bytes 6152 | tf_op jit(solution)/shard_map/ppermute | solution.py:36
  24.5 0.3 %collective-permute-start.15 = (f32[1,512]{1,0:T(1,128)S(1)}, f32[1,512]{1,0:T(1,128)S(1)}, u32[]{:S(2)}, u32[]{:S(2)}) collective-permute-start(f32[1,512]{1,0:T(1,128)S(1)} %get-tuple-element.47.refs_4_), channel_id=1, source_target_pairs={{0,3},{1,2},{2,1},{3,0},{4,7},{5,6},{6,5},{7,4},{8,11},{9,10},{10,... | collective-permute-start | bytes 6152 | tf_op jit(solution)/shard_map/ppermute | solution.py:36
  24.8 0.0 collective-permute-done.13.refs_5_
  24.8 1.8 %collective-permute-done.14.refs_6_ = f32[1,512]{1,0:T(1,128)S(1)} collective-permute-done((f32[1,512]{1,0:T(1,128)S(1)}, f32[1,512]{1,0:T(1,128)S(1)}, u32[]{:S(2)}, u32[]{:S(2)}) %collective-permute-start.14) | collective-permute-done | bytes 2080 | tf_op jit(solution)/shard_map/ppermute | solution.py:36
  26.6 0.9 %collective-permute-done.15.refs_7_ = f32[1,512]{1,0:T(1,128)S(1)} collective-permute-done((f32[1,512]{1,0:T(1,128)S(1)}, f32[1,512]{1,0:T(1,128)S(1)}, u32[]{:S(2)}, u32[]{:S(2)}) %collective-permute-start.15) | collective-permute-done | bytes 2080 | tf_op jit(solution)/shard_map/ppermute | solution.py:36
  27.5 1.4 %norm.1 = bf16[512,1024]{1,0:T(8,128)(2,1)} custom-call(s32[1]{0:T(128)} %bitcast.place_ref, f32[256,512]{1,0:T(8,128)S(1)} %get-tuple-element.38.refs_0_, f32[256,512]{1,0:T(8,128)S(1)} %get-tuple-element.42.refs_1_, f32[256,512]{1,0:T(8,128)S(1)} %get-tuple-element.45.refs_2_, f32[256,512]{1,0:T(8,128)S(1)} %get-tuple-element.46.refs_3_, ...), custom_call_target="tpu_custom_call" | custom-call | flops 1048576 | bytes 1048576 | tf_op jit(solution)/shard_map/norm/pallas_call | solution.py:282
  (2 shorter events, 0.1 us)
Async XLA Ops:
  0.0 17.1 %copy-start = (bf16[512,1024]{1,0:T(8,128)(2,1)S(1)}, bf16[512,1024]{1,0:T(8,128)(2,1)}, u32[]{:S(2)}) copy-start(bf16[512,1024]{1,0:T(8,128)(2,1)} %q_ref.9) | copy-start | bytes 3145732
  2.3 4.3 %collective-permute-start = (bf16[2,128,128]{2,1,0:T(8,128)(2,1)S(1)}, bf16[2,128,128]{2,1,0:T(8,128)(2,1)S(1)}, u32[]{:S(2)}, u32[]{:S(2)}) collective-permute-start(bf16[2,128,128]{2,1,0:T(8,128)(2,1)S(1)} %get-tuple-element.27), channel_id=1, source_target_pairs={{0,4},{4,0},{8,12},{12,8},{16,20},{20,16},{24,28},{28,24},{1,5},{5... | collective-permute-start | bytes 196616 | tf_op jit(solution)/shard_map/ppermute | solution.py:36
  3.9 4.3 %collective-permute-start.2 = (bf16[2,128,128]{2,1,0:T(8,128)(2,1)S(1)}, bf16[2,128,128]{2,1,0:T(8,128)(2,1)S(1)}, u32[]{:S(2)}, u32[]{:S(2)}) collective-permute-start(bf16[2,128,128]{2,1,0:T(8,128)(2,1)S(1)} %get-tuple-element.30), channel_id=1, source_target_pairs={{0,8},{1,9},{2,10},{3,11},{4,12},{5,13},{6,14},{7,15},{8,0},{9,1},... | collective-permute-start | bytes 196616 | tf_op jit(solution)/shard_map/ppermute | solution.py:46
  3.9 4.3 %collective-permute-start.3 = (bf16[2,128,128]{2,1,0:T(8,128)(2,1)S(1)}, bf16[2,128,128]{2,1,0:T(8,128)(2,1)S(1)}, u32[]{:S(2)}, u32[]{:S(2)}) collective-permute-start(bf16[2,128,128]{2,1,0:T(8,128)(2,1)S(1)} %get-tuple-element.31), channel_id=1, source_target_pairs={{0,12},{1,13},{2,14},{3,15},{4,8},{5,9},{6,10},{7,11},{8,4},{9,5},... | collective-permute-start | bytes 196616 | tf_op jit(solution)/shard_map/ppermute | solution.py:46
  4.4 5.6 %collective-permute-start.4 = (bf16[2,128,128]{2,1,0:T(8,128)(2,1)S(1)}, bf16[2,128,128]{2,1,0:T(8,128)(2,1)S(1)}, u32[]{:S(2)}, u32[]{:S(2)}) collective-permute-start(bf16[2,128,128]{2,1,0:T(8,128)(2,1)S(1)} %get-tuple-element.30), channel_id=1, source_target_pairs={{0,1},{1,0},{2,3},{3,2},{4,5},{5,4},{6,7},{7,6},{8,9},{9,8},{10,11... | collective-permute-start | bytes 196616 | tf_op jit(solution)/shard_map/ppermute | solution.py:46
  4.9 5.3 %collective-permute-start.5 = (bf16[2,128,128]{2,1,0:T(8,128)(2,1)S(1)}, bf16[2,128,128]{2,1,0:T(8,128)(2,1)S(1)}, u32[]{:S(2)}, u32[]{:S(2)}) collective-permute-start(bf16[2,128,128]{2,1,0:T(8,128)(2,1)S(1)} %get-tuple-element.31), channel_id=1, source_target_pairs={{0,1},{1,0},{2,3},{3,2},{4,5},{5,4},{6,7},{7,6},{8,9},{9,8},{10,11... | collective-permute-start | bytes 196616 | tf_op jit(solution)/shard_map/ppermute | solution.py:46
  6.6 13.3 %collective-permute-start.1 = (bf16[6,128,128]{2,1,0:T(8,128)(2,1)S(1)}, bf16[6,128,128]{2,1,0:T(8,128)(2,1)S(1)}, u32[]{:S(2)}, u32[]{:S(2)}) collective-permute-start(bf16[6,128,128]{2,1,0:T(8,128)(2,1)S(1)} %get-tuple-element.28), channel_id=1, source_target_pairs={{0,4},{4,0},{8,12},{12,8},{16,20},{20,16},{24,28},{28,24},{1,5},{5... | collective-permute-start | bytes 589832 | tf_op jit(solution)/shard_map/ppermute | solution.py:36
  8.2 8.9 %copy-start.1 = (f32[5,8,512]{2,1,0:T(8,128)S(1)}, f32[5,8,512]{2,1,0:T(8,128)}, u32[]{:S(2)}) copy-start(f32[5,8,512]{2,1,0:T(8,128)} %w_ref.9) | copy-start | bytes 245764
  8.2 5.9 %collective-permute-start.9 = (bf16[2,128,128]{2,1,0:T(8,128)(2,1)S(1)}, bf16[2,128,128]{2,1,0:T(8,128)(2,1)S(1)}, u32[]{:S(2)}, u32[]{:S(2)}) collective-permute-start(bf16[2,128,128]{2,1,0:T(8,128)(2,1)S(1)} %sums.1), channel_id=1, source_target_pairs={{0,16},{4,20},{8,24},{12,28},{16,0},{20,4},{24,8},{28,12},{1,17},{... | collective-permute-start | bytes 196616 | tf_op jit(solution)/shard_map/ppermute | solution.py:36
  10.2 5.1 %collective-permute-start.6 = (bf16[2,128,128]{2,1,0:T(8,128)(2,1)S(1)}, bf16[2,128,128]{2,1,0:T(8,128)(2,1)S(1)}, u32[]{:S(2)}, u32[]{:S(2)}) collective-permute-start(bf16[2,128,128]{2,1,0:T(8,128)(2,1)S(1)} %left.1.refs_2_), channel_id=1, source_target_pairs={{0,1},{1,0},{2,3},{3,2},{4,5},{5,4},{6,7},{7,6},{8,12},{9,13},{10,... | collective-permute-start | bytes 196616 | tf_op jit(solution)/shard_map/ppermute | solution.py:46
  11.5 6.8 %collective-permute-start.7 = (bf16[2,128,128]{2,1,0:T(8,128)(2,1)S(1)}, bf16[2,128,128]{2,1,0:T(8,128)(2,1)S(1)}, u32[]{:S(2)}, u32[]{:S(2)}) collective-permute-start(bf16[2,128,128]{2,1,0:T(8,128)(2,1)S(1)} %left.1.refs_2_), channel_id=1, source_target_pairs={{0,8},{4,12},{8,0},{12,4},{16,24},{20,28},{24,16},{28,20},{1,9},{5... | collective-permute-start | bytes 196616 | tf_op jit(solution)/shard_map/ppermute | solution.py:36
  12.2 7.8 %collective-permute-start.8 = (bf16[2,128,128]{2,1,0:T(8,128)(2,1)S(1)}, bf16[2,128,128]{2,1,0:T(8,128)(2,1)S(1)}, u32[]{:S(2)}, u32[]{:S(2)}) collective-permute-start(bf16[2,128,128]{2,1,0:T(8,128)(2,1)S(1)} %left.1.refs_2_), channel_id=1, source_target_pairs={{0,12},{4,8},{8,4},{12,0},{16,28},{20,24},{24,20},{28,16},{1,13},{... | collective-permute-start | bytes 196616 | tf_op jit(solution)/shard_map/ppermute | solution.py:36
  14.2 6.7 %collective-permute-start.10 = (bf16[2,128,128]{2,1,0:T(8,128)(2,1)S(1)}, bf16[2,128,128]{2,1,0:T(8,128)(2,1)S(1)}, u32[]{:S(2)}, u32[]{:S(2)}) collective-permute-start(bf16[2,128,128]{2,1,0:T(8,128)(2,1)S(1)} %collective-permute-done.9.refs_6_), channel_id=1, source_target_pairs={{0,1},{1,0},{2,3},{3,2},{4,5},{5,4},{6,7},{7,6},{8,9},{9,8},{10,11... | collective-permute-start | bytes 196616 | tf_op jit(solution)/shard_map/ppermute | solution.py:46
  15.3 5.6 %collective-permute-start.11 = (bf16[2,128,128]{2,1,0:T(8,128)(2,1)S(1)}, bf16[2,128,128]{2,1,0:T(8,128)(2,1)S(1)}, u32[]{:S(2)}, u32[]{:S(2)}) collective-permute-start(bf16[2,128,128]{2,1,0:T(8,128)(2,1)S(1)} %collective-permute-done.9.refs_6_), channel_id=1, source_target_pairs={{0,1},{1,0},{2,3},{3,2},{4,5},{5,4},{6,7},{7,6},{8,9},{9,8},{10,11... | collective-permute-start | bytes 196616 | tf_op jit(solution)/shard_map/ppermute | solution.py:46
  17.2 1.7 %copy-start.2 = (f32[1024]{0:T(1024)S(1)}, f32[1024]{0:T(1024)}, u32[]{:S(2)}) copy-start(f32[1024]{0:T(1024)} %param.9) | copy-start | bytes 12292
  18.3 4.3 %collective-permute-start.12 = (bf16[2,128,128]{2,1,0:T(8,128)(2,1)S(1)}, bf16[2,128,128]{2,1,0:T(8,128)(2,1)S(1)}, u32[]{:S(2)}, u32[]{:S(2)}) collective-permute-start(bf16[2,128,128]{2,1,0:T(8,128)(2,1)S(1)} %collective-permute-done.9.refs_6_), channel_id=1, source_target_pairs={{0,1},{1,0},{2,3},{3,2},{4,5},{5,4},{6,7},{7,6},{8,9},{9,8},{10,11... | collective-permute-start | bytes 196616 | tf_op jit(solution)/shard_map/ppermute | solution.py:46
  22.9 1.9 %collective-permute-start.13 = (f32[1,512]{1,0:T(1,128)S(1)}, f32[1,512]{1,0:T(1,128)S(1)}, u32[]{:S(2)}, u32[]{:S(2)}) collective-permute-start(f32[1,512]{1,0:T(1,128)S(1)} %get-tuple-element.47.refs_4_), channel_id=1, source_target_pairs={{0,1},{1,0},{2,3},{3,2},{4,5},{5,4},{6,7},{7,6},{8,9},{9,8},{10,11... | collective-permute-start | bytes 6152 | tf_op jit(solution)/shard_map/ppermute | solution.py:36
  23.0 3.7 %collective-permute-start.14 = (f32[1,512]{1,0:T(1,128)S(1)}, f32[1,512]{1,0:T(1,128)S(1)}, u32[]{:S(2)}, u32[]{:S(2)}) collective-permute-start(f32[1,512]{1,0:T(1,128)S(1)} %get-tuple-element.47.refs_4_), channel_id=1, source_target_pairs={{0,2},{1,3},{2,0},{3,1},{4,6},{5,7},{6,4},{7,5},{8,10},{9,11},{10,... | collective-permute-start | bytes 6152 | tf_op jit(solution)/shard_map/ppermute | solution.py:36
  24.5 3.0 %collective-permute-start.15 = (f32[1,512]{1,0:T(1,128)S(1)}, f32[1,512]{1,0:T(1,128)S(1)}, u32[]{:S(2)}, u32[]{:S(2)}) collective-permute-start(f32[1,512]{1,0:T(1,128)S(1)} %get-tuple-element.47.refs_4_), channel_id=1, source_target_pairs={{0,3},{1,2},{2,1},{3,0},{4,7},{5,6},{6,5},{7,4},{8,11},{9,10},{10,... | collective-permute-start | bytes 6152 | tf_op jit(solution)/shard_map/ppermute | solution.py:36

commit v11 on v10

--- a/solution.py
+++ b/solution.py
@@ -105,8 +105,11 @@
 def intra_kernel(group, groups, place_ref, q_ref, w_ref, k_all, v_all, *refs):
     out_refs = refs[-len(groups) :]
     if len(refs) > len(groups):
-        gain_ref, kept_ref = refs[:2]
-        kept_ref[...] = gain_ref[...]
+        gain_ref, column_ref = refs[:2]
+        heads = gain_ref.shape[1] // HEAD_DIM
+        for head in range(heads):
+            rows = jnp.broadcast_to(gain_ref[:, column(head)], (HEAD_DIM, HEAD_DIM))
+            column_ref[column(head), :] = jnp.transpose(rows, (1, 0))
     count = q_ref.shape[0] // STRETCH
     local_bits = count.bit_length() - 1
     place = place_ref[0] & (QUAD - 1)
@@ -160,16 +163,20 @@
 
 def norm_kernel(group, full_width, place_ref, *refs):
     total_refs, share_refs, (gain_ref, out_hbm, buf, sems) = refs[:QUAD], refs[QUAD:-4], refs[-4:]
-    width = group * HEAD_DIM
     place = place_ref[0] & (QUAD - 1)
+    rows = buf.shape[0]
     scale = lax.rsqrt(functools.reduce(jnp.add, (ref[...] for ref in share_refs)) / full_width + EPSILON)
     copies = []
     for r in range(QUAD):
-        cols = pl.ds(pl.multiple_of((place ^ r) * width, width), width)
-        x = jnp.transpose(total_refs[r][...] * scale, (1, 0))
-        buf[r] = (x * gain_ref[:, cols]).astype(BF16)
-        copies.append(pltpu.make_async_copy(buf.at[r], out_hbm.at[:, cols], sems.at[r]))
-        copies[-1].start()
+        for j in range(group):
+            start = pl.multiple_of(((place ^ r) * group + j) * HEAD_DIM, HEAD_DIM)
+            here = pl.ds(start, HEAD_DIM)
+            gain = jnp.concatenate([gain_ref[here, :]] * (rows // HEAD_DIM), axis=1)
+            x = (total_refs[r][column(j), :] * scale * gain).astype(BF16)
+            spot = column(r * group + j)
+            buf[:, spot] = jnp.transpose(x, (1, 0))
+            copies.append(pltpu.make_async_copy(buf.at[:, spot], out_hbm.at[:, here], sems.at[r * group + j]))
+            copies[-1].start()
     for copy in copies:
         copy.wait()
 
@@ -207,11 +214,11 @@
     near = exchanged(rest, "seq", 1)
 
     totals = {}
-    for number, groups in enumerate(((3, 1), (2, 0))):
-        extra = [norm_gain.reshape(1, width)] if number == 0 else []
+    for number, groups in enumerate(((3,), (1, 2, 0))):
+        extra = [norm_gain.reshape(1, width)] if number == 1 else []
         outs = pl.pallas_call(
             functools.partial(intra_kernel, group, groups),
-            out_shape=(sds((1, width), F32),) * len(extra) + (part_shape,) * len(groups),
+            out_shape=(sds((width, HEAD_DIM), F32),) * len(extra) + (part_shape,) * len(groups),
             in_specs=[SMEM] + [VMEM] * (4 + len(extra)),
             out_specs=(VMEM,) * (len(extra) + len(groups)),
             compiler_params=params(),
@@ -284,7 +291,7 @@
         out_shape=sds((rows, width), BF16),
         in_specs=[SMEM] + [VMEM] * (QUAD + len(shares) + 1),
         out_specs=ANY,
-        scratch_shapes=[pltpu.VMEM((QUAD,) + panel, BF16), pltpu.SemaphoreType.DMA((QUAD,))],
+        scratch_shapes=[pltpu.VMEM((rows, width), BF16), pltpu.SemaphoreType.DMA((QUAD * group,))],
         compiler_params=params(),
         cost_estimate=cost(2 * rows * width, 2 * rows * width),
         name="norm",

time: 29.4 us -> 28.9 us (0.983)
  the two profiles are of different devices: /device:TPU:24 before, /device:TPU:0 now
where the time goes in v11:
time: 28.9 us; the launch traced here: 28.7 us
  starting transfers between devices  13 us (45%)
  waiting for transfers between devices  8.38 us (29%)
  Pallas kernels  7.19 us (25%)
    ppermute x8, starting transfers between devices, exchanged(): return lax.ppermute(block, axis, [(i, i ^ mask) for i in range(count)])  10.2 us
    ppermute x8, waiting for transfers between devices, exchanged(): return lax.ppermute(block, axis, [(i, i ^ mask) for i in range(count)])  5.79 us
    ppermute x8, starting transfers between devices, exchanged_in(): return lax.ppermute(block, ('seq', 'head'), route)  2.76 us
    ppermute x8, waiting for transfers between devices, exchanged_in(): return lax.ppermute(block, ('seq', 'head'), route)  2.59 us
    pallas_call x1, Pallas kernels, local(): pl.pallas_call(functools.partial(states_kernel, group), out_shape=(sds((Q...  2.3 us
    pallas_call x2, Pallas kernels, local(): pl.pallas_call(functools.partial(intra_kernel, group, groups), out_shape=...  2.22 us
    pallas_call x3, Pallas kernels, readout(): pl.pallas_call(kernel, out_shape=tuple(shapes), in_specs=[SMEM] + [VMEM]...  1.45 us
    pallas_call x1, Pallas kernels, local(): pl.pallas_call(functools.partial(norm_kernel, group, full_width), out_sha...  1.13 us
  transfers between devices with their start and end apart: 16, of which 6 were waited for; matrix products, arithmetic and copies ran while one was open for 0% of the time, Pallas kernels for 12%

profile of v11, /device:TPU:0, one launch (start us, length us, event | category | flops | bytes accessed | tf_op | source)
XLA Modules:
  0.0 28.7 jit_solution(7576498462906336556)
XLA Ops:
  0.0 0.0 copy-start
  0.0 2.3 %states.1 = (bf16[4,512,256]{2,1,0:T(8,128)(2,1)S(1)}, bf16[4,512,256]{2,1,0:T(8,128)(2,1)S(1)}, f32[2,128,128]{2,1,0:T(8,128)S(1)}, bf16[2,128,128]{2,1,0:T(8,1...) custom-call(s32[1]{0:T(128)} %bitcast.place_ref, ...), custom_call_target="tpu_custom_call" | custom-call | flops 134217728 | bytes 2097152 | tf_op jit(solution)/shard_map/states/pallas_call | solution.py:198
  2.3 3.1 %collective-permute-start = (bf16[2,128,128]{2,1,0:T(8,128)(2,1)S(1)}, bf16[2,128,128]{2,1,0:T(8,128)(2,1)S(1)}, u32[]{:S(2)}, u32[]{:S(2)}) collective-permute-start(bf16[2,128,128]{2,1,0:T(8,128)(2,1)S(1)} %get-tuple-element.26), channel_id=1, source_target_pairs={{0,4},{4,0},{8,12},{12,8},{16,20},{20,16},{24,28},{28,24},{1,5},{5... | collective-permute-start | bytes 196616 | tf_op jit(solution)/shard_map/ppermute | solution.py:36
  5.4 1.6 %collective-permute-start.2 = (bf16[2,128,128]{2,1,0:T(8,128)(2,1)S(1)}, bf16[2,128,128]{2,1,0:T(8,128)(2,1)S(1)}, u32[]{:S(2)}, u32[]{:S(2)}) collective-permute-start(bf16[2,128,128]{2,1,0:T(8,128)(2,1)S(1)} %get-tuple-element.29), channel_id=1, source_target_pairs={{0,8},{1,9},{2,10},{3,11},{4,12},{5,13},{6,14},{7,15},{8,0},{9,1},... | collective-permute-start | bytes 196616 | tf_op jit(solution)/shard_map/ppermute | solution.py:46
  6.9 0.0 collective-permute-start.3
  7.0 0.0 collective-permute-start.4
  7.0 0.5 %collective-permute-start.5 = (bf16[2,128,128]{2,1,0:T(8,128)(2,1)S(1)}, bf16[2,128,128]{2,1,0:T(8,128)(2,1)S(1)}, u32[]{:S(2)}, u32[]{:S(2)}) collective-permute-start(bf16[2,128,128]{2,1,0:T(8,128)(2,1)S(1)} %get-tuple-element.30), channel_id=1, source_target_pairs={{0,1},{1,0},{2,3},{3,2},{4,5},{5,4},{6,7},{7,6},{8,9},{9,8},{10,11... | collective-permute-start | bytes 196616 | tf_op jit(solution)/shard_map/ppermute | solution.py:46
  7.5 0.2 collective-permute-done.one_ref.refs_0_
  7.6 2.0 %collective-permute-start.1 = (bf16[6,128,128]{2,1,0:T(8,128)(2,1)S(1)}, bf16[6,128,128]{2,1,0:T(8,128)(2,1)S(1)}, u32[]{:S(2)}, u32[]{:S(2)}) collective-permute-start(bf16[6,128,128]{2,1,0:T(8,128)(2,1)S(1)} %get-tuple-element.27), channel_id=1, source_target_pairs={{0,4},{4,0},{8,12},{12,8},{16,20},{20,16},{24,28},{28,24},{1,5},{5... | collective-permute-start | bytes 589832 | tf_op jit(solution)/shard_map/ppermute | solution.py:36
  9.6 0.5 %collective-permute-done.2.early2_ref.two_ref = bf16[2,128,128]{2,1,0:T(8,128)(2,1)S(1)} collective-permute-done((bf16[2,128,128]{2,1,0:T(8,128)(2,1)S(1)}, bf16[2,128,128]{2,1,0:T(8,128)(2,1)S(1)}, u32[]{:S(2)}, u32[]{:S(2)}) %collective-permute-start.2) | collective-permute-done | bytes 65568 | tf_op jit(solution)/shard_map/ppermute | solution.py:46
  10.2 2.0 %collective-permute-done.3.early3_ref.three_ref = bf16[2,128,128]{2,1,0:T(8,128)(2,1)S(1)} collective-permute-done((bf16[2,128,128]{2,1,0:T(8,128)(2,1)S(1)}, bf16[2,128,128]{2,1,0:T(8,128)(2,1)S(1)}, u32[]{:S(2)}, u32[]{:S(2)}) %collective-permute-start.3) | collective-permute-done | bytes 65568 | tf_op jit(solution)/shard_map/ppermute | solution.py:46
  12.2 0.0 copy-start.1
  12.3 0.1 collective-permute-start.9
  12.3 0.0 collective-permute-done.4.late2_ref
  12.4 0.0 collective-permute-done.5.late3_ref
  12.4 0.1 collective-permute-start.6
  12.5 2.1 %collective-permute-start.7 = (bf16[2,128,128]{2,1,0:T(8,128)(2,1)S(1)}, bf16[2,128,128]{2,1,0:T(8,128)(2,1)S(1)}, u32[]{:S(2)}, u32[]{:S(2)}) collective-permute-start(bf16[2,128,128]{2,1,0:T(8,128)(2,1)S(1)} %left.1.refs_2_), channel_id=1, source_target_pairs={{0,8},{4,12},{8,0},{12,4},{16,24},{20,28},{24,16},{28,20},{1,9},{5... | collective-permute-start | bytes 196616 | tf_op jit(solution)/shard_map/ppermute | solution.py:36
  14.6 1.0 %collective-permute-start.8 = (bf16[2,128,128]{2,1,0:T(8,128)(2,1)S(1)}, bf16[2,128,128]{2,1,0:T(8,128)(2,1)S(1)}, u32[]{:S(2)}, u32[]{:S(2)}) collective-permute-start(bf16[2,128,128]{2,1,0:T(8,128)(2,1)S(1)} %left.1.refs_2_), channel_id=1, source_target_pairs={{0,12},{4,8},{8,4},{12,0},{16,28},{20,24},{24,20},{28,16},{1,13},{... | collective-permute-start | bytes 196616 | tf_op jit(solution)/shard_map/ppermute | solution.py:36
  15.5 2.6 %collective-permute-done.9.refs_6_ = bf16[2,128,128]{2,1,0:T(8,128)(2,1)S(1)} collective-permute-done((bf16[2,128,128]{2,1,0:T(8,128)(2,1)S(1)}, bf16[2,128,128]{2,1,0:T(8,128)(2,1)S(1)}, u32[]{:S(2)}, u32[]{:S(2)}) %collective-permute-start.9) | collective-permute-done | bytes 65568 | tf_op jit(solution)/shard_map/ppermute | solution.py:36
  18.1 0.0 collective-permute-start.10
  18.1 0.0 collective-permute-done.6.refs_3_
  18.1 0.5 %collective-permute-start.11 = (bf16[2,128,128]{2,1,0:T(8,128)(2,1)S(1)}, bf16[2,128,128]{2,1,0:T(8,128)(2,1)S(1)}, u32[]{:S(2)}, u32[]{:S(2)}) collective-permute-start(bf16[2,128,128]{2,1,0:T(8,128)(2,1)S(1)} %collective-permute-done.9.refs_6_), channel_id=1, source_target_pairs={{0,1},{1,0},{2,3},{3,2},{4,5},{5,4},{6,7},{7,6},{8,9},{9,8},{10,11... | collective-permute-start | bytes 196616 | tf_op jit(solution)/shard_map/ppermute | solution.py:46
  18.7 0.0 copy-done
  18.7 0.0 copy-done.1
  18.7 0.0 copy-start.2
  18.7 0.7 %intra.2.refs_7_ = f32[256,512]{1,0:T(8,128)S(1)} custom-call(s32[1]{0:T(128)} %bitcast.place_ref, bf16[512,1024]{1,0:T(8,128)(2,1)S(1)} %copy-done, f32[5,8,512]{2,1,0:T(8,128)S(1)} %copy-done.1, bf16[4,512,256]{2,1,0:T(8,128)(2,1)S(1)} %get-tuple-element.31.k_all, bf16[4,512,256]{2,1,0:T(8,128)(2,1)S(1)} %get-tuple-element.32.v_all), custom_call_target="tpu_custom_call" | custom-call | flops 402653184 | bytes 1048576 | tf_op jit(solution)/shard_map/intra/pallas_call | solution.py:219
  19.4 0.0 collective-permute-done.7.refs_4_
  19.4 0.1 collective-permute-start.12
  19.5 0.0 copy-done.2
  19.5 1.5 %intra.3 = (f32[1024,128]{1,0:T(8,128)S(1)}, f32[256,512]{1,0:T(8,128)S(1)}, f32[256,512]{1,0:T(8,128)S(1)}, f32[256,512]{1,0:T(8,128)S(1)}) custom-call(s32[1]{0:T(128)} %bitcast.place_ref, bf16[512,1024]{1,0:T(8,128)(2,1)S(1)} %copy-done, f32[5,8,512]{2,1,0:T(8,128)S(1)} %copy-done.1, bf16[4,512,256]{2,1,0:T(8,128)(2,1)S(1)} %get-tuple-element.31.k_all, ...), custom_call_target="tpu_custom_call" | custom-call | flops 402653184 | bytes 1048576 | tf_op jit(solution)/shard_map/intra/pallas_call | solution.py:219
  21.0 0.0 collective-permute-done.8.refs_5_
  21.0 0.0 collective-permute-done.1.refs_1_
  21.0 0.8 %shard_map.55 = (f32[256,512]{1,0:T(8,128)S(1)}, f32[256,512]{1,0:T(8,128)S(1)}, f32[256,512]{1,0:T(8,128)S(1)}, f32[256,512]{1,0:T(8,128)S(1)}, f32[8,512]{1,0:T(8,128)S(1)}) custom-call(s32[1]{0:T(128)} %bitcast.place_ref, bf16[512,1024]{1,0:T(8,128)(2,1)S(1)} %copy-done, f32[5,8,512]{2,1,0:T(8,128)S(1)} %copy-done.1, ...), custom_call_target="tpu_custom_call" | custom-call | flops 268435456 | bytes 4194304 | tf_op jit(solution)/shard_map/pallas_call | solution.py:270
  21.9 0.0 collective-permute-done.10.refs_0_
  21.9 0.0 collective-permute-done.11.refs_1_
  21.9 0.3 %shard_map.56 = (f32[256,512]{1,0:T(8,128)S(1)}, f32[256,512]{1,0:T(8,128)S(1)}, f32[8,512]{1,0:T(8,128)S(1)}) custom-call(s32[1]{0:T(128)} %bitcast.place_ref, bf16[512,1024]{1,0:T(8,128)(2,1)S(1)} %copy-done, f32[5,8,512]{2,1,0:T(8,128)S(1)} %copy-done.1, bf16[2,128,128]{2,1,0:T(8,128)(2,1)S(1)} %collective-permute-done.10.refs_0_, ...), custom_call_target="tpu_custom_call" | custom-call | flops 134217728 | bytes 2097152 | tf_op jit(solution)/shard_map/pallas_call | solution.py:270
  22.2 0.0 collective-permute-done.12.refs_0_
  22.3 0.3 shard_map.57
  22.5 0.6 %collective-permute-start.13 = (f32[1,512]{1,0:T(1,128)S(1)}, f32[1,512]{1,0:T(1,128)S(1)}, u32[]{:S(2)}, u32[]{:S(2)}) collective-permute-start(f32[1,512]{1,0:T(1,128)S(1)} %get-tuple-element.45.refs_4_), channel_id=1, source_target_pairs={{0,1},{1,0},{2,3},{3,2},{4,5},{5,4},{6,7},{7,6},{8,9},{9,8},{10,11... | collective-permute-start | bytes 6152 | tf_op jit(solution)/shard_map/ppermute | solution.py:36
  23.1 1.5 %collective-permute-start.14 = (f32[1,512]{1,0:T(1,128)S(1)}, f32[1,512]{1,0:T(1,128)S(1)}, u32[]{:S(2)}, u32[]{:S(2)}) collective-permute-start(f32[1,512]{1,0:T(1,128)S(1)} %get-tuple-element.45.refs_4_), channel_id=1, source_target_pairs={{0,2},{1,3},{2,0},{3,1},{4,6},{5,7},{6,4},{7,5},{8,10},{9,11},{10,... | collective-permute-start | bytes 6152 | tf_op jit(solution)/shard_map/ppermute | solution.py:36
  24.6 0.0 collective-permute-start.15
  24.6 0.0 collective-permute-done.13.refs_5_
  24.6 2.1 %collective-permute-done.14.refs_6_ = f32[1,512]{1,0:T(1,128)S(1)} collective-permute-done((f32[1,512]{1,0:T(1,128)S(1)}, f32[1,512]{1,0:T(1,128)S(1)}, u32[]{:S(2)}, u32[]{:S(2)}) %collective-permute-start.14) | collective-permute-done | bytes 2080 | tf_op jit(solution)/shard_map/ppermute | solution.py:36
  26.7 0.9 %collective-permute-done.15.refs_7_ = f32[1,512]{1,0:T(1,128)S(1)} collective-permute-done((f32[1,512]{1,0:T(1,128)S(1)}, f32[1,512]{1,0:T(1,128)S(1)}, u32[]{:S(2)}, u32[]{:S(2)}) %collective-permute-start.15) | collective-permute-done | bytes 2080 | tf_op jit(solution)/shard_map/ppermute | solution.py:36
  27.6 1.1 %norm.1 = bf16[512,1024]{1,0:T(8,128)(2,1)} custom-call(s32[1]{0:T(128)} %bitcast.place_ref, f32[256,512]{1,0:T(8,128)S(1)} %get-tuple-element.36.refs_0_, f32[256,512]{1,0:T(8,128)S(1)} %get-tuple-element.40.refs_1_, f32[256,512]{1,0:T(8,128)S(1)} %get-tuple-element.43.refs_2_, f32[256,512]{1,0:T(8,128)S(1)} %get-tuple-element.44.refs_3_, ...), custom_call_target="tpu_custom_call" | custom-call | flops 1048576 | bytes 1048576 | tf_op jit(solution)/shard_map/norm/pallas_call | solution.py:289
  (2 shorter events, 0.1 us)
Async XLA Ops:
  0.0 18.7 %copy-start = (bf16[512,1024]{1,0:T(8,128)(2,1)S(1)}, bf16[512,1024]{1,0:T(8,128)(2,1)}, u32[]{:S(2)}) copy-start(bf16[512,1024]{1,0:T(8,128)(2,1)} %q_ref.9) | copy-start | bytes 3145732
  2.3 5.3 %collective-permute-start = (bf16[2,128,128]{2,1,0:T(8,128)(2,1)S(1)}, bf16[2,128,128]{2,1,0:T(8,128)(2,1)S(1)}, u32[]{:S(2)}, u32[]{:S(2)}) collective-permute-start(bf16[2,128,128]{2,1,0:T(8,128)(2,1)S(1)} %get-tuple-element.26), channel_id=1, source_target_pairs={{0,4},{4,0},{8,12},{12,8},{16,20},{20,16},{24,28},{28,24},{1,5},{5... | collective-permute-start | bytes 196616 | tf_op jit(solution)/shard_map/ppermute | solution.py:36
  5.4 4.8 %collective-permute-start.2 = (bf16[2,128,128]{2,1,0:T(8,128)(2,1)S(1)}, bf16[2,128,128]{2,1,0:T(8,128)(2,1)S(1)}, u32[]{:S(2)}, u32[]{:S(2)}) collective-permute-start(bf16[2,128,128]{2,1,0:T(8,128)(2,1)S(1)} %get-tuple-element.29), channel_id=1, source_target_pairs={{0,8},{1,9},{2,10},{3,11},{4,12},{5,13},{6,14},{7,15},{8,0},{9,1},... | collective-permute-start | bytes 196616 | tf_op jit(solution)/shard_map/ppermute | solution.py:46
  6.9 5.3 %collective-permute-start.3 = (bf16[2,128,128]{2,1,0:T(8,128)(2,1)S(1)}, bf16[2,128,128]{2,1,0:T(8,128)(2,1)S(1)}, u32[]{:S(2)}, u32[]{:S(2)}) collective-permute-start(bf16[2,128,128]{2,1,0:T(8,128)(2,1)S(1)} %get-tuple-element.30), channel_id=1, source_target_pairs={{0,12},{1,13},{2,14},{3,15},{4,8},{5,9},{6,10},{7,11},{8,4},{9,5},... | collective-permute-start | bytes 196616 | tf_op jit(solution)/shard_map/ppermute | solution.py:46
  7.0 5.4 %collective-permute-start.4 = (bf16[2,128,128]{2,1,0:T(8,128)(2,1)S(1)}, bf16[2,128,128]{2,1,0:T(8,128)(2,1)S(1)}, u32[]{:S(2)}, u32[]{:S(2)}) collective-permute-start(bf16[2,128,128]{2,1,0:T(8,128)(2,1)S(1)} %get-tuple-element.29), channel_id=1, source_target_pairs={{0,1},{1,0},{2,3},{3,2},{4,5},{5,4},{6,7},{7,6},{8,9},{9,8},{10,11... | collective-permute-start | bytes 196616 | tf_op jit(solution)/shard_map/ppermute | solution.py:46
  7.0 5.4 %collective-permute-start.5 = (bf16[2,128,128]{2,1,0:T(8,128)(2,1)S(1)}, bf16[2,128,128]{2,1,0:T(8,128)(2,1)S(1)}, u32[]{:S(2)}, u32[]{:S(2)}) collective-permute-start(bf16[2,128,128]{2,1,0:T(8,128)(2,1)S(1)} %get-tuple-element.30), channel_id=1, source_target_pairs={{0,1},{1,0},{2,3},{3,2},{4,5},{5,4},{6,7},{7,6},{8,9},{9,8},{10,11... | collective-permute-start | bytes 196616 | tf_op jit(solution)/shard_map/ppermute | solution.py:46
  7.6 13.4 %collective-permute-start.1 = (bf16[6,128,128]{2,1,0:T(8,128)(2,1)S(1)}, bf16[6,128,128]{2,1,0:T(8,128)(2,1)S(1)}, u32[]{:S(2)}, u32[]{:S(2)}) collective-permute-start(bf16[6,128,128]{2,1,0:T(8,128)(2,1)S(1)} %get-tuple-element.27), channel_id=1, source_target_pairs={{0,4},{4,0},{8,12},{12,8},{16,20},{20,16},{24,28},{28,24},{1,5},{5... | collective-permute-start | bytes 589832 | tf_op jit(solution)/shard_map/ppermute | solution.py:36
  12.2 6.4 %copy-start.1 = (f32[5,8,512]{2,1,0:T(8,128)S(1)}, f32[5,8,512]{2,1,0:T(8,128)}, u32[]{:S(2)}) copy-start(f32[5,8,512]{2,1,0:T(8,128)} %w_ref.9) | copy-start | bytes 245764
  12.3 5.9 %collective-permute-start.9 = (bf16[2,128,128]{2,1,0:T(8,128)(2,1)S(1)}, bf16[2,128,128]{2,1,0:T(8,128)(2,1)S(1)}, u32[]{:S(2)}, u32[]{:S(2)}) collective-permute-start(bf16[2,128,128]{2,1,0:T(8,128)(2,1)S(1)} %sums.1), channel_id=1, source_target_pairs={{0,16},{4,20},{8,24},{12,28},{16,0},{20,4},{24,8},{28,12},{1,17},{... | collective-permute-start | bytes 196616 | tf_op jit(solution)/shard_map/ppermute | solution.py:36
  12.4 5.7 %collective-permute-start.6 = (bf16[2,128,128]{2,1,0:T(8,128)(2,1)S(1)}, bf16[2,128,128]{2,1,0:T(8,128)(2,1)S(1)}, u32[]{:S(2)}, u32[]{:S(2)}) collective-permute-start(bf16[2,128,128]{2,1,0:T(8,128)(2,1)S(1)} %left.1.refs_2_), channel_id=1, source_target_pairs={{0,1},{1,0},{2,3},{3,2},{4,5},{5,4},{6,7},{7,6},{8,12},{9,13},{10,... | collective-permute-start | bytes 196616 | tf_op jit(solution)/shard_map/ppermute | solution.py:46
  12.5 6.9 %collective-permute-start.7 = (bf16[2,128,128]{2,1,0:T(8,128)(2,1)S(1)}, bf16[2,128,128]{2,1,0:T(8,128)(2,1)S(1)}, u32[]{:S(2)}, u32[]{:S(2)}) collective-permute-start(bf16[2,128,128]{2,1,0:T(8,128)(2,1)S(1)} %left.1.refs_2_), channel_id=1, source_target_pairs={{0,8},{4,12},{8,0},{12,4},{16,24},{20,28},{24,16},{28,20},{1,9},{5... | collective-permute-start | bytes 196616 | tf_op jit(solution)/shard_map/ppermute | solution.py:36
  14.6 6.5 %collective-permute-start.8 = (bf16[2,128,128]{2,1,0:T(8,128)(2,1)S(1)}, bf16[2,128,128]{2,1,0:T(8,128)(2,1)S(1)}, u32[]{:S(2)}, u32[]{:S(2)}) collective-permute-start(bf16[2,128,128]{2,1,0:T(8,128)(2,1)S(1)} %left.1.refs_2_), channel_id=1, source_target_pairs={{0,12},{4,8},{8,4},{12,0},{16,28},{20,24},{24,20},{28,16},{1,13},{... | collective-permute-start | bytes 196616 | tf_op jit(solution)/shard_map/ppermute | solution.py:36
  18.1 3.7 %collective-permute-start.10 = (bf16[2,128,128]{2,1,0:T(8,128)(2,1)S(1)}, bf16[2,128,128]{2,1,0:T(8,128)(2,1)S(1)}, u32[]{:S(2)}, u32[]{:S(2)}) collective-permute-start(bf16[2,128,128]{2,1,0:T(8,128)(2,1)S(1)} %collective-permute-done.9.refs_6_), channel_id=1, source_target_pairs={{0,1},{1,0},{2,3},{3,2},{4,5},{5,4},{6,7},{7,6},{8,9},{9,8},{10,11... | collective-permute-start | bytes 196616 | tf_op jit(solution)/shard_map/ppermute | solution.py:46
  18.1 3.7 %collective-permute-start.11 = (bf16[2,128,128]{2,1,0:T(8,128)(2,1)S(1)}, bf16[2,128,128]{2,1,0:T(8,128)(2,1)S(1)}, u32[]{:S(2)}, u32[]{:S(2)}) collective-permute-start(bf16[2,128,128]{2,1,0:T(8,128)(2,1)S(1)} %collective-permute-done.9.refs_6_), channel_id=1, source_target_pairs={{0,1},{1,0},{2,3},{3,2},{4,5},{5,4},{6,7},{7,6},{8,9},{9,8},{10,11... | collective-permute-start | bytes 196616 | tf_op jit(solution)/shard_map/ppermute | solution.py:46
  18.7 0.8 %copy-start.2 = (f32[1024]{0:T(1024)S(1)}, f32[1024]{0:T(1024)}, u32[]{:S(2)}) copy-start(f32[1024]{0:T(1024)} %param.9) | copy-start | bytes 12292
  19.4 2.8 %collective-permute-start.12 = (bf16[2,128,128]{2,1,0:T(8,128)(2,1)S(1)}, bf16[2,128,128]{2,1,0:T(8,128)(2,1)S(1)}, u32[]{:S(2)}, u32[]{:S(2)}) collective-permute-start(bf16[2,128,128]{2,1,0:T(8,128)(2,1)S(1)} %collective-permute-done.9.refs_6_), channel_id=1, source_target_pairs={{0,1},{1,0},{2,3},{3,2},{4,5},{5,4},{6,7},{7,6},{8,9},{9,8},{10,11... | collective-permute-start | bytes 196616 | tf_op jit(solution)/shard_map/ppermute | solution.py:46
  22.5 2.0 %collective-permute-start.13 = (f32[1,512]{1,0:T(1,128)S(1)}, f32[1,512]{1,0:T(1,128)S(1)}, u32[]{:S(2)}, u32[]{:S(2)}) collective-permute-start(f32[1,512]{1,0:T(1,128)S(1)} %get-tuple-element.45.refs_4_), channel_id=1, source_target_pairs={{0,1},{1,0},{2,3},{3,2},{4,5},{5,4},{6,7},{7,6},{8,9},{9,8},{10,11... | collective-permute-start | bytes 6152 | tf_op jit(solution)/shard_map/ppermute | solution.py:36
  23.1 3.6 %collective-permute-start.14 = (f32[1,512]{1,0:T(1,128)S(1)}, f32[1,512]{1,0:T(1,128)S(1)}, u32[]{:S(2)}, u32[]{:S(2)}) collective-permute-start(f32[1,512]{1,0:T(1,128)S(1)} %get-tuple-element.45.refs_4_), channel_id=1, source_target_pairs={{0,2},{1,3},{2,0},{3,1},{4,6},{5,7},{6,4},{7,5},{8,10},{9,11},{10,... | collective-permute-start | bytes 6152 | tf_op jit(solution)/shard_map/ppermute | solution.py:36
  24.6 3.0 %collective-permute-start.15 = (f32[1,512]{1,0:T(1,128)S(1)}, f32[1,512]{1,0:T(1,128)S(1)}, u32[]{:S(2)}, u32[]{:S(2)}) collective-permute-start(f32[1,512]{1,0:T(1,128)S(1)} %get-tuple-element.45.refs_4_), channel_id=1, source_target_pairs={{0,3},{1,2},{2,1},{3,0},{4,7},{5,6},{6,5},{7,4},{8,11},{9,10},{10,... | collective-permute-start | bytes 6152 | tf_op jit(solution)/shard_map/ppermute | solution.py:36

commit v12 on v11

--- a/solution.py
+++ b/solution.py
@@ -93,7 +93,8 @@
     sent_ref[...] = total.astype(BF16)
 
 
-def left_kernel(seq, place_ref, own_ref, one_ref, early2_ref, early3_ref, late2_ref, late3_ref, left_ref):
+def left_kernel(seq, place_ref, own_ref, one_ref, early2_ref, early3_ref, late2_ref, late3_ref, gain_ref, left_ref, kept_ref):
+    kept_ref[...] = gain_ref[...]
     last_quad = place_ref[0] >= seq - QUAD
     two = jnp.where(last_quad, late2_ref[...], early2_ref[...])
     three = jnp.where(last_quad, late3_ref[...], early3_ref[...])
@@ -102,23 +103,15 @@
     left_ref[...] = jnp.where(place_ref[0] >> 1 & 1 == 1, other, pair).astype(BF16)
 
 
-def intra_kernel(group, groups, place_ref, q_ref, w_ref, k_all, v_all, *refs):
-    out_refs = refs[-len(groups) :]
-    if len(refs) > len(groups):
-        gain_ref, column_ref = refs[:2]
-        heads = gain_ref.shape[1] // HEAD_DIM
-        for head in range(heads):
-            rows = jnp.broadcast_to(gain_ref[:, column(head)], (HEAD_DIM, HEAD_DIM))
-            column_ref[column(head), :] = jnp.transpose(rows, (1, 0))
+def intra_of(group, place, q_ref, w_ref, k_all, v_all, out_refs):
     count = q_ref.shape[0] // STRETCH
     local_bits = count.bit_length() - 1
-    place = place_ref[0] & (QUAD - 1)
     causal = lax.broadcasted_iota(jnp.int32, (STRETCH, STRETCH), 0) <= lax.broadcasted_iota(
         jnp.int32, (STRETCH, STRETCH), 1
     )
-    for r, out_ref in zip(groups, out_refs):
+    for r, out_ref in enumerate(out_refs):
         for j in range(group):
-            head = (place ^ r) * group + j
+            head = (place & (QUAD - 1) ^ r) * group + j
             cols = pl.ds(pl.multiple_of(head * HEAD_DIM, HEAD_DIM), HEAD_DIM)
             states = []
             for c in range(count):
@@ -136,7 +129,29 @@
                     states.append(tn(v, k))
 
 
-def readout_kernel(group, first, work, n_states, carry, finish, place_ref, q_ref, w_ref, *refs):
+def intra_early_kernel(group, place_ref, *refs):
+    @pl.when(place_ref[0] < QUAD)
+    def _():
+        intra_of(group, place_ref[0], *refs[:4], refs[4:])
+
+
+def intra_late_kernel(group, place_ref, q_ref, w_ref, k_all, v_all, gain_ref, *refs):
+    done_refs, column_ref, out_refs = refs[:QUAD], refs[QUAD], refs[QUAD + 1 :]
+    for head in range(QUAD * group):
+        rows = jnp.broadcast_to(gain_ref[:, column(head)], (HEAD_DIM, HEAD_DIM))
+        column_ref[column(head), :] = jnp.transpose(rows, (1, 0))
+
+    @pl.when(place_ref[0] < QUAD)
+    def _():
+        for done_ref, out_ref in zip(done_refs, out_refs):
+            out_ref[...] = done_ref[...]
+
+    @pl.when(place_ref[0] >= QUAD)
+    def _():
+        intra_of(group, place_ref[0], q_ref, w_ref, k_all, v_all, out_refs)
+
+
+def readout_of(group, first, work, n_states, carry, finish, place_ref, q_ref, w_ref, *refs):
     n = len(work)
     state_refs, total_refs, refs = refs[:n_states], refs[n_states : n_states + n], refs[n_states + n :]
     carried_ref = refs[0] if carry else None
@@ -161,6 +176,14 @@
         squares_ref[:, here] = jnp.sum(squares, axis=0, keepdims=True) if finish else squares
 
 
+def readout_kernel(group, first, work, lacks, *args):
+    low = any(bit < 2 for _, _, reads in work for bit, _, _ in reads)
+    fewer = tuple((r, complete, tuple(read for read in reads if low and read[0] >= 2)) for r, complete, reads in work)
+    place = args[3][0]
+    for present, some in ((True, work), (False, fewer)):
+        pl.when(lacks(place) != present)(functools.partial(readout_of, group, first, some, *args))
+
+
 def norm_kernel(group, full_width, place_ref, *refs):
     total_refs, share_refs, (gain_ref, out_hbm, buf, sems) = refs[:QUAD], refs[QUAD:-4], refs[-4:]
     place = place_ref[0] & (QUAD - 1)
@@ -213,22 +236,17 @@
     late2 = exchanged_in(two, 2, lambda s, seq: s >= seq - QUAD)
     near = exchanged(rest, "seq", 1)
 
-    totals = {}
-    for number, groups in enumerate(((3,), (1, 2, 0))):
-        extra = [norm_gain.reshape(1, width)] if number == 1 else []
-        outs = pl.pallas_call(
-            functools.partial(intra_kernel, group, groups),
-            out_shape=(sds((width, HEAD_DIM), F32),) * len(extra) + (part_shape,) * len(groups),
-            in_specs=[SMEM] + [VMEM] * (4 + len(extra)),
-            out_specs=(VMEM,) * (len(extra) + len(groups)),
-            compiler_params=params(),
-            cost_estimate=cost(3 * rows * STRETCH * width, 2 * rows * width),
-            name="intra",
-        )(place, queries, level_weights, k_all, v_all, *extra)
-        if extra:
-            gain, *outs = outs
-        totals |= dict(zip(groups, outs))
-
+    args = (place, queries, level_weights, k_all, v_all)
+    work_cost = cost(6 * rows * STRETCH * width, 4 * rows * width)
+    outs = pl.pallas_call(
+        functools.partial(intra_early_kernel, group),
+        out_shape=(part_shape,) * QUAD,
+        in_specs=[SMEM] + [VMEM] * 4,
+        out_specs=(VMEM,) * QUAD,
+        compiler_params=params(),
+        cost_estimate=work_cost,
+        name="intra_early",
+    )(*args)
     sums, *running = pl.pallas_call(
         sums_kernel,
         out_shape=(sds(block, BF16),) + (sds(block, F32),) * (seq_bits > 3),
@@ -244,27 +262,42 @@
             running = [running[0] + upper[-1].astype(F32)]
             sums = running[0].astype(BF16)
         upper.append(exchanged(sums, "seq", 1 << bit))
-    left_pair = pl.pallas_call(
+    left_pair, gain = pl.pallas_call(
         functools.partial(left_kernel, lax.axis_size("seq")),
-        out_shape=sds(block, BF16),
-        in_specs=[SMEM] + [VMEM] * 6,
-        out_specs=VMEM,
+        out_shape=(sds(block, BF16), sds((1, width), F32)),
+        in_specs=[SMEM] + [VMEM] * 7,
+        out_specs=(VMEM,) * 2,
         compiler_params=params(),
         cost_estimate=cost(4 * group * HEAD_DIM**2, 16 * group * HEAD_DIM**2),
         name="left",
-    )(place, own, taken1, early2, early3, late2, late3)
+    )(place, own, taken1, early2, early3, late2, late3, norm_gain.reshape(1, width))
     top = jnp.concatenate(upper, axis=0) if len(upper) > 1 else upper[0]
     tops = {0: top} | {r: exchanged_in(top, r, lambda s, seq: s >= QUAD) for r in (3, 1, 2)}
 
+    gain, *outs = pl.pallas_call(
+        functools.partial(intra_late_kernel, group),
+        out_shape=(sds((width, HEAD_DIM), F32),) + (part_shape,) * QUAD,
+        in_specs=[SMEM] + [VMEM] * (5 + QUAD),
+        out_specs=(VMEM,) * (1 + QUAD),
+        compiler_params=params(),
+        cost_estimate=work_cost,
+        name="intra_late",
+    )(*args, gain, *outs)
+    totals = dict(enumerate(outs))
+
     middle = {0: left_pair} | {r: exchanged(left_pair, "seq", r) for r in (3, 2)}
     middle[1] = exchanged_in(left_pair, 1, lambda s, seq: s >> 1 & 1 == 1)
 
     def top_reads(ref):
         return tuple((bit, ref, (bit - 2) * group) for bit in range(2, seq_bits))
 
-    def readout(work, states, squares, finish=False):
+    def readout(label, work, states, squares, finish=False):
         n, carry = len(work), squares is not None
-        kernel = functools.partial(readout_kernel, group, 1 + local_bits, work, len(states), carry, finish)
+
+        def lacks(place):
+            return place & (QUAD - 1) == 0 if label == "far" else place < QUAD
+
+        kernel = functools.partial(readout_kernel, group, 1 + local_bits, work, lacks, len(states), carry, finish)
         ins = [place, queries, level_weights, *states, *(totals[r] for r, _, _ in work)] + [squares] * carry
         shapes = [part_shape] * n + [sds((1 if finish else 8, rows), F32)]
         outs = pl.pallas_call(
@@ -280,9 +313,9 @@
 
     below = {0: ((0, 0, 0), (1, 2, 0))} | {r: ((0, 1, (r - 1) * group), (1, 2 + r, 0)) for r in (1, 2, 3)}
     work = tuple((r, r == 0, below[r] + (top_reads(6) if r == 0 else ())) for r in (3, 1, 2, 0))
-    squares = readout(work, (taken1, near, *(middle[r] for r in range(QUAD)), top), None)
-    squares = readout(((3, True, top_reads(0)), (1, True, top_reads(1))), (tops[3], tops[1]), squares)
-    squares = readout(((2, True, top_reads(0)),), (tops[2],), squares, finish=True)
+    squares = readout("far", work, (taken1, near, *(middle[r] for r in range(QUAD)), top), None)
+    squares = readout("mid", ((3, True, top_reads(0)), (1, True, top_reads(1))), (tops[3], tops[1]), squares)
+    squares = readout("last", ((2, True, top_reads(0)),), (tops[2],), squares, finish=True)
 
     shares = [squares] + [exchanged(squares, "head", mask) for mask in range(1, lax.axis_size("head"))]
 

time: 28.9 us -> 31.4 us (1.087)
  the two profiles are of different devices: /device:TPU:0 before, /device:TPU:17 now
where the time goes in v12:
time: 31.4 us; the launch traced here: 31.3 us
  starting transfers between devices  15.5 us (49%)
  waiting for transfers between devices  9.03 us (29%)
  Pallas kernels  6.57 us (21%)
    ppermute x8, starting transfers between devices, exchanged_in(): return lax.ppermute(block, ('seq', 'head'), route)  7.99 us
    ppermute x8, starting transfers between devices, exchanged(): return lax.ppermute(block, axis, [(i, i ^ mask) for i in range(count)])  7.54 us
    ppermute x8, waiting for transfers between devices, exchanged(): return lax.ppermute(block, axis, [(i, i ^ mask) for i in range(count)])  5.15 us
    ppermute x8, waiting for transfers between devices, exchanged_in(): return lax.ppermute(block, ('seq', 'head'), route)  3.87 us
    pallas_call x1, Pallas kernels, local(): pl.pallas_call(functools.partial(states_kernel, group), out_shape=(sds((Q...  2.3 us
    pallas_call x1, Pallas kernels, local(): pl.pallas_call(functools.partial(intra_late_kernel, group), out_shape=(sd...  2.09 us
    pallas_call x1, Pallas kernels, local(): pl.pallas_call(functools.partial(norm_kernel, group, full_width), out_sha...  1.14 us
    pallas_call x3, Pallas kernels, readout(): pl.pallas_call(kernel, out_shape=tuple(shapes), in_specs=[SMEM] + [VMEM]...  0.95 us
  transfers between devices with their start and end apart: 16, of which 6 were waited for; matrix products, arithmetic and copies ran while one was open for 0% of the time, Pallas kernels for 9%

profile of v12, /device:TPU:17, one launch (start us, length us, event | category | flops | bytes accessed | tf_op | source)
XLA Modules:
  0.0 31.3 jit_solution(3267072195894205481)
XLA Ops:
  0.0 0.0 copy-start
  0.0 2.3 %states.1 = (bf16[4,512,256]{2,1,0:T(8,128)(2,1)S(1)}, bf16[4,512,256]{2,1,0:T(8,128)(2,1)S(1)}, f32[2,128,128]{2,1,0:T(8,128)S(1)}, bf16[2,128,128]{2,1,0:T(8,1...) custom-call(s32[1]{0:T(128)} %bitcast.place_ref.args_0_, ...), custom_call_target="tpu_custom_call" | custom-call | flops 134217728 | bytes 2097152 | tf_op jit(solution)/shard_map/states/pallas_call | solution.py:221
  2.3 1.3 %collective-permute-start = (bf16[2,128,128]{2,1,0:T(8,128)(2,1)S(1)}, bf16[2,128,128]{2,1,0:T(8,128)(2,1)S(1)}, u32[]{:S(2)}, u32[]{:S(2)}) collective-permute-start(bf16[2,128,128]{2,1,0:T(8,128)(2,1)S(1)} %get-tuple-element.33), channel_id=1, source_target_pairs={{0,4},{4,0},{8,12},{12,8},{16,20},{20,16},{24,28},{28,24},{1,5},{5... | collective-permute-start | bytes 196616 | tf_op jit(solution)/shard_map/ppermute | solution.py:36
  3.6 0.0 copy-start.2
  3.6 1.0 %collective-permute-start.2 = (bf16[2,128,128]{2,1,0:T(8,128)(2,1)S(1)}, bf16[2,128,128]{2,1,0:T(8,128)(2,1)S(1)}, u32[]{:S(2)}, u32[]{:S(2)}) collective-permute-start(bf16[2,128,128]{2,1,0:T(8,128)(2,1)S(1)} %get-tuple-element.36), channel_id=1, source_target_pairs={{0,8},{1,9},{2,10},{3,11},{4,12},{5,13},{6,14},{7,15},{8,0},{9,1},... | collective-permute-start | bytes 196616 | tf_op jit(solution)/shard_map/ppermute | solution.py:46
  4.6 0.0 collective-permute-start.3
  4.6 1.3 %collective-permute-start.4 = (bf16[2,128,128]{2,1,0:T(8,128)(2,1)S(1)}, bf16[2,128,128]{2,1,0:T(8,128)(2,1)S(1)}, u32[]{:S(2)}, u32[]{:S(2)}) collective-permute-start(bf16[2,128,128]{2,1,0:T(8,128)(2,1)S(1)} %get-tuple-element.36), channel_id=1, source_target_pairs={{0,1},{1,0},{2,3},{3,2},{4,5},{5,4},{6,7},{7,6},{8,9},{9,8},{10,11... | collective-permute-start | bytes 196616 | tf_op jit(solution)/shard_map/ppermute | solution.py:46
  5.9 0.1 collective-permute-start.5
  6.0 0.0 collective-permute-done.one_ref.args_3_
  6.0 1.2 %collective-permute-start.1 = (bf16[6,128,128]{2,1,0:T(8,128)(2,1)S(1)}, bf16[6,128,128]{2,1,0:T(8,128)(2,1)S(1)}, u32[]{:S(2)}, u32[]{:S(2)}) collective-permute-start(bf16[6,128,128]{2,1,0:T(8,128)(2,1)S(1)} %get-tuple-element.34), channel_id=1, source_target_pairs={{0,4},{4,0},{8,12},{12,8},{16,20},{20,16},{24,28},{28,24},{1,5},{5... | collective-permute-start | bytes 589832 | tf_op jit(solution)/shard_map/ppermute | solution.py:36
  7.2 0.0 collective-permute-done.2.early2_ref.two_ref
  7.2 0.0 collective-permute-done.3.early3_ref.three_ref
  7.2 0.5 %collective-permute-done.4.late2_ref = bf16[2,128,128]{2,1,0:T(8,128)(2,1)S(1)} collective-permute-done((bf16[2,128,128]{2,1,0:T(8,128)(2,1)S(1)}, bf16[2,128,128]{2,1,0:T(8,128)(2,1)S(1)}, u32[]{:S(2)}, u32[]{:S(2)}) %collective-permute-start.4) | collective-permute-done | bytes 65568 | tf_op jit(solution)/shard_map/ppermute | solution.py:46
  7.7 2.3 %collective-permute-done.5.late3_ref = bf16[2,128,128]{2,1,0:T(8,128)(2,1)S(1)} collective-permute-done((bf16[2,128,128]{2,1,0:T(8,128)(2,1)S(1)}, bf16[2,128,128]{2,1,0:T(8,128)(2,1)S(1)}, u32[]{:S(2)}, u32[]{:S(2)}) %collective-permute-start.5) | collective-permute-done | bytes 65568 | tf_op jit(solution)/shard_map/ppermute | solution.py:46
  10.0 0.0 copy-done.2
  10.0 0.0 copy-start.1
  10.1 2.0 %collective-permute-start.6 = (bf16[2,128,128]{2,1,0:T(8,128)(2,1)S(1)}, bf16[2,128,128]{2,1,0:T(8,128)(2,1)S(1)}, u32[]{:S(2)}, u32[]{:S(2)}) collective-permute-start(bf16[2,128,128]{2,1,0:T(8,128)(2,1)S(1)} %get-tuple-element.38.args_5_), channel_id=1, source_target_pairs={{0,1},{1,0},{2,3},{3,2},{4,5},{5,4},{6,7},{7,6},{8,12},{9,13},{10,... | collective-permute-start | bytes 196616 | tf_op jit(solution)/shard_map/ppermute | solution.py:46
  12.1 0.0 collective-permute-start.7
  12.1 0.1 collective-permute-start.9
  12.2 0.0 copy-done
  12.2 0.0 copy-done.1
  12.2 1.4 %collective-permute-start.8 = (bf16[2,128,128]{2,1,0:T(8,128)(2,1)S(1)}, bf16[2,128,128]{2,1,0:T(8,128)(2,1)S(1)}, u32[]{:S(2)}, u32[]{:S(2)}) collective-permute-start(bf16[2,128,128]{2,1,0:T(8,128)(2,1)S(1)} %get-tuple-element.38.args_5_), channel_id=1, source_target_pairs={{0,12},{4,8},{8,4},{12,0},{16,28},{20,24},{24,20},{28,16},{1,13},{... | collective-permute-start | bytes 196616 | tf_op jit(solution)/shard_map/ppermute | solution.py:36
  13.6 2.6 %collective-permute-done.9.args_9_ = bf16[2,128,128]{2,1,0:T(8,128)(2,1)S(1)} collective-permute-done((bf16[2,128,128]{2,1,0:T(8,128)(2,1)S(1)}, bf16[2,128,128]{2,1,0:T(8,128)(2,1)S(1)}, u32[]{:S(2)}, u32[]{:S(2)}) %collective-permute-start.9) | collective-permute-done | bytes 65568 | tf_op jit(solution)/shard_map/ppermute | solution.py:36
  16.2 2.5 %collective-permute-start.10 = (bf16[2,128,128]{2,1,0:T(8,128)(2,1)S(1)}, bf16[2,128,128]{2,1,0:T(8,128)(2,1)S(1)}, u32[]{:S(2)}, u32[]{:S(2)}) collective-permute-start(bf16[2,128,128]{2,1,0:T(8,128)(2,1)S(1)} %collective-permute-done.9.args_9_), channel_id=1, source_target_pairs={{0,1},{1,0},{2,3},{3,2},{4,5},{5,4},{6,7},{7,6},{8,9},{9,8},{10,11... | collective-permute-start | bytes 196616 | tf_op jit(solution)/shard_map/ppermute | solution.py:46
  18.8 0.0 collective-permute-done.6.args_6_
  18.8 1.1 %collective-permute-start.11 = (bf16[2,128,128]{2,1,0:T(8,128)(2,1)S(1)}, bf16[2,128,128]{2,1,0:T(8,128)(2,1)S(1)}, u32[]{:S(2)}, u32[]{:S(2)}) collective-permute-start(bf16[2,128,128]{2,1,0:T(8,128)(2,1)S(1)} %collective-permute-done.9.args_9_), channel_id=1, source_target_pairs={{0,1},{1,0},{2,3},{3,2},{4,5},{5,4},{6,7},{7,6},{8,9},{9,8},{10,11... | collective-permute-start | bytes 196616 | tf_op jit(solution)/shard_map/ppermute | solution.py:46
  19.8 0.0 collective-permute-done.7.args_7_
  19.9 0.0 collective-permute-start.12
  19.9 2.1 %intra_late.1 = (f32[1024,128]{1,0:T(8,128)S(1)}, f32[256,512]{1,0:T(8,128)S(1)}, f32[256,512]{1,0:T(8,128)S(1)}, f32[256,512]{1,0:T(8,128)S(1)}, f32[256,512]{1,0:T(8,128)S(1)}) custom-call(s32[1]{0:T(128)} %bitcast.place_ref.args_0_, bf16[512,1024]{1,0:T(8,128)(2,1)S(1)} %copy-done, f32[5,8,512]{2,1,0:T(8,128)S(1)} %copy-done.1, ...), custom_call_target="tpu_custom_call" | custom-call | flops 805306368 | bytes 2097152 | tf_op jit(solution)/shard_map/intra_late/pallas_call | solution.py:277
  22.0 0.0 collective-permute-done.8.args_8_
  22.0 0.0 collective-permute-done.1.args_4_
  22.0 0.3 %shard_map.55 = (f32[256,512]{1,0:T(8,128)S(1)}, f32[256,512]{1,0:T(8,128)S(1)}, f32[256,512]{1,0:T(8,128)S(1)}, f32[256,512]{1,0:T(8,128)S(1)}, f32[8,512]{1,0:T(8,128)S(1)}) custom-call(s32[1]{0:T(128)} %bitcast.place_ref.args_0_, bf16[512,1024]{1,0:T(8,128)(2,1)S(1)} %copy-done, f32[5,8,512]{2,1,0:T(8,128)S(1)} %copy-done.1, ...), custom_call_target="tpu_custom_call" | custom-call | flops 268435456 | bytes 4194304 | tf_op jit(solution)/shard_map/pallas_call | solution.py:303
  22.3 0.0 collective-permute-done.10.args_3_
  22.3 0.0 collective-permute-done.11.args_4_
  22.3 0.3 %shard_map.56 = (f32[256,512]{1,0:T(8,128)S(1)}, f32[256,512]{1,0:T(8,128)S(1)}, f32[8,512]{1,0:T(8,128)S(1)}) custom-call(s32[1]{0:T(128)} %bitcast.place_ref.args_0_, bf16[512,1024]{1,0:T(8,128)(2,1)S(1)} %copy-done, f32[5,8,512]{2,1,0:T(8,128)S(1)} %copy-done.1, bf16[2,128,128]{2,1,0:T(8,128)(2,1)S(1)} %collective-permute-done.10.args_3_, ...), custom_call_target="tpu_custom_call" | custom-call | flops 134217728 | bytes 2097152 | tf_op jit(solution)/shard_map/pallas_call | solution.py:303
  22.7 1.1 %collective-permute-done.12.args_3_ = bf16[2,128,128]{2,1,0:T(8,128)(2,1)S(1)} collective-permute-done((bf16[2,128,128]{2,1,0:T(8,128)(2,1)S(1)}, bf16[2,128,128]{2,1,0:T(8,128)(2,1)S(1)}, u32[]{:S(2)}, u32[]{:S(2)}) %collective-permute-start.12) | collective-permute-done | bytes 65568 | tf_op jit(solution)/shard_map/ppermute | solution.py:46
  23.8 0.3 shard_map.57
  24.1 1.8 %collective-permute-start.13 = (f32[1,512]{1,0:T(1,128)S(1)}, f32[1,512]{1,0:T(1,128)S(1)}, u32[]{:S(2)}, u32[]{:S(2)}) collective-permute-start(f32[1,512]{1,0:T(1,128)S(1)} %get-tuple-element.59.refs_4_), channel_id=1, source_target_pairs={{0,1},{1,0},{2,3},{3,2},{4,5},{5,4},{6,7},{7,6},{8,9},{9,8},{10,11... | collective-permute-start | bytes 6152 | tf_op jit(solution)/shard_map/ppermute | solution.py:36
  25.9 1.2 %collective-permute-start.14 = (f32[1,512]{1,0:T(1,128)S(1)}, f32[1,512]{1,0:T(1,128)S(1)}, u32[]{:S(2)}, u32[]{:S(2)}) collective-permute-start(f32[1,512]{1,0:T(1,128)S(1)} %get-tuple-element.59.refs_4_), channel_id=1, source_target_pairs={{0,2},{1,3},{2,0},{3,1},{4,6},{5,7},{6,4},{7,5},{8,10},{9,11},{10,... | collective-permute-start | bytes 6152 | tf_op jit(solution)/shard_map/ppermute | solution.py:36
  27.1 0.5 %collective-permute-start.15 = (f32[1,512]{1,0:T(1,128)S(1)}, f32[1,512]{1,0:T(1,128)S(1)}, u32[]{:S(2)}, u32[]{:S(2)}) collective-permute-start(f32[1,512]{1,0:T(1,128)S(1)} %get-tuple-element.59.refs_4_), channel_id=1, source_target_pairs={{0,3},{1,2},{2,1},{3,0},{4,7},{5,6},{6,5},{7,4},{8,11},{9,10},{10,... | collective-permute-start | bytes 6152 | tf_op jit(solution)/shard_map/ppermute | solution.py:36
  27.6 0.0 collective-permute-done.13.refs_5_
  27.6 0.7 %collective-permute-done.14.refs_6_ = f32[1,512]{1,0:T(1,128)S(1)} collective-permute-done((f32[1,512]{1,0:T(1,128)S(1)}, f32[1,512]{1,0:T(1,128)S(1)}, u32[]{:S(2)}, u32[]{:S(2)}) %collective-permute-start.14) | collective-permute-done | bytes 2080 | tf_op jit(solution)/shard_map/ppermute | solution.py:36
  28.4 1.8 %collective-permute-done.15.refs_7_ = f32[1,512]{1,0:T(1,128)S(1)} collective-permute-done((f32[1,512]{1,0:T(1,128)S(1)}, f32[1,512]{1,0:T(1,128)S(1)}, u32[]{:S(2)}, u32[]{:S(2)}) %collective-permute-start.15) | collective-permute-done | bytes 2080 | tf_op jit(solution)/shard_map/ppermute | solution.py:36
  30.1 1.1 %norm.1 = bf16[512,1024]{1,0:T(8,128)(2,1)} custom-call(s32[1]{0:T(128)} %bitcast.place_ref.args_0_, f32[256,512]{1,0:T(8,128)S(1)} %get-tuple-element.50.refs_0_, f32[256,512]{1,0:T(8,128)S(1)} %get-tuple-element.54.refs_1_, f32[256,512]{1,0:T(8,128)S(1)} %get-tuple-element.57.refs_2_, f32[256,512]{1,0:T(8,128)S(1)} %get-tuple-element.58.refs_3_, ...), custom_call_target="tpu_custom_call" | custom-call | flops 1048576 | bytes 1048576 | tf_op jit(solution)/shard_map/norm/pallas_call | solution.py:322
  (3 shorter events, 0.1 us)
Async XLA Ops:
  0.0 12.2 %copy-start = (bf16[512,1024]{1,0:T(8,128)(2,1)S(1)}, bf16[512,1024]{1,0:T(8,128)(2,1)}, u32[]{:S(2)}) copy-start(bf16[512,1024]{1,0:T(8,128)(2,1)} %args_1_.8) | copy-start | bytes 3145732
  2.3 3.7 %collective-permute-start = (bf16[2,128,128]{2,1,0:T(8,128)(2,1)S(1)}, bf16[2,128,128]{2,1,0:T(8,128)(2,1)S(1)}, u32[]{:S(2)}, u32[]{:S(2)}) collective-permute-start(bf16[2,128,128]{2,1,0:T(8,128)(2,1)S(1)} %get-tuple-element.33), channel_id=1, source_target_pairs={{0,4},{4,0},{8,12},{12,8},{16,20},{20,16},{24,28},{28,24},{1,5},{5... | collective-permute-start | bytes 196616 | tf_op jit(solution)/shard_map/ppermute | solution.py:36
  3.6 6.4 %copy-start.2 = (f32[1024]{0:T(1024)S(1)}, f32[1024]{0:T(1024)}, u32[]{:S(2)}) copy-start(f32[1024]{0:T(1024)} %param.9) | copy-start | bytes 12292
  3.6 3.6 %collective-permute-start.2 = (bf16[2,128,128]{2,1,0:T(8,128)(2,1)S(1)}, bf16[2,128,128]{2,1,0:T(8,128)(2,1)S(1)}, u32[]{:S(2)}, u32[]{:S(2)}) collective-permute-start(bf16[2,128,128]{2,1,0:T(8,128)(2,1)S(1)} %get-tuple-element.36), channel_id=1, source_target_pairs={{0,8},{1,9},{2,10},{3,11},{4,12},{5,13},{6,14},{7,15},{8,0},{9,1},... | collective-permute-start | bytes 196616 | tf_op jit(solution)/shard_map/ppermute | solution.py:46
  4.6 2.7 %collective-permute-start.3 = (bf16[2,128,128]{2,1,0:T(8,128)(2,1)S(1)}, bf16[2,128,128]{2,1,0:T(8,128)(2,1)S(1)}, u32[]{:S(2)}, u32[]{:S(2)}) collective-permute-start(bf16[2,128,128]{2,1,0:T(8,128)(2,1)S(1)} %get-tuple-element.37), channel_id=1, source_target_pairs={{0,12},{1,13},{2,14},{3,15},{4,8},{5,9},{6,10},{7,11},{8,4},{9,5},... | collective-permute-start | bytes 196616 | tf_op jit(solution)/shard_map/ppermute | solution.py:46
  4.6 3.1 %collective-permute-start.4 = (bf16[2,128,128]{2,1,0:T(8,128)(2,1)S(1)}, bf16[2,128,128]{2,1,0:T(8,128)(2,1)S(1)}, u32[]{:S(2)}, u32[]{:S(2)}) collective-permute-start(bf16[2,128,128]{2,1,0:T(8,128)(2,1)S(1)} %get-tuple-element.36), channel_id=1, source_target_pairs={{0,1},{1,0},{2,3},{3,2},{4,5},{5,4},{6,7},{7,6},{8,9},{9,8},{10,11... | collective-permute-start | bytes 196616 | tf_op jit(solution)/shard_map/ppermute | solution.py:46
  5.9 4.1 %collective-permute-start.5 = (bf16[2,128,128]{2,1,0:T(8,128)(2,1)S(1)}, bf16[2,128,128]{2,1,0:T(8,128)(2,1)S(1)}, u32[]{:S(2)}, u32[]{:S(2)}) collective-permute-start(bf16[2,128,128]{2,1,0:T(8,128)(2,1)S(1)} %get-tuple-element.37), channel_id=1, source_target_pairs={{0,1},{1,0},{2,3},{3,2},{4,5},{5,4},{6,7},{7,6},{8,9},{9,8},{10,11... | collective-permute-start | bytes 196616 | tf_op jit(solution)/shard_map/ppermute | solution.py:46
  6.0 16.0 %collective-permute-start.1 = (bf16[6,128,128]{2,1,0:T(8,128)(2,1)S(1)}, bf16[6,128,128]{2,1,0:T(8,128)(2,1)S(1)}, u32[]{:S(2)}, u32[]{:S(2)}) collective-permute-start(bf16[6,128,128]{2,1,0:T(8,128)(2,1)S(1)} %get-tuple-element.34), channel_id=1, source_target_pairs={{0,4},{4,0},{8,12},{12,8},{16,20},{20,16},{24,28},{28,24},{1,5},{5... | collective-permute-start | bytes 589832 | tf_op jit(solution)/shard_map/ppermute | solution.py:36
  10.0 2.1 %copy-start.1 = (f32[5,8,512]{2,1,0:T(8,128)S(1)}, f32[5,8,512]{2,1,0:T(8,128)}, u32[]{:S(2)}) copy-start(f32[5,8,512]{2,1,0:T(8,128)} %args_2_.8) | copy-start | bytes 245764
  10.1 8.7 %collective-permute-start.6 = (bf16[2,128,128]{2,1,0:T(8,128)(2,1)S(1)}, bf16[2,128,128]{2,1,0:T(8,128)(2,1)S(1)}, u32[]{:S(2)}, u32[]{:S(2)}) collective-permute-start(bf16[2,128,128]{2,1,0:T(8,128)(2,1)S(1)} %get-tuple-element.38.args_5_), channel_id=1, source_target_pairs={{0,1},{1,0},{2,3},{3,2},{4,5},{5,4},{6,7},{7,6},{8,12},{9,13},{10,... | collective-permute-start | bytes 196616 | tf_op jit(solution)/shard_map/ppermute | solution.py:46
  12.1 7.8 %collective-permute-start.7 = (bf16[2,128,128]{2,1,0:T(8,128)(2,1)S(1)}, bf16[2,128,128]{2,1,0:T(8,128)(2,1)S(1)}, u32[]{:S(2)}, u32[]{:S(2)}) collective-permute-start(bf16[2,128,128]{2,1,0:T(8,128)(2,1)S(1)} %get-tuple-element.38.args_5_), channel_id=1, source_target_pairs={{0,8},{4,12},{8,0},{12,4},{16,24},{20,28},{24,16},{28,20},{1,9},{5... | collective-permute-start | bytes 196616 | tf_op jit(solution)/shard_map/ppermute | solution.py:36
  12.1 4.1 %collective-permute-start.9 = (bf16[2,128,128]{2,1,0:T(8,128)(2,1)S(1)}, bf16[2,128,128]{2,1,0:T(8,128)(2,1)S(1)}, u32[]{:S(2)}, u32[]{:S(2)}) collective-permute-start(bf16[2,128,128]{2,1,0:T(8,128)(2,1)S(1)} %sums.1), channel_id=1, source_target_pairs={{0,16},{4,20},{8,24},{12,28},{16,0},{20,4},{24,8},{28,12},{1,17},{... | collective-permute-start | bytes 196616 | tf_op jit(solution)/shard_map/ppermute | solution.py:36
  12.2 9.7 %collective-permute-start.8 = (bf16[2,128,128]{2,1,0:T(8,128)(2,1)S(1)}, bf16[2,128,128]{2,1,0:T(8,128)(2,1)S(1)}, u32[]{:S(2)}, u32[]{:S(2)}) collective-permute-start(bf16[2,128,128]{2,1,0:T(8,128)(2,1)S(1)} %get-tuple-element.38.args_5_), channel_id=1, source_target_pairs={{0,12},{4,8},{8,4},{12,0},{16,28},{20,24},{24,20},{28,16},{1,13},{... | collective-permute-start | bytes 196616 | tf_op jit(solution)/shard_map/ppermute | solution.py:36
  16.2 6.1 %collective-permute-start.10 = (bf16[2,128,128]{2,1,0:T(8,128)(2,1)S(1)}, bf16[2,128,128]{2,1,0:T(8,128)(2,1)S(1)}, u32[]{:S(2)}, u32[]{:S(2)}) collective-permute-start(bf16[2,128,128]{2,1,0:T(8,128)(2,1)S(1)} %collective-permute-done.9.args_9_), channel_id=1, source_target_pairs={{0,1},{1,0},{2,3},{3,2},{4,5},{5,4},{6,7},{7,6},{8,9},{9,8},{10,11... | collective-permute-start | bytes 196616 | tf_op jit(solution)/shard_map/ppermute | solution.py:46
  18.8 3.6 %collective-permute-start.11 = (bf16[2,128,128]{2,1,0:T(8,128)(2,1)S(1)}, bf16[2,128,128]{2,1,0:T(8,128)(2,1)S(1)}, u32[]{:S(2)}, u32[]{:S(2)}) collective-permute-start(bf16[2,128,128]{2,1,0:T(8,128)(2,1)S(1)} %collective-permute-done.9.args_9_), channel_id=1, source_target_pairs={{0,1},{1,0},{2,3},{3,2},{4,5},{5,4},{6,7},{7,6},{8,9},{9,8},{10,11... | collective-permute-start | bytes 196616 | tf_op jit(solution)/shard_map/ppermute | solution.py:46
  19.9 4.0 %collective-permute-start.12 = (bf16[2,128,128]{2,1,0:T(8,128)(2,1)S(1)}, bf16[2,128,128]{2,1,0:T(8,128)(2,1)S(1)}, u32[]{:S(2)}, u32[]{:S(2)}) collective-permute-start(bf16[2,128,128]{2,1,0:T(8,128)(2,1)S(1)} %collective-permute-done.9.args_9_), channel_id=1, source_target_pairs={{0,1},{1,0},{2,3},{3,2},{4,5},{5,4},{6,7},{7,6},{8,9},{9,8},{10,11... | collective-permute-start | bytes 196616 | tf_op jit(solution)/shard_map/ppermute | solution.py:46
  24.1 3.6 %collective-permute-start.13 = (f32[1,512]{1,0:T(1,128)S(1)}, f32[1,512]{1,0:T(1,128)S(1)}, u32[]{:S(2)}, u32[]{:S(2)}) collective-permute-start(f32[1,512]{1,0:T(1,128)S(1)} %get-tuple-element.59.refs_4_), channel_id=1, source_target_pairs={{0,1},{1,0},{2,3},{3,2},{4,5},{5,4},{6,7},{7,6},{8,9},{9,8},{10,11... | collective-permute-start | bytes 6152 | tf_op jit(solution)/shard_map/ppermute | solution.py:36
  25.9 2.4 %collective-permute-start.14 = (f32[1,512]{1,0:T(1,128)S(1)}, f32[1,512]{1,0:T(1,128)S(1)}, u32[]{:S(2)}, u32[]{:S(2)}) collective-permute-start(f32[1,512]{1,0:T(1,128)S(1)} %get-tuple-element.59.refs_4_), channel_id=1, source_target_pairs={{0,2},{1,3},{2,0},{3,1},{4,6},{5,7},{6,4},{7,5},{8,10},{9,11},{10,... | collective-permute-start | bytes 6152 | tf_op jit(solution)/shard_map/ppermute | solution.py:36
  27.1 3.0 %collective-permute-start.15 = (f32[1,512]{1,0:T(1,128)S(1)}, f32[1,512]{1,0:T(1,128)S(1)}, u32[]{:S(2)}, u32[]{:S(2)}) collective-permute-start(f32[1,512]{1,0:T(1,128)S(1)} %get-tuple-element.59.refs_4_), channel_id=1, source_target_pairs={{0,3},{1,2},{2,1},{3,0},{4,7},{5,6},{6,5},{7,4},{8,11},{9,10},{10,... | collective-permute-start | bytes 6152 | tf_op jit(solution)/shard_map/ppermute | solution.py:36

commit v13 on v12

--- a/solution.py
+++ b/solution.py
@@ -177,7 +177,7 @@
 
 
 def readout_kernel(group, first, work, lacks, *args):
-    low = any(bit < 2 for _, _, reads in work for bit, _, _ in reads)
+    low = any(bit == 0 for _, _, reads in work for bit, _, _ in reads)
     fewer = tuple((r, complete, tuple(read for read in reads if low and read[0] >= 2)) for r, complete, reads in work)
     place = args[3][0]
     for present, some in ((True, work), (False, fewer)):
@@ -295,7 +295,7 @@
         n, carry = len(work), squares is not None
 
         def lacks(place):
-            return place & (QUAD - 1) == 0 if label == "far" else place < QUAD
+            return {"far": place & (QUAD - 1) == 0, "mid": place < 2, "last": place < QUAD}[label]
 
         kernel = functools.partial(readout_kernel, group, 1 + local_bits, work, lacks, len(states), carry, finish)
         ins = [place, queries, level_weights, *states, *(totals[r] for r, _, _ in work)] + [squares] * carry
@@ -311,10 +311,12 @@
         totals.update({r: out for (r, _, _), out in zip(work, outs)})
         return outs[n]
 
-    below = {0: ((0, 0, 0), (1, 2, 0))} | {r: ((0, 1, (r - 1) * group), (1, 2 + r, 0)) for r in (1, 2, 3)}
-    work = tuple((r, r == 0, below[r] + (top_reads(6) if r == 0 else ())) for r in (3, 1, 2, 0))
-    squares = readout("far", work, (taken1, near, *(middle[r] for r in range(QUAD)), top), None)
-    squares = readout("mid", ((3, True, top_reads(0)), (1, True, top_reads(1))), (tops[3], tops[1]), squares)
+    below = {0: ((0, 0, 0), (1, 2, 0)), 1: ((0, 1, 0),)}
+    below |= {r: ((0, 1, (r - 1) * group), (1, 1 + r, 0)) for r in (2, 3)}
+    work = tuple((r, r == 0, below[r] + (top_reads(5) if r == 0 else ())) for r in (3, 1, 2, 0))
+    squares = readout("far", work, (taken1, near, middle[0], middle[2], middle[3], top), None)
+    work = (3, True, top_reads(0)), (1, True, ((1, 2, 0), *top_reads(1)))
+    squares = readout("mid", work, (tops[3], tops[1], middle[1]), squares)
     squares = readout("last", ((2, True, top_reads(0)),), (tops[2],), squares, finish=True)
 
     shares = [squares] + [exchanged(squares, "head", mask) for mask in range(1, lax.axis_size("head"))]

time: 31.4 us -> 32.8 us (1.045)
  starting transfers between devices: 15.5 us -> 18.5 us
  waiting for transfers between devices: 9.03 us -> 7.32 us
    ppermute x8, starting transfers between devices: 7.54 us -> 11.4 us  [exchanged(): return lax.ppermute(block, axis, [(i, i ^ mask) for i in range(count)])]
    ppermute x8, waiting for transfers between devices: 3.87 us -> 2.77 us  [exchanged_in(): return lax.ppermute(block, ('seq', 'head'), route)]
    ppermute x8, starting transfers between devices: 7.99 us -> 7.12 us  [exchanged_in(): return lax.ppermute(block, ('seq', 'head'), route)]
    ppermute x8, waiting for transfers between devices: 5.15 us -> 4.56 us  [exchanged(): return lax.ppermute(block, axis, [(i, i ^ mask) for i in range(count)])]
  transfers between devices with their start and end apart: 16 -> 16, of which waited for: 6 -> 5; matrix products, arithmetic and copies ran while one was open for 0% -> 0% of each run, Pallas kernels for 9% -> 9%
where the time goes in v13:
time: 32.8 us; the launch traced here: 32.6 us
  starting transfers between devices  18.5 us (56%)
  waiting for transfers between devices  7.32 us (22%)
  Pallas kernels  6.64 us (20%)
    ppermute x8, starting transfers between devices, exchanged(): return lax.ppermute(block, axis, [(i, i ^ mask) for i in range(count)])  11.4 us
    ppermute x8, starting transfers between devices, exchanged_in(): return lax.ppermute(block, ('seq', 'head'), route)  7.12 us
    ppermute x8, waiting for transfers between devices, exchanged(): return lax.ppermute(block, axis, [(i, i ^ mask) for i in range(count)])  4.56 us
    ppermute x8, waiting for transfers between devices, exchanged_in(): return lax.ppermute(block, ('seq', 'head'), route)  2.77 us
    pallas_call x1, Pallas kernels, local(): pl.pallas_call(functools.partial(states_kernel, group), out_shape=(sds((Q...  2.3 us
    pallas_call x1, Pallas kernels, local(): pl.pallas_call(functools.partial(intra_late_kernel, group), out_shape=(sd...  2.09 us
    pallas_call x1, Pallas kernels, local(): pl.pallas_call(functools.partial(norm_kernel, group, full_width), out_sha...  1.14 us
    pallas_call x3, Pallas kernels, readout(): pl.pallas_call(kernel, out_shape=tuple(shapes), in_specs=[SMEM] + [VMEM]...  1.02 us
  transfers between devices with their start and end apart: 16, of which 5 were waited for; matrix products, arithmetic and copies ran while one was open for 0% of the time, Pallas kernels for 9%

profile of v13, /device:TPU:17, one launch (start us, length us, event | category | flops | bytes accessed | tf_op | source)
XLA Modules:
  0.0 32.6 jit_solution(1820316177124388805)
XLA Ops:
  0.0 0.0 copy-start
  0.0 2.3 %states.1 = (bf16[4,512,256]{2,1,0:T(8,128)(2,1)S(1)}, bf16[4,512,256]{2,1,0:T(8,128)(2,1)S(1)}, f32[2,128,128]{2,1,0:T(8,128)S(1)}, bf16[2,128,128]{2,1,0:T(8,1...) custom-call(s32[1]{0:T(128)} %bitcast.place_ref.args_0_, ...), custom_call_target="tpu_custom_call" | custom-call | flops 134217728 | bytes 2097152 | tf_op jit(solution)/shard_map/states/pallas_call | solution.py:221
  2.3 1.3 %collective-permute-start = (bf16[2,128,128]{2,1,0:T(8,128)(2,1)S(1)}, bf16[2,128,128]{2,1,0:T(8,128)(2,1)S(1)}, u32[]{:S(2)}, u32[]{:S(2)}) collective-permute-start(bf16[2,128,128]{2,1,0:T(8,128)(2,1)S(1)} %get-tuple-element.33), channel_id=1, source_target_pairs={{0,4},{4,0},{8,12},{12,8},{16,20},{20,16},{24,28},{28,24},{1,5},{5... | collective-permute-start | bytes 196616 | tf_op jit(solution)/shard_map/ppermute | solution.py:36
  3.6 0.0 copy-start.2
  3.6 1.0 %collective-permute-start.2 = (bf16[2,128,128]{2,1,0:T(8,128)(2,1)S(1)}, bf16[2,128,128]{2,1,0:T(8,128)(2,1)S(1)}, u32[]{:S(2)}, u32[]{:S(2)}) collective-permute-start(bf16[2,128,128]{2,1,0:T(8,128)(2,1)S(1)} %get-tuple-element.36), channel_id=1, source_target_pairs={{0,8},{1,9},{2,10},{3,11},{4,12},{5,13},{6,14},{7,15},{8,0},{9,1},... | collective-permute-start | bytes 196616 | tf_op jit(solution)/shard_map/ppermute | solution.py:46
  4.6 0.0 collective-permute-start.3
  4.6 1.3 %collective-permute-start.4 = (bf16[2,128,128]{2,1,0:T(8,128)(2,1)S(1)}, bf16[2,128,128]{2,1,0:T(8,128)(2,1)S(1)}, u32[]{:S(2)}, u32[]{:S(2)}) collective-permute-start(bf16[2,128,128]{2,1,0:T(8,128)(2,1)S(1)} %get-tuple-element.36), channel_id=1, source_target_pairs={{0,1},{1,0},{2,3},{3,2},{4,5},{5,4},{6,7},{7,6},{8,9},{9,8},{10,11... | collective-permute-start | bytes 196616 | tf_op jit(solution)/shard_map/ppermute | solution.py:46
  5.9 0.1 collective-permute-start.5
  6.0 0.0 collective-permute-done.one_ref.args_3_
  6.0 1.2 %collective-permute-start.1 = (bf16[6,128,128]{2,1,0:T(8,128)(2,1)S(1)}, bf16[6,128,128]{2,1,0:T(8,128)(2,1)S(1)}, u32[]{:S(2)}, u32[]{:S(2)}) collective-permute-start(bf16[6,128,128]{2,1,0:T(8,128)(2,1)S(1)} %get-tuple-element.34), channel_id=1, source_target_pairs={{0,4},{4,0},{8,12},{12,8},{16,20},{20,16},{24,28},{28,24},{1,5},{5... | collective-permute-start | bytes 589832 | tf_op jit(solution)/shard_map/ppermute | solution.py:36
  7.2 0.0 collective-permute-done.2.early2_ref.two_ref
  7.2 0.0 collective-permute-done.3.early3_ref.three_ref
  7.2 0.5 %collective-permute-done.4.late2_ref = bf16[2,128,128]{2,1,0:T(8,128)(2,1)S(1)} collective-permute-done((bf16[2,128,128]{2,1,0:T(8,128)(2,1)S(1)}, bf16[2,128,128]{2,1,0:T(8,128)(2,1)S(1)}, u32[]{:S(2)}, u32[]{:S(2)}) %collective-permute-start.4) | collective-permute-done | bytes 65568 | tf_op jit(solution)/shard_map/ppermute | solution.py:46
  7.7 2.3 %collective-permute-done.5.late3_ref = bf16[2,128,128]{2,1,0:T(8,128)(2,1)S(1)} collective-permute-done((bf16[2,128,128]{2,1,0:T(8,128)(2,1)S(1)}, bf16[2,128,128]{2,1,0:T(8,128)(2,1)S(1)}, u32[]{:S(2)}, u32[]{:S(2)}) %collective-permute-start.5) | collective-permute-done | bytes 65568 | tf_op jit(solution)/shard_map/ppermute | solution.py:46
  10.0 0.0 copy-done.2
  10.0 0.0 copy-start.1
  10.1 0.8 %collective-permute-start.6 = (bf16[2,128,128]{2,1,0:T(8,128)(2,1)S(1)}, bf16[2,128,128]{2,1,0:T(8,128)(2,1)S(1)}, u32[]{:S(2)}, u32[]{:S(2)}) collective-permute-start(bf16[2,128,128]{2,1,0:T(8,128)(2,1)S(1)} %get-tuple-element.38.args_5_), channel_id=1, source_target_pairs={{0,8},{4,12},{8,0},{12,4},{16,24},{20,28},{24,16},{28,20},{1,9},{5... | collective-permute-start | bytes 196616 | tf_op jit(solution)/shard_map/ppermute | solution.py:36
  10.8 1.1 %collective-permute-start.7 = (bf16[2,128,128]{2,1,0:T(8,128)(2,1)S(1)}, bf16[2,128,128]{2,1,0:T(8,128)(2,1)S(1)}, u32[]{:S(2)}, u32[]{:S(2)}) collective-permute-start(bf16[2,128,128]{2,1,0:T(8,128)(2,1)S(1)} %get-tuple-element.38.args_5_), channel_id=1, source_target_pairs={{0,12},{4,8},{8,4},{12,0},{16,28},{20,24},{24,20},{28,16},{1,13},{... | collective-permute-start | bytes 196616 | tf_op jit(solution)/shard_map/ppermute | solution.py:36
  12.0 0.1 collective-permute-start.8
  12.1 0.0 copy-done
  12.1 0.0 copy-done.1
  12.1 2.0 %collective-permute-start.11 = (bf16[2,128,128]{2,1,0:T(8,128)(2,1)S(1)}, bf16[2,128,128]{2,1,0:T(8,128)(2,1)S(1)}, u32[]{:S(2)}, u32[]{:S(2)}) collective-permute-start(bf16[2,128,128]{2,1,0:T(8,128)(2,1)S(1)} %get-tuple-element.38.args_5_), channel_id=1, source_target_pairs={{0,1},{1,0},{2,3},{3,2},{4,5},{5,4},{6,7},{7,6},{8,12},{9,13},{10,... | collective-permute-start | bytes 196616 | tf_op jit(solution)/shard_map/ppermute | solution.py:46
  14.1 2.0 %collective-permute-done.8.args_8_ = bf16[2,128,128]{2,1,0:T(8,128)(2,1)S(1)} collective-permute-done((bf16[2,128,128]{2,1,0:T(8,128)(2,1)S(1)}, bf16[2,128,128]{2,1,0:T(8,128)(2,1)S(1)}, u32[]{:S(2)}, u32[]{:S(2)}) %collective-permute-start.8) | collective-permute-done | bytes 65568 | tf_op jit(solution)/shard_map/ppermute | solution.py:36
  16.2 1.6 %collective-permute-start.9 = (bf16[2,128,128]{2,1,0:T(8,128)(2,1)S(1)}, bf16[2,128,128]{2,1,0:T(8,128)(2,1)S(1)}, u32[]{:S(2)}, u32[]{:S(2)}) collective-permute-start(bf16[2,128,128]{2,1,0:T(8,128)(2,1)S(1)} %collective-permute-done.8.args_8_), channel_id=1, source_target_pairs={{0,1},{1,0},{2,3},{3,2},{4,5},{5,4},{6,7},{7,6},{8,9},{9,8},{10,11... | collective-permute-start | bytes 196616 | tf_op jit(solution)/shard_map/ppermute | solution.py:46
  17.8 0.0 collective-permute-done.6.args_6_
  17.8 0.8 %collective-permute-start.10 = (bf16[2,128,128]{2,1,0:T(8,128)(2,1)S(1)}, bf16[2,128,128]{2,1,0:T(8,128)(2,1)S(1)}, u32[]{:S(2)}, u32[]{:S(2)}) collective-permute-start(bf16[2,128,128]{2,1,0:T(8,128)(2,1)S(1)} %collective-permute-done.8.args_8_), channel_id=1, source_target_pairs={{0,1},{1,0},{2,3},{3,2},{4,5},{5,4},{6,7},{7,6},{8,9},{9,8},{10,11... | collective-permute-start | bytes 196616 | tf_op jit(solution)/shard_map/ppermute | solution.py:46
  18.6 0.0 collective-permute-done.7.args_7_
  18.6 0.3 collective-permute-start.12
  18.9 2.1 %intra_late.1 = (f32[1024,128]{1,0:T(8,128)S(1)}, f32[256,512]{1,0:T(8,128)S(1)}, f32[256,512]{1,0:T(8,128)S(1)}, f32[256,512]{1,0:T(8,128)S(1)}, f32[256,512]{1,0:T(8,128)S(1)}) custom-call(s32[1]{0:T(128)} %bitcast.place_ref.args_0_, bf16[512,1024]{1,0:T(8,128)(2,1)S(1)} %copy-done, f32[5,8,512]{2,1,0:T(8,128)S(1)} %copy-done.1, ...), custom_call_target="tpu_custom_call" | custom-call | flops 805306368 | bytes 2097152 | tf_op jit(solution)/shard_map/intra_late/pallas_call | solution.py:277
  21.0 0.0 collective-permute-done.1.args_4_
  21.0 0.3 %shard_map.55 = (f32[256,512]{1,0:T(8,128)S(1)}, f32[256,512]{1,0:T(8,128)S(1)}, f32[256,512]{1,0:T(8,128)S(1)}, f32[256,512]{1,0:T(8,128)S(1)}, f32[8,512]{1,0:T(8,128)S(1)}) custom-call(s32[1]{0:T(128)} %bitcast.place_ref.args_0_, bf16[512,1024]{1,0:T(8,128)(2,1)S(1)} %copy-done, f32[5,8,512]{2,1,0:T(8,128)S(1)} %copy-done.1, ...), custom_call_target="tpu_custom_call" | custom-call | flops 268435456 | bytes 4194304 | tf_op jit(solution)/shard_map/pallas_call | solution.py:303
  21.4 0.0 collective-permute-done.11.args_5_
  21.4 0.0 collective-permute-done.9.args_3_
  21.4 0.0 collective-permute-done.10.args_4_
  21.4 0.4 %shard_map.56 = (f32[256,512]{1,0:T(8,128)S(1)}, f32[256,512]{1,0:T(8,128)S(1)}, f32[8,512]{1,0:T(8,128)S(1)}) custom-call(s32[1]{0:T(128)} %bitcast.place_ref.args_0_, bf16[512,1024]{1,0:T(8,128)(2,1)S(1)} %copy-done, f32[5,8,512]{2,1,0:T(8,128)S(1)} %copy-done.1, bf16[2,128,128]{2,1,0:T(8,128)(2,1)S(1)} %collective-permute-done.9.args_3_, ...), custom_call_target="tpu_custom_call" | custom-call | flops 134217728 | bytes 2097152 | tf_op jit(solution)/shard_map/pallas_call | solution.py:303
  21.8 0.0 collective-permute-done.12.args_3_
  21.8 0.3 shard_map.57
  22.1 5.2 %collective-permute-start.13 = (f32[1,512]{1,0:T(1,128)S(1)}, f32[1,512]{1,0:T(1,128)S(1)}, u32[]{:S(2)}, u32[]{:S(2)}) collective-permute-start(f32[1,512]{1,0:T(1,128)S(1)} %get-tuple-element.59.refs_4_), channel_id=1, source_target_pairs={{0,1},{1,0},{2,3},{3,2},{4,5},{5,4},{6,7},{7,6},{8,9},{9,8},{10,11... | collective-permute-start | bytes 6152 | tf_op jit(solution)/shard_map/ppermute | solution.py:36
  27.3 1.2 %collective-permute-start.14 = (f32[1,512]{1,0:T(1,128)S(1)}, f32[1,512]{1,0:T(1,128)S(1)}, u32[]{:S(2)}, u32[]{:S(2)}) collective-permute-start(f32[1,512]{1,0:T(1,128)S(1)} %get-tuple-element.59.refs_4_), channel_id=1, source_target_pairs={{0,2},{1,3},{2,0},{3,1},{4,6},{5,7},{6,4},{7,5},{8,10},{9,11},{10,... | collective-permute-start | bytes 6152 | tf_op jit(solution)/shard_map/ppermute | solution.py:36
  28.5 0.5 %collective-permute-start.15 = (f32[1,512]{1,0:T(1,128)S(1)}, f32[1,512]{1,0:T(1,128)S(1)}, u32[]{:S(2)}, u32[]{:S(2)}) collective-permute-start(f32[1,512]{1,0:T(1,128)S(1)} %get-tuple-element.59.refs_4_), channel_id=1, source_target_pairs={{0,3},{1,2},{2,1},{3,0},{4,7},{5,6},{6,5},{7,4},{8,11},{9,10},{10,... | collective-permute-start | bytes 6152 | tf_op jit(solution)/shard_map/ppermute | solution.py:36
  29.0 0.0 collective-permute-done.13.refs_5_
  29.0 0.7 %collective-permute-done.14.refs_6_ = f32[1,512]{1,0:T(1,128)S(1)} collective-permute-done((f32[1,512]{1,0:T(1,128)S(1)}, f32[1,512]{1,0:T(1,128)S(1)}, u32[]{:S(2)}, u32[]{:S(2)}) %collective-permute-start.14) | collective-permute-done | bytes 2080 | tf_op jit(solution)/shard_map/ppermute | solution.py:36
  29.7 1.8 %collective-permute-done.15.refs_7_ = f32[1,512]{1,0:T(1,128)S(1)} collective-permute-done((f32[1,512]{1,0:T(1,128)S(1)}, f32[1,512]{1,0:T(1,128)S(1)}, u32[]{:S(2)}, u32[]{:S(2)}) %collective-permute-start.15) | collective-permute-done | bytes 2080 | tf_op jit(solution)/shard_map/ppermute | solution.py:36
  31.5 1.1 %norm.1 = bf16[512,1024]{1,0:T(8,128)(2,1)} custom-call(s32[1]{0:T(128)} %bitcast.place_ref.args_0_, f32[256,512]{1,0:T(8,128)S(1)} %get-tuple-element.50.refs_0_, f32[256,512]{1,0:T(8,128)S(1)} %get-tuple-element.54.refs_1_, f32[256,512]{1,0:T(8,128)S(1)} %get-tuple-element.57.refs_2_, f32[256,512]{1,0:T(8,128)S(1)} %get-tuple-element.58.refs_3_, ...), custom_call_target="tpu_custom_call" | custom-call | flops 1048576 | bytes 1048576 | tf_op jit(solution)/shard_map/norm/pallas_call | solution.py:324
  (3 shorter events, 0.1 us)
Async XLA Ops:
  0.0 12.1 %copy-start = (bf16[512,1024]{1,0:T(8,128)(2,1)S(1)}, bf16[512,1024]{1,0:T(8,128)(2,1)}, u32[]{:S(2)}) copy-start(bf16[512,1024]{1,0:T(8,128)(2,1)} %args_1_.8) | copy-start | bytes 3145732
  2.3 3.7 %collective-permute-start = (bf16[2,128,128]{2,1,0:T(8,128)(2,1)S(1)}, bf16[2,128,128]{2,1,0:T(8,128)(2,1)S(1)}, u32[]{:S(2)}, u32[]{:S(2)}) collective-permute-start(bf16[2,128,128]{2,1,0:T(8,128)(2,1)S(1)} %get-tuple-element.33), channel_id=1, source_target_pairs={{0,4},{4,0},{8,12},{12,8},{16,20},{20,16},{24,28},{28,24},{1,5},{5... | collective-permute-start | bytes 196616 | tf_op jit(solution)/shard_map/ppermute | solution.py:36
  3.6 6.4 %copy-start.2 = (f32[1024]{0:T(1024)S(1)}, f32[1024]{0:T(1024)}, u32[]{:S(2)}) copy-start(f32[1024]{0:T(1024)} %param.9) | copy-start | bytes 12292
  3.6 3.6 %collective-permute-start.2 = (bf16[2,128,128]{2,1,0:T(8,128)(2,1)S(1)}, bf16[2,128,128]{2,1,0:T(8,128)(2,1)S(1)}, u32[]{:S(2)}, u32[]{:S(2)}) collective-permute-start(bf16[2,128,128]{2,1,0:T(8,128)(2,1)S(1)} %get-tuple-element.36), channel_id=1, source_target_pairs={{0,8},{1,9},{2,10},{3,11},{4,12},{5,13},{6,14},{7,15},{8,0},{9,1},... | collective-permute-start | bytes 196616 | tf_op jit(solution)/shard_map/ppermute | solution.py:46
  4.6 2.7 %collective-permute-start.3 = (bf16[2,128,128]{2,1,0:T(8,128)(2,1)S(1)}, bf16[2,128,128]{2,1,0:T(8,128)(2,1)S(1)}, u32[]{:S(2)}, u32[]{:S(2)}) collective-permute-start(bf16[2,128,128]{2,1,0:T(8,128)(2,1)S(1)} %get-tuple-element.37), channel_id=1, source_target_pairs={{0,12},{1,13},{2,14},{3,15},{4,8},{5,9},{6,10},{7,11},{8,4},{9,5},... | collective-permute-start | bytes 196616 | tf_op jit(solution)/shard_map/ppermute | solution.py:46
  4.6 3.1 %collective-permute-start.4 = (bf16[2,128,128]{2,1,0:T(8,128)(2,1)S(1)}, bf16[2,128,128]{2,1,0:T(8,128)(2,1)S(1)}, u32[]{:S(2)}, u32[]{:S(2)}) collective-permute-start(bf16[2,128,128]{2,1,0:T(8,128)(2,1)S(1)} %get-tuple-element.36), channel_id=1, source_target_pairs={{0,1},{1,0},{2,3},{3,2},{4,5},{5,4},{6,7},{7,6},{8,9},{9,8},{10,11... | collective-permute-start | bytes 196616 | tf_op jit(solution)/shard_map/ppermute | solution.py:46
  5.9 4.1 %collective-permute-start.5 = (bf16[2,128,128]{2,1,0:T(8,128)(2,1)S(1)}, bf16[2,128,128]{2,1,0:T(8,128)(2,1)S(1)}, u32[]{:S(2)}, u32[]{:S(2)}) collective-permute-start(bf16[2,128,128]{2,1,0:T(8,128)(2,1)S(1)} %get-tuple-element.37), channel_id=1, source_target_pairs={{0,1},{1,0},{2,3},{3,2},{4,5},{5,4},{6,7},{7,6},{8,9},{9,8},{10,11... | collective-permute-start | bytes 196616 | tf_op jit(solution)/shard_map/ppermute | solution.py:46
  6.0 15.0 %collective-permute-start.1 = (bf16[6,128,128]{2,1,0:T(8,128)(2,1)S(1)}, bf16[6,128,128]{2,1,0:T(8,128)(2,1)S(1)}, u32[]{:S(2)}, u32[]{:S(2)}) collective-permute-start(bf16[6,128,128]{2,1,0:T(8,128)(2,1)S(1)} %get-tuple-element.34), channel_id=1, source_target_pairs={{0,4},{4,0},{8,12},{12,8},{16,20},{20,16},{24,28},{28,24},{1,5},{5... | collective-permute-start | bytes 589832 | tf_op jit(solution)/shard_map/ppermute | solution.py:36
  10.0 2.0 %copy-start.1 = (f32[5,8,512]{2,1,0:T(8,128)S(1)}, f32[5,8,512]{2,1,0:T(8,128)}, u32[]{:S(2)}) copy-start(f32[5,8,512]{2,1,0:T(8,128)} %args_2_.8) | copy-start | bytes 245764
  10.1 7.8 %collective-permute-start.6 = (bf16[2,128,128]{2,1,0:T(8,128)(2,1)S(1)}, bf16[2,128,128]{2,1,0:T(8,128)(2,1)S(1)}, u32[]{:S(2)}, u32[]{:S(2)}) collective-permute-start(bf16[2,128,128]{2,1,0:T(8,128)(2,1)S(1)} %get-tuple-element.38.args_5_), channel_id=1, source_target_pairs={{0,8},{4,12},{8,0},{12,4},{16,24},{20,28},{24,16},{28,20},{1,9},{5... | collective-permute-start | bytes 196616 | tf_op jit(solution)/shard_map/ppermute | solution.py:36
  10.8 7.8 %collective-permute-start.7 = (bf16[2,128,128]{2,1,0:T(8,128)(2,1)S(1)}, bf16[2,128,128]{2,1,0:T(8,128)(2,1)S(1)}, u32[]{:S(2)}, u32[]{:S(2)}) collective-permute-start(bf16[2,128,128]{2,1,0:T(8,128)(2,1)S(1)} %get-tuple-element.38.args_5_), channel_id=1, source_target_pairs={{0,12},{4,8},{8,4},{12,0},{16,28},{20,24},{24,20},{28,16},{1,13},{... | collective-permute-start | bytes 196616 | tf_op jit(solution)/shard_map/ppermute | solution.py:36
  12.0 4.2 %collective-permute-start.8 = (bf16[2,128,128]{2,1,0:T(8,128)(2,1)S(1)}, bf16[2,128,128]{2,1,0:T(8,128)(2,1)S(1)}, u32[]{:S(2)}, u32[]{:S(2)}) collective-permute-start(bf16[2,128,128]{2,1,0:T(8,128)(2,1)S(1)} %sums.1), channel_id=1, source_target_pairs={{0,16},{4,20},{8,24},{12,28},{16,0},{20,4},{24,8},{28,12},{1,17},{... | collective-permute-start | bytes 196616 | tf_op jit(solution)/shard_map/ppermute | solution.py:36
  12.1 9.3 %collective-permute-start.11 = (bf16[2,128,128]{2,1,0:T(8,128)(2,1)S(1)}, bf16[2,128,128]{2,1,0:T(8,128)(2,1)S(1)}, u32[]{:S(2)}, u32[]{:S(2)}) collective-permute-start(bf16[2,128,128]{2,1,0:T(8,128)(2,1)S(1)} %get-tuple-element.38.args_5_), channel_id=1, source_target_pairs={{0,1},{1,0},{2,3},{3,2},{4,5},{5,4},{6,7},{7,6},{8,12},{9,13},{10,... | collective-permute-start | bytes 196616 | tf_op jit(solution)/shard_map/ppermute | solution.py:46
  16.2 5.2 %collective-permute-start.9 = (bf16[2,128,128]{2,1,0:T(8,128)(2,1)S(1)}, bf16[2,128,128]{2,1,0:T(8,128)(2,1)S(1)}, u32[]{:S(2)}, u32[]{:S(2)}) collective-permute-start(bf16[2,128,128]{2,1,0:T(8,128)(2,1)S(1)} %collective-permute-done.8.args_8_), channel_id=1, source_target_pairs={{0,1},{1,0},{2,3},{3,2},{4,5},{5,4},{6,7},{7,6},{8,9},{9,8},{10,11... | collective-permute-start | bytes 196616 | tf_op jit(solution)/shard_map/ppermute | solution.py:46
  17.8 3.6 %collective-permute-start.10 = (bf16[2,128,128]{2,1,0:T(8,128)(2,1)S(1)}, bf16[2,128,128]{2,1,0:T(8,128)(2,1)S(1)}, u32[]{:S(2)}, u32[]{:S(2)}) collective-permute-start(bf16[2,128,128]{2,1,0:T(8,128)(2,1)S(1)} %collective-permute-done.8.args_8_), channel_id=1, source_target_pairs={{0,1},{1,0},{2,3},{3,2},{4,5},{5,4},{6,7},{7,6},{8,9},{9,8},{10,11... | collective-permute-start | bytes 196616 | tf_op jit(solution)/shard_map/ppermute | solution.py:46
  18.6 3.2 %collective-permute-start.12 = (bf16[2,128,128]{2,1,0:T(8,128)(2,1)S(1)}, bf16[2,128,128]{2,1,0:T(8,128)(2,1)S(1)}, u32[]{:S(2)}, u32[]{:S(2)}) collective-permute-start(bf16[2,128,128]{2,1,0:T(8,128)(2,1)S(1)} %collective-permute-done.8.args_8_), channel_id=1, source_target_pairs={{0,1},{1,0},{2,3},{3,2},{4,5},{5,4},{6,7},{7,6},{8,9},{9,8},{10,11... | collective-permute-start | bytes 196616 | tf_op jit(solution)/shard_map/ppermute | solution.py:46
  22.1 6.9 %collective-permute-start.13 = (f32[1,512]{1,0:T(1,128)S(1)}, f32[1,512]{1,0:T(1,128)S(1)}, u32[]{:S(2)}, u32[]{:S(2)}) collective-permute-start(f32[1,512]{1,0:T(1,128)S(1)} %get-tuple-element.59.refs_4_), channel_id=1, source_target_pairs={{0,1},{1,0},{2,3},{3,2},{4,5},{5,4},{6,7},{7,6},{8,9},{9,8},{10,11... | collective-permute-start | bytes 6152 | tf_op jit(solution)/shard_map/ppermute | solution.py:36
  27.3 2.4 %collective-permute-start.14 = (f32[1,512]{1,0:T(1,128)S(1)}, f32[1,512]{1,0:T(1,128)S(1)}, u32[]{:S(2)}, u32[]{:S(2)}) collective-permute-start(f32[1,512]{1,0:T(1,128)S(1)} %get-tuple-element.59.refs_4_), channel_id=1, source_target_pairs={{0,2},{1,3},{2,0},{3,1},{4,6},{5,7},{6,4},{7,5},{8,10},{9,11},{10,... | collective-permute-start | bytes 6152 | tf_op jit(solution)/shard_map/ppermute | solution.py:36
  28.5 3.0 %collective-permute-start.15 = (f32[1,512]{1,0:T(1,128)S(1)}, f32[1,512]{1,0:T(1,128)S(1)}, u32[]{:S(2)}, u32[]{:S(2)}) collective-permute-start(f32[1,512]{1,0:T(1,128)S(1)} %get-tuple-element.59.refs_4_), channel_id=1, source_target_pairs={{0,3},{1,2},{2,1},{3,0},{4,7},{5,6},{6,5},{7,4},{8,11},{9,10},{10,... | collective-permute-start | bytes 6152 | tf_op jit(solution)/shard_map/ppermute | solution.py:36

commit v14 on v13

--- a/solution.py
+++ b/solution.py
@@ -93,8 +93,7 @@
     sent_ref[...] = total.astype(BF16)
 
 
-def left_kernel(seq, place_ref, own_ref, one_ref, early2_ref, early3_ref, late2_ref, late3_ref, gain_ref, left_ref, kept_ref):
-    kept_ref[...] = gain_ref[...]
+def left_kernel(seq, place_ref, own_ref, one_ref, early2_ref, early3_ref, late2_ref, late3_ref, left_ref):
     last_quad = place_ref[0] >= seq - QUAD
     two = jnp.where(last_quad, late2_ref[...], early2_ref[...])
     three = jnp.where(last_quad, late3_ref[...], early3_ref[...])
@@ -103,13 +102,13 @@
     left_ref[...] = jnp.where(place_ref[0] >> 1 & 1 == 1, other, pair).astype(BF16)
 
 
-def intra_of(group, place, q_ref, w_ref, k_all, v_all, out_refs):
+def intra_of(group, groups, place, q_ref, w_ref, k_all, v_all, out_refs):
     count = q_ref.shape[0] // STRETCH
     local_bits = count.bit_length() - 1
     causal = lax.broadcasted_iota(jnp.int32, (STRETCH, STRETCH), 0) <= lax.broadcasted_iota(
         jnp.int32, (STRETCH, STRETCH), 1
     )
-    for r, out_ref in enumerate(out_refs):
+    for r, out_ref in zip(groups, out_refs):
         for j in range(group):
             head = (place & (QUAD - 1) ^ r) * group + j
             cols = pl.ds(pl.multiple_of(head * HEAD_DIM, HEAD_DIM), HEAD_DIM)
@@ -129,26 +128,56 @@
                     states.append(tn(v, k))
 
 
-def intra_early_kernel(group, place_ref, *refs):
-    @pl.when(place_ref[0] < QUAD)
-    def _():
-        intra_of(group, place_ref[0], *refs[:4], refs[4:])
-
-
-def intra_late_kernel(group, place_ref, q_ref, w_ref, k_all, v_all, gain_ref, *refs):
+def lowest(place):
+    return place < QUAD
+
+
+def busy(place):
+    return (place >= QUAD) & (place >> 1 & 1 == 1)
+
+
+def intra_first_kernel(group, place_ref, *refs):
+    gain_ref, kept_ref, out_ref = refs[4:]
+    kept_ref[...] = gain_ref[...]
+
+    @pl.when(busy(place_ref[0]))
+    def _():
+        intra_of(group, (3,), place_ref[0], *refs[:4], (out_ref,))
+
+
+def intra_second_kernel(group, place_ref, *refs):
+    args, out_refs = refs[:4], refs[4:]
+
+    @pl.when(lowest(place_ref[0]))
+    def _():
+        intra_of(group, range(QUAD), place_ref[0], *args, out_refs)
+
+    @pl.when(busy(place_ref[0]))
+    def _():
+        intra_of(group, (1,), place_ref[0], *args, out_refs[1:2])
+
+
+def intra_last_kernel(group, place_ref, q_ref, w_ref, k_all, v_all, gain_ref, first_ref, *refs):
+    args = (q_ref, w_ref, k_all, v_all)
     done_refs, column_ref, out_refs = refs[:QUAD], refs[QUAD], refs[QUAD + 1 :]
     for head in range(QUAD * group):
         rows = jnp.broadcast_to(gain_ref[:, column(head)], (HEAD_DIM, HEAD_DIM))
         column_ref[column(head), :] = jnp.transpose(rows, (1, 0))
 
-    @pl.when(place_ref[0] < QUAD)
+    @pl.when(lowest(place_ref[0]))
     def _():
         for done_ref, out_ref in zip(done_refs, out_refs):
             out_ref[...] = done_ref[...]
 
-    @pl.when(place_ref[0] >= QUAD)
-    def _():
-        intra_of(group, place_ref[0], q_ref, w_ref, k_all, v_all, out_refs)
+    @pl.when(busy(place_ref[0]))
+    def _():
+        out_refs[3][...] = first_ref[...]
+        out_refs[1][...] = done_refs[1][...]
+        intra_of(group, (2, 0), place_ref[0], *args, (out_refs[2], out_refs[0]))
+
+    @pl.when(jnp.logical_not(lowest(place_ref[0]) | busy(place_ref[0])))
+    def _():
+        intra_of(group, range(QUAD), place_ref[0], *args, out_refs)
 
 
 def readout_of(group, first, work, n_states, carry, finish, place_ref, q_ref, w_ref, *refs):
@@ -238,15 +267,25 @@
 
     args = (place, queries, level_weights, k_all, v_all)
     work_cost = cost(6 * rows * STRETCH * width, 4 * rows * width)
+    gain, first = pl.pallas_call(
+        functools.partial(intra_first_kernel, group),
+        out_shape=(sds((1, width), F32), part_shape),
+        in_specs=[SMEM] + [VMEM] * 5,
+        out_specs=(VMEM,) * 2,
+        compiler_params=params(),
+        cost_estimate=work_cost,
+        name="intra_first",
+    )(*args, norm_gain.reshape(1, width))
     outs = pl.pallas_call(
-        functools.partial(intra_early_kernel, group),
+        functools.partial(intra_second_kernel, group),
         out_shape=(part_shape,) * QUAD,
         in_specs=[SMEM] + [VMEM] * 4,
         out_specs=(VMEM,) * QUAD,
         compiler_params=params(),
         cost_estimate=work_cost,
-        name="intra_early",
+        name="intra_second",
     )(*args)
+
     sums, *running = pl.pallas_call(
         sums_kernel,
         out_shape=(sds(block, BF16),) + (sds(block, F32),) * (seq_bits > 3),
@@ -262,27 +301,27 @@
             running = [running[0] + upper[-1].astype(F32)]
             sums = running[0].astype(BF16)
         upper.append(exchanged(sums, "seq", 1 << bit))
-    left_pair, gain = pl.pallas_call(
+    left_pair = pl.pallas_call(
         functools.partial(left_kernel, lax.axis_size("seq")),
-        out_shape=(sds(block, BF16), sds((1, width), F32)),
-        in_specs=[SMEM] + [VMEM] * 7,
-        out_specs=(VMEM,) * 2,
+        out_shape=sds(block, BF16),
+        in_specs=[SMEM] + [VMEM] * 6,
+        out_specs=VMEM,
         compiler_params=params(),
         cost_estimate=cost(4 * group * HEAD_DIM**2, 16 * group * HEAD_DIM**2),
         name="left",
-    )(place, own, taken1, early2, early3, late2, late3, norm_gain.reshape(1, width))
+    )(place, own, taken1, early2, early3, late2, late3)
     top = jnp.concatenate(upper, axis=0) if len(upper) > 1 else upper[0]
     tops = {0: top} | {r: exchanged_in(top, r, lambda s, seq: s >= QUAD) for r in (3, 1, 2)}
 
     gain, *outs = pl.pallas_call(
-        functools.partial(intra_late_kernel, group),
+        functools.partial(intra_last_kernel, group),
         out_shape=(sds((width, HEAD_DIM), F32),) + (part_shape,) * QUAD,
-        in_specs=[SMEM] + [VMEM] * (5 + QUAD),
+        in_specs=[SMEM] + [VMEM] * (6 + QUAD),
         out_specs=(VMEM,) * (1 + QUAD),
         compiler_params=params(),
         cost_estimate=work_cost,
-        name="intra_late",
-    )(*args, gain, *outs)
+        name="intra_last",
+    )(*args, gain, first, *outs)
     totals = dict(enumerate(outs))
 
     middle = {0: left_pair} | {r: exchanged(left_pair, "seq", r) for r in (3, 2)}

time: 32.8 us -> 32.8 us (level)
  starting transfers between devices: 18.5 us -> 17.7 us
  waiting for transfers between devices: 7.32 us -> 7.87 us
    ppermute x8, starting transfers between devices: 11.4 us -> 10.4 us  [exchanged(): return lax.ppermute(block, axis, [(i, i ^ mask) for i in range(count)])]
    ppermute x8, waiting for transfers between devices: 2.77 us -> 3.15 us  [exchanged_in(): return lax.ppermute(block, ('seq', 'head'), route)]
    pallas_call x2 -> x3, Pallas kernels: 2.1 us -> 2.1 us  [the longest x1 2.1 us: local(): pl.pallas_call(functools.partial(intra_last_kernel, group), out_shape=(sd...]
  transfers between devices with their start and end apart: 16 -> 16, of which waited for: 5 -> 6; matrix products, arithmetic and copies ran while one was open for 0% -> 0% of each run, Pallas kernels for 9% -> 9%
where the time goes in v14:
time: 32.8 us; the launch traced here: 32.6 us
  starting transfers between devices  17.7 us (54%)
  waiting for transfers between devices  7.87 us (24%)
  Pallas kernels  6.64 us (20%)
    ppermute x8, starting transfers between devices, exchanged(): return lax.ppermute(block, axis, [(i, i ^ mask) for i in range(count)])  10.4 us
    ppermute x8, starting transfers between devices, exchanged_in(): return lax.ppermute(block, ('seq', 'head'), route)  7.35 us
    ppermute x8, waiting for transfers between devices, exchanged(): return lax.ppermute(block, axis, [(i, i ^ mask) for i in range(count)])  4.72 us
    ppermute x8, waiting for transfers between devices, exchanged_in(): return lax.ppermute(block, ('seq', 'head'), route)  3.15 us
    pallas_call x1, Pallas kernels, local(): pl.pallas_call(functools.partial(states_kernel, group), out_shape=(sds((Q...  2.3 us
    pallas_call x1, Pallas kernels, local(): pl.pallas_call(functools.partial(intra_last_kernel, group), out_shape=(sd...  2.1 us
    pallas_call x1, Pallas kernels, local(): pl.pallas_call(functools.partial(norm_kernel, group, full_width), out_sha...  1.14 us
    pallas_call x3, Pallas kernels, readout(): pl.pallas_call(kernel, out_shape=tuple(shapes), in_specs=[SMEM] + [VMEM]...  1.02 us
  transfers between devices with their start and end apart: 16, of which 6 were waited for; matrix products, arithmetic and copies ran while one was open for 0% of the time, Pallas kernels for 9%

profile of v14, /device:TPU:17, one launch (start us, length us, event | category | flops | bytes accessed | tf_op | source)
XLA Modules:
  0.0 32.6 jit_solution(2015758024666575812)
XLA Ops:
  0.0 0.0 copy-start
  0.0 0.0 copy-start.1
  0.0 2.3 %states.1 = (bf16[4,512,256]{2,1,0:T(8,128)(2,1)S(1)}, bf16[4,512,256]{2,1,0:T(8,128)(2,1)S(1)}, f32[2,128,128]{2,1,0:T(8,128)S(1)}, bf16[2,128,128]{2,1,0:T(8,1...) custom-call(s32[1]{0:T(128)} %bitcast.place_ref.args_0_, ...), custom_call_target="tpu_custom_call" | custom-call | flops 134217728 | bytes 2097152 | tf_op jit(solution)/shard_map/states/pallas_call | solution.py:250
  2.3 1.3 %collective-permute-start = (bf16[2,128,128]{2,1,0:T(8,128)(2,1)S(1)}, bf16[2,128,128]{2,1,0:T(8,128)(2,1)S(1)}, u32[]{:S(2)}, u32[]{:S(2)}) collective-permute-start(bf16[2,128,128]{2,1,0:T(8,128)(2,1)S(1)} %get-tuple-element.33), channel_id=1, source_target_pairs={{0,4},{4,0},{8,12},{12,8},{16,20},{20,16},{24,28},{28,24},{1,5},{5... | collective-permute-start | bytes 196616 | tf_op jit(solution)/shard_map/ppermute | solution.py:36
  3.6 1.0 %collective-permute-start.2 = (bf16[2,128,128]{2,1,0:T(8,128)(2,1)S(1)}, bf16[2,128,128]{2,1,0:T(8,128)(2,1)S(1)}, u32[]{:S(2)}, u32[]{:S(2)}) collective-permute-start(bf16[2,128,128]{2,1,0:T(8,128)(2,1)S(1)} %get-tuple-element.36), channel_id=1, source_target_pairs={{0,8},{1,9},{2,10},{3,11},{4,12},{5,13},{6,14},{7,15},{8,0},{9,1},... | collective-permute-start | bytes 196616 | tf_op jit(solution)/shard_map/ppermute | solution.py:46
  4.6 1.3 %collective-permute-start.4 = (bf16[2,128,128]{2,1,0:T(8,128)(2,1)S(1)}, bf16[2,128,128]{2,1,0:T(8,128)(2,1)S(1)}, u32[]{:S(2)}, u32[]{:S(2)}) collective-permute-start(bf16[2,128,128]{2,1,0:T(8,128)(2,1)S(1)} %get-tuple-element.36), channel_id=1, source_target_pairs={{0,1},{1,0},{2,3},{3,2},{4,5},{5,4},{6,7},{7,6},{8,9},{9,8},{10,11... | collective-permute-start | bytes 196616 | tf_op jit(solution)/shard_map/ppermute | solution.py:46
  5.9 0.3 collective-permute-start.3
  6.2 0.1 collective-permute-start.5
  6.3 0.0 collective-permute-done.one_ref.args_3_
  6.3 1.2 %collective-permute-start.1 = (bf16[6,128,128]{2,1,0:T(8,128)(2,1)S(1)}, bf16[6,128,128]{2,1,0:T(8,128)(2,1)S(1)}, u32[]{:S(2)}, u32[]{:S(2)}) collective-permute-start(bf16[6,128,128]{2,1,0:T(8,128)(2,1)S(1)} %get-tuple-element.34), channel_id=1, source_target_pairs={{0,4},{4,0},{8,12},{12,8},{16,20},{20,16},{24,28},{28,24},{1,5},{5... | collective-permute-start | bytes 589832 | tf_op jit(solution)/shard_map/ppermute | solution.py:36
  7.5 0.0 copy-done
  7.5 0.0 copy-done.1
  7.5 0.0 collective-permute-done.2.early2_ref.two_ref
  7.5 0.0 collective-permute-done.3.early3_ref.three_ref
  7.5 0.7 %collective-permute-done.4.late2_ref = bf16[2,128,128]{2,1,0:T(8,128)(2,1)S(1)} collective-permute-done((bf16[2,128,128]{2,1,0:T(8,128)(2,1)S(1)}, bf16[2,128,128]{2,1,0:T(8,128)(2,1)S(1)}, u32[]{:S(2)}, u32[]{:S(2)}) %collective-permute-start.4) | collective-permute-done | bytes 65568 | tf_op jit(solution)/shard_map/ppermute | solution.py:46
  8.2 2.3 %collective-permute-done.5.late3_ref = bf16[2,128,128]{2,1,0:T(8,128)(2,1)S(1)} collective-permute-done((bf16[2,128,128]{2,1,0:T(8,128)(2,1)S(1)}, bf16[2,128,128]{2,1,0:T(8,128)(2,1)S(1)}, u32[]{:S(2)}, u32[]{:S(2)}) %collective-permute-start.5) | collective-permute-done | bytes 65568 | tf_op jit(solution)/shard_map/ppermute | solution.py:46
  10.5 0.2 collective-permute-start.6
  10.8 1.3 %collective-permute-start.7 = (bf16[2,128,128]{2,1,0:T(8,128)(2,1)S(1)}, bf16[2,128,128]{2,1,0:T(8,128)(2,1)S(1)}, u32[]{:S(2)}, u32[]{:S(2)}) collective-permute-start(bf16[2,128,128]{2,1,0:T(8,128)(2,1)S(1)} %left.1.args_5_), channel_id=1, source_target_pairs={{0,12},{4,8},{8,4},{12,0},{16,28},{20,24},{24,20},{28,16},{1,13},{... | collective-permute-start | bytes 196616 | tf_op jit(solution)/shard_map/ppermute | solution.py:36
  12.0 0.0 copy-start.2
  12.1 0.3 %collective-permute-start.8 = (bf16[2,128,128]{2,1,0:T(8,128)(2,1)S(1)}, bf16[2,128,128]{2,1,0:T(8,128)(2,1)S(1)}, u32[]{:S(2)}, u32[]{:S(2)}) collective-permute-start(bf16[2,128,128]{2,1,0:T(8,128)(2,1)S(1)} %sums.1), channel_id=1, source_target_pairs={{0,16},{4,20},{8,24},{12,28},{16,0},{20,4},{24,8},{28,12},{1,17},{... | collective-permute-start | bytes 196616 | tf_op jit(solution)/shard_map/ppermute | solution.py:36
  12.4 0.3 copy-done.2
  12.7 1.7 %collective-permute-start.11 = (bf16[2,128,128]{2,1,0:T(8,128)(2,1)S(1)}, bf16[2,128,128]{2,1,0:T(8,128)(2,1)S(1)}, u32[]{:S(2)}, u32[]{:S(2)}) collective-permute-start(bf16[2,128,128]{2,1,0:T(8,128)(2,1)S(1)} %left.1.args_5_), channel_id=1, source_target_pairs={{0,1},{1,0},{2,3},{3,2},{4,5},{5,4},{6,7},{7,6},{8,12},{9,13},{10,... | collective-permute-start | bytes 196616 | tf_op jit(solution)/shard_map/ppermute | solution.py:46
  14.4 2.2 %collective-permute-done.8.args_8_ = bf16[2,128,128]{2,1,0:T(8,128)(2,1)S(1)} collective-permute-done((bf16[2,128,128]{2,1,0:T(8,128)(2,1)S(1)}, bf16[2,128,128]{2,1,0:T(8,128)(2,1)S(1)}, u32[]{:S(2)}, u32[]{:S(2)}) %collective-permute-start.8) | collective-permute-done | bytes 65568 | tf_op jit(solution)/shard_map/ppermute | solution.py:36
  16.6 0.9 %collective-permute-start.9 = (bf16[2,128,128]{2,1,0:T(8,128)(2,1)S(1)}, bf16[2,128,128]{2,1,0:T(8,128)(2,1)S(1)}, u32[]{:S(2)}, u32[]{:S(2)}) collective-permute-start(bf16[2,128,128]{2,1,0:T(8,128)(2,1)S(1)} %collective-permute-done.8.args_8_), channel_id=1, source_target_pairs={{0,1},{1,0},{2,3},{3,2},{4,5},{5,4},{6,7},{7,6},{8,9},{9,8},{10,11... | collective-permute-start | bytes 196616 | tf_op jit(solution)/shard_map/ppermute | solution.py:46
  17.5 0.0 collective-permute-done.6.args_6_
  17.5 2.1 %collective-permute-start.10 = (bf16[2,128,128]{2,1,0:T(8,128)(2,1)S(1)}, bf16[2,128,128]{2,1,0:T(8,128)(2,1)S(1)}, u32[]{:S(2)}, u32[]{:S(2)}) collective-permute-start(bf16[2,128,128]{2,1,0:T(8,128)(2,1)S(1)} %collective-permute-done.8.args_8_), channel_id=1, source_target_pairs={{0,1},{1,0},{2,3},{3,2},{4,5},{5,4},{6,7},{7,6},{8,9},{9,8},{10,11... | collective-permute-start | bytes 196616 | tf_op jit(solution)/shard_map/ppermute | solution.py:46
  19.6 0.0 collective-permute-done.7.args_7_
  19.6 0.0 collective-permute-start.12
  19.6 2.1 %intra_last.1 = (f32[1024,128]{1,0:T(8,128)S(1)}, f32[256,512]{1,0:T(8,128)S(1)}, f32[256,512]{1,0:T(8,128)S(1)}, f32[256,512]{1,0:T(8,128)S(1)}, f32[256,512]{1,0:T(8,128)S(1)}) custom-call(s32[1]{0:T(128)} %bitcast.place_ref.args_0_, bf16[512,1024]{1,0:T(8,128)(2,1)S(1)} %copy-done, f32[5,8,512]{2,1,0:T(8,128)S(1)} %copy-done.1, ...), custom_call_target="tpu_custom_call" | custom-call | flops 805306368 | bytes 2097152 | tf_op jit(solution)/shard_map/intra_last/pallas_call | solution.py:316
  21.7 0.0 collective-permute-done.1.args_4_
  21.7 0.3 %shard_map.55 = (f32[256,512]{1,0:T(8,128)S(1)}, f32[256,512]{1,0:T(8,128)S(1)}, f32[256,512]{1,0:T(8,128)S(1)}, f32[256,512]{1,0:T(8,128)S(1)}, f32[8,512]{1,0:T(8,128)S(1)}) custom-call(s32[1]{0:T(128)} %bitcast.place_ref.args_0_, bf16[512,1024]{1,0:T(8,128)(2,1)S(1)} %copy-done, f32[5,8,512]{2,1,0:T(8,128)S(1)} %copy-done.1, ...), custom_call_target="tpu_custom_call" | custom-call | flops 268435456 | bytes 4194304 | tf_op jit(solution)/shard_map/pallas_call | solution.py:342
  22.1 0.0 collective-permute-done.11.args_5_
  22.1 0.0 collective-permute-done.9.args_3_
  22.1 0.0 collective-permute-done.10.args_4_
  22.1 0.4 %shard_map.56 = (f32[256,512]{1,0:T(8,128)S(1)}, f32[256,512]{1,0:T(8,128)S(1)}, f32[8,512]{1,0:T(8,128)S(1)}) custom-call(s32[1]{0:T(128)} %bitcast.place_ref.args_0_, bf16[512,1024]{1,0:T(8,128)(2,1)S(1)} %copy-done, f32[5,8,512]{2,1,0:T(8,128)S(1)} %copy-done.1, bf16[2,128,128]{2,1,0:T(8,128)(2,1)S(1)} %collective-permute-done.9.args_3_, ...), custom_call_target="tpu_custom_call" | custom-call | flops 134217728 | bytes 2097152 | tf_op jit(solution)/shard_map/pallas_call | solution.py:342
  22.5 0.2 collective-permute-done.12.args_3_
  22.7 0.3 shard_map.57
  23.0 4.3 %collective-permute-start.13 = (f32[1,512]{1,0:T(1,128)S(1)}, f32[1,512]{1,0:T(1,128)S(1)}, u32[]{:S(2)}, u32[]{:S(2)}) collective-permute-start(f32[1,512]{1,0:T(1,128)S(1)} %get-tuple-element.59.refs_4_), channel_id=1, source_target_pairs={{0,1},{1,0},{2,3},{3,2},{4,5},{5,4},{6,7},{7,6},{8,9},{9,8},{10,11... | collective-permute-start | bytes 6152 | tf_op jit(solution)/shard_map/ppermute | solution.py:36
  27.3 1.2 %collective-permute-start.14 = (f32[1,512]{1,0:T(1,128)S(1)}, f32[1,512]{1,0:T(1,128)S(1)}, u32[]{:S(2)}, u32[]{:S(2)}) collective-permute-start(f32[1,512]{1,0:T(1,128)S(1)} %get-tuple-element.59.refs_4_), channel_id=1, source_target_pairs={{0,2},{1,3},{2,0},{3,1},{4,6},{5,7},{6,4},{7,5},{8,10},{9,11},{10,... | collective-permute-start | bytes 6152 | tf_op jit(solution)/shard_map/ppermute | solution.py:36
  28.5 0.5 %collective-permute-start.15 = (f32[1,512]{1,0:T(1,128)S(1)}, f32[1,512]{1,0:T(1,128)S(1)}, u32[]{:S(2)}, u32[]{:S(2)}) collective-permute-start(f32[1,512]{1,0:T(1,128)S(1)} %get-tuple-element.59.refs_4_), channel_id=1, source_target_pairs={{0,3},{1,2},{2,1},{3,0},{4,7},{5,6},{6,5},{7,4},{8,11},{9,10},{10,... | collective-permute-start | bytes 6152 | tf_op jit(solution)/shard_map/ppermute | solution.py:36
  29.0 0.0 collective-permute-done.13.refs_5_
  29.0 0.7 %collective-permute-done.14.refs_6_ = f32[1,512]{1,0:T(1,128)S(1)} collective-permute-done((f32[1,512]{1,0:T(1,128)S(1)}, f32[1,512]{1,0:T(1,128)S(1)}, u32[]{:S(2)}, u32[]{:S(2)}) %collective-permute-start.14) | collective-permute-done | bytes 2080 | tf_op jit(solution)/shard_map/ppermute | solution.py:36
  29.7 1.8 %collective-permute-done.15.refs_7_ = f32[1,512]{1,0:T(1,128)S(1)} collective-permute-done((f32[1,512]{1,0:T(1,128)S(1)}, f32[1,512]{1,0:T(1,128)S(1)}, u32[]{:S(2)}, u32[]{:S(2)}) %collective-permute-start.15) | collective-permute-done | bytes 2080 | tf_op jit(solution)/shard_map/ppermute | solution.py:36
  31.5 1.1 %norm.1 = bf16[512,1024]{1,0:T(8,128)(2,1)} custom-call(s32[1]{0:T(128)} %bitcast.place_ref.args_0_, f32[256,512]{1,0:T(8,128)S(1)} %get-tuple-element.50.refs_0_, f32[256,512]{1,0:T(8,128)S(1)} %get-tuple-element.54.refs_1_, f32[256,512]{1,0:T(8,128)S(1)} %get-tuple-element.57.refs_2_, f32[256,512]{1,0:T(8,128)S(1)} %get-tuple-element.58.refs_3_, ...), custom_call_target="tpu_custom_call" | custom-call | flops 1048576 | bytes 1048576 | tf_op jit(solution)/shard_map/norm/pallas_call | solution.py:363
  (4 shorter events, 0.1 us)
Async XLA Ops:
  0.0 7.5 %copy-start = (bf16[512,1024]{1,0:T(8,128)(2,1)S(1)}, bf16[512,1024]{1,0:T(8,128)(2,1)}, u32[]{:S(2)}) copy-start(bf16[512,1024]{1,0:T(8,128)(2,1)} %args_1_.8) | copy-start | bytes 3145732
  0.0 7.5 %copy-start.1 = (f32[5,8,512]{2,1,0:T(8,128)S(1)}, f32[5,8,512]{2,1,0:T(8,128)}, u32[]{:S(2)}) copy-start(f32[5,8,512]{2,1,0:T(8,128)} %args_2_.8) | copy-start | bytes 245764
  2.3 4.0 %collective-permute-start = (bf16[2,128,128]{2,1,0:T(8,128)(2,1)S(1)}, bf16[2,128,128]{2,1,0:T(8,128)(2,1)S(1)}, u32[]{:S(2)}, u32[]{:S(2)}) collective-permute-start(bf16[2,128,128]{2,1,0:T(8,128)(2,1)S(1)} %get-tuple-element.33), channel_id=1, source_target_pairs={{0,4},{4,0},{8,12},{12,8},{16,20},{20,16},{24,28},{28,24},{1,5},{5... | collective-permute-start | bytes 196616 | tf_op jit(solution)/shard_map/ppermute | solution.py:36
  3.6 3.9 %collective-permute-start.2 = (bf16[2,128,128]{2,1,0:T(8,128)(2,1)S(1)}, bf16[2,128,128]{2,1,0:T(8,128)(2,1)S(1)}, u32[]{:S(2)}, u32[]{:S(2)}) collective-permute-start(bf16[2,128,128]{2,1,0:T(8,128)(2,1)S(1)} %get-tuple-element.36), channel_id=1, source_target_pairs={{0,8},{1,9},{2,10},{3,11},{4,12},{5,13},{6,14},{7,15},{8,0},{9,1},... | collective-permute-start | bytes 196616 | tf_op jit(solution)/shard_map/ppermute | solution.py:46
  4.6 3.6 %collective-permute-start.4 = (bf16[2,128,128]{2,1,0:T(8,128)(2,1)S(1)}, bf16[2,128,128]{2,1,0:T(8,128)(2,1)S(1)}, u32[]{:S(2)}, u32[]{:S(2)}) collective-permute-start(bf16[2,128,128]{2,1,0:T(8,128)(2,1)S(1)} %get-tuple-element.36), channel_id=1, source_target_pairs={{0,1},{1,0},{2,3},{3,2},{4,5},{5,4},{6,7},{7,6},{8,9},{9,8},{10,11... | collective-permute-start | bytes 196616 | tf_op jit(solution)/shard_map/ppermute | solution.py:46
  5.9 1.7 %collective-permute-start.3 = (bf16[2,128,128]{2,1,0:T(8,128)(2,1)S(1)}, bf16[2,128,128]{2,1,0:T(8,128)(2,1)S(1)}, u32[]{:S(2)}, u32[]{:S(2)}) collective-permute-start(bf16[2,128,128]{2,1,0:T(8,128)(2,1)S(1)} %get-tuple-element.37), channel_id=1, source_target_pairs={{0,12},{1,13},{2,14},{3,15},{4,8},{5,9},{6,10},{7,11},{8,4},{9,5},... | collective-permute-start | bytes 196616 | tf_op jit(solution)/shard_map/ppermute | solution.py:46
  6.2 4.3 %collective-permute-start.5 = (bf16[2,128,128]{2,1,0:T(8,128)(2,1)S(1)}, bf16[2,128,128]{2,1,0:T(8,128)(2,1)S(1)}, u32[]{:S(2)}, u32[]{:S(2)}) collective-permute-start(bf16[2,128,128]{2,1,0:T(8,128)(2,1)S(1)} %get-tuple-element.37), channel_id=1, source_target_pairs={{0,1},{1,0},{2,3},{3,2},{4,5},{5,4},{6,7},{7,6},{8,9},{9,8},{10,11... | collective-permute-start | bytes 196616 | tf_op jit(solution)/shard_map/ppermute | solution.py:46
  6.3 15.4 %collective-permute-start.1 = (bf16[6,128,128]{2,1,0:T(8,128)(2,1)S(1)}, bf16[6,128,128]{2,1,0:T(8,128)(2,1)S(1)}, u32[]{:S(2)}, u32[]{:S(2)}) collective-permute-start(bf16[6,128,128]{2,1,0:T(8,128)(2,1)S(1)} %get-tuple-element.34), channel_id=1, source_target_pairs={{0,4},{4,0},{8,12},{12,8},{16,20},{20,16},{24,28},{28,24},{1,5},{5... | collective-permute-start | bytes 589832 | tf_op jit(solution)/shard_map/ppermute | solution.py:36
  10.5 7.0 %collective-permute-start.6 = (bf16[2,128,128]{2,1,0:T(8,128)(2,1)S(1)}, bf16[2,128,128]{2,1,0:T(8,128)(2,1)S(1)}, u32[]{:S(2)}, u32[]{:S(2)}) collective-permute-start(bf16[2,128,128]{2,1,0:T(8,128)(2,1)S(1)} %left.1.args_5_), channel_id=1, source_target_pairs={{0,8},{4,12},{8,0},{12,4},{16,24},{20,28},{24,16},{28,20},{1,9},{5... | collective-permute-start | bytes 196616 | tf_op jit(solution)/shard_map/ppermute | solution.py:36
  10.8 8.8 %collective-permute-start.7 = (bf16[2,128,128]{2,1,0:T(8,128)(2,1)S(1)}, bf16[2,128,128]{2,1,0:T(8,128)(2,1)S(1)}, u32[]{:S(2)}, u32[]{:S(2)}) collective-permute-start(bf16[2,128,128]{2,1,0:T(8,128)(2,1)S(1)} %left.1.args_5_), channel_id=1, source_target_pairs={{0,12},{4,8},{8,4},{12,0},{16,28},{20,24},{24,20},{28,16},{1,13},{... | collective-permute-start | bytes 196616 | tf_op jit(solution)/shard_map/ppermute | solution.py:36
  12.0 0.7 %copy-start.2 = (f32[1024]{0:T(1024)S(1)}, f32[1024]{0:T(1024)}, u32[]{:S(2)}) copy-start(f32[1024]{0:T(1024)} %param.9) | copy-start | bytes 12292
  12.1 4.6 %collective-permute-start.8 = (bf16[2,128,128]{2,1,0:T(8,128)(2,1)S(1)}, bf16[2,128,128]{2,1,0:T(8,128)(2,1)S(1)}, u32[]{:S(2)}, u32[]{:S(2)}) collective-permute-start(bf16[2,128,128]{2,1,0:T(8,128)(2,1)S(1)} %sums.1), channel_id=1, source_target_pairs={{0,16},{4,20},{8,24},{12,28},{16,0},{20,4},{24,8},{28,12},{1,17},{... | collective-permute-start | bytes 196616 | tf_op jit(solution)/shard_map/ppermute | solution.py:36
  12.7 9.4 %collective-permute-start.11 = (bf16[2,128,128]{2,1,0:T(8,128)(2,1)S(1)}, bf16[2,128,128]{2,1,0:T(8,128)(2,1)S(1)}, u32[]{:S(2)}, u32[]{:S(2)}) collective-permute-start(bf16[2,128,128]{2,1,0:T(8,128)(2,1)S(1)} %left.1.args_5_), channel_id=1, source_target_pairs={{0,1},{1,0},{2,3},{3,2},{4,5},{5,4},{6,7},{7,6},{8,12},{9,13},{10,... | collective-permute-start | bytes 196616 | tf_op jit(solution)/shard_map/ppermute | solution.py:46
  16.6 5.5 %collective-permute-start.9 = (bf16[2,128,128]{2,1,0:T(8,128)(2,1)S(1)}, bf16[2,128,128]{2,1,0:T(8,128)(2,1)S(1)}, u32[]{:S(2)}, u32[]{:S(2)}) collective-permute-start(bf16[2,128,128]{2,1,0:T(8,128)(2,1)S(1)} %collective-permute-done.8.args_8_), channel_id=1, source_target_pairs={{0,1},{1,0},{2,3},{3,2},{4,5},{5,4},{6,7},{7,6},{8,9},{9,8},{10,11... | collective-permute-start | bytes 196616 | tf_op jit(solution)/shard_map/ppermute | solution.py:46
  17.5 4.6 %collective-permute-start.10 = (bf16[2,128,128]{2,1,0:T(8,128)(2,1)S(1)}, bf16[2,128,128]{2,1,0:T(8,128)(2,1)S(1)}, u32[]{:S(2)}, u32[]{:S(2)}) collective-permute-start(bf16[2,128,128]{2,1,0:T(8,128)(2,1)S(1)} %collective-permute-done.8.args_8_), channel_id=1, source_target_pairs={{0,1},{1,0},{2,3},{3,2},{4,5},{5,4},{6,7},{7,6},{8,9},{9,8},{10,11... | collective-permute-start | bytes 196616 | tf_op jit(solution)/shard_map/ppermute | solution.py:46
  19.6 3.1 %collective-permute-start.12 = (bf16[2,128,128]{2,1,0:T(8,128)(2,1)S(1)}, bf16[2,128,128]{2,1,0:T(8,128)(2,1)S(1)}, u32[]{:S(2)}, u32[]{:S(2)}) collective-permute-start(bf16[2,128,128]{2,1,0:T(8,128)(2,1)S(1)} %collective-permute-done.8.args_8_), channel_id=1, source_target_pairs={{0,1},{1,0},{2,3},{3,2},{4,5},{5,4},{6,7},{7,6},{8,9},{9,8},{10,11... | collective-permute-start | bytes 196616 | tf_op jit(solution)/shard_map/ppermute | solution.py:46
  23.0 6.0 %collective-permute-start.13 = (f32[1,512]{1,0:T(1,128)S(1)}, f32[1,512]{1,0:T(1,128)S(1)}, u32[]{:S(2)}, u32[]{:S(2)}) collective-permute-start(f32[1,512]{1,0:T(1,128)S(1)} %get-tuple-element.59.refs_4_), channel_id=1, source_target_pairs={{0,1},{1,0},{2,3},{3,2},{4,5},{5,4},{6,7},{7,6},{8,9},{9,8},{10,11... | collective-permute-start | bytes 6152 | tf_op jit(solution)/shard_map/ppermute | solution.py:36
  27.3 2.4 %collective-permute-start.14 = (f32[1,512]{1,0:T(1,128)S(1)}, f32[1,512]{1,0:T(1,128)S(1)}, u32[]{:S(2)}, u32[]{:S(2)}) collective-permute-start(f32[1,512]{1,0:T(1,128)S(1)} %get-tuple-element.59.refs_4_), channel_id=1, source_target_pairs={{0,2},{1,3},{2,0},{3,1},{4,6},{5,7},{6,4},{7,5},{8,10},{9,11},{10,... | collective-permute-start | bytes 6152 | tf_op jit(solution)/shard_map/ppermute | solution.py:36
  28.5 3.0 %collective-permute-start.15 = (f32[1,512]{1,0:T(1,128)S(1)}, f32[1,512]{1,0:T(1,128)S(1)}, u32[]{:S(2)}, u32[]{:S(2)}) collective-permute-start(f32[1,512]{1,0:T(1,128)S(1)} %get-tuple-element.59.refs_4_), channel_id=1, source_target_pairs={{0,3},{1,2},{2,1},{3,0},{4,7},{5,6},{6,5},{7,4},{8,11},{9,10},{10,... | collective-permute-start | bytes 6152 | tf_op jit(solution)/shard_map/ppermute | solution.py:36

commit v15 on v14

--- a/solution.py
+++ b/solution.py
@@ -93,6 +93,11 @@
     sent_ref[...] = total.astype(BF16)
 
 
+def join_kernel(top_ref, left_ref, joined_ref):
+    joined_ref[: top_ref.shape[0]] = top_ref[...]
+    joined_ref[top_ref.shape[0] :] = left_ref[...]
+
+
 def left_kernel(seq, place_ref, own_ref, one_ref, early2_ref, early3_ref, late2_ref, late3_ref, left_ref):
     last_quad = place_ref[0] >= seq - QUAD
     two = jnp.where(last_quad, late2_ref[...], early2_ref[...])
@@ -311,7 +316,17 @@
         name="left",
     )(place, own, taken1, early2, early3, late2, late3)
     top = jnp.concatenate(upper, axis=0) if len(upper) > 1 else upper[0]
-    tops = {0: top} | {r: exchanged_in(top, r, lambda s, seq: s >= QUAD) for r in (3, 1, 2)}
+    tops = {r: exchanged_in(top, r, lambda s, seq: s >= QUAD) for r in (3, 2)}
+    joined = pl.pallas_call(
+        join_kernel,
+        out_shape=sds((top.shape[0] + group,) + block[1:], BF16),
+        in_specs=[VMEM] * 2,
+        out_specs=VMEM,
+        compiler_params=params(),
+        cost_estimate=cost(0, 16 * group * HEAD_DIM**2),
+        name="join",
+    )(top, left_pair)
+    tops[1] = exchanged_in(joined, 1, lambda s, seq: s >= 2)
 
     gain, *outs = pl.pallas_call(
         functools.partial(intra_last_kernel, group),
@@ -325,7 +340,6 @@
     totals = dict(enumerate(outs))
 
     middle = {0: left_pair} | {r: exchanged(left_pair, "seq", r) for r in (3, 2)}
-    middle[1] = exchanged_in(left_pair, 1, lambda s, seq: s >> 1 & 1 == 1)
 
     def top_reads(ref):
         return tuple((bit, ref, (bit - 2) * group) for bit in range(2, seq_bits))
@@ -354,8 +368,8 @@
     below |= {r: ((0, 1, (r - 1) * group), (1, 1 + r, 0)) for r in (2, 3)}
     work = tuple((r, r == 0, below[r] + (top_reads(5) if r == 0 else ())) for r in (3, 1, 2, 0))
     squares = readout("far", work, (taken1, near, middle[0], middle[2], middle[3], top), None)
-    work = (3, True, top_reads(0)), (1, True, ((1, 2, 0), *top_reads(1)))
-    squares = readout("mid", work, (tops[3], tops[1], middle[1]), squares)
+    work = (3, True, top_reads(0)), (1, True, ((1, 1, top.shape[0]), *top_reads(1)))
+    squares = readout("mid", work, (tops[3], tops[1]), squares)
     squares = readout("last", ((2, True, top_reads(0)),), (tops[2],), squares, finish=True)
 
     shares = [squares] + [exchanged(squares, "head", mask) for mask in range(1, lax.axis_size("head"))]

time: 32.8 us -> 30.5 us (0.930)
  the two profiles are of different devices: /device:TPU:17 before, /device:TPU:0 now
where the time goes in v15:
time: 30.5 us; the launch traced here: 30.3 us
  starting transfers between devices  11.5 us (38%)
  waiting for transfers between devices  11.1 us (36%)
  Pallas kernels  6.25 us (20%)
  local copies, waits for them, and re-layouts  1.35 us (4%)
    ppermute x8, starting transfers between devices, exchanged(): return lax.ppermute(block, axis, [(i, i ^ mask) for i in range(count)])  8.85 us
    ppermute x8, waiting for transfers between devices, exchanged(): return lax.ppermute(block, axis, [(i, i ^ mask) for i in range(count)])  8.47 us
    ppermute x7, starting transfers between devices, exchanged_in(): return lax.ppermute(block, ('seq', 'head'), route)  2.67 us
    ppermute x7, waiting for transfers between devices, exchanged_in(): return lax.ppermute(block, ('seq', 'head'), route)  2.59 us
    pallas_call x1, Pallas kernels, local(): pl.pallas_call(functools.partial(states_kernel, group), out_shape=(sds((Q...  2.3 us
    pallas_call x1, Pallas kernels, local(): pl.pallas_call(functools.partial(intra_second_kernel, group), out_shape=(...  1.9 us
    unnamed x6, local copies, waits for them, and re-layouts  1.35 us
    pallas_call x1, Pallas kernels, local(): pl.pallas_call(functools.partial(norm_kernel, group, full_width), out_sha...  1.14 us
  transfers between devices with their start and end apart: 15, of which 7 were waited for; matrix products, arithmetic and copies ran while one was open for 0% of the time, Pallas kernels for 9%

profile of v15, /device:TPU:0, one launch (start us, length us, event | category | flops | bytes accessed | tf_op | source)
XLA Modules:
  0.0 30.3 jit_solution(12794610141077519222)
XLA Ops:
  0.0 0.0 copy-start
  0.0 2.3 %states.1 = (bf16[4,512,256]{2,1,0:T(8,128)(2,1)S(1)}, bf16[4,512,256]{2,1,0:T(8,128)(2,1)S(1)}, f32[2,128,128]{2,1,0:T(8,128)S(1)}, bf16[2,128,128]{2,1,0:T(8,1...) custom-call(s32[1]{0:T(128)} %bitcast.place_ref.args_0_, ...), custom_call_target="tpu_custom_call" | custom-call | flops 134217728 | bytes 2097152 | tf_op jit(solution)/shard_map/states/pallas_call | solution.py:255
  2.3 3.1 %collective-permute-start = (bf16[2,128,128]{2,1,0:T(8,128)(2,1)S(1)}, bf16[2,128,128]{2,1,0:T(8,128)(2,1)S(1)}, u32[]{:S(2)}, u32[]{:S(2)}) collective-permute-start(bf16[2,128,128]{2,1,0:T(8,128)(2,1)S(1)} %get-tuple-element.33), channel_id=1, source_target_pairs={{0,4},{4,0},{8,12},{12,8},{16,20},{20,16},{24,28},{28,24},{1,5},{5... | collective-permute-start | bytes 196616 | tf_op jit(solution)/shard_map/ppermute | solution.py:36
  5.4 1.6 %collective-permute-start.2 = (bf16[2,128,128]{2,1,0:T(8,128)(2,1)S(1)}, bf16[2,128,128]{2,1,0:T(8,128)(2,1)S(1)}, u32[]{:S(2)}, u32[]{:S(2)}) collective-permute-start(bf16[2,128,128]{2,1,0:T(8,128)(2,1)S(1)} %get-tuple-element.36), channel_id=1, source_target_pairs={{0,8},{1,9},{2,10},{3,11},{4,12},{5,13},{6,14},{7,15},{8,0},{9,1},... | collective-permute-start | bytes 196616 | tf_op jit(solution)/shard_map/ppermute | solution.py:46
  6.9 0.0 collective-permute-start.3
  7.0 0.0 collective-permute-start.4
  7.0 0.5 %collective-permute-start.5 = (bf16[2,128,128]{2,1,0:T(8,128)(2,1)S(1)}, bf16[2,128,128]{2,1,0:T(8,128)(2,1)S(1)}, u32[]{:S(2)}, u32[]{:S(2)}) collective-permute-start(bf16[2,128,128]{2,1,0:T(8,128)(2,1)S(1)} %get-tuple-element.37), channel_id=1, source_target_pairs={{0,1},{1,0},{2,3},{3,2},{4,5},{5,4},{6,7},{7,6},{8,9},{9,8},{10,11... | collective-permute-start | bytes 196616 | tf_op jit(solution)/shard_map/ppermute | solution.py:46
  7.5 0.2 collective-permute-done.one_ref.args_3_
  7.6 2.0 %collective-permute-start.1 = (bf16[6,128,128]{2,1,0:T(8,128)(2,1)S(1)}, bf16[6,128,128]{2,1,0:T(8,128)(2,1)S(1)}, u32[]{:S(2)}, u32[]{:S(2)}) collective-permute-start(bf16[6,128,128]{2,1,0:T(8,128)(2,1)S(1)} %get-tuple-element.34), channel_id=1, source_target_pairs={{0,4},{4,0},{8,12},{12,8},{16,20},{20,16},{24,28},{28,24},{1,5},{5... | collective-permute-start | bytes 589832 | tf_op jit(solution)/shard_map/ppermute | solution.py:36
  9.6 0.5 %collective-permute-done.2.early2_ref.two_ref = bf16[2,128,128]{2,1,0:T(8,128)(2,1)S(1)} collective-permute-done((bf16[2,128,128]{2,1,0:T(8,128)(2,1)S(1)}, bf16[2,128,128]{2,1,0:T(8,128)(2,1)S(1)}, u32[]{:S(2)}, u32[]{:S(2)}) %collective-permute-start.2) | collective-permute-done | bytes 65568 | tf_op jit(solution)/shard_map/ppermute | solution.py:46
  10.2 2.0 %collective-permute-done.3.early3_ref.three_ref = bf16[2,128,128]{2,1,0:T(8,128)(2,1)S(1)} collective-permute-done((bf16[2,128,128]{2,1,0:T(8,128)(2,1)S(1)}, bf16[2,128,128]{2,1,0:T(8,128)(2,1)S(1)}, u32[]{:S(2)}, u32[]{:S(2)}) %collective-permute-start.3) | collective-permute-done | bytes 65568 | tf_op jit(solution)/shard_map/ppermute | solution.py:46
  12.2 0.0 copy-start.1
  12.3 0.1 collective-permute-start.8
  12.3 0.0 copy-done
  12.3 0.8 %copy-done.1 = f32[5,8,512]{2,1,0:T(8,128)S(1)} copy-done((f32[5,8,512]{2,1,0:T(8,128)S(1)}, f32[5,8,512]{2,1,0:T(8,128)}, u32[]{:S(2)}) %copy-start.1) | copy-done | bytes 81944
  13.1 1.9 %intra_second.1 = (f32[256,512]{1,0:T(8,128)S(1)}, f32[256,512]{1,0:T(8,128)S(1)}, f32[256,512]{1,0:T(8,128)S(1)}, f32[256,512]{1,0:T(8,128)S(1)}) custom-call(s32[1]{0:T(128)} %bitcast.place_ref.args_0_, bf16[512,1024]{1,0:T(8,128)(2,1)S(1)} %copy-done, f32[5,8,512]{2,1,0:T(8,128)S(1)} %copy-done.1, ...), custom_call_target="tpu_custom_call" | custom-call | flops 805306368 | bytes 2097152 | tf_op jit(solution)/shard_map/intra_second/pallas_call | solution.py:284
  15.0 0.0 collective-permute-done.4.late2_ref
  15.0 0.0 collective-permute-done.5.late3_ref
  15.1 0.9 %collective-permute-start.6 = (bf16[2,128,128]{2,1,0:T(8,128)(2,1)S(1)}, bf16[2,128,128]{2,1,0:T(8,128)(2,1)S(1)}, u32[]{:S(2)}, u32[]{:S(2)}) collective-permute-start(bf16[2,128,128]{2,1,0:T(8,128)(2,1)S(1)} %left.1.args_5_.left_ref), channel_id=1, source_target_pairs={{0,8},{4,12},{8,0},{12,4},{16,24},{20,28},{24,16},{28,20},{1,9},{5... | collective-permute-start | bytes 196616 | tf_op jit(solution)/shard_map/ppermute | solution.py:36
  16.0 2.1 %collective-permute-done.8.args_8_.top_ref = bf16[2,128,128]{2,1,0:T(8,128)(2,1)S(1)} collective-permute-done((bf16[2,128,128]{2,1,0:T(8,128)(2,1)S(1)}, bf16[2,128,128]{2,1,0:T(8,128)(2,1)S(1)}, u32[]{:S(2)}, u32[]{:S(2)}) %collective-permute-start.8) | collective-permute-done | bytes 65568 | tf_op jit(solution)/shard_map/ppermute | solution.py:36
  18.1 0.0 copy-start.2
  18.1 0.1 collective-permute-start.10
  18.2 0.6 %copy-done.2 = f32[1024]{0:T(1024)S(1)} copy-done((f32[1024]{0:T(1024)S(1)}, f32[1024]{0:T(1024)}, u32[]{:S(2)}) %copy-start.2) | copy-done | bytes 4120
  18.8 0.9 %collective-permute-start.7 = (bf16[2,128,128]{2,1,0:T(8,128)(2,1)S(1)}, bf16[2,128,128]{2,1,0:T(8,128)(2,1)S(1)}, u32[]{:S(2)}, u32[]{:S(2)}) collective-permute-start(bf16[2,128,128]{2,1,0:T(8,128)(2,1)S(1)} %left.1.args_5_.left_ref), channel_id=1, source_target_pairs={{0,12},{4,8},{8,4},{12,0},{16,28},{20,24},{24,20},{28,16},{1,13},{... | collective-permute-start | bytes 196616 | tf_op jit(solution)/shard_map/ppermute | solution.py:36
  19.6 0.0 collective-permute-start.9
  19.6 0.0 collective-permute-done.6.args_6_
  19.7 0.5 %collective-permute-start.11 = (bf16[2,128,128]{2,1,0:T(8,128)(2,1)S(1)}, bf16[2,128,128]{2,1,0:T(8,128)(2,1)S(1)}, u32[]{:S(2)}, u32[]{:S(2)}) collective-permute-start(bf16[2,128,128]{2,1,0:T(8,128)(2,1)S(1)} %collective-permute-done.8.args_8_.top_ref), channel_id=1, source_target_pairs={{0,1},{1,0},{2,3},{3,2},{4,5},{5,4},{6,7},{7,6},{8,9},{9,8},{10,11... | collective-permute-start | bytes 196616 | tf_op jit(solution)/shard_map/ppermute | solution.py:46
  20.2 0.3 %intra_last.1 = (f32[1024,128]{1,0:T(8,128)S(1)}, f32[256,512]{1,0:T(8,128)S(1)}, f32[256,512]{1,0:T(8,128)S(1)}, f32[256,512]{1,0:T(8,128)S(1)}, f32[256,512]{1,0:T(8,128)S(1)}) custom-call(s32[1]{0:T(128)} %bitcast.place_ref.args_0_, bf16[512,1024]{1,0:T(8,128)(2,1)S(1)} %copy-done, f32[5,8,512]{2,1,0:T(8,128)S(1)} %copy-done.1, ...), custom_call_target="tpu_custom_call" | custom-call | flops 805306368 | bytes 2097152 | tf_op jit(solution)/shard_map/intra_last/pallas_call | solution.py:331
  20.5 3.5 %collective-permute-done.7.args_7_ = bf16[2,128,128]{2,1,0:T(8,128)(2,1)S(1)} collective-permute-done((bf16[2,128,128]{2,1,0:T(8,128)(2,1)S(1)}, bf16[2,128,128]{2,1,0:T(8,128)(2,1)S(1)}, u32[]{:S(2)}, u32[]{:S(2)}) %collective-permute-start.7) | collective-permute-done | bytes 65568 | tf_op jit(solution)/shard_map/ppermute | solution.py:36
  24.0 0.0 collective-permute-done.1.args_4_
  24.0 0.3 %shard_map.55 = (f32[256,512]{1,0:T(8,128)S(1)}, f32[256,512]{1,0:T(8,128)S(1)}, f32[256,512]{1,0:T(8,128)S(1)}, f32[256,512]{1,0:T(8,128)S(1)}, f32[8,512]{1,0:T(8,128)S(1)}) custom-call(s32[1]{0:T(128)} %bitcast.place_ref.args_0_, bf16[512,1024]{1,0:T(8,128)(2,1)S(1)} %copy-done, f32[5,8,512]{2,1,0:T(8,128)S(1)} %copy-done.1, ...), custom_call_target="tpu_custom_call" | custom-call | flops 268435456 | bytes 4194304 | tf_op jit(solution)/shard_map/pallas_call | solution.py:356
  24.3 0.0 collective-permute-done.9.args_3_
  24.3 0.0 collective-permute-done.10.args_4_
  24.3 0.1 shard_map.56
  24.4 0.0 collective-permute-done.11.args_3_
  24.5 0.1 shard_map.57
  24.5 0.1 collective-permute-start.12
  24.6 1.6 %collective-permute-start.13 = (f32[1,512]{1,0:T(1,128)S(1)}, f32[1,512]{1,0:T(1,128)S(1)}, u32[]{:S(2)}, u32[]{:S(2)}) collective-permute-start(f32[1,512]{1,0:T(1,128)S(1)} %get-tuple-element.59.refs_4_), channel_id=1, source_target_pairs={{0,2},{1,3},{2,0},{3,1},{4,6},{5,7},{6,4},{7,5},{8,10},{9,11},{10,... | collective-permute-start | bytes 6152 | tf_op jit(solution)/shard_map/ppermute | solution.py:36
  26.2 0.3 collective-permute-start.14
  26.5 0.0 collective-permute-done.12.refs_5_
  26.5 1.8 %collective-permute-done.13.refs_6_ = f32[1,512]{1,0:T(1,128)S(1)} collective-permute-done((f32[1,512]{1,0:T(1,128)S(1)}, f32[1,512]{1,0:T(1,128)S(1)}, u32[]{:S(2)}, u32[]{:S(2)}) %collective-permute-start.13) | collective-permute-done | bytes 2080 | tf_op jit(solution)/shard_map/ppermute | solution.py:36
  28.3 0.9 %collective-permute-done.14.refs_7_ = f32[1,512]{1,0:T(1,128)S(1)} collective-permute-done((f32[1,512]{1,0:T(1,128)S(1)}, f32[1,512]{1,0:T(1,128)S(1)}, u32[]{:S(2)}, u32[]{:S(2)}) %collective-permute-start.14) | collective-permute-done | bytes 2080 | tf_op jit(solution)/shard_map/ppermute | solution.py:36
  29.2 1.1 %norm.1 = bf16[512,1024]{1,0:T(8,128)(2,1)} custom-call(s32[1]{0:T(128)} %bitcast.place_ref.args_0_, f32[256,512]{1,0:T(8,128)S(1)} %get-tuple-element.50.refs_0_, f32[256,512]{1,0:T(8,128)S(1)} %get-tuple-element.54.refs_1_, f32[256,512]{1,0:T(8,128)S(1)} %get-tuple-element.57.refs_2_, f32[256,512]{1,0:T(8,128)S(1)} %get-tuple-element.58.refs_3_, ...), custom_call_target="tpu_custom_call" | custom-call | flops 1048576 | bytes 1048576 | tf_op jit(solution)/shard_map/norm/pallas_call | solution.py:377
  (4 shorter events, 0.1 us)
Async XLA Ops:
  0.0 12.3 %copy-start = (bf16[512,1024]{1,0:T(8,128)(2,1)S(1)}, bf16[512,1024]{1,0:T(8,128)(2,1)}, u32[]{:S(2)}) copy-start(bf16[512,1024]{1,0:T(8,128)(2,1)} %args_1_.8) | copy-start | bytes 3145732
  2.3 5.3 %collective-permute-start = (bf16[2,128,128]{2,1,0:T(8,128)(2,1)S(1)}, bf16[2,128,128]{2,1,0:T(8,128)(2,1)S(1)}, u32[]{:S(2)}, u32[]{:S(2)}) collective-permute-start(bf16[2,128,128]{2,1,0:T(8,128)(2,1)S(1)} %get-tuple-element.33), channel_id=1, source_target_pairs={{0,4},{4,0},{8,12},{12,8},{16,20},{20,16},{24,28},{28,24},{1,5},{5... | collective-permute-start | bytes 196616 | tf_op jit(solution)/shard_map/ppermute | solution.py:36
  5.4 4.8 %collective-permute-start.2 = (bf16[2,128,128]{2,1,0:T(8,128)(2,1)S(1)}, bf16[2,128,128]{2,1,0:T(8,128)(2,1)S(1)}, u32[]{:S(2)}, u32[]{:S(2)}) collective-permute-start(bf16[2,128,128]{2,1,0:T(8,128)(2,1)S(1)} %get-tuple-element.36), channel_id=1, source_target_pairs={{0,8},{1,9},{2,10},{3,11},{4,12},{5,13},{6,14},{7,15},{8,0},{9,1},... | collective-permute-start | bytes 196616 | tf_op jit(solution)/shard_map/ppermute | solution.py:46
  6.9 5.3 %collective-permute-start.3 = (bf16[2,128,128]{2,1,0:T(8,128)(2,1)S(1)}, bf16[2,128,128]{2,1,0:T(8,128)(2,1)S(1)}, u32[]{:S(2)}, u32[]{:S(2)}) collective-permute-start(bf16[2,128,128]{2,1,0:T(8,128)(2,1)S(1)} %get-tuple-element.37), channel_id=1, source_target_pairs={{0,12},{1,13},{2,14},{3,15},{4,8},{5,9},{6,10},{7,11},{8,4},{9,5},... | collective-permute-start | bytes 196616 | tf_op jit(solution)/shard_map/ppermute | solution.py:46
  7.0 8.1 %collective-permute-start.4 = (bf16[2,128,128]{2,1,0:T(8,128)(2,1)S(1)}, bf16[2,128,128]{2,1,0:T(8,128)(2,1)S(1)}, u32[]{:S(2)}, u32[]{:S(2)}) collective-permute-start(bf16[2,128,128]{2,1,0:T(8,128)(2,1)S(1)} %get-tuple-element.36), channel_id=1, source_target_pairs={{0,1},{1,0},{2,3},{3,2},{4,5},{5,4},{6,7},{7,6},{8,9},{9,8},{10,11... | collective-permute-start | bytes 196616 | tf_op jit(solution)/shard_map/ppermute | solution.py:46
  7.0 8.1 %collective-permute-start.5 = (bf16[2,128,128]{2,1,0:T(8,128)(2,1)S(1)}, bf16[2,128,128]{2,1,0:T(8,128)(2,1)S(1)}, u32[]{:S(2)}, u32[]{:S(2)}) collective-permute-start(bf16[2,128,128]{2,1,0:T(8,128)(2,1)S(1)} %get-tuple-element.37), channel_id=1, source_target_pairs={{0,1},{1,0},{2,3},{3,2},{4,5},{5,4},{6,7},{7,6},{8,9},{9,8},{10,11... | collective-permute-start | bytes 196616 | tf_op jit(solution)/shard_map/ppermute | solution.py:46
  7.6 16.3 %collective-permute-start.1 = (bf16[6,128,128]{2,1,0:T(8,128)(2,1)S(1)}, bf16[6,128,128]{2,1,0:T(8,128)(2,1)S(1)}, u32[]{:S(2)}, u32[]{:S(2)}) collective-permute-start(bf16[6,128,128]{2,1,0:T(8,128)(2,1)S(1)} %get-tuple-element.34), channel_id=1, source_target_pairs={{0,4},{4,0},{8,12},{12,8},{16,20},{20,16},{24,28},{28,24},{1,5},{5... | collective-permute-start | bytes 589832 | tf_op jit(solution)/shard_map/ppermute | solution.py:36
  12.2 0.9 %copy-start.1 = (f32[5,8,512]{2,1,0:T(8,128)S(1)}, f32[5,8,512]{2,1,0:T(8,128)}, u32[]{:S(2)}) copy-start(f32[5,8,512]{2,1,0:T(8,128)} %args_2_.8) | copy-start | bytes 245764
  12.3 5.9 %collective-permute-start.8 = (bf16[2,128,128]{2,1,0:T(8,128)(2,1)S(1)}, bf16[2,128,128]{2,1,0:T(8,128)(2,1)S(1)}, u32[]{:S(2)}, u32[]{:S(2)}) collective-permute-start(bf16[2,128,128]{2,1,0:T(8,128)(2,1)S(1)} %sums.1), channel_id=1, source_target_pairs={{0,16},{4,20},{8,24},{12,28},{16,0},{20,4},{24,8},{28,12},{1,17},{... | collective-permute-start | bytes 196616 | tf_op jit(solution)/shard_map/ppermute | solution.py:36
  15.1 4.6 %collective-permute-start.6 = (bf16[2,128,128]{2,1,0:T(8,128)(2,1)S(1)}, bf16[2,128,128]{2,1,0:T(8,128)(2,1)S(1)}, u32[]{:S(2)}, u32[]{:S(2)}) collective-permute-start(bf16[2,128,128]{2,1,0:T(8,128)(2,1)S(1)} %left.1.args_5_.left_ref), channel_id=1, source_target_pairs={{0,8},{4,12},{8,0},{12,4},{16,24},{20,28},{24,16},{28,20},{1,9},{5... | collective-permute-start | bytes 196616 | tf_op jit(solution)/shard_map/ppermute | solution.py:36
  18.1 0.7 %copy-start.2 = (f32[1024]{0:T(1024)S(1)}, f32[1024]{0:T(1024)}, u32[]{:S(2)}) copy-start(f32[1024]{0:T(1024)} %param.9) | copy-start | bytes 12292
  18.1 6.2 %collective-permute-start.10 = (bf16[4,128,128]{2,1,0:T(8,128)(2,1)S(1)}, bf16[4,128,128]{2,1,0:T(8,128)(2,1)S(1)}, u32[]{:S(2)}, u32[]{:S(2)}) collective-permute-start(bf16[4,128,128]{2,1,0:T(8,128)(2,1)S(1)} %join.1), channel_id=1, source_target_pairs={{0,1},{1,0},{2,3},{3,2},{4,5},{5,4},{6,7},{7,6},{8,12},{9,13},{10,... | collective-permute-start | bytes 393224 | tf_op jit(solution)/shard_map/ppermute | solution.py:46
  18.8 5.2 %collective-permute-start.7 = (bf16[2,128,128]{2,1,0:T(8,128)(2,1)S(1)}, bf16[2,128,128]{2,1,0:T(8,128)(2,1)S(1)}, u32[]{:S(2)}, u32[]{:S(2)}) collective-permute-start(bf16[2,128,128]{2,1,0:T(8,128)(2,1)S(1)} %left.1.args_5_.left_ref), channel_id=1, source_target_pairs={{0,12},{4,8},{8,4},{12,0},{16,28},{20,24},{24,20},{28,16},{1,13},{... | collective-permute-start | bytes 196616 | tf_op jit(solution)/shard_map/ppermute | solution.py:36
  19.6 4.6 %collective-permute-start.9 = (bf16[2,128,128]{2,1,0:T(8,128)(2,1)S(1)}, bf16[2,128,128]{2,1,0:T(8,128)(2,1)S(1)}, u32[]{:S(2)}, u32[]{:S(2)}) collective-permute-start(bf16[2,128,128]{2,1,0:T(8,128)(2,1)S(1)} %collective-permute-done.8.args_8_.top_ref), channel_id=1, source_target_pairs={{0,1},{1,0},{2,3},{3,2},{4,5},{5,4},{6,7},{7,6},{8,9},{9,8},{10,11... | collective-permute-start | bytes 196616 | tf_op jit(solution)/shard_map/ppermute | solution.py:46
  19.7 4.8 %collective-permute-start.11 = (bf16[2,128,128]{2,1,0:T(8,128)(2,1)S(1)}, bf16[2,128,128]{2,1,0:T(8,128)(2,1)S(1)}, u32[]{:S(2)}, u32[]{:S(2)}) collective-permute-start(bf16[2,128,128]{2,1,0:T(8,128)(2,1)S(1)} %collective-permute-done.8.args_8_.top_ref), channel_id=1, source_target_pairs={{0,1},{1,0},{2,3},{3,2},{4,5},{5,4},{6,7},{7,6},{8,9},{9,8},{10,11... | collective-permute-start | bytes 196616 | tf_op jit(solution)/shard_map/ppermute | solution.py:46
  24.5 1.9 %collective-permute-start.12 = (f32[1,512]{1,0:T(1,128)S(1)}, f32[1,512]{1,0:T(1,128)S(1)}, u32[]{:S(2)}, u32[]{:S(2)}) collective-permute-start(f32[1,512]{1,0:T(1,128)S(1)} %get-tuple-element.59.refs_4_), channel_id=1, source_target_pairs={{0,1},{1,0},{2,3},{3,2},{4,5},{5,4},{6,7},{7,6},{8,9},{9,8},{10,11... | collective-permute-start | bytes 6152 | tf_op jit(solution)/shard_map/ppermute | solution.py:36
  24.6 3.7 %collective-permute-start.13 = (f32[1,512]{1,0:T(1,128)S(1)}, f32[1,512]{1,0:T(1,128)S(1)}, u32[]{:S(2)}, u32[]{:S(2)}) collective-permute-start(f32[1,512]{1,0:T(1,128)S(1)} %get-tuple-element.59.refs_4_), channel_id=1, source_target_pairs={{0,2},{1,3},{2,0},{3,1},{4,6},{5,7},{6,4},{7,5},{8,10},{9,11},{10,... | collective-permute-start | bytes 6152 | tf_op jit(solution)/shard_map/ppermute | solution.py:36
  26.2 3.0 %collective-permute-start.14 = (f32[1,512]{1,0:T(1,128)S(1)}, f32[1,512]{1,0:T(1,128)S(1)}, u32[]{:S(2)}, u32[]{:S(2)}) collective-permute-start(f32[1,512]{1,0:T(1,128)S(1)} %get-tuple-element.59.refs_4_), channel_id=1, source_target_pairs={{0,3},{1,2},{2,1},{3,0},{4,7},{5,6},{6,5},{7,4},{8,11},{9,10},{10,... | collective-permute-start | bytes 6152 | tf_op jit(solution)/shard_map/ppermute | solution.py:36

commit v16 on v15

--- a/solution.py
+++ b/solution.py
@@ -151,15 +151,9 @@
 
 
 def intra_second_kernel(group, place_ref, *refs):
-    args, out_refs = refs[:4], refs[4:]
-
     @pl.when(lowest(place_ref[0]))
     def _():
-        intra_of(group, range(QUAD), place_ref[0], *args, out_refs)
-
-    @pl.when(busy(place_ref[0]))
-    def _():
-        intra_of(group, (1,), place_ref[0], *args, out_refs[1:2])
+        intra_of(group, range(QUAD), place_ref[0], *refs[:4], refs[4:])
 
 
 def intra_last_kernel(group, place_ref, q_ref, w_ref, k_all, v_all, gain_ref, first_ref, *refs):
@@ -177,8 +171,7 @@
     @pl.when(busy(place_ref[0]))
     def _():
         out_refs[3][...] = first_ref[...]
-        out_refs[1][...] = done_refs[1][...]
-        intra_of(group, (2, 0), place_ref[0], *args, (out_refs[2], out_refs[0]))
+        intra_of(group, range(3), place_ref[0], *args, out_refs[:3])
 
     @pl.when(jnp.logical_not(lowest(place_ref[0]) | busy(place_ref[0])))
     def _():

time: 30.5 us -> 30.5 us (level)
  no operation moved by 1% of the time
where the time goes in v16:
time: 30.5 us; the launch traced here: 30.3 us
  starting transfers between devices  11.5 us (38%)
  waiting for transfers between devices  11.1 us (36%)
  Pallas kernels  6.24 us (20%)
  local copies, waits for them, and re-layouts  1.35 us (4%)
    ppermute x8, starting transfers between devices, exchanged(): return lax.ppermute(block, axis, [(i, i ^ mask) for i in range(count)])  8.85 us
    ppermute x8, waiting for transfers between devices, exchanged(): return lax.ppermute(block, axis, [(i, i ^ mask) for i in range(count)])  8.48 us
    ppermute x7, starting transfers between devices, exchanged_in(): return lax.ppermute(block, ('seq', 'head'), route)  2.67 us
    ppermute x7, waiting for transfers between devices, exchanged_in(): return lax.ppermute(block, ('seq', 'head'), route)  2.59 us
    pallas_call x1, Pallas kernels, local(): pl.pallas_call(functools.partial(states_kernel, group), out_shape=(sds((Q...  2.3 us
    pallas_call x1, Pallas kernels, local(): pl.pallas_call(functools.partial(intra_second_kernel, group), out_shape=(...  1.89 us
    unnamed x6, local copies, waits for them, and re-layouts  1.35 us
    pallas_call x1, Pallas kernels, local(): pl.pallas_call(functools.partial(norm_kernel, group, full_width), out_sha...  1.14 us
  transfers between devices with their start and end apart: 15, of which 7 were waited for; matrix products, arithmetic and copies ran while one was open for 0% of the time, Pallas kernels for 9%

profile of v16, /device:TPU:0, one launch (start us, length us, event | category | flops | bytes accessed | tf_op | source)
XLA Modules:
  0.0 30.3 jit_solution(3839768586854251500)
XLA Ops:
  0.0 0.0 copy-start
  0.0 2.3 %states.1 = (bf16[4,512,256]{2,1,0:T(8,128)(2,1)S(1)}, bf16[4,512,256]{2,1,0:T(8,128)(2,1)S(1)}, f32[2,128,128]{2,1,0:T(8,128)S(1)}, bf16[2,128,128]{2,1,0:T(8,1...) custom-call(s32[1]{0:T(128)} %bitcast.place_ref.args_0_, ...), custom_call_target="tpu_custom_call" | custom-call | flops 134217728 | bytes 2097152 | tf_op jit(solution)/shard_map/states/pallas_call | solution.py:248
  2.3 3.1 %collective-permute-start = (bf16[2,128,128]{2,1,0:T(8,128)(2,1)S(1)}, bf16[2,128,128]{2,1,0:T(8,128)(2,1)S(1)}, u32[]{:S(2)}, u32[]{:S(2)}) collective-permute-start(bf16[2,128,128]{2,1,0:T(8,128)(2,1)S(1)} %get-tuple-element.33), channel_id=1, source_target_pairs={{0,4},{4,0},{8,12},{12,8},{16,20},{20,16},{24,28},{28,24},{1,5},{5... | collective-permute-start | bytes 196616 | tf_op jit(solution)/shard_map/ppermute | solution.py:36
  5.4 1.6 %collective-permute-start.2 = (bf16[2,128,128]{2,1,0:T(8,128)(2,1)S(1)}, bf16[2,128,128]{2,1,0:T(8,128)(2,1)S(1)}, u32[]{:S(2)}, u32[]{:S(2)}) collective-permute-start(bf16[2,128,128]{2,1,0:T(8,128)(2,1)S(1)} %get-tuple-element.36), channel_id=1, source_target_pairs={{0,8},{1,9},{2,10},{3,11},{4,12},{5,13},{6,14},{7,15},{8,0},{9,1},... | collective-permute-start | bytes 196616 | tf_op jit(solution)/shard_map/ppermute | solution.py:46
  6.9 0.0 collective-permute-start.3
  7.0 0.0 collective-permute-start.4
  7.0 0.5 %collective-permute-start.5 = (bf16[2,128,128]{2,1,0:T(8,128)(2,1)S(1)}, bf16[2,128,128]{2,1,0:T(8,128)(2,1)S(1)}, u32[]{:S(2)}, u32[]{:S(2)}) collective-permute-start(bf16[2,128,128]{2,1,0:T(8,128)(2,1)S(1)} %get-tuple-element.37), channel_id=1, source_target_pairs={{0,1},{1,0},{2,3},{3,2},{4,5},{5,4},{6,7},{7,6},{8,9},{9,8},{10,11... | collective-permute-start | bytes 196616 | tf_op jit(solution)/shard_map/ppermute | solution.py:46
  7.5 0.2 collective-permute-done.one_ref.args_3_
  7.6 2.0 %collective-permute-start.1 = (bf16[6,128,128]{2,1,0:T(8,128)(2,1)S(1)}, bf16[6,128,128]{2,1,0:T(8,128)(2,1)S(1)}, u32[]{:S(2)}, u32[]{:S(2)}) collective-permute-start(bf16[6,128,128]{2,1,0:T(8,128)(2,1)S(1)} %get-tuple-element.34), channel_id=1, source_target_pairs={{0,4},{4,0},{8,12},{12,8},{16,20},{20,16},{24,28},{28,24},{1,5},{5... | collective-permute-start | bytes 589832 | tf_op jit(solution)/shard_map/ppermute | solution.py:36
  9.6 0.5 %collective-permute-done.2.early2_ref.two_ref = bf16[2,128,128]{2,1,0:T(8,128)(2,1)S(1)} collective-permute-done((bf16[2,128,128]{2,1,0:T(8,128)(2,1)S(1)}, bf16[2,128,128]{2,1,0:T(8,128)(2,1)S(1)}, u32[]{:S(2)}, u32[]{:S(2)}) %collective-permute-start.2) | collective-permute-done | bytes 65568 | tf_op jit(solution)/shard_map/ppermute | solution.py:46
  10.2 2.0 %collective-permute-done.3.early3_ref.three_ref = bf16[2,128,128]{2,1,0:T(8,128)(2,1)S(1)} collective-permute-done((bf16[2,128,128]{2,1,0:T(8,128)(2,1)S(1)}, bf16[2,128,128]{2,1,0:T(8,128)(2,1)S(1)}, u32[]{:S(2)}, u32[]{:S(2)}) %collective-permute-start.3) | collective-permute-done | bytes 65568 | tf_op jit(solution)/shard_map/ppermute | solution.py:46
  12.2 0.0 copy-start.1
  12.3 0.1 collective-permute-start.8
  12.3 0.0 copy-done
  12.3 0.8 %copy-done.1 = f32[5,8,512]{2,1,0:T(8,128)S(1)} copy-done((f32[5,8,512]{2,1,0:T(8,128)S(1)}, f32[5,8,512]{2,1,0:T(8,128)}, u32[]{:S(2)}) %copy-start.1) | copy-done | bytes 81944
  13.1 1.9 %intra_second.1 = (f32[256,512]{1,0:T(8,128)S(1)}, f32[256,512]{1,0:T(8,128)S(1)}, f32[256,512]{1,0:T(8,128)S(1)}, f32[256,512]{1,0:T(8,128)S(1)}) custom-call(s32[1]{0:T(128)} %bitcast.place_ref.args_0_, bf16[512,1024]{1,0:T(8,128)(2,1)S(1)} %copy-done, f32[5,8,512]{2,1,0:T(8,128)S(1)} %copy-done.1, ...), custom_call_target="tpu_custom_call" | custom-call | flops 805306368 | bytes 2097152 | tf_op jit(solution)/shard_map/intra_second/pallas_call | solution.py:277
  15.0 0.0 collective-permute-done.4.late2_ref
  15.0 0.0 collective-permute-done.5.late3_ref
  15.1 0.9 %collective-permute-start.6 = (bf16[2,128,128]{2,1,0:T(8,128)(2,1)S(1)}, bf16[2,128,128]{2,1,0:T(8,128)(2,1)S(1)}, u32[]{:S(2)}, u32[]{:S(2)}) collective-permute-start(bf16[2,128,128]{2,1,0:T(8,128)(2,1)S(1)} %left.1.args_5_.left_ref), channel_id=1, source_target_pairs={{0,8},{4,12},{8,0},{12,4},{16,24},{20,28},{24,16},{28,20},{1,9},{5... | collective-permute-start | bytes 196616 | tf_op jit(solution)/shard_map/ppermute | solution.py:36
  16.0 2.1 %collective-permute-done.8.args_8_.top_ref = bf16[2,128,128]{2,1,0:T(8,128)(2,1)S(1)} collective-permute-done((bf16[2,128,128]{2,1,0:T(8,128)(2,1)S(1)}, bf16[2,128,128]{2,1,0:T(8,128)(2,1)S(1)}, u32[]{:S(2)}, u32[]{:S(2)}) %collective-permute-start.8) | collective-permute-done | bytes 65568 | tf_op jit(solution)/shard_map/ppermute | solution.py:36
  18.1 0.0 copy-start.2
  18.1 0.1 collective-permute-start.10
  18.2 0.6 %copy-done.2 = f32[1024]{0:T(1024)S(1)} copy-done((f32[1024]{0:T(1024)S(1)}, f32[1024]{0:T(1024)}, u32[]{:S(2)}) %copy-start.2) | copy-done | bytes 4120
  18.8 0.9 %collective-permute-start.7 = (bf16[2,128,128]{2,1,0:T(8,128)(2,1)S(1)}, bf16[2,128,128]{2,1,0:T(8,128)(2,1)S(1)}, u32[]{:S(2)}, u32[]{:S(2)}) collective-permute-start(bf16[2,128,128]{2,1,0:T(8,128)(2,1)S(1)} %left.1.args_5_.left_ref), channel_id=1, source_target_pairs={{0,12},{4,8},{8,4},{12,0},{16,28},{20,24},{24,20},{28,16},{1,13},{... | collective-permute-start | bytes 196616 | tf_op jit(solution)/shard_map/ppermute | solution.py:36
  19.6 0.0 collective-permute-start.9
  19.6 0.0 collective-permute-done.6.args_6_
  19.7 0.5 %collective-permute-start.11 = (bf16[2,128,128]{2,1,0:T(8,128)(2,1)S(1)}, bf16[2,128,128]{2,1,0:T(8,128)(2,1)S(1)}, u32[]{:S(2)}, u32[]{:S(2)}) collective-permute-start(bf16[2,128,128]{2,1,0:T(8,128)(2,1)S(1)} %collective-permute-done.8.args_8_.top_ref), channel_id=1, source_target_pairs={{0,1},{1,0},{2,3},{3,2},{4,5},{5,4},{6,7},{7,6},{8,9},{9,8},{10,11... | collective-permute-start | bytes 196616 | tf_op jit(solution)/shard_map/ppermute | solution.py:46
  20.2 0.3 %intra_last.1 = (f32[1024,128]{1,0:T(8,128)S(1)}, f32[256,512]{1,0:T(8,128)S(1)}, f32[256,512]{1,0:T(8,128)S(1)}, f32[256,512]{1,0:T(8,128)S(1)}, f32[256,512]{1,0:T(8,128)S(1)}) custom-call(s32[1]{0:T(128)} %bitcast.place_ref.args_0_, bf16[512,1024]{1,0:T(8,128)(2,1)S(1)} %copy-done, f32[5,8,512]{2,1,0:T(8,128)S(1)} %copy-done.1, ...), custom_call_target="tpu_custom_call" | custom-call | flops 805306368 | bytes 2097152 | tf_op jit(solution)/shard_map/intra_last/pallas_call | solution.py:324
  20.5 3.5 %collective-permute-done.7.args_7_ = bf16[2,128,128]{2,1,0:T(8,128)(2,1)S(1)} collective-permute-done((bf16[2,128,128]{2,1,0:T(8,128)(2,1)S(1)}, bf16[2,128,128]{2,1,0:T(8,128)(2,1)S(1)}, u32[]{:S(2)}, u32[]{:S(2)}) %collective-permute-start.7) | collective-permute-done | bytes 65568 | tf_op jit(solution)/shard_map/ppermute | solution.py:36
  24.0 0.0 collective-permute-done.1.args_4_
  24.0 0.3 %shard_map.55 = (f32[256,512]{1,0:T(8,128)S(1)}, f32[256,512]{1,0:T(8,128)S(1)}, f32[256,512]{1,0:T(8,128)S(1)}, f32[256,512]{1,0:T(8,128)S(1)}, f32[8,512]{1,0:T(8,128)S(1)}) custom-call(s32[1]{0:T(128)} %bitcast.place_ref.args_0_, bf16[512,1024]{1,0:T(8,128)(2,1)S(1)} %copy-done, f32[5,8,512]{2,1,0:T(8,128)S(1)} %copy-done.1, ...), custom_call_target="tpu_custom_call" | custom-call | flops 268435456 | bytes 4194304 | tf_op jit(solution)/shard_map/pallas_call | solution.py:349
  24.3 0.0 collective-permute-done.9.args_3_
  24.3 0.0 collective-permute-done.10.args_4_
  24.3 0.1 shard_map.56
  24.4 0.0 collective-permute-done.11.args_3_
  24.5 0.1 shard_map.57
  24.5 0.1 collective-permute-start.12
  24.6 1.6 %collective-permute-start.13 = (f32[1,512]{1,0:T(1,128)S(1)}, f32[1,512]{1,0:T(1,128)S(1)}, u32[]{:S(2)}, u32[]{:S(2)}) collective-permute-start(f32[1,512]{1,0:T(1,128)S(1)} %get-tuple-element.59.refs_4_), channel_id=1, source_target_pairs={{0,2},{1,3},{2,0},{3,1},{4,6},{5,7},{6,4},{7,5},{8,10},{9,11},{10,... | collective-permute-start | bytes 6152 | tf_op jit(solution)/shard_map/ppermute | solution.py:36
  26.2 0.3 collective-permute-start.14
  26.5 0.0 collective-permute-done.12.refs_5_
  26.5 1.8 %collective-permute-done.13.refs_6_ = f32[1,512]{1,0:T(1,128)S(1)} collective-permute-done((f32[1,512]{1,0:T(1,128)S(1)}, f32[1,512]{1,0:T(1,128)S(1)}, u32[]{:S(2)}, u32[]{:S(2)}) %collective-permute-start.13) | collective-permute-done | bytes 2080 | tf_op jit(solution)/shard_map/ppermute | solution.py:36
  28.3 0.9 %collective-permute-done.14.refs_7_ = f32[1,512]{1,0:T(1,128)S(1)} collective-permute-done((f32[1,512]{1,0:T(1,128)S(1)}, f32[1,512]{1,0:T(1,128)S(1)}, u32[]{:S(2)}, u32[]{:S(2)}) %collective-permute-start.14) | collective-permute-done | bytes 2080 | tf_op jit(solution)/shard_map/ppermute | solution.py:36
  29.2 1.1 %norm.1 = bf16[512,1024]{1,0:T(8,128)(2,1)} custom-call(s32[1]{0:T(128)} %bitcast.place_ref.args_0_, f32[256,512]{1,0:T(8,128)S(1)} %get-tuple-element.50.refs_0_, f32[256,512]{1,0:T(8,128)S(1)} %get-tuple-element.54.refs_1_, f32[256,512]{1,0:T(8,128)S(1)} %get-tuple-element.57.refs_2_, f32[256,512]{1,0:T(8,128)S(1)} %get-tuple-element.58.refs_3_, ...), custom_call_target="tpu_custom_call" | custom-call | flops 1048576 | bytes 1048576 | tf_op jit(solution)/shard_map/norm/pallas_call | solution.py:370
  (4 shorter events, 0.1 us)
Async XLA Ops:
  0.0 12.3 %copy-start = (bf16[512,1024]{1,0:T(8,128)(2,1)S(1)}, bf16[512,1024]{1,0:T(8,128)(2,1)}, u32[]{:S(2)}) copy-start(bf16[512,1024]{1,0:T(8,128)(2,1)} %args_1_.8) | copy-start | bytes 3145732
  2.3 5.3 %collective-permute-start = (bf16[2,128,128]{2,1,0:T(8,128)(2,1)S(1)}, bf16[2,128,128]{2,1,0:T(8,128)(2,1)S(1)}, u32[]{:S(2)}, u32[]{:S(2)}) collective-permute-start(bf16[2,128,128]{2,1,0:T(8,128)(2,1)S(1)} %get-tuple-element.33), channel_id=1, source_target_pairs={{0,4},{4,0},{8,12},{12,8},{16,20},{20,16},{24,28},{28,24},{1,5},{5... | collective-permute-start | bytes 196616 | tf_op jit(solution)/shard_map/ppermute | solution.py:36
  5.4 4.8 %collective-permute-start.2 = (bf16[2,128,128]{2,1,0:T(8,128)(2,1)S(1)}, bf16[2,128,128]{2,1,0:T(8,128)(2,1)S(1)}, u32[]{:S(2)}, u32[]{:S(2)}) collective-permute-start(bf16[2,128,128]{2,1,0:T(8,128)(2,1)S(1)} %get-tuple-element.36), channel_id=1, source_target_pairs={{0,8},{1,9},{2,10},{3,11},{4,12},{5,13},{6,14},{7,15},{8,0},{9,1},... | collective-permute-start | bytes 196616 | tf_op jit(solution)/shard_map/ppermute | solution.py:46
  6.9 5.3 %collective-permute-start.3 = (bf16[2,128,128]{2,1,0:T(8,128)(2,1)S(1)}, bf16[2,128,128]{2,1,0:T(8,128)(2,1)S(1)}, u32[]{:S(2)}, u32[]{:S(2)}) collective-permute-start(bf16[2,128,128]{2,1,0:T(8,128)(2,1)S(1)} %get-tuple-element.37), channel_id=1, source_target_pairs={{0,12},{1,13},{2,14},{3,15},{4,8},{5,9},{6,10},{7,11},{8,4},{9,5},... | collective-permute-start | bytes 196616 | tf_op jit(solution)/shard_map/ppermute | solution.py:46
  7.0 8.0 %collective-permute-start.4 = (bf16[2,128,128]{2,1,0:T(8,128)(2,1)S(1)}, bf16[2,128,128]{2,1,0:T(8,128)(2,1)S(1)}, u32[]{:S(2)}, u32[]{:S(2)}) collective-permute-start(bf16[2,128,128]{2,1,0:T(8,128)(2,1)S(1)} %get-tuple-element.36), channel_id=1, source_target_pairs={{0,1},{1,0},{2,3},{3,2},{4,5},{5,4},{6,7},{7,6},{8,9},{9,8},{10,11... | collective-permute-start | bytes 196616 | tf_op jit(solution)/shard_map/ppermute | solution.py:46
  7.0 8.1 %collective-permute-start.5 = (bf16[2,128,128]{2,1,0:T(8,128)(2,1)S(1)}, bf16[2,128,128]{2,1,0:T(8,128)(2,1)S(1)}, u32[]{:S(2)}, u32[]{:S(2)}) collective-permute-start(bf16[2,128,128]{2,1,0:T(8,128)(2,1)S(1)} %get-tuple-element.37), channel_id=1, source_target_pairs={{0,1},{1,0},{2,3},{3,2},{4,5},{5,4},{6,7},{7,6},{8,9},{9,8},{10,11... | collective-permute-start | bytes 196616 | tf_op jit(solution)/shard_map/ppermute | solution.py:46
  7.6 16.3 %collective-permute-start.1 = (bf16[6,128,128]{2,1,0:T(8,128)(2,1)S(1)}, bf16[6,128,128]{2,1,0:T(8,128)(2,1)S(1)}, u32[]{:S(2)}, u32[]{:S(2)}) collective-permute-start(bf16[6,128,128]{2,1,0:T(8,128)(2,1)S(1)} %get-tuple-element.34), channel_id=1, source_target_pairs={{0,4},{4,0},{8,12},{12,8},{16,20},{20,16},{24,28},{28,24},{1,5},{5... | collective-permute-start | bytes 589832 | tf_op jit(solution)/shard_map/ppermute | solution.py:36
  12.2 0.9 %copy-start.1 = (f32[5,8,512]{2,1,0:T(8,128)S(1)}, f32[5,8,512]{2,1,0:T(8,128)}, u32[]{:S(2)}) copy-start(f32[5,8,512]{2,1,0:T(8,128)} %args_2_.8) | copy-start | bytes 245764
  12.3 5.9 %collective-permute-start.8 = (bf16[2,128,128]{2,1,0:T(8,128)(2,1)S(1)}, bf16[2,128,128]{2,1,0:T(8,128)(2,1)S(1)}, u32[]{:S(2)}, u32[]{:S(2)}) collective-permute-start(bf16[2,128,128]{2,1,0:T(8,128)(2,1)S(1)} %sums.1), channel_id=1, source_target_pairs={{0,16},{4,20},{8,24},{12,28},{16,0},{20,4},{24,8},{28,12},{1,17},{... | collective-permute-start | bytes 196616 | tf_op jit(solution)/shard_map/ppermute | solution.py:36
  15.1 4.6 %collective-permute-start.6 = (bf16[2,128,128]{2,1,0:T(8,128)(2,1)S(1)}, bf16[2,128,128]{2,1,0:T(8,128)(2,1)S(1)}, u32[]{:S(2)}, u32[]{:S(2)}) collective-permute-start(bf16[2,128,128]{2,1,0:T(8,128)(2,1)S(1)} %left.1.args_5_.left_ref), channel_id=1, source_target_pairs={{0,8},{4,12},{8,0},{12,4},{16,24},{20,28},{24,16},{28,20},{1,9},{5... | collective-permute-start | bytes 196616 | tf_op jit(solution)/shard_map/ppermute | solution.py:36
  18.1 0.7 %copy-start.2 = (f32[1024]{0:T(1024)S(1)}, f32[1024]{0:T(1024)}, u32[]{:S(2)}) copy-start(f32[1024]{0:T(1024)} %param.9) | copy-start | bytes 12292
  18.1 6.2 %collective-permute-start.10 = (bf16[4,128,128]{2,1,0:T(8,128)(2,1)S(1)}, bf16[4,128,128]{2,1,0:T(8,128)(2,1)S(1)}, u32[]{:S(2)}, u32[]{:S(2)}) collective-permute-start(bf16[4,128,128]{2,1,0:T(8,128)(2,1)S(1)} %join.1), channel_id=1, source_target_pairs={{0,1},{1,0},{2,3},{3,2},{4,5},{5,4},{6,7},{7,6},{8,12},{9,13},{10,... | collective-permute-start | bytes 393224 | tf_op jit(solution)/shard_map/ppermute | solution.py:46
  18.8 5.2 %collective-permute-start.7 = (bf16[2,128,128]{2,1,0:T(8,128)(2,1)S(1)}, bf16[2,128,128]{2,1,0:T(8,128)(2,1)S(1)}, u32[]{:S(2)}, u32[]{:S(2)}) collective-permute-start(bf16[2,128,128]{2,1,0:T(8,128)(2,1)S(1)} %left.1.args_5_.left_ref), channel_id=1, source_target_pairs={{0,12},{4,8},{8,4},{12,0},{16,28},{20,24},{24,20},{28,16},{1,13},{... | collective-permute-start | bytes 196616 | tf_op jit(solution)/shard_map/ppermute | solution.py:36
  19.6 4.6 %collective-permute-start.9 = (bf16[2,128,128]{2,1,0:T(8,128)(2,1)S(1)}, bf16[2,128,128]{2,1,0:T(8,128)(2,1)S(1)}, u32[]{:S(2)}, u32[]{:S(2)}) collective-permute-start(bf16[2,128,128]{2,1,0:T(8,128)(2,1)S(1)} %collective-permute-done.8.args_8_.top_ref), channel_id=1, source_target_pairs={{0,1},{1,0},{2,3},{3,2},{4,5},{5,4},{6,7},{7,6},{8,9},{9,8},{10,11... | collective-permute-start | bytes 196616 | tf_op jit(solution)/shard_map/ppermute | solution.py:46
  19.7 4.8 %collective-permute-start.11 = (bf16[2,128,128]{2,1,0:T(8,128)(2,1)S(1)}, bf16[2,128,128]{2,1,0:T(8,128)(2,1)S(1)}, u32[]{:S(2)}, u32[]{:S(2)}) collective-permute-start(bf16[2,128,128]{2,1,0:T(8,128)(2,1)S(1)} %collective-permute-done.8.args_8_.top_ref), channel_id=1, source_target_pairs={{0,1},{1,0},{2,3},{3,2},{4,5},{5,4},{6,7},{7,6},{8,9},{9,8},{10,11... | collective-permute-start | bytes 196616 | tf_op jit(solution)/shard_map/ppermute | solution.py:46
  24.5 1.9 %collective-permute-start.12 = (f32[1,512]{1,0:T(1,128)S(1)}, f32[1,512]{1,0:T(1,128)S(1)}, u32[]{:S(2)}, u32[]{:S(2)}) collective-permute-start(f32[1,512]{1,0:T(1,128)S(1)} %get-tuple-element.59.refs_4_), channel_id=1, source_target_pairs={{0,1},{1,0},{2,3},{3,2},{4,5},{5,4},{6,7},{7,6},{8,9},{9,8},{10,11... | collective-permute-start | bytes 6152 | tf_op jit(solution)/shard_map/ppermute | solution.py:36
  24.6 3.7 %collective-permute-start.13 = (f32[1,512]{1,0:T(1,128)S(1)}, f32[1,512]{1,0:T(1,128)S(1)}, u32[]{:S(2)}, u32[]{:S(2)}) collective-permute-start(f32[1,512]{1,0:T(1,128)S(1)} %get-tuple-element.59.refs_4_), channel_id=1, source_target_pairs={{0,2},{1,3},{2,0},{3,1},{4,6},{5,7},{6,4},{7,5},{8,10},{9,11},{10,... | collective-permute-start | bytes 6152 | tf_op jit(solution)/shard_map/ppermute | solution.py:36
  26.2 3.0 %collective-permute-start.14 = (f32[1,512]{1,0:T(1,128)S(1)}, f32[1,512]{1,0:T(1,128)S(1)}, u32[]{:S(2)}, u32[]{:S(2)}) collective-permute-start(f32[1,512]{1,0:T(1,128)S(1)} %get-tuple-element.59.refs_4_), channel_id=1, source_target_pairs={{0,3},{1,2},{2,1},{3,0},{4,7},{5,6},{6,5},{7,4},{8,11},{9,10},{10,... | collective-permute-start | bytes 6152 | tf_op jit(solution)/shard_map/ppermute | solution.py:36
